TPU v7x, 128 devices: a whole 4x4x4 slice. The times are simulated.
128 devices in a mesh: dp: 2 (over core), section: 4 (over z), depth: 16 (over y, x).
Axes of the slice: x: 4, y: 4, z: 4, core: 2. Of those that a mesh axis runs over, the one named last changes fastest.
Arguments:
- volume: bfloat16 [2, 32, 32, 32, 128], P('dp', 'depth'), may hold values from -6 to 6
- weights: bfloat16 [4, 3456, 128], P('section'), may hold values from -0.15625 to 0.15625
- biases: bfloat16 [4, 128], P('section'), may hold values from -3 to 3
- cotangent: bfloat16 [2, 32, 32, 32, 128], P('dp', 'depth'), may hold values from -6 to 6
Outputs:
- section_outputs: bfloat16 [4, 2, 32, 32, 32, 128], P('section', 'dp', 'depth')
- input_grads: bfloat16 [4, 2, 32, 32, 32, 128], P('section', 'dp', 'depth')
- weight_grads: float32 [4, 3456, 128], P('section')
- bias_grads: float32 [4, 128], P('section')
All inputs are finite; a program needn't handle non-finite values.
Results may differ from a plain program's by a relative error of at most 0.025.
Values may be sent and summed in bfloat16 or wider, within the bound.
No kernel may reach another device: no remote copies, remote signals or barrier semaphores. Data moves between devices by JAX's collectives and lax.ppermute only.
A program may use at most 128 MiB of HBM per device.

v0:
```python
import math

import jax
import jax.numpy as jnp
from jax import lax
from jax.experimental import pallas as pl
from jax.experimental.pallas import tpu as pltpu
from jax.sharding import PartitionSpec as P


BF = jnp.bfloat16
F32 = jnp.float32

SMEM = pl.BlockSpec(memory_space=pltpu.SMEM)
VMEM = pl.BlockSpec(memory_space=pltpu.VMEM)
ANY = pl.BlockSpec(memory_space=pl.ANY)


def sds(shape, dtype=BF):
    return jax.ShapeDtypeStruct(shape, dtype)


def call(body, out, n_any_or_specs, scratch, out_specs=None, vmem=20):
    return pl.pallas_call(
        body,
        grid=(1,),
        out_shape=out,
        in_specs=n_any_or_specs,
        out_specs=out_specs if out_specs is not None else jax.tree.map(lambda _: VMEM, out),
        scratch_shapes=scratch,
        compiler_params=pltpu.CompilerParams(vmem_limit_bytes=vmem * 1024 * 1024),
    )


def column(w_ref, t, C=128):
    return jnp.concatenate(
        [
            jnp.concatenate([w_ref[t, (3 * k + c) * C : (3 * k + c + 1) * C] for c in range(3)], axis=1)
            for k in range(9)
        ],
        axis=0,
    )


def conv_plane(x_ref, p, wide, nr):
    W, C = x_ref.shape[2], x_ref.shape[3]
    m = nr * W
    lhs = jnp.concatenate(
        [x_ref[p + a, b : b + nr].reshape(m, C) for a in range(3) for b in range(3)], axis=1
    )
    y = jnp.dot(lhs, wide, preferred_element_type=F32)
    x_pos = lax.broadcasted_iota(jnp.int32, (m, C), 0) % W
    left = jnp.where(x_pos == 0, 0.0, pltpu.roll(y[:, :C], 1, 0))
    right = jnp.where(x_pos == W - 1, 0.0, pltpu.roll(y[:, 2 * C :], m - 1, 0))
    return y[:, C : 2 * C] + left + right


def inside(nr, W, C, first_row, H, plane, D):
    row = first_row + lax.broadcasted_iota(jnp.int32, (nr * W, C), 0) // W
    return (row >= 0) & (row < H) & (plane >= 0) & (plane < D)


def slope(pre):
    q = jax.nn.sigmoid(pre)
    return q * (1.0 + pre * (1.0 - q))


def assemble(dst, lo, own, hi, d, last):
    zero = jnp.zeros(lo.shape, BF)
    dst[0:2] = jnp.where(d > 0, lo[...], zero)
    dst[2:4] = own[...]
    dst[4:6] = jnp.where(d < last, hi[...], zero)


def halves(s, c, t, own, got, swp, dst, sem, half):
    mine = pl.multiple_of(c * half, 16)
    other = pl.multiple_of((1 - c) * half, 16)
    k = (s + 4 - t) % 4

    def pair(first, second):
        return (
            pltpu.make_async_copy(first, dst.at[pl.ds(mine, half)], sem.at[0]),
            pltpu.make_async_copy(second, dst.at[pl.ds(other, half)], sem.at[1]),
        )

    def start():
        @pl.when(k == 0)
        def _():
            for cp in pair(own.at[pl.ds(mine, half)], own.at[pl.ds(other, half)]):
                cp.start()

        for i in range(3):

            @pl.when(k == i + 1)
            def _():
                for cp in pair(got[i].at[pl.ds(0, half)], swp[i].at[pl.ds(0, half)]):
                    cp.start()

    def wait():
        for cp in pair(own.at[pl.ds(mine, half)], own.at[pl.ds(other, half)]):
            cp.wait()

    return start, wait


def bias_of(s, t, own_bias, got_bias):
    k = (s + 4 - t) % 4
    row = own_bias[...].astype(F32)
    for i in range(3):
        row = jnp.where(k == i + 1, got_bias[i][0:1].astype(F32), row)
    return row


def shards(volume, weights, biases, cotangent):
    n_sec = lax.axis_size("section")
    n_dep = lax.axis_size("depth")
    n_dp = lax.axis_size("dp")
    s = lax.axis_index("section")
    d = lax.axis_index("depth")
    c = lax.axis_index("dp")
    assert n_sec == 4 and n_dep == 16 and n_dp == 2
    PL, H, W, C = volume.shape[1:]
    assert PL == 2
    R = H // n_sec
    D = PL * n_dep
    last = n_dep - 1
    grad_scale = 1.0 / math.sqrt(n_dp * D * H * W)
    idx = jnp.stack([s, d, c]).astype(jnp.int32)
    TAP = 27 * C
    HALF = TAP // 2
    HB = HALF + 16

    def sec(v, k):
        return lax.ppermute(v, "section", [(i, (i + k) % n_sec) for i in range(n_sec)])

    def dep(v, k):
        return lax.ppermute(v, "depth", [(i, (i + k) % n_dep) for i in range(n_dep)])

    def swap(v):
        return lax.ppermute(v, "dp", [(0, 1), (1, 0)])

    def xdep(v, k):
        return lax.ppermute(v, "depth", [(i, i // 4 * 4 + (i + k) % 4) for i in range(n_dep)])

    def ydep(v, k):
        return lax.ppermute(v, "depth", [(i, (i + 4 * k) % n_dep) for i in range(n_dep)])

    def window(v, ext):
        padded = jnp.pad(v, ((0, 0), (ext, ext), (0, 0), (0, 0)))
        return lax.dynamic_slice_in_dim(padded, s * R, R + 2 * ext, 1)

    h0 = window(volume[0], 8)
    h0_lo, h0_hi = dep(h0, 1), dep(h0, -1)

    own_w = weights[0]

    def prepare(idx, w, b, out):
        out[0:HALF] = w[idx[2]]
        out[HALF:] = jnp.broadcast_to(b[...], (16, C))

    own_half = call(prepare, sds((HB, C)), [SMEM, VMEM, VMEM], [], VMEM)(idx, own_w.reshape(2, HALF, C), biases)
    got = [sec(own_half, k) for k in (1, 3, 2)]
    got = [got[0], got[2], got[1]]
    swapped = [swap(g) for g in got]
    all_w = (own_w, *got, *swapped)
    W_SPECS = [ANY] * 7
    got_b = tuple(g[HALF:] for g in got)
    all_b = (biases, *got_b)

    cot = window(cotangent[0], 4)

    def turn(idx, own, g1, g2, g3, s1, s2, s3, out, buf, sem):
        steps = [
            halves(idx[0], idx[2], t, own, (g1, g2, g3), (s1, s2, s3), buf.at[t], sem.at[t], HALF) for t in range(4)
        ]
        for start, _ in steps:
            start()
        for t in (3, 2, 1, 0):
            steps[t][1]()

            def one(j, _):
                out[t, pl.ds(pl.multiple_of(j * C, C), C)] = buf[t, pl.ds(pl.multiple_of((26 - j) * C, C), C)].T
                return 0

            lax.fori_loop(0, 27, one, 0, unroll=3)

    def k1(idx, own, lo, hi, ow, g1, g2, g3, s1, s2, s3, ob, b1_, b2_, b3_, h0e, pre0, h1e, pre1, h2, x, h1, w, sem):
        s_, d_ = idx[0], idx[1]
        steps = [
            halves(s_, idx[2], t, ow, (g1, g2, g3), (s1, s2, s3), w.at[t], sem.at[t], HALF) for t in range(2)
        ]
        for start, _ in steps:
            start()
        assemble(x, lo, own, hi, d_, last)
        h0e[...] = x[1:5, 8 : 8 + R]
        steps[0][1]()
        wide = column(w, 0)
        b0 = bias_of(s_, 0, ob, (b1_, b2_, b3_))

        def one(p, _):
            pre = conv_plane(x, p, wide, R + 14) + b0
            h = jnp.where(inside(R + 14, W, C, s_ * R - 7, H, 2 * d_ - 1 + p, D), pre * jax.nn.sigmoid(pre), 0.0)
            h = h.astype(BF).reshape(R + 14, W, C)
            h1[p] = h
            h1e[p] = h[7 : 7 + R]
            pre0[p] = pre[6 * W : (16 + 0) * W].astype(BF).reshape(R + 2, W, C)
            return 0

        lax.fori_loop(0, 4, one, 0)
        steps[1][1]()
        wide1 = column(w, 1)
        b1 = bias_of(s_, 1, ob, (b1_, b2_, b3_))

        def two(p, _):
            pre = conv_plane(h1, p, wide1, R + 12) + b1
            h = jnp.where(inside(R + 12, W, C, s_ * R - 6, H, 2 * d_ + p, D), pre * jax.nn.sigmoid(pre), 0.0)
            h2[p] = h.astype(BF).reshape(R + 12, W, C)
            pre1[p] = pre[4 * W : 16 * W].astype(BF).reshape(R + 4, W, C)
            return 0

        lax.fori_loop(0, 2, two, 0)

    h0e, pre0, h1e, pre1, h2 = call(
        k1,
        (
            sds((4, R, W, C)),
            sds((4, R + 2, W, C)),
            sds((4, R, W, C)),
            sds((2, R + 4, W, C)),
            sds((2, R + 12, W, C)),
        ),
        [SMEM, VMEM, VMEM, VMEM] + W_SPECS + [VMEM] * 4,
        [
            pltpu.VMEM((6, R + 16, W, C), BF),
            pltpu.VMEM((4, R + 14, W, C), BF),
            pltpu.VMEM((2, TAP, C), BF),
            pltpu.SemaphoreType.DMA((2, 2)),
        ],
    )(idx, h0, h0_lo, h0_hi, *all_w, *all_b)

    h2_lo, h2_hi = dep(h2, 1), dep(h2, -1)

    wturn = call(
        turn, sds((4, TAP, C)), [SMEM] + W_SPECS, [pltpu.VMEM((4, TAP, C), BF), pltpu.SemaphoreType.DMA((4, 2))], VMEM
    )(idx, *all_w)
    h2_lo, h2_hi, wturn = lax.optimization_barrier((h2_lo, h2_hi, wturn))

    def k2(idx, own, lo, hi, ow, g1, g2, g3, s1, s2, s3, ob, b1_, b2_, b3_, cot, h2e, pre2, h3e, h4, d3, x, h3, w, sem):
        s_, d_ = idx[0], idx[1]
        steps = [
            halves(s_, idx[2], t + 2, ow, (g1, g2, g3), (s1, s2, s3), w.at[t], sem.at[t], HALF) for t in range(2)
        ]
        for start, _ in steps:
            start()
        assemble(x, lo, own, hi, d_, last)
        h2e[...] = x[1:5, 6 : 6 + R]
        steps[0][1]()
        wide = column(w, 0)
        b0 = bias_of(s_, 2, ob, (b1_, b2_, b3_))

        def one(p, _):
            pre = conv_plane(x, p, wide, R + 10) + b0
            h = jnp.where(inside(R + 10, W, C, s_ * R - 5, H, 2 * d_ - 1 + p, D), pre * jax.nn.sigmoid(pre), 0.0)
            h = h.astype(BF).reshape(R + 10, W, C)
            h3[p] = h
            h3e[p] = h[5 : 5 + R]
            pre2[p] = pre[2 * W : 16 * W].astype(BF).reshape(R + 6, W, C)
            return 0

        lax.fori_loop(0, 4, one, 0)
        steps[1][1]()
        wide1 = column(w, 1)
        b1 = bias_of(s_, 3, ob, (b1_, b2_, b3_))

        def two(p, _):
            pre = conv_plane(h3, p, wide1, R + 8) + b1
            h = (pre * jax.nn.sigmoid(pre)).astype(BF).reshape(R + 8, W, C)
            h4[p] = h[4 : 4 + R]
            g = cot[p].reshape((R + 8) * W, C).astype(F32)
            dl = g * slope(pre.astype(BF).astype(F32))
            dl = jnp.where(inside(R + 8, W, C, s_ * R - 4, H, 2 * d_ + p, D), dl, 0.0)
            d3[p] = dl.astype(BF).reshape(R + 8, W, C)
            return 0

        lax.fori_loop(0, 2, two, 0)

    h2e, pre2, h3e, h4, d3 = call(
        k2,
        (
            sds((4, R, W, C)),
            sds((4, R + 6, W, C)),
            sds((4, R, W, C)),
            sds((2, R, W, C)),
            sds((2, R + 8, W, C)),
        ),
        [SMEM, VMEM, VMEM, VMEM] + W_SPECS + [VMEM] * 5,
        [
            pltpu.VMEM((6, R + 12, W, C), BF),
            pltpu.VMEM((4, R + 10, W, C), BF),
            pltpu.VMEM((2, TAP, C), BF),
            pltpu.SemaphoreType.DMA((2, 2)),
        ],
    )(idx, h2, h2_lo, h2_hi, *all_w, *all_b, cot)

    d3_lo, d3_hi = dep(d3, 1), dep(d3, -1)

    def pack(idx, x0, x1, x2, x3, x4, own, a1, a2, a3):
        xs = (x0, x1, x2, x3)
        for k, out in enumerate((own, a1, a2, a3)):
            for t in range(4):

                @pl.when((idx[0] + k) % 4 == t)
                def _():
                    out[0:4] = xs[t][...]
                    out[4:6] = x4[...] if t == 3 else xs[t + 1][1:3]

    six = sds((6, R, W, C))
    h_own, *h_send = call(pack, (six,) * 4, [SMEM] + [VMEM] * 5, [])(idx, h0e, h1e, h2e, h3e, h4)
    h_got = [sec(h_send[k - 1], k) for k in (1, 2, 3)]

    def backward_pair(e0, final_delta):
        n1, n2 = R + 2 * e0 - 2, R + 2 * e0 - 4

        def body(idx, own, lo, hi, w, pre_a, *rest):
            if final_delta:
                pre_b, ga, da, gb, db, x, dbuf = rest
            else:
                d1_, d2_, d3_, g2_, g3_, *sends, ga, da, gb, x, dbuf = rest
            s_, d_ = idx[0], idx[1]
            assemble(x, lo, own, hi, d_, last)
            wide = column(w, 1)

            def one(p, _):
                g = conv_plane(x, p, wide, n1).astype(BF)
                dl = g.astype(F32) * slope(pre_a[p].reshape(n1 * W, C).astype(F32))
                dl = jnp.where(inside(n1, W, C, s_ * R - e0 + 1, H, 2 * d_ - 1 + p, D), dl, 0.0)
                dl = dl.astype(BF).reshape(n1, W, C)
                dbuf[p] = dl
                gr = g.reshape(n1, W, C)

                @pl.when((p > 0) & (p < 3))
                def _():
                    ga[p - 1] = gr[e0 - 1 : e0 - 1 + R]
                    da[p - 1] = dl[e0 - 1 : e0 - 1 + R]

                return 0

            lax.fori_loop(0, 4, one, 0)
            wide1 = column(w, 0)

            def two(p, _):
                g = conv_plane(dbuf, p, wide1, n2).astype(BF)
                gr = g.reshape(n2, W, C)
                gb[p] = gr[e0 - 2 : e0 - 2 + R]
                if final_delta:
                    dl = g.astype(F32) * slope(pre_b[p].reshape(n2 * W, C).astype(F32))
                    dl = jnp.where(inside(n2, W, C, s_ * R - e0 + 2, H, 2 * d_ + p, D), dl, 0.0)
                    db[p] = dl.astype(BF).reshape(n2, W, C)
                return 0

            lax.fori_loop(0, 2, two, 0)
            if not final_delta:
                ds = (da[...], d1_[:, 2 : 2 + R], d2_[...], d3_[:, 4 : 4 + R])
                gs = (gb[...], ga[...], g2_[...], g3_[...])
                for k in range(4):
                    for t in range(4):

                        @pl.when((s_ + k) % 4 == t)
                        def _():
                            sends[k][...] = ds[t]
                            sends[4 + k][...] = gs[t]

        piece = sds((2, R, W, C))
        out = (piece, piece, piece, sds((2, n2, W, C))) if final_delta else (piece,) * 8
        held = [] if final_delta else [pltpu.VMEM(piece.shape, BF)] * 3
        return call(
            body,
            out,
            [SMEM, VMEM, VMEM, VMEM, pl.BlockSpec((2, TAP, C), lambda _: (1 if final_delta else 0, 0, 0)), VMEM]
            + [VMEM] * (1 if final_delta else 5),
            held + [pltpu.VMEM((6, R + 2 * e0, W, C), BF), pltpu.VMEM((4, n1, W, C), BF)],
        )

    g3, d2, g2, d1 = backward_pair(4, True)(idx, d3, d3_lo, d3_hi, wturn, pre2, pre1)
    d1_lo, d1_hi = dep(d1, 1), dep(d1, -1)
    sends = backward_pair(2, False)(idx, d1, d1_lo, d1_hi, wturn, pre0, d1, d2, d3, g2, g3)
    d_got = [sec(sends[k], k) for k in (1, 2, 3)]
    g_got = [sec(sends[4 + k], k) for k in (1, 2, 3)]

    ROWS = TAP + C

    def kw(idx, x0, x1, x2, x3, e0, e1, e2, e3, keep, away, x, dl, wide, out):
        s_ = idx[0]
        x[:, 0] = jnp.zeros((4, W, C), BF)
        x[:, H + 1] = jnp.zeros((4, W, C), BF)
        for k, (xs, es) in enumerate(((x0, e0), (x1, e1), (x2, e2), (x3, e3))):
            row = ((s_ + 4 - k) % 4) * R
            x[:, pl.ds(row + 1, R)] = xs[0:4]
            dl[:, pl.ds(row, R)] = es[...]
        acc_b = jnp.zeros((1, C), F32)
        m = H * W
        pos = lax.broadcasted_iota(jnp.int32, (m, C), 0) % W
        for p in range(2):
            v = dl[p].reshape(m, C).astype(F32)
            acc_b = acc_b + jnp.sum(v, axis=0, keepdims=True)
            wide[p, :, 0:C] = jnp.where(pos == W - 1, 0.0, pltpu.roll(v, m - 1, 0)).astype(BF)
            wide[p, :, C : 2 * C] = dl[p].reshape(m, C)
            wide[p, :, 2 * C :] = jnp.where(pos == 0, 0.0, pltpu.roll(v, 1, 0)).astype(BF)

        def one(k, _):
            a, b = k // 3, k % 3
            acc = jnp.zeros((C, 3 * C), F32)
            for p in range(2):
                acc = acc + lax.dot_general(
                    x[p + a, pl.ds(b, H)].reshape(m, C),
                    wide[p],
                    (((0,), (0,)), ((), ())),
                    preferred_element_type=F32,
                )
            for j in range(3):
                out[3 * k + j] = acc[:, j * C : (j + 1) * C]
            return 0

        lax.fori_loop(0, 9, one, 0)
        first = lax.broadcasted_iota(jnp.int32, (C, C), 0) == 0
        out[27] = jnp.where(first, jnp.broadcast_to(acc_b, (C, C)), 0.0)
        keep[...] = out[pl.ds(idx[2] * 14, 14)].reshape(RH, C)
        away[...] = out[pl.ds((1 - idx[2]) * 14, 14)].reshape(RH, C).astype(BF)

    RH, RQ = ROWS // 2, ROWS // 8
    keep, away = call(
        kw,
        (sds((RH, C), F32), sds((RH, C))),
        [SMEM] + [VMEM] * 8,
        [
            pltpu.VMEM((4, H + 2, W, C), BF),
            pltpu.VMEM((2, H, W, C), BF),
            pltpu.VMEM((2, H * W, 3 * C), BF),
            pltpu.VMEM((28, C, C), F32),
        ],
    )(idx, h_own, *h_got, sends[0], *d_got)

    recv = swap(away)

    def split(idx, keep, recv, mine, q1, q2, q3, buf):
        x = idx[1] % 4
        buf[...] = keep[...].reshape(4, RQ, C) + recv[...].reshape(4, RQ, C).astype(F32)
        mine[...] = buf[x]
        for k, q in enumerate((q1, q2, q3), 1):
            q[...] = buf[(x + k) % 4].astype(BF)

    quart = sds((RQ, C))
    q, *qs = call(
        split, (sds((RQ, C), F32), quart, quart, quart), [SMEM, VMEM, VMEM], [pltpu.VMEM((4, RQ, C), F32)]
    )(idx, keep, recv)
    xs = [xdep(qs[k - 1], k) for k in (1, 2, 3)]
    for v in xs:
        q = q + v.astype(F32)
    q = q.astype(BF)
    ys = [ydep(q, k) for k in (1, 2, 3)]

    def ordered(idx, q0, q1, q2, q3, out, buf):
        y = idx[1] // 4
        for k, r in enumerate((q0, q1, q2, q3)):
            buf[k] = r[...].astype(F32)
        acc = buf[y % 4]
        for j in range(1, 4):
            acc = acc + buf[(y + 4 - j) % 4]
        out[...] = acc.astype(BF)

    q = call(ordered, sds((RQ, C)), [SMEM] + [VMEM] * 4, [pltpu.VMEM((4, RQ, C), F32)], VMEM)(idx, q, *ys)
    qs = [q] + [xdep(q, k) for k in (1, 2, 3)]

    def join(idx, q0, q1, q2, q3, out):
        x = idx[1] % 4
        for k, r in enumerate((q0, q1, q2, q3)):
            out[(x + 4 - k) % 4] = r[...]

    half = call(join, sds((4, RQ, C)), [SMEM] + [VMEM] * 4, [], VMEM)(idx, *qs)
    other = swap(half)

    def finish(idx, mine, theirs, w_out, b_out, buf):
        buf[idx[2]] = mine[...].reshape(RH, C)
        buf[1 - idx[2]] = theirs[...].reshape(RH, C)
        w_out[0:RH] = buf[0].astype(F32) * grad_scale
        w_out[RH:] = buf[1, 0 : TAP - RH].astype(F32) * grad_scale
        b_out[...] = buf[1, TAP - RH : TAP - RH + 8].astype(F32) * grad_scale

    w_grad, b_grad = call(
        finish, (sds((TAP, C), F32), sds((8, C), F32)), [SMEM, VMEM, VMEM], [pltpu.VMEM((2, RH, C), BF)]
    )(idx, half, other)

    def place(idx, a0, a1, a2, a3, b0, b1, b2, b3, oa, ob, sem):
        copies = []
        for k, (va, vb) in enumerate(((a0, b0), (a1, b1), (a2, b2), (a3, b3))):
            row = ((idx[0] + 4 - k) % 4) * R
            copies.append(pltpu.make_async_copy(va.at[4:6], oa.at[:, pl.ds(row, R)], sem.at[2 * k]))
            copies.append(pltpu.make_async_copy(vb, ob.at[:, pl.ds(row, R)], sem.at[2 * k + 1]))
        for cp in copies:
            cp.start()
        for cp in copies:
            cp.wait()

    full = sds((2, H, W, C))
    out_h, out_g = call(
        place, (full, full), [SMEM] + [ANY] * 8, [pltpu.SemaphoreType.DMA((8,))], (ANY, ANY)
    )(idx, h_own, *h_got, sends[4], *g_got)
    return out_h[None, None], out_g[None, None], w_grad[None], b_grad[0:1]


def solution(mesh):
    in_specs = (
        P("dp", "depth", None, None, None),
        P("section", None, None),
        P("section", None),
        P("dp", "depth", None, None, None),
    )
    out_specs = (
        P("section", "dp", "depth", None, None, None),
        P("section", "dp", "depth", None, None, None),
        P("section", None, None),
        P("section", None),
    )

    return jax.shard_map(shards, mesh=mesh, in_specs=in_specs, out_specs=out_specs, check_vma=False)
```

profile of v0, /device:TPU:1, one launch (start us, length us, event | category | flops | bytes accessed | tf_op | source)
XLA Modules:
  0.0 180.2 jit_solution(6957085701289185214)
XLA Ops:
  0.7 1.2 copy-done
  2.5 1.3 shard_map.75
  3.9 4.6 %collective-permute-start.4 = (bf16[1744,128]{1,0:T(8,128)(2,1)}, bf16[1744,128]{1,0:T(8,128)(2,1)S(1)}, u32[]{:S(2)}, u32[]{:S(2)}) collective-permute-start(bf16[1744,128]{1,0:T(8,128)(2,1)} %shard_map.75), channel_id=1, source_target_pairs={{0,48},{16,0},{32,16},{48,32},{1,49},{17,1},{33,17},{49,33},{2,50}... | collective-permute-start | bytes 1339400 | tf_op jit(solution)/shard_map/ppermute | solution.py:134
  9.2 18.0 %collective-permute-done.4.g3 = bf16[1744,128]{1,0:T(8,128)(2,1)S(1)} collective-permute-done((bf16[1744,128]{1,0:T(8,128)(2,1)}, bf16[1744,128]{1,0:T(8,128)(2,1)S(1)}, u32[]{:S(2)}, u32[]{:S(2)}) %collective-permute-start.4) | collective-permute-done | bytes 446496 | tf_op jit(solution)/shard_map/ppermute | solution.py:134
  27.1 1.7 collective-permute-start.7
  28.8 2.5 %collective-permute-done.2.g1 = bf16[1744,128]{1,0:T(8,128)(2,1)S(1)} collective-permute-done((bf16[1744,128]{1,0:T(8,128)(2,1)}, bf16[1744,128]{1,0:T(8,128)(2,1)S(1)}, u32[]{:S(2)}, u32[]{:S(2)}) %collective-permute-start.2) | collective-permute-done | bytes 446496 | tf_op jit(solution)/shard_map/ppermute | solution.py:134
  32.1 1.0 pad_dynamic-slice_fusion.own
  33.1 5.0 %collective-permute-start.1 = (bf16[2,24,32,128]{3,2,1,0:T(8,128)(2,1)S(1)}, bf16[2,24,32,128]{3,2,1,0:T(8,128)(2,1)S(1)}, u32[]{:S(2)}, u32[]{:S(2)}) collective-permute-start(bf16[2,24,32,128]{3,2,1,0:T(8,128)(2,1)S(1)} %pad_dynamic-slice_fusion.own), channel_id=1, source_target_pairs={{0,15},{1,0},{2,1},{3,2},{4,3},{5,4},{6,5},{7,6},{8,7},{9,8},{10,9... | collective-permute-start | bytes 1179656 | tf_op jit(solution)/shard_map/ppermute | solution.py:137
  38.1 8.5 %collective-permute-done.1.hi = bf16[2,24,32,128]{3,2,1,0:T(8,128)(2,1)S(1)} collective-permute-done((bf16[2,24,32,128]{3,2,1,0:T(8,128)(2,1)S(1)}, bf16[2,24,32,128]{3,2,1,0:T(8,128)(2,1)S(1)}, u32[]{:S(2)}, u32[]{:S(2)}) %collective-permute-start.1) | collective-permute-done | bytes 393248 | tf_op jit(solution)/shard_map/ppermute | solution.py:137
  46.6 5.2 %collective-permute-done.lo = bf16[2,24,32,128]{3,2,1,0:T(8,128)(2,1)S(1)} collective-permute-done((bf16[2,24,32,128]{3,2,1,0:T(8,128)(2,1)S(1)}, bf16[2,24,32,128]{3,2,1,0:T(8,128)(2,1)S(1)}, u32[]{:S(2)}, u32[]{:S(2)}) %collective-permute-start) | collective-permute-done | bytes 393248 | tf_op jit(solution)/shard_map/ppermute | solution.py:137
  51.9 1.3 copy-done.1
  53.9 8.8 %shard_map.76 = (bf16[4,8,32,128]{3,2,1,0:T(8,128)(2,1)S(1)}, bf16[4,10,32,128]{3,2,1,0:T(8,128)(2,1)S(1)}, bf16[4,8,32,128]{3,2,1,0:T(8,128)(2,1)S(1)}, bf16[2,...) custom-call(s32[3]{0:T(128)S(1)} %pad_add_fusion.idx, bf16[2,24,32,128]{3,2,1,0:T(8,128)(2,1)S(1)} %pad_dynamic-slice_fusion.own, ...), custom_call_target="tpu_custom_call" | custom-call | tf_op jit(solution)/shard_map/pallas_call | solution.py:223
  65.8 1.2 collective-permute-start.8
  67.0 1.0 pad_dynamic-slice_fusion.1.cot
  68.0 1.0 copy-done.4
  69.0 5.9 %shard_map.77.w = bf16[4,3456,128]{2,1,0:T(8,128)(2,1)S(1)} custom-call(s32[3]{0:T(128)S(1)} %pad_add_fusion.idx, bf16[3456,128]{1,0:T(8,128)(2,1)S(1)} %bitcast.12, bf16[1744,128]{1,0:T(8,128)(2,1)S(1)} %collective-permute-done.2.g1, bf16[1744,128]{1,0:T(8,128)(2,1)S(1)} %collective-permute-done.3.g2, bf16[1744,128]{1,0:T(8,128)(2,1)S(1)} %collective-permute-done.4.g3, ...), custom_call_target="tpu_custom_call" | custom-call | tf_op jit(solution)/shard_map/pallas_call | solution.py:243
  74.9 2.5 %collective-permute-done.8.lo = bf16[2,20,32,128]{3,2,1,0:T(8,128)(2,1)} collective-permute-done((bf16[2,20,32,128]{3,2,1,0:T(8,128)(2,1)S(1)}, bf16[2,20,32,128]{3,2,1,0:T(8,128)(2,1)}, u32[]{:S(2)}, u32[]{:S(2)}) %collective-permute-start.8) | collective-permute-done | bytes 327712 | tf_op jit(solution)/shard_map/ppermute | solution.py:137
  77.4 8.4 %shard_map.78 = (bf16[4,8,32,128]{3,2,1,0:T(8,128)(2,1)S(1)}, bf16[4,14,32,128]{3,2,1,0:T(8,128)(2,1)S(1)}, bf16[4,8,32,128]{3,2,1,0:T(8,128)(2,1)S(1)}, bf16[2,...) custom-call(s32[3]{0:T(128)S(1)} %pad_add_fusion.idx, bf16[2,20,32,128]{3,2,1,0:T(8,128)(2,1)S(1)} %get-tuple-element.45.own, ...), custom_call_target="tpu_custom_call" | custom-call | tf_op jit(solution)/shard_map/pallas_call | solution.py:287
  85.8 1.3 collective-permute-start.14
  88.2 1.8 collective-permute-start.11
  90.0 0.9 collective-permute-start.12
  91.7 4.8 %collective-permute-done.13.lo = bf16[2,16,32,128]{3,2,1,0:T(8,128)(2,1)S(1)} collective-permute-done((bf16[2,16,32,128]{3,2,1,0:T(8,128)(2,1)S(1)}, bf16[2,16,32,128]{3,2,1,0:T(8,128)(2,1)S(1)}, u32[]{:S(2)}, u32[]{:S(2)}) %collective-permute-start.13) | collective-permute-done | bytes 262176 | tf_op jit(solution)/shard_map/ppermute | solution.py:137
  96.6 5.5 %shard_map.80 = (bf16[2,8,32,128]{3,2,1,0:T(8,128)(2,1)S(1)}, bf16[2,8,32,128]{3,2,1,0:T(8,128)(2,1)S(1)}, bf16[2,8,32,128]{3,2,1,0:T(8,128)(2,1)S(1)}, bf16[2,12,32,128]{3,2,1,0:T(8,128)(2,1)S(1)}) custom-call(s32[3]{0:T(128)S(1)} %pad_add_fusion.idx, bf16[2,16,32,128]{3,2,1,0:T(8,128)(2,1)S(1)} %get-tuple-element.55.own.rest_2_, ...), custom_call_target="tpu_custom_call" | custom-call | tf_op jit(solution)/shard_map/pallas_call | solution.py:384
  102.5 1.2 collective-permute-start.15
  103.7 3.3 %collective-permute-done.16.hi = bf16[2,12,32,128]{3,2,1,0:T(8,128)(2,1)S(1)} collective-permute-done((bf16[2,12,32,128]{3,2,1,0:T(8,128)(2,1)S(1)}, bf16[2,12,32,128]{3,2,1,0:T(8,128)(2,1)S(1)}, u32[]{:S(2)}, u32[]{:S(2)}) %collective-permute-start.16) | collective-permute-done | bytes 196640 | tf_op jit(solution)/shard_map/ppermute | solution.py:137
  107.0 3.3 %collective-permute-done.15.lo = bf16[2,12,32,128]{3,2,1,0:T(8,128)(2,1)S(1)} collective-permute-done((bf16[2,12,32,128]{3,2,1,0:T(8,128)(2,1)S(1)}, bf16[2,12,32,128]{3,2,1,0:T(8,128)(2,1)S(1)}, u32[]{:S(2)}, u32[]{:S(2)}) %collective-permute-start.15) | collective-permute-done | bytes 196640 | tf_op jit(solution)/shard_map/ppermute | solution.py:137
  110.3 4.6 %shard_map.81 = (bf16[2,8,32,128]{3,2,1,0:T(8,128)(2,1)S(1)}, bf16[2,8,32,128]{3,2,1,0:T(8,128)(2,1)S(1)}, bf16[2,8,32,128]{3,2,1,0:T(8,128)(2,1)S(1)}, bf16[2,8...) custom-call(s32[3]{0:T(128)S(1)} %pad_add_fusion.idx, ...), custom_call_target="tpu_custom_call" | custom-call | tf_op jit(solution)/shard_map/pallas_call | solution.py:386
  115.0 1.8 collective-permute-start.21
  116.8 1.3 collective-permute-start.22
  118.1 3.4 %collective-permute-done.20.e1 = bf16[2,8,32,128]{3,2,1,0:T(8,128)(2,1)S(1)} collective-permute-done((bf16[2,8,32,128]{3,2,1,0:T(8,128)(2,1)S(1)}, bf16[2,8,32,128]{3,2,1,0:T(8,128)(2,1)S(1)}, u32[]{:S(2)}, u32[]{:S(2)}) %collective-permute-start.20) | collective-permute-done | bytes 131104 | tf_op jit(solution)/shard_map/ppermute | solution.py:134
  122.0 5.8 %shard_map.83 = (f32[1792,128]{1,0:T(8,128)S(1)}, bf16[1792,128]{1,0:T(8,128)(2,1)S(1)}) custom-call(s32[3]{0:T(128)S(1)} %pad_add_fusion.idx, bf16[6,8,32,128]{3,2,1,0:T(8,128)(2,1)S(1)} %get-tuple-element.51.a0.x0, bf16[6,8,32,128]{3,2,1,0:T(8,128)(2,1)S(1)} %collective-permute-done.10.a1.x1, bf16[6,8,32,128]{3,2,1,0:T(8,128)(2,1)S(1)} %collective-permute-done.11.a2.x2, ...), custom_call_target="tpu_custom_call" | custom-call | tf_op jit(solution)/shard_map/pallas_call | solution.py:431
  127.8 5.2 %collective-permute-start.23 = (bf16[1792,128]{1,0:T(8,128)(2,1)S(1)}, bf16[1792,128]{1,0:T(8,128)(2,1)S(1)}, u32[]{:S(2)}, u32[]{:S(2)}) collective-permute-start(bf16[1792,128]{1,0:T(8,128)(2,1)S(1)} %get-tuple-element.75), channel_id=1, source_target_pairs={{0,64},{64,0},{1,65},{65,1},{2,66},{66,2},{3,67},{67,3},{4,68},{68... | collective-permute-start | bytes 1376264 | tf_op jit(solution)/shard_map/ppermute | solution.py:140
  133.0 1.4 collective-permute-done.23.recv
  135.3 2.6 %collective-permute-start.26 = (bf16[448,128]{1,0:T(8,128)(2,1)S(1)}, bf16[448,128]{1,0:T(8,128)(2,1)S(1)}, u32[]{:S(2)}, u32[]{:S(2)}) collective-permute-start(bf16[448,128]{1,0:T(8,128)(2,1)S(1)} %get-tuple-element.79), channel_id=1, source_target_pairs={{0,3},{1,0},{2,1},{3,2},{4,7},{5,4},{6,5},{7,6},{8,11},{9,8},{10,9... | collective-permute-start | bytes 344072 | tf_op jit(solution)/shard_map/ppermute | solution.py:143
  137.9 5.7 %collective-permute-done.24 = bf16[448,128]{1,0:T(8,128)(2,1)S(1)} collective-permute-done((bf16[448,128]{1,0:T(8,128)(2,1)S(1)}, bf16[448,128]{1,0:T(8,128)(2,1)S(1)}, u32[]{:S(2)}, u32[]{:S(2)}) %collective-permute-start.24) | collective-permute-done | bytes 114720 | tf_op jit(solution)/shard_map/ppermute | solution.py:143
  143.8 1.4 collective-permute-start.27
  145.2 2.2 %collective-permute-done.29.q3 = bf16[448,128]{1,0:T(8,128)(2,1)S(1)} collective-permute-done((bf16[448,128]{1,0:T(8,128)(2,1)S(1)}, bf16[448,128]{1,0:T(8,128)(2,1)S(1)}, u32[]{:S(2)}, u32[]{:S(2)}) %collective-permute-start.29) | collective-permute-done | bytes 114720 | tf_op jit(solution)/shard_map/ppermute | solution.py:146
  147.4 1.6 collective-permute-done.28.q2
  149.0 2.1 %collective-permute-done.27.q1 = bf16[448,128]{1,0:T(8,128)(2,1)S(1)} collective-permute-done((bf16[448,128]{1,0:T(8,128)(2,1)S(1)}, bf16[448,128]{1,0:T(8,128)(2,1)S(1)}, u32[]{:S(2)}, u32[]{:S(2)}) %collective-permute-start.27) | collective-permute-done | bytes 114720 | tf_op jit(solution)/shard_map/ppermute | solution.py:146
  151.8 4.5 %collective-permute-start.32 = (bf16[448,128]{1,0:T(8,128)(2,1)S(1)}, bf16[448,128]{1,0:T(8,128)(2,1)S(1)}, u32[]{:S(2)}, u32[]{:S(2)}) collective-permute-start(bf16[448,128]{1,0:T(8,128)(2,1)S(1)} %shard_map.85.q0), channel_id=1, source_target_pairs={{0,3},{1,0},{2,1},{3,2},{4,7},{5,4},{6,5},{7,6},{8,11},{9,8},{10,9... | collective-permute-start | bytes 344072 | tf_op jit(solution)/shard_map/ppermute | solution.py:143
  156.9 3.9 %collective-permute-done.32.q3 = bf16[448,128]{1,0:T(8,128)(2,1)S(1)} collective-permute-done((bf16[448,128]{1,0:T(8,128)(2,1)S(1)}, bf16[448,128]{1,0:T(8,128)(2,1)S(1)}, u32[]{:S(2)}, u32[]{:S(2)}) %collective-permute-start.32) | collective-permute-done | bytes 114720 | tf_op jit(solution)/shard_map/ppermute | solution.py:143
  161.5 3.2 %collective-permute-done.30.q1 = bf16[448,128]{1,0:T(8,128)(2,1)S(1)} collective-permute-done((bf16[448,128]{1,0:T(8,128)(2,1)S(1)}, bf16[448,128]{1,0:T(8,128)(2,1)S(1)}, u32[]{:S(2)}, u32[]{:S(2)}) %collective-permute-start.30) | collective-permute-done | bytes 114720 | tf_op jit(solution)/shard_map/ppermute | solution.py:143
  166.1 0.9 collective-permute-start.17
  167.0 2.7 %collective-permute-start.18 = (bf16[2,8,32,128]{3,2,1,0:T(8,128)(2,1)S(1)}, bf16[2,8,32,128]{3,2,1,0:T(8,128)(2,1)S(1)}, u32[]{:S(2)}, u32[]{:S(2)}) collective-permute-start(bf16[2,8,32,128]{3,2,1,0:T(8,128)(2,1)S(1)} %get-tuple-element.66), channel_id=1, source_target_pairs={{0,32},{16,48},{32,0},{48,16},{1,33},{17,49},{33,1},{49,17},{2,34}... | collective-permute-start | bytes 393224 | tf_op jit(solution)/shard_map/ppermute | solution.py:134
  169.8 2.5 %collective-permute-done.17.b1 = bf16[2,8,32,128]{3,2,1,0:T(8,128)(2,1)S(1)} collective-permute-done((bf16[2,8,32,128]{3,2,1,0:T(8,128)(2,1)S(1)}, bf16[2,8,32,128]{3,2,1,0:T(8,128)(2,1)S(1)}, u32[]{:S(2)}, u32[]{:S(2)}) %collective-permute-start.17) | collective-permute-done | bytes 131104 | tf_op jit(solution)/shard_map/ppermute | solution.py:134
  172.3 3.7 %collective-permute-done.18.b2 = bf16[2,8,32,128]{3,2,1,0:T(8,128)(2,1)S(1)} collective-permute-done((bf16[2,8,32,128]{3,2,1,0:T(8,128)(2,1)S(1)}, bf16[2,8,32,128]{3,2,1,0:T(8,128)(2,1)S(1)}, u32[]{:S(2)}, u32[]{:S(2)}) %collective-permute-start.18) | collective-permute-done | bytes 131104 | tf_op jit(solution)/shard_map/ppermute | solution.py:134
  176.0 1.6 shard_map.82
  177.6 2.0 %shard_map.87 = (f32[3456,128]{1,0:T(8,128)}, f32[8,128]{1,0:T(8,128)S(1)}) custom-call(s32[3]{0:T(128)S(1)} %pad_add_fusion.idx, bf16[4,448,128]{2,1,0:T(8,128)(2,1)S(1)} %shard_map.86.mine, bf16[4,448,128]{2,1,0:T(8,128)(2,1)S(1)} %collective-permute-done.33.theirs), custom_call_target="tpu_custom_call" | custom-call | tf_op jit(solution)/shard_map/pallas_call | solution.py:489
  (73 shorter events, 14.2 us)
Async XLA Ops:
  0.7 1.2 copy-start
  3.9 64.1 %copy-start.2 = (bf16[1,3456,128]{2,1,0:T(8,128)(2,1)S(1)}, bf16[1,3456,128]{2,1,0:T(8,128)(2,1)}, u32[]{:S(2)}) copy-start(bf16[1,3456,128]{2,1,0:T(8,128)(2,1)} %param.5) | copy-start | bytes 2654212
  3.9 23.3 %collective-permute-start.4 = (bf16[1744,128]{1,0:T(8,128)(2,1)}, bf16[1744,128]{1,0:T(8,128)(2,1)S(1)}, u32[]{:S(2)}, u32[]{:S(2)}) collective-permute-start(bf16[1744,128]{1,0:T(8,128)(2,1)} %shard_map.75), channel_id=1, source_target_pairs={{0,48},{16,0},{32,16},{48,32},{1,49},{17,1},{33,17},{49,33},{2,50}... | collective-permute-start | bytes 1339400 | tf_op jit(solution)/shard_map/ppermute | solution.py:134
  8.5 20.4 %collective-permute-start.3 = (bf16[1744,128]{1,0:T(8,128)(2,1)}, bf16[1744,128]{1,0:T(8,128)(2,1)S(1)}, u32[]{:S(2)}, u32[]{:S(2)}) collective-permute-start(bf16[1744,128]{1,0:T(8,128)(2,1)} %shard_map.75), channel_id=1, source_target_pairs={{0,32},{16,48},{32,0},{48,16},{1,33},{17,49},{33,1},{49,17},{2,34}... | collective-permute-start | bytes 1339400 | tf_op jit(solution)/shard_map/ppermute | solution.py:134
  8.5 22.9 %collective-permute-start.2 = (bf16[1744,128]{1,0:T(8,128)(2,1)}, bf16[1744,128]{1,0:T(8,128)(2,1)S(1)}, u32[]{:S(2)}, u32[]{:S(2)}) collective-permute-start(bf16[1744,128]{1,0:T(8,128)(2,1)} %shard_map.75), channel_id=1, source_target_pairs={{0,16},{16,32},{32,48},{48,0},{1,17},{17,33},{33,49},{49,1},{2,18}... | collective-permute-start | bytes 1339400 | tf_op jit(solution)/shard_map/ppermute | solution.py:134
  27.1 24.7 %collective-permute-start.7 = (bf16[1744,128]{1,0:T(8,128)(2,1)S(1)}, bf16[1744,128]{1,0:T(8,128)(2,1)S(1)}, u32[]{:S(2)}, u32[]{:S(2)}) collective-permute-start(bf16[1744,128]{1,0:T(8,128)(2,1)S(1)} %collective-permute-done.4.g3), channel_id=1, source_target_pairs={{0,64},{64,0},{1,65},{65,1},{2,66},{66,2},{3,67},{67,3},{4,68},{68... | collective-permute-start | bytes 1339400 | tf_op jit(solution)/shard_map/ppermute | solution.py:140
  28.8 23.0 %collective-permute-start.6 = (bf16[1744,128]{1,0:T(8,128)(2,1)S(1)}, bf16[1744,128]{1,0:T(8,128)(2,1)S(1)}, u32[]{:S(2)}, u32[]{:S(2)}) collective-permute-start(bf16[1744,128]{1,0:T(8,128)(2,1)S(1)} %collective-permute-done.3.g2), channel_id=1, source_target_pairs={{0,64},{64,0},{1,65},{65,1},{2,66},{66,2},{3,67},{67,3},{4,68},{68... | collective-permute-start | bytes 1339400 | tf_op jit(solution)/shard_map/ppermute | solution.py:140
  31.3 20.5 %collective-permute-start.5 = (bf16[1744,128]{1,0:T(8,128)(2,1)S(1)}, bf16[1744,128]{1,0:T(8,128)(2,1)S(1)}, u32[]{:S(2)}, u32[]{:S(2)}) collective-permute-start(bf16[1744,128]{1,0:T(8,128)(2,1)S(1)} %collective-permute-done.2.g1), channel_id=1, source_target_pairs={{0,64},{64,0},{1,65},{65,1},{2,66},{66,2},{3,67},{67,3},{4,68},{68... | collective-permute-start | bytes 1339400 | tf_op jit(solution)/shard_map/ppermute | solution.py:140
  33.1 13.5 %collective-permute-start.1 = (bf16[2,24,32,128]{3,2,1,0:T(8,128)(2,1)S(1)}, bf16[2,24,32,128]{3,2,1,0:T(8,128)(2,1)S(1)}, u32[]{:S(2)}, u32[]{:S(2)}) collective-permute-start(bf16[2,24,32,128]{3,2,1,0:T(8,128)(2,1)S(1)} %pad_dynamic-slice_fusion.own), channel_id=1, source_target_pairs={{0,15},{1,0},{2,1},{3,2},{4,3},{5,4},{6,5},{7,6},{8,7},{9,8},{10,9... | collective-permute-start | bytes 1179656 | tf_op jit(solution)/shard_map/ppermute | solution.py:137
  38.1 13.7 %collective-permute-start = (bf16[2,24,32,128]{3,2,1,0:T(8,128)(2,1)S(1)}, bf16[2,24,32,128]{3,2,1,0:T(8,128)(2,1)S(1)}, u32[]{:S(2)}, u32[]{:S(2)}) collective-permute-start(bf16[2,24,32,128]{3,2,1,0:T(8,128)(2,1)S(1)} %pad_dynamic-slice_fusion.own), channel_id=1, source_target_pairs={{0,1},{1,2},{2,3},{3,4},{4,5},{5,6},{6,7},{7,8},{8,9},{9,10},{10,1... | collective-permute-start | bytes 1179656 | tf_op jit(solution)/shard_map/ppermute | solution.py:137
  51.9 10.9 %copy-start.3 = (bf16[1744,128]{1,0:T(8,128)(2,1)}, bf16[1744,128]{1,0:T(8,128)(2,1)S(1)}, u32[]{:S(2)}) copy-start(bf16[1744,128]{1,0:T(8,128)(2,1)S(1)} %collective-permute-done.5.s1) | copy-start | bytes 1339396
  51.9 1.3 copy-start.1
  62.7 0.7 copy-start.5
  63.4 0.7 copy-start.7
  64.1 0.7 copy-start.9
  64.8 0.7 copy-start.11
  65.5 9.4 %collective-permute-start.9 = (bf16[2,20,32,128]{3,2,1,0:T(8,128)(2,1)S(1)}, bf16[2,20,32,128]{3,2,1,0:T(8,128)(2,1)}, u32[]{:S(2)}, u32[]{:S(2)}) collective-permute-start(bf16[2,20,32,128]{3,2,1,0:T(8,128)(2,1)S(1)} %get-tuple-element.45.own), channel_id=1, source_target_pairs={{0,15},{1,0},{2,1},{3,2},{4,3},{5,4},{6,5},{7,6},{8,7},{9,8},{10,9... | collective-permute-start | bytes 983048 | tf_op jit(solution)/shard_map/ppermute | solution.py:137
  65.8 11.6 %collective-permute-start.8 = (bf16[2,20,32,128]{3,2,1,0:T(8,128)(2,1)S(1)}, bf16[2,20,32,128]{3,2,1,0:T(8,128)(2,1)}, u32[]{:S(2)}, u32[]{:S(2)}) collective-permute-start(bf16[2,20,32,128]{3,2,1,0:T(8,128)(2,1)S(1)} %get-tuple-element.45.own), channel_id=1, source_target_pairs={{0,1},{1,2},{2,3},{3,4},{4,5},{5,6},{6,7},{7,8},{8,9},{9,10},{10,1... | collective-permute-start | bytes 983048 | tf_op jit(solution)/shard_map/ppermute | solution.py:137
  68.0 1.0 copy-start.4
  69.0 8.4 %copy-start.15 = (bf16[1,128]{1,0:T(2,128)(2,1)S(1)}, bf16[1,128]{1,0:T(2,128)(2,1)}, u32[]{:S(2)}) copy-start(bf16[1,128]{1,0:T(2,128)(2,1)} %ob.3) | copy-start | bytes 772
  74.9 12.5 %copy-start.8 = (bf16[4,8,32,128]{3,2,1,0:T(8,128)(2,1)S(1)}, bf16[4,8,32,128]{3,2,1,0:T(8,128)(2,1)}, u32[]{:S(2)}) copy-start(bf16[4,8,32,128]{3,2,1,0:T(8,128)(2,1)} %copy-done.7) | copy-start | bytes 786436
  74.9 12.5 %copy-start.10 = (bf16[4,8,32,128]{3,2,1,0:T(8,128)(2,1)S(1)}, bf16[4,8,32,128]{3,2,1,0:T(8,128)(2,1)}, u32[]{:S(2)}) copy-start(bf16[4,8,32,128]{3,2,1,0:T(8,128)(2,1)} %copy-done.9) | copy-start | bytes 786436
  74.9 21.7 %copy-start.12 = (bf16[2,12,32,128]{3,2,1,0:T(8,128)(2,1)S(1)}, bf16[2,12,32,128]{3,2,1,0:T(8,128)(2,1)}, u32[]{:S(2)}) copy-start(bf16[2,12,32,128]{3,2,1,0:T(8,128)(2,1)} %copy-done.11) | copy-start | bytes 589828
  85.8 24.5 %copy-start.6 = (bf16[4,10,32,128]{3,2,1,0:T(8,128)(2,1)S(1)}, bf16[4,10,32,128]{3,2,1,0:T(8,128)(2,1)}, u32[]{:S(2)}) copy-start(bf16[4,10,32,128]{3,2,1,0:T(8,128)(2,1)} %copy-done.5) | copy-start | bytes 983044
  85.8 5.9 %collective-permute-start.14 = (bf16[2,16,32,128]{3,2,1,0:T(8,128)(2,1)S(1)}, bf16[2,16,32,128]{3,2,1,0:T(8,128)(2,1)S(1)}, u32[]{:S(2)}, u32[]{:S(2)}) collective-permute-start(bf16[2,16,32,128]{3,2,1,0:T(8,128)(2,1)S(1)} %get-tuple-element.55.own.rest_2_), channel_id=1, source_target_pairs={{0,15},{1,0},{2,1},{3,2},{4,3},{5,4},{6,5},{7,6},{8,7},{9,8},{10,9... | collective-permute-start | bytes 786440 | tf_op jit(solution)/shard_map/ppermute | solution.py:137
  87.1 9.5 %collective-permute-start.13 = (bf16[2,16,32,128]{3,2,1,0:T(8,128)(2,1)S(1)}, bf16[2,16,32,128]{3,2,1,0:T(8,128)(2,1)S(1)}, u32[]{:S(2)}, u32[]{:S(2)}) collective-permute-start(bf16[2,16,32,128]{3,2,1,0:T(8,128)(2,1)S(1)} %get-tuple-element.55.own.rest_2_), channel_id=1, source_target_pairs={{0,1},{1,2},{2,3},{3,4},{4,5},{5,6},{6,7},{7,8},{8,9},{9,10},{10,1... | collective-permute-start | bytes 786440 | tf_op jit(solution)/shard_map/ppermute | solution.py:137
  88.2 28.6 %collective-permute-start.10 = (bf16[6,8,32,128]{3,2,1,0:T(8,128)(2,1)S(1)}, bf16[6,8,32,128]{3,2,1,0:T(8,128)(2,1)S(1)}, u32[]{:S(2)}, u32[]{:S(2)}) collective-permute-start(bf16[6,8,32,128]{3,2,1,0:T(8,128)(2,1)S(1)} %get-tuple-element.52), channel_id=1, source_target_pairs={{0,16},{16,32},{32,48},{48,0},{1,17},{17,33},{33,49},{49,1},{2,18}... | collective-permute-start | bytes 1179656 | tf_op jit(solution)/shard_map/ppermute | solution.py:134
  88.2 29.8 %collective-permute-start.11 = (bf16[6,8,32,128]{3,2,1,0:T(8,128)(2,1)S(1)}, bf16[6,8,32,128]{3,2,1,0:T(8,128)(2,1)S(1)}, u32[]{:S(2)}, u32[]{:S(2)}) collective-permute-start(bf16[6,8,32,128]{3,2,1,0:T(8,128)(2,1)S(1)} %get-tuple-element.53), channel_id=1, source_target_pairs={{0,32},{16,48},{32,0},{48,16},{1,33},{17,49},{33,1},{49,17},{2,34}... | collective-permute-start | bytes 1179656 | tf_op jit(solution)/shard_map/ppermute | solution.py:134
  90.0 28.0 %collective-permute-start.12 = (bf16[6,8,32,128]{3,2,1,0:T(8,128)(2,1)S(1)}, bf16[6,8,32,128]{3,2,1,0:T(8,128)(2,1)S(1)}, u32[]{:S(2)}, u32[]{:S(2)}) collective-permute-start(bf16[6,8,32,128]{3,2,1,0:T(8,128)(2,1)S(1)} %get-tuple-element.54), channel_id=1, source_target_pairs={{0,48},{16,0},{32,16},{48,32},{1,49},{17,1},{33,17},{49,33},{2,50}... | collective-permute-start | bytes 1179656 | tf_op jit(solution)/shard_map/ppermute | solution.py:134
  102.1 4.9 %collective-permute-start.16 = (bf16[2,12,32,128]{3,2,1,0:T(8,128)(2,1)S(1)}, bf16[2,12,32,128]{3,2,1,0:T(8,128)(2,1)S(1)}, u32[]{:S(2)}, u32[]{:S(2)}) collective-permute-start(bf16[2,12,32,128]{3,2,1,0:T(8,128)(2,1)S(1)} %get-tuple-element.59.own.rest_0_), channel_id=1, source_target_pairs={{0,15},{1,0},{2,1},{3,2},{4,3},{5,4},{6,5},{7,6},{8,7},{9,8},{10,9... | collective-permute-start | bytes 589832 | tf_op jit(solution)/shard_map/ppermute | solution.py:137
  102.5 7.8 %collective-permute-start.15 = (bf16[2,12,32,128]{3,2,1,0:T(8,128)(2,1)S(1)}, bf16[2,12,32,128]{3,2,1,0:T(8,128)(2,1)S(1)}, u32[]{:S(2)}, u32[]{:S(2)}) collective-permute-start(bf16[2,12,32,128]{3,2,1,0:T(8,128)(2,1)S(1)} %get-tuple-element.59.own.rest_0_), channel_id=1, source_target_pairs={{0,1},{1,2},{2,3},{3,4},{4,5},{5,6},{6,7},{7,8},{8,9},{9,10},{10,1... | collective-permute-start | bytes 589832 | tf_op jit(solution)/shard_map/ppermute | solution.py:137
  114.9 6.5 %collective-permute-start.20 = (bf16[2,8,32,128]{3,2,1,0:T(8,128)(2,1)S(1)}, bf16[2,8,32,128]{3,2,1,0:T(8,128)(2,1)S(1)}, u32[]{:S(2)}, u32[]{:S(2)}) collective-permute-start(bf16[2,8,32,128]{3,2,1,0:T(8,128)(2,1)S(1)} %get-tuple-element.71), channel_id=1, source_target_pairs={{0,16},{16,32},{32,48},{48,0},{1,17},{17,33},{33,49},{49,1},{2,18}... | collective-permute-start | bytes 393224 | tf_op jit(solution)/shard_map/ppermute | solution.py:134
  115.0 6.4 %collective-permute-start.21 = (bf16[2,8,32,128]{3,2,1,0:T(8,128)(2,1)S(1)}, bf16[2,8,32,128]{3,2,1,0:T(8,128)(2,1)S(1)}, u32[]{:S(2)}, u32[]{:S(2)}) collective-permute-start(bf16[2,8,32,128]{3,2,1,0:T(8,128)(2,1)S(1)} %get-tuple-element.72), channel_id=1, source_target_pairs={{0,32},{16,48},{32,0},{48,16},{1,33},{17,49},{33,1},{49,17},{2,34}... | collective-permute-start | bytes 393224 | tf_op jit(solution)/shard_map/ppermute | solution.py:134
  116.8 5.2 %collective-permute-start.22 = (bf16[2,8,32,128]{3,2,1,0:T(8,128)(2,1)S(1)}, bf16[2,8,32,128]{3,2,1,0:T(8,128)(2,1)S(1)}, u32[]{:S(2)}, u32[]{:S(2)}) collective-permute-start(bf16[2,8,32,128]{3,2,1,0:T(8,128)(2,1)S(1)} %get-tuple-element.73), channel_id=1, source_target_pairs={{0,48},{16,0},{32,16},{48,32},{1,49},{17,1},{33,17},{49,33},{2,50}... | collective-permute-start | bytes 393224 | tf_op jit(solution)/shard_map/ppermute | solution.py:134
  127.8 6.7 %collective-permute-start.23 = (bf16[1792,128]{1,0:T(8,128)(2,1)S(1)}, bf16[1792,128]{1,0:T(8,128)(2,1)S(1)}, u32[]{:S(2)}, u32[]{:S(2)}) collective-permute-start(bf16[1792,128]{1,0:T(8,128)(2,1)S(1)} %get-tuple-element.75), channel_id=1, source_target_pairs={{0,64},{64,0},{1,65},{65,1},{2,66},{66,2},{3,67},{67,3},{4,68},{68... | collective-permute-start | bytes 1376264 | tf_op jit(solution)/shard_map/ppermute | solution.py:140
  135.2 8.4 %collective-permute-start.24 = (bf16[448,128]{1,0:T(8,128)(2,1)S(1)}, bf16[448,128]{1,0:T(8,128)(2,1)S(1)}, u32[]{:S(2)}, u32[]{:S(2)}) collective-permute-start(bf16[448,128]{1,0:T(8,128)(2,1)S(1)} %get-tuple-element.77), channel_id=1, source_target_pairs={{0,1},{1,2},{2,3},{3,0},{4,5},{5,6},{6,7},{7,4},{8,9},{9,10},{10,1... | collective-permute-start | bytes 344072 | tf_op jit(solution)/shard_map/ppermute | solution.py:143
  135.2 8.3 %collective-permute-start.25 = (bf16[448,128]{1,0:T(8,128)(2,1)S(1)}, bf16[448,128]{1,0:T(8,128)(2,1)S(1)}, u32[]{:S(2)}, u32[]{:S(2)}) collective-permute-start(bf16[448,128]{1,0:T(8,128)(2,1)S(1)} %get-tuple-element.78), channel_id=1, source_target_pairs={{0,2},{1,3},{2,0},{3,1},{4,6},{5,7},{6,4},{7,5},{8,10},{9,11},{10,... | collective-permute-start | bytes 344072 | tf_op jit(solution)/shard_map/ppermute | solution.py:143
  135.3 8.3 %collective-permute-start.26 = (bf16[448,128]{1,0:T(8,128)(2,1)S(1)}, bf16[448,128]{1,0:T(8,128)(2,1)S(1)}, u32[]{:S(2)}, u32[]{:S(2)}) collective-permute-start(bf16[448,128]{1,0:T(8,128)(2,1)S(1)} %get-tuple-element.79), channel_id=1, source_target_pairs={{0,3},{1,0},{2,1},{3,2},{4,7},{5,4},{6,5},{7,6},{8,11},{9,8},{10,9... | collective-permute-start | bytes 344072 | tf_op jit(solution)/shard_map/ppermute | solution.py:143
  143.7 3.7 %collective-permute-start.29 = (bf16[448,128]{1,0:T(8,128)(2,1)S(1)}, bf16[448,128]{1,0:T(8,128)(2,1)S(1)}, u32[]{:S(2)}, u32[]{:S(2)}) collective-permute-start(bf16[448,128]{1,0:T(8,128)(2,1)S(1)} %add_convert_fusion.q0), channel_id=1, source_target_pairs={{0,12},{1,13},{2,14},{3,15},{4,0},{5,1},{6,2},{7,3},{8,4},{9,5},{1... | collective-permute-start | bytes 344072 | tf_op jit(solution)/shard_map/ppermute | solution.py:146
  143.8 5.3 %collective-permute-start.28 = (bf16[448,128]{1,0:T(8,128)(2,1)S(1)}, bf16[448,128]{1,0:T(8,128)(2,1)S(1)}, u32[]{:S(2)}, u32[]{:S(2)}) collective-permute-start(bf16[448,128]{1,0:T(8,128)(2,1)S(1)} %add_convert_fusion.q0), channel_id=1, source_target_pairs={{0,8},{1,9},{2,10},{3,11},{4,12},{5,13},{6,14},{7,15},{8,0},{9,1},... | collective-permute-start | bytes 344072 | tf_op jit(solution)/shard_map/ppermute | solution.py:146
  143.8 7.2 %collective-permute-start.27 = (bf16[448,128]{1,0:T(8,128)(2,1)S(1)}, bf16[448,128]{1,0:T(8,128)(2,1)S(1)}, u32[]{:S(2)}, u32[]{:S(2)}) collective-permute-start(bf16[448,128]{1,0:T(8,128)(2,1)S(1)} %add_convert_fusion.q0), channel_id=1, source_target_pairs={{0,4},{1,5},{2,6},{3,7},{4,8},{5,9},{6,10},{7,11},{8,12},{9,13},{1... | collective-permute-start | bytes 344072 | tf_op jit(solution)/shard_map/ppermute | solution.py:146
  151.8 9.1 %collective-permute-start.32 = (bf16[448,128]{1,0:T(8,128)(2,1)S(1)}, bf16[448,128]{1,0:T(8,128)(2,1)S(1)}, u32[]{:S(2)}, u32[]{:S(2)}) collective-permute-start(bf16[448,128]{1,0:T(8,128)(2,1)S(1)} %shard_map.85.q0), channel_id=1, source_target_pairs={{0,3},{1,0},{2,1},{3,2},{4,7},{5,4},{6,5},{7,6},{8,11},{9,8},{10,9... | collective-permute-start | bytes 344072 | tf_op jit(solution)/shard_map/ppermute | solution.py:143
  156.2 5.2 %collective-permute-start.31 = (bf16[448,128]{1,0:T(8,128)(2,1)S(1)}, bf16[448,128]{1,0:T(8,128)(2,1)S(1)}, u32[]{:S(2)}, u32[]{:S(2)}) collective-permute-start(bf16[448,128]{1,0:T(8,128)(2,1)S(1)} %shard_map.85.q0), channel_id=1, source_target_pairs={{0,2},{1,3},{2,0},{3,1},{4,6},{5,7},{6,4},{7,5},{8,10},{9,11},{10,... | collective-permute-start | bytes 344072 | tf_op jit(solution)/shard_map/ppermute | solution.py:143
  156.2 8.4 %collective-permute-start.30 = (bf16[448,128]{1,0:T(8,128)(2,1)S(1)}, bf16[448,128]{1,0:T(8,128)(2,1)S(1)}, u32[]{:S(2)}, u32[]{:S(2)}) collective-permute-start(bf16[448,128]{1,0:T(8,128)(2,1)S(1)} %shard_map.85.q0), channel_id=1, source_target_pairs={{0,1},{1,2},{2,3},{3,0},{4,5},{5,6},{6,7},{7,4},{8,9},{9,10},{10,1... | collective-permute-start | bytes 344072 | tf_op jit(solution)/shard_map/ppermute | solution.py:143
  165.3 12.3 %collective-permute-start.33 = (bf16[4,448,128]{2,1,0:T(8,128)(2,1)S(1)}, bf16[4,448,128]{2,1,0:T(8,128)(2,1)S(1)}, u32[]{:S(2)}, u32[]{:S(2)}) collective-permute-start(bf16[4,448,128]{2,1,0:T(8,128)(2,1)S(1)} %shard_map.86.mine), channel_id=1, source_target_pairs={{0,64},{64,0},{1,65},{65,1},{2,66},{66,2},{3,67},{67,3},{4,68},{68... | collective-permute-start | bytes 1376264 | tf_op jit(solution)/shard_map/ppermute | solution.py:140
  166.1 6.2 %collective-permute-start.17 = (bf16[2,8,32,128]{3,2,1,0:T(8,128)(2,1)S(1)}, bf16[2,8,32,128]{3,2,1,0:T(8,128)(2,1)S(1)}, u32[]{:S(2)}, u32[]{:S(2)}) collective-permute-start(bf16[2,8,32,128]{3,2,1,0:T(8,128)(2,1)S(1)} %get-tuple-element.65), channel_id=1, source_target_pairs={{0,16},{16,32},{32,48},{48,0},{1,17},{17,33},{33,49},{49,1},{2,18}... | collective-permute-start | bytes 393224 | tf_op jit(solution)/shard_map/ppermute | solution.py:134
  167.0 9.0 %collective-permute-start.18 = (bf16[2,8,32,128]{3,2,1,0:T(8,128)(2,1)S(1)}, bf16[2,8,32,128]{3,2,1,0:T(8,128)(2,1)S(1)}, u32[]{:S(2)}, u32[]{:S(2)}) collective-permute-start(bf16[2,8,32,128]{3,2,1,0:T(8,128)(2,1)S(1)} %get-tuple-element.66), channel_id=1, source_target_pairs={{0,32},{16,48},{32,0},{48,16},{1,33},{17,49},{33,1},{49,17},{2,34}... | collective-permute-start | bytes 393224 | tf_op jit(solution)/shard_map/ppermute | solution.py:134
  169.7 6.3 %collective-permute-start.19 = (bf16[2,8,32,128]{3,2,1,0:T(8,128)(2,1)S(1)}, bf16[2,8,32,128]{3,2,1,0:T(8,128)(2,1)S(1)}, u32[]{:S(2)}, u32[]{:S(2)}) collective-permute-start(bf16[2,8,32,128]{3,2,1,0:T(8,128)(2,1)S(1)} %get-tuple-element.67), channel_id=1, source_target_pairs={{0,48},{16,0},{32,16},{48,32},{1,49},{17,1},{33,17},{49,33},{2,50}... | collective-permute-start | bytes 393224 | tf_op jit(solution)/shard_map/ppermute | solution.py:134
  (2 other events, 1.3 us)
where the time goes:
time: 180 us
  waiting for transfers between devices  80 us (44%)
  Pallas kernels  46.7 us (26%)
  starting transfers between devices  42.3 us (24%)
  local copies, waits for them, and re-layouts  10.1 us (6%)
    ppermute x12, waiting for transfers between devices, sec(): lax.ppermute(v, 'section', [(i, (i + k) % n_sec) for i in range(n_sec)])  30.7 us
    ppermute x8, waiting for transfers between devices, dep(): lax.ppermute(v, 'depth', [(i, (i + k) % n_dep) for i in range(n_dep)])  28.5 us
    ppermute x12, starting transfers between devices, sec(): lax.ppermute(v, 'section', [(i, (i + k) % n_sec) for i in range(n_sec)])  14.8 us
    ppermute x6, waiting for transfers between devices, xdep(): lax.ppermute(v, 'depth', [(i, i // 4 * 4 + (i + k) % 4) for i in range(n_...  13.5 us
    ppermute x8, starting transfers between devices, dep(): lax.ppermute(v, 'depth', [(i, (i + k) % n_dep) for i in range(n_dep)])  9.54 us
    pallas_call x1, Pallas kernels, shards(): call(k1, (sds((4, R, W, C)), sds((4, R + 2, W, C)), sds((4, R, W, C)), sd...  8.84 us
    ppermute x5, starting transfers between devices, swap(): return lax.ppermute(v, 'dp', [(0, 1), (1, 0)])  8.56 us
    pallas_call x1, Pallas kernels, shards(): call(k2, (sds((4, R, W, C)), sds((4, R + 6, W, C)), sds((4, R, W, C)), sd...  8.38 us
  transfers between devices with their start and end apart: 34, of which 21 were waited for; matrix products, arithmetic and copies ran while one was open for 1% of the time, Pallas kernels for 10%

commit v1 on v0

--- a/solution.py
+++ b/solution.py
@@ -14,6 +14,11 @@
 SMEM = pl.BlockSpec(memory_space=pltpu.SMEM)
 VMEM = pl.BlockSpec(memory_space=pltpu.VMEM)
 ANY = pl.BlockSpec(memory_space=pl.ANY)
+HBM = pl.BlockSpec(memory_space=pltpu.HBM)
+
+
+def in_hbm(x):
+    return pltpu.with_memory_space_constraint(x, pltpu.HBM)
 
 
 def sds(shape, dtype=BF):
@@ -105,7 +110,7 @@
 
 def bias_of(s, t, own_bias, got_bias):
     k = (s + 4 - t) % 4
-    row = own_bias[...].astype(F32)
+    row = own_bias[0:1].astype(F32)
     for i in range(3):
         row = jnp.where(k == i + 1, got_bias[i][0:1].astype(F32), row)
     return row
@@ -145,29 +150,40 @@
     def ydep(v, k):
         return lax.ppermute(v, "depth", [(i, (i + 4 * k) % n_dep) for i in range(n_dep)])
 
-    def window(v, ext):
-        padded = jnp.pad(v, ((0, 0), (ext, ext), (0, 0), (0, 0)))
-        return lax.dynamic_slice_in_dim(padded, s * R, R + 2 * ext, 1)
-
-    h0 = window(volume[0], 8)
+    own_w = weights[0]
+
+    def prepare(vol, w, b, h0, half, pad, row, sem):
+        s_, c_ = lax.axis_index("section"), lax.axis_index("dp")
+        pull_w = pltpu.make_async_copy(w.at[c_], half.at[pl.ds(0, HALF)], sem.at[0])
+        pull_v = pltpu.make_async_copy(vol, pad.at[:, pl.ds(8, H)], sem.at[1])
+        pull_b = pltpu.make_async_copy(b, row, sem.at[2])
+        pull_w.start()
+        pull_v.start()
+        pull_b.start()
+        pad[:, 0:8] = jnp.zeros((PL, 8, W, C), BF)
+        pad[:, H + 8 :] = jnp.zeros((PL, 8, W, C), BF)
+        pull_b.wait()
+        half[HALF:] = jnp.broadcast_to(row[...], (16, C))
+        pull_v.wait()
+        h0[...] = pad[:, pl.ds(s_ * R, R + 16)]
+        pull_w.wait()
+
+    h0, own_half = call(
+        prepare,
+        (sds((PL, R + 16, W, C)), sds((HB, C))),
+        [HBM, HBM, HBM],
+        [pltpu.VMEM((PL, H + 16, W, C), BF), pltpu.VMEM((1, C), BF), pltpu.SemaphoreType.DMA((3,))],
+    )(in_hbm(volume[0]), in_hbm(own_w.reshape(2, HALF, C)), in_hbm(biases))
     h0_lo, h0_hi = dep(h0, 1), dep(h0, -1)
 
-    own_w = weights[0]
-
-    def prepare(idx, w, b, out):
-        out[0:HALF] = w[idx[2]]
-        out[HALF:] = jnp.broadcast_to(b[...], (16, C))
-
-    own_half = call(prepare, sds((HB, C)), [SMEM, VMEM, VMEM], [], VMEM)(idx, own_w.reshape(2, HALF, C), biases)
-    got = [sec(own_half, k) for k in (1, 3, 2)]
-    got = [got[0], got[2], got[1]]
+    near = [sec(own_half, k) for k in (1, 3)]
+    got = [near[0], sec(own_half, 2), near[1]]
     swapped = [swap(g) for g in got]
     all_w = (own_w, *got, *swapped)
-    W_SPECS = [ANY] * 7
-    got_b = tuple(g[HALF:] for g in got)
-    all_b = (biases, *got_b)
-
-    cot = window(cotangent[0], 4)
+    W_SPECS = [HBM] + [ANY] * 6
+    all_b = (own_half, *got)
+    tail_rows = pl.BlockSpec((16, C), lambda _: (HALF // 16, 0))
+    B_SPECS = [tail_rows] * 4
 
     def turn(idx, own, g1, g2, g3, s1, s2, s3, out, buf, sem):
         steps = [
@@ -194,11 +210,10 @@
         assemble(x, lo, own, hi, d_, last)
         h0e[...] = x[1:5, 8 : 8 + R]
         steps[0][1]()
-        wide = column(w, 0)
         b0 = bias_of(s_, 0, ob, (b1_, b2_, b3_))
 
         def one(p, _):
-            pre = conv_plane(x, p, wide, R + 14) + b0
+            pre = conv_plane(x, p, column(w, 0), R + 14) + b0
             h = jnp.where(inside(R + 14, W, C, s_ * R - 7, H, 2 * d_ - 1 + p, D), pre * jax.nn.sigmoid(pre), 0.0)
             h = h.astype(BF).reshape(R + 14, W, C)
             h1[p] = h
@@ -208,11 +223,10 @@
 
         lax.fori_loop(0, 4, one, 0)
         steps[1][1]()
-        wide1 = column(w, 1)
         b1 = bias_of(s_, 1, ob, (b1_, b2_, b3_))
 
         def two(p, _):
-            pre = conv_plane(h1, p, wide1, R + 12) + b1
+            pre = conv_plane(h1, p, column(w, 1), R + 12) + b1
             h = jnp.where(inside(R + 12, W, C, s_ * R - 6, H, 2 * d_ + p, D), pre * jax.nn.sigmoid(pre), 0.0)
             h2[p] = h.astype(BF).reshape(R + 12, W, C)
             pre1[p] = pre[4 * W : 16 * W].astype(BF).reshape(R + 4, W, C)
@@ -229,7 +243,7 @@
             sds((2, R + 4, W, C)),
             sds((2, R + 12, W, C)),
         ),
-        [SMEM, VMEM, VMEM, VMEM] + W_SPECS + [VMEM] * 4,
+        [SMEM, VMEM, VMEM, VMEM] + W_SPECS + B_SPECS,
         [
             pltpu.VMEM((6, R + 16, W, C), BF),
             pltpu.VMEM((4, R + 14, W, C), BF),
@@ -245,7 +259,7 @@
     )(idx, *all_w)
     h2_lo, h2_hi, wturn = lax.optimization_barrier((h2_lo, h2_hi, wturn))
 
-    def k2(idx, own, lo, hi, ow, g1, g2, g3, s1, s2, s3, ob, b1_, b2_, b3_, cot, h2e, pre2, h3e, h4, d3, x, h3, w, sem):
+    def k2(idx, own, lo, hi, ow, g1, g2, g3, s1, s2, s3, ob, b1_, b2_, b3_, cot, h2e, pre2, h3e, h4, d3, x, h3, w, gpad, sem):
         s_, d_ = idx[0], idx[1]
         steps = [
             halves(s_, idx[2], t + 2, ow, (g1, g2, g3), (s1, s2, s3), w.at[t], sem.at[t], HALF) for t in range(2)
@@ -254,12 +268,12 @@
             start()
         assemble(x, lo, own, hi, d_, last)
         h2e[...] = x[1:5, 6 : 6 + R]
+        gpad[:, 4 : 4 + H] = cot[...]
         steps[0][1]()
-        wide = column(w, 0)
         b0 = bias_of(s_, 2, ob, (b1_, b2_, b3_))
 
         def one(p, _):
-            pre = conv_plane(x, p, wide, R + 10) + b0
+            pre = conv_plane(x, p, column(w, 0), R + 10) + b0
             h = jnp.where(inside(R + 10, W, C, s_ * R - 5, H, 2 * d_ - 1 + p, D), pre * jax.nn.sigmoid(pre), 0.0)
             h = h.astype(BF).reshape(R + 10, W, C)
             h3[p] = h
@@ -269,14 +283,13 @@
 
         lax.fori_loop(0, 4, one, 0)
         steps[1][1]()
-        wide1 = column(w, 1)
         b1 = bias_of(s_, 3, ob, (b1_, b2_, b3_))
 
         def two(p, _):
-            pre = conv_plane(h3, p, wide1, R + 8) + b1
+            pre = conv_plane(h3, p, column(w, 1), R + 8) + b1
             h = (pre * jax.nn.sigmoid(pre)).astype(BF).reshape(R + 8, W, C)
             h4[p] = h[4 : 4 + R]
-            g = cot[p].reshape((R + 8) * W, C).astype(F32)
+            g = gpad[p, pl.ds(s_ * R, R + 8)].reshape((R + 8) * W, C).astype(F32)
             dl = g * slope(pre.astype(BF).astype(F32))
             dl = jnp.where(inside(R + 8, W, C, s_ * R - 4, H, 2 * d_ + p, D), dl, 0.0)
             d3[p] = dl.astype(BF).reshape(R + 8, W, C)
@@ -293,14 +306,15 @@
             sds((2, R, W, C)),
             sds((2, R + 8, W, C)),
         ),
-        [SMEM, VMEM, VMEM, VMEM] + W_SPECS + [VMEM] * 5,
+        [SMEM, VMEM, VMEM, VMEM] + W_SPECS + B_SPECS + [VMEM],
         [
             pltpu.VMEM((6, R + 12, W, C), BF),
             pltpu.VMEM((4, R + 10, W, C), BF),
             pltpu.VMEM((2, TAP, C), BF),
+            pltpu.VMEM((PL, H + 8, W, C), BF),
             pltpu.SemaphoreType.DMA((2, 2)),
         ],
-    )(idx, h2, h2_lo, h2_hi, *all_w, *all_b, cot)
+    )(idx, h2, h2_lo, h2_hi, *all_w, *all_b, cotangent[0])
 
     d3_lo, d3_hi = dep(d3, 1), dep(d3, -1)
 
@@ -318,110 +332,154 @@
     h_own, *h_send = call(pack, (six,) * 4, [SMEM] + [VMEM] * 5, [])(idx, h0e, h1e, h2e, h3e, h4)
     h_got = [sec(h_send[k - 1], k) for k in (1, 2, 3)]
 
-    def backward_pair(e0, final_delta):
-        n1, n2 = R + 2 * e0 - 2, R + 2 * e0 - 4
-
-        def body(idx, own, lo, hi, w, pre_a, *rest):
-            if final_delta:
-                pre_b, ga, da, gb, db, x, dbuf = rest
-            else:
-                d1_, d2_, d3_, g2_, g3_, *sends, ga, da, gb, x, dbuf = rest
-            s_, d_ = idx[0], idx[1]
-            assemble(x, lo, own, hi, d_, last)
-            wide = column(w, 1)
-
-            def one(p, _):
-                g = conv_plane(x, p, wide, n1).astype(BF)
-                dl = g.astype(F32) * slope(pre_a[p].reshape(n1 * W, C).astype(F32))
-                dl = jnp.where(inside(n1, W, C, s_ * R - e0 + 1, H, 2 * d_ - 1 + p, D), dl, 0.0)
-                dl = dl.astype(BF).reshape(n1, W, C)
-                dbuf[p] = dl
-                gr = g.reshape(n1, W, C)
-
-                @pl.when((p > 0) & (p < 3))
+    def wturn_of(t):
+        return pl.BlockSpec((1, TAP, C), lambda _: (t, 0, 0))
+
+    piece = sds((2, R, W, C))
+
+    def delta_of(g, pre, p, n, first_row, plane):
+        dl = g.astype(F32) * slope(pre[p].reshape(n * W, C).astype(F32))
+        dl = jnp.where(inside(n, W, C, first_row, H, plane, D), dl, 0.0)
+        return dl.astype(BF).reshape(n, W, C)
+
+    def send_all(s_, outs, values):
+        for k in range(4):
+            for t in range(4):
+
+                @pl.when((s_ + k) % 4 == t)
                 def _():
-                    ga[p - 1] = gr[e0 - 1 : e0 - 1 + R]
-                    da[p - 1] = dl[e0 - 1 : e0 - 1 + R]
-
-                return 0
-
-            lax.fori_loop(0, 4, one, 0)
-            wide1 = column(w, 0)
-
-            def two(p, _):
-                g = conv_plane(dbuf, p, wide1, n2).astype(BF)
-                gr = g.reshape(n2, W, C)
-                gb[p] = gr[e0 - 2 : e0 - 2 + R]
-                if final_delta:
-                    dl = g.astype(F32) * slope(pre_b[p].reshape(n2 * W, C).astype(F32))
-                    dl = jnp.where(inside(n2, W, C, s_ * R - e0 + 2, H, 2 * d_ + p, D), dl, 0.0)
-                    db[p] = dl.astype(BF).reshape(n2, W, C)
-                return 0
-
-            lax.fori_loop(0, 2, two, 0)
-            if not final_delta:
-                ds = (da[...], d1_[:, 2 : 2 + R], d2_[...], d3_[:, 4 : 4 + R])
-                gs = (gb[...], ga[...], g2_[...], g3_[...])
-                for k in range(4):
-                    for t in range(4):
-
-                        @pl.when((s_ + k) % 4 == t)
-                        def _():
-                            sends[k][...] = ds[t]
-                            sends[4 + k][...] = gs[t]
-
-        piece = sds((2, R, W, C))
-        out = (piece, piece, piece, sds((2, n2, W, C))) if final_delta else (piece,) * 8
-        held = [] if final_delta else [pltpu.VMEM(piece.shape, BF)] * 3
-        return call(
-            body,
-            out,
-            [SMEM, VMEM, VMEM, VMEM, pl.BlockSpec((2, TAP, C), lambda _: (1 if final_delta else 0, 0, 0)), VMEM]
-            + [VMEM] * (1 if final_delta else 5),
-            held + [pltpu.VMEM((6, R + 2 * e0, W, C), BF), pltpu.VMEM((4, n1, W, C), BF)],
+                    outs[k][...] = values[t]()
+
+    def k3(idx, own, lo, hi, wa, wb, pre_a, pre_b, ga, da, gb, db, x, dbuf):
+        s_, d_ = idx[0], idx[1]
+        assemble(x, lo, own, hi, d_, last)
+
+        def one(p, _):
+            g = conv_plane(x, p, column(wa, 0), R + 6).astype(BF)
+            dl = delta_of(g, pre_a, p, R + 6, s_ * R - 3, 2 * d_ - 1 + p)
+            dbuf[p] = dl
+
+            @pl.when((p > 0) & (p < 3))
+            def _():
+                ga[p - 1] = g.reshape(R + 6, W, C)[3 : 3 + R]
+                da[p - 1] = dl[3 : 3 + R]
+
+            return 0
+
+        lax.fori_loop(0, 4, one, 0)
+
+        def two(p, _):
+            g = conv_plane(dbuf, p, column(wb, 0), R + 4).astype(BF)
+            gb[p] = g.reshape(R + 4, W, C)[2 : 2 + R]
+            db[p] = delta_of(g, pre_b, p, R + 4, s_ * R - 2, 2 * d_ + p)
+            return 0
+
+        lax.fori_loop(0, 2, two, 0)
+
+    g3, d2, g2, d1 = call(
+        k3,
+        (piece, piece, piece, sds((2, R + 4, W, C))),
+        [SMEM, VMEM, VMEM, VMEM, wturn_of(3), wturn_of(2), VMEM, VMEM],
+        [pltpu.VMEM((6, R + 8, W, C), BF), pltpu.VMEM((4, R + 6, W, C), BF)],
+    )(idx, d3, d3_lo, d3_hi, wturn, wturn, pre2, pre1)
+    d1_lo, d1_hi = dep(d1, 1), dep(d1, -1)
+
+    def k4a(idx, own, lo, hi, wa, pre_a, e1, e2, e3, g1, dbuf, *rest):
+        *sends, x = rest
+        s_, d_ = idx[0], idx[1]
+        assemble(x, lo, own, hi, d_, last)
+
+        def one(p, _):
+            g = conv_plane(x, p, column(wa, 0), R + 2).astype(BF)
+            dbuf[p] = delta_of(g, pre_a, p, R + 2, s_ * R - 1, 2 * d_ - 1 + p)
+
+            @pl.when((p > 0) & (p < 3))
+            def _():
+                g1[p - 1] = g.reshape(R + 2, W, C)[1 : 1 + R]
+
+            return 0
+
+        lax.fori_loop(0, 4, one, 0)
+        send_all(
+            s_,
+            sends,
+            (
+                lambda: dbuf[1:3, 1 : 1 + R],
+                lambda: e1[:, 2 : 2 + R],
+                lambda: e2[...],
+                lambda: e3[:, 4 : 4 + R],
+            ),
         )
 
-    g3, d2, g2, d1 = backward_pair(4, True)(idx, d3, d3_lo, d3_hi, wturn, pre2, pre1)
-    d1_lo, d1_hi = dep(d1, 1), dep(d1, -1)
-    sends = backward_pair(2, False)(idx, d1, d1_lo, d1_hi, wturn, pre0, d1, d2, d3, g2, g3)
-    d_got = [sec(sends[k], k) for k in (1, 2, 3)]
-    g_got = [sec(sends[4 + k], k) for k in (1, 2, 3)]
-
-    ROWS = TAP + C
-
-    def kw(idx, x0, x1, x2, x3, e0, e1, e2, e3, keep, away, x, dl, wide, out):
-        s_ = idx[0]
+    g1, d0, *d_send = call(
+        k4a,
+        (piece, sds((4, R + 2, W, C))) + (piece,) * 4,
+        [SMEM, VMEM, VMEM, VMEM, wturn_of(1), VMEM, VMEM, VMEM, VMEM],
+        [pltpu.VMEM((6, R + 4, W, C), BF)],
+    )(idx, d1, d1_lo, d1_hi, wturn, pre0, d1, d2, d3)
+    d_got = [sec(d_send[k], k) for k in (1, 3, 2)]
+    d_got = [d_got[0], d_got[2], d_got[1]]
+
+    def k4b(idx, dbuf, wb, g1, g2, g3, *rest):
+        *sends, g0 = rest
+
+        def two(p, _):
+            g0[p] = conv_plane(dbuf, p, column(wb, 0), R).astype(BF).reshape(R, W, C)
+            return 0
+
+        lax.fori_loop(0, 2, two, 0)
+        send_all(idx[0], sends, (lambda: g0[...], lambda: g1[...], lambda: g2[...], lambda: g3[...]))
+
+    g_send = call(
+        k4b, (piece,) * 4, [SMEM, VMEM, wturn_of(0), VMEM, VMEM, VMEM], [pltpu.VMEM(piece.shape, BF)]
+    )(idx, d0, wturn, g1, g2, g3)
+    g_got = []
+    for k in (1, 2, 3):
+        g_got.append(sec(g_send[k], k))
+
+    def kx(idx, x0, x1, x2, x3, x):
         x[:, 0] = jnp.zeros((4, W, C), BF)
         x[:, H + 1] = jnp.zeros((4, W, C), BF)
-        for k, (xs, es) in enumerate(((x0, e0), (x1, e1), (x2, e2), (x3, e3))):
-            row = ((s_ + 4 - k) % 4) * R
-            x[:, pl.ds(row + 1, R)] = xs[0:4]
-            dl[:, pl.ds(row, R)] = es[...]
-        acc_b = jnp.zeros((1, C), F32)
-        m = H * W
+        for k, xs in enumerate((x0, x1, x2, x3)):
+            x[:, pl.ds(((idx[0] + 4 - k) % 4) * R + 1, R)] = xs[0:4]
+
+    x_all = call(kx, sds((4, H + 2, W, C)), [SMEM] + [VMEM] * 4, [], VMEM)(idx, h_own, *h_got)
+
+    ROWS = TAP + C
+
+    def kw(idx, x, e0, e1, e2, e3, keep, away, dl, wide, out):
+        s_ = idx[0]
+        for k, es in enumerate((e0, e1, e2, e3)):
+            dl[:, pl.ds(((s_ + 4 - k) % 4) * R, R)] = es[...]
+        m = 4 * W
         pos = lax.broadcasted_iota(jnp.int32, (m, C), 0) % W
-        for p in range(2):
-            v = dl[p].reshape(m, C).astype(F32)
-            acc_b = acc_b + jnp.sum(v, axis=0, keepdims=True)
-            wide[p, :, 0:C] = jnp.where(pos == W - 1, 0.0, pltpu.roll(v, m - 1, 0)).astype(BF)
-            wide[p, :, C : 2 * C] = dl[p].reshape(m, C)
-            wide[p, :, 2 * C :] = jnp.where(pos == 0, 0.0, pltpu.roll(v, 1, 0)).astype(BF)
-
-        def one(k, _):
-            a, b = k // 3, k % 3
-            acc = jnp.zeros((C, 3 * C), F32)
+
+        def spread(i, acc):
             for p in range(2):
+                v16 = dl[p, pl.ds(i * 4, 4)].reshape(m, C)
+                v = v16.astype(F32)
+                at = pl.ds(pl.multiple_of(i * m, m), m)
+                wide[p, at, 0:C] = jnp.where(pos == W - 1, 0.0, pltpu.roll(v, m - 1, 0)).astype(BF)
+                wide[p, at, C : 2 * C] = v16
+                wide[p, at, 2 * C :] = jnp.where(pos == 0, 0.0, pltpu.roll(v, 1, 0)).astype(BF)
+                acc = acc + jnp.sum(v.reshape(m // 8, 8, C), axis=0)
+            return acc
+
+        acc_b = jnp.sum(lax.fori_loop(0, H // 4, spread, jnp.zeros((8, C), F32)), axis=0, keepdims=True)
+
+        def one(a, _):
+            acc = jnp.zeros((3 * C, 3 * C), F32)
+            for p in range(2):
+                lhs = jnp.concatenate([x[p + a, b : b + H].reshape(H * W, C) for b in range(3)], axis=1)
                 acc = acc + lax.dot_general(
-                    x[p + a, pl.ds(b, H)].reshape(m, C),
-                    wide[p],
-                    (((0,), (0,)), ((), ())),
-                    preferred_element_type=F32,
+                    lhs, wide[p], (((0,), (0,)), ((), ())), preferred_element_type=F32
                 )
-            for j in range(3):
-                out[3 * k + j] = acc[:, j * C : (j + 1) * C]
-            return 0
-
-        lax.fori_loop(0, 9, one, 0)
+            for b in range(3):
+                for j in range(3):
+                    out[9 * a + 3 * b + j] = acc[b * C : (b + 1) * C, j * C : (j + 1) * C]
+            return 0
+
+        lax.fori_loop(0, 3, one, 0)
         first = lax.broadcasted_iota(jnp.int32, (C, C), 0) == 0
         out[27] = jnp.where(first, jnp.broadcast_to(acc_b, (C, C)), 0.0)
         keep[...] = out[pl.ds(idx[2] * 14, 14)].reshape(RH, C)
@@ -431,14 +489,13 @@
     keep, away = call(
         kw,
         (sds((RH, C), F32), sds((RH, C))),
-        [SMEM] + [VMEM] * 8,
+        [SMEM] + [VMEM] * 5,
         [
-            pltpu.VMEM((4, H + 2, W, C), BF),
             pltpu.VMEM((2, H, W, C), BF),
             pltpu.VMEM((2, H * W, 3 * C), BF),
             pltpu.VMEM((28, C, C), F32),
         ],
-    )(idx, h_own, *h_got, sends[0], *d_got)
+    )(idx, x_all, d_send[0], *d_got)
 
     recv = swap(away)
 
@@ -479,18 +536,7 @@
     half = call(join, sds((4, RQ, C)), [SMEM] + [VMEM] * 4, [], VMEM)(idx, *qs)
     other = swap(half)
 
-    def finish(idx, mine, theirs, w_out, b_out, buf):
-        buf[idx[2]] = mine[...].reshape(RH, C)
-        buf[1 - idx[2]] = theirs[...].reshape(RH, C)
-        w_out[0:RH] = buf[0].astype(F32) * grad_scale
-        w_out[RH:] = buf[1, 0 : TAP - RH].astype(F32) * grad_scale
-        b_out[...] = buf[1, TAP - RH : TAP - RH + 8].astype(F32) * grad_scale
-
-    w_grad, b_grad = call(
-        finish, (sds((TAP, C), F32), sds((8, C), F32)), [SMEM, VMEM, VMEM], [pltpu.VMEM((2, RH, C), BF)]
-    )(idx, half, other)
-
-    def place(idx, a0, a1, a2, a3, b0, b1, b2, b3, oa, ob, sem):
+    def place(idx, a0, a1, a2, a3, b0, b1, b2, b3, mine, oa, ob, w_out, buf, sem):
         copies = []
         for k, (va, vb) in enumerate(((a0, b0), (a1, b1), (a2, b2), (a3, b3))):
             row = ((idx[0] + 4 - k) % 4) * R
@@ -498,14 +544,79 @@
             copies.append(pltpu.make_async_copy(vb, ob.at[:, pl.ds(row, R)], sem.at[2 * k + 1]))
         for cp in copies:
             cp.start()
+        buf[...] = mine[...].reshape(RH, C).astype(F32) * grad_scale
+        for c_, n in ((0, RH), (1, TAP - RH)):
+
+            @pl.when(idx[2] == c_)
+            def _():
+                cp = pltpu.make_async_copy(
+                    buf.at[pl.ds(0, n)], w_out.at[pl.ds(c_ * RH, n)], sem.at[8]
+                )
+                cp.start()
+                cp.wait()
+
         for cp in copies:
             cp.wait()
 
     full = sds((2, H, W, C))
-    out_h, out_g = call(
-        place, (full, full), [SMEM] + [ANY] * 8, [pltpu.SemaphoreType.DMA((8,))], (ANY, ANY)
-    )(idx, h_own, *h_got, sends[4], *g_got)
-    return out_h[None, None], out_g[None, None], w_grad[None], b_grad[0:1]
+    out_h, out_g, w_part = call(
+        place,
+        (full, full, sds((TAP, C), F32)),
+        [SMEM] + [ANY] * 8 + [VMEM],
+        [pltpu.VMEM((RH, C), F32), pltpu.SemaphoreType.DMA((9,))],
+        (ANY, ANY, ANY),
+    )(idx, h_own, *h_got, g_send[0], *g_got, half)
+
+    def finish(idx, mine, theirs, w_in, w_out, b_out, buf, sem):
+        parts = 4
+        row = TAP - RH
+        c_ = idx[2]
+        step = RH // parts
+        for i in range(parts):
+            buf[i * step : (i + 1) * step] = theirs[...].reshape(RH, C)[i * step : (i + 1) * step].astype(F32) * grad_scale
+            n = min(step, row - i * step)
+
+            @pl.when(c_ == 1)
+            def _():
+                pltpu.make_async_copy(
+                    buf.at[pl.ds(i * step, step)], w_out.at[pl.ds(i * step, step)], sem.at[i]
+                ).start()
+
+            @pl.when(c_ == 0)
+            def _():
+                pltpu.make_async_copy(
+                    buf.at[pl.ds(i * step, n)], w_out.at[pl.ds(RH + i * step, n)], sem.at[i]
+                ).start()
+
+        own_b = mine[3, RQ - C : RQ - C + 8].astype(F32) * grad_scale
+        b_out[...] = jnp.where(c_ == 1, own_b, buf[row : row + 8])[0:1]
+        for i in range(parts):
+            n = min(step, row - i * step)
+
+            @pl.when(c_ == 1)
+            def _():
+                pltpu.make_async_copy(
+                    buf.at[pl.ds(i * step, step)], w_out.at[pl.ds(i * step, step)], sem.at[i]
+                ).wait()
+
+            @pl.when(c_ == 0)
+            def _():
+                pltpu.make_async_copy(
+                    buf.at[pl.ds(i * step, n)], w_out.at[pl.ds(RH + i * step, n)], sem.at[i]
+                ).wait()
+
+    w_grad, b_grad = pl.pallas_call(
+        finish,
+        name="finish",
+        grid=(1,),
+        out_shape=(sds((TAP, C), F32), sds((1, C), F32)),
+        in_specs=[SMEM, VMEM, VMEM, ANY],
+        out_specs=(ANY, VMEM),
+        scratch_shapes=[pltpu.VMEM((RH, C), F32), pltpu.SemaphoreType.DMA((4,))],
+        input_output_aliases={3: 0},
+        compiler_params=pltpu.CompilerParams(vmem_limit_bytes=20 * 1024 * 1024),
+    )(idx, half, other, w_part)
+    return out_h[None, None], out_g[None, None], w_grad[None], b_grad
 
 
 def solution(mesh):

time: 180 us -> 171 us (0.950)
  local copies, waits for them, and re-layouts: 10.1 us -> 1.79 us
  waiting for transfers between devices: 80 us -> 77.8 us
    unnamed x32 -> x10, local copies, waits for them, and re-layouts: 7.65 us -> 1.79 us
    ppermute x12, waiting for transfers between devices: 30.7 us -> 28.6 us  [sec(): lax.ppermute(v, 'section', [(i, (i + k) % n_sec) for i in range(n_sec)])]
    dynamic_slice x2 -> x0, local copies, waits for them, and re-layouts: 1.97 us -> none  [window(): return lax.dynamic_slice_in_dim(padded, s * R, R + 2 * ext, 1)]
    pallas_call x6 -> x8, Pallas kernels: 20.8 us -> 20.3 us  [the longest x1 5.45 us: shards(): call(k3, (piece, piece, piece, sds((2, R + 4, W, C))), [SMEM, VMEM, VMEM,...]
  transfers between devices with their start and end apart: 34 -> 34, of which waited for: 21 -> 21; matrix products, arithmetic and copies ran while one was open for 1% -> 0% of each run, Pallas kernels for 10% -> 12%
where the time goes in v1:
time: 171 us
  waiting for transfers between devices  77.8 us (45%)
  Pallas kernels  46.5 us (27%)
  starting transfers between devices  43.3 us (25%)
  local copies, waits for them, and re-layouts  1.79 us (1%)
    ppermute x12, waiting for transfers between devices, sec(): lax.ppermute(v, 'section', [(i, (i + k) % n_sec) for i in range(n_sec)])  28.6 us
    ppermute x8, waiting for transfers between devices, dep(): lax.ppermute(v, 'depth', [(i, (i + k) % n_dep) for i in range(n_dep)])  28.4 us
    ppermute x12, starting transfers between devices, sec(): lax.ppermute(v, 'section', [(i, (i + k) % n_sec) for i in range(n_sec)])  15.5 us
    ppermute x6, waiting for transfers between devices, xdep(): lax.ppermute(v, 'depth', [(i, i // 4 * 4 + (i + k) % 4) for i in range(n_...  13.5 us
    ppermute x8, starting transfers between devices, dep(): lax.ppermute(v, 'depth', [(i, (i + k) % n_dep) for i in range(n_dep)])  9.54 us
    pallas_call x1, Pallas kernels, shards(): call(k1, (sds((4, R, W, C)), sds((4, R + 2, W, C)), sds((4, R, W, C)), sd...  9.31 us
    ppermute x5, starting transfers between devices, swap(): return lax.ppermute(v, 'dp', [(0, 1), (1, 0)])  8.86 us
    ppermute x6, starting transfers between devices, xdep(): lax.ppermute(v, 'depth', [(i, i // 4 * 4 + (i + k) % 4) for i in range(n_...  7.89 us
  transfers between devices with their start and end apart: 34, of which 21 were waited for; matrix products, arithmetic and copies ran while one was open for 0% of the time, Pallas kernels for 12%

profile of v1, /device:TPU:1, one launch (start us, length us, event | category | flops | bytes accessed | tf_op | source)
XLA Modules:
  0.0 170.6 jit_solution(2681707104296127939)
XLA Ops:
  0.6 1.3 shard_map.75
  2.0 4.6 %collective-permute-start.4 = (bf16[1744,128]{1,0:T(8,128)(2,1)S(1)}, bf16[1744,128]{1,0:T(8,128)(2,1)S(1)}, u32[]{:S(2)}, u32[]{:S(2)}) collective-permute-start(bf16[1744,128]{1,0:T(8,128)(2,1)S(1)} %get-tuple-element.49.ob), channel_id=1, source_target_pairs={{0,48},{16,0},{32,16},{48,32},{1,49},{17,1},{33,17},{49,33},{2,50}... | collective-permute-start | bytes 1339400 | tf_op jit(solution)/shard_map/ppermute | solution.py:139
  8.1 16.9 %collective-permute-done.4.g3.b3_ = bf16[1744,128]{1,0:T(8,128)(2,1)S(1)} collective-permute-done((bf16[1744,128]{1,0:T(8,128)(2,1)S(1)}, bf16[1744,128]{1,0:T(8,128)(2,1)S(1)}, u32[]{:S(2)}, u32[]{:S(2)}) %collective-permute-start.4) | collective-permute-done | bytes 446496 | tf_op jit(solution)/shard_map/ppermute | solution.py:139
  25.0 1.7 collective-permute-start.7
  26.7 2.6 %collective-permute-done.2.g1.b1_ = bf16[1744,128]{1,0:T(8,128)(2,1)S(1)} collective-permute-done((bf16[1744,128]{1,0:T(8,128)(2,1)S(1)}, bf16[1744,128]{1,0:T(8,128)(2,1)S(1)}, u32[]{:S(2)}, u32[]{:S(2)}) %collective-permute-start.2) | collective-permute-done | bytes 446496 | tf_op jit(solution)/shard_map/ppermute | solution.py:139
  29.3 0.8 collective-permute-start.5
  30.1 4.9 %collective-permute-start.1 = (bf16[2,24,32,128]{3,2,1,0:T(8,128)(2,1)S(1)}, bf16[2,24,32,128]{3,2,1,0:T(8,128)(2,1)}, u32[]{:S(2)}, u32[]{:S(2)}) collective-permute-start(bf16[2,24,32,128]{3,2,1,0:T(8,128)(2,1)S(1)} %get-tuple-element.48.own), channel_id=1, source_target_pairs={{0,15},{1,0},{2,1},{3,2},{4,3},{5,4},{6,5},{7,6},{8,7},{9,8},{10,9... | collective-permute-start | bytes 1179656 | tf_op jit(solution)/shard_map/ppermute | solution.py:142
  35.1 8.4 %collective-permute-done.1.hi = bf16[2,24,32,128]{3,2,1,0:T(8,128)(2,1)} collective-permute-done((bf16[2,24,32,128]{3,2,1,0:T(8,128)(2,1)S(1)}, bf16[2,24,32,128]{3,2,1,0:T(8,128)(2,1)}, u32[]{:S(2)}, u32[]{:S(2)}) %collective-permute-start.1) | collective-permute-done | bytes 393248 | tf_op jit(solution)/shard_map/ppermute | solution.py:142
  43.5 5.3 %collective-permute-done.lo = bf16[2,24,32,128]{3,2,1,0:T(8,128)(2,1)} collective-permute-done((bf16[2,24,32,128]{3,2,1,0:T(8,128)(2,1)S(1)}, bf16[2,24,32,128]{3,2,1,0:T(8,128)(2,1)}, u32[]{:S(2)}, u32[]{:S(2)}) %collective-permute-start) | collective-permute-done | bytes 393248 | tf_op jit(solution)/shard_map/ppermute | solution.py:142
  48.8 1.0 copy-done.2
  49.8 9.3 %shard_map.76 = (bf16[4,8,32,128]{3,2,1,0:T(8,128)(2,1)S(1)}, bf16[4,10,32,128]{3,2,1,0:T(8,128)(2,1)S(1)}, bf16[4,8,32,128]{3,2,1,0:T(8,128)(2,1)S(1)}, bf16[2,...) custom-call(s32[3]{0:T(128)S(1)} %pad_add_fusion.idx, bf16[2,24,32,128]{3,2,1,0:T(8,128)(2,1)S(1)} %get-tuple-element.48.own, ...), custom_call_target="tpu_custom_call" | custom-call | tf_op jit(solution)/shard_map/pallas_call | solution.py:237
  59.5 1.2 collective-permute-start.8
  60.7 6.6 %shard_map.77.wa.wb = bf16[4,3456,128]{2,1,0:T(8,128)(2,1)S(1)} custom-call(s32[3]{0:T(128)S(1)} %pad_add_fusion.idx, bf16[3456,128]{1,0:T(8,128)(2,1)S(1)} %bitcast.12, bf16[1744,128]{1,0:T(8,128)(2,1)S(1)} %collective-permute-done.2.g1.b1_, bf16[1744,128]{1,0:T(8,128)(2,1)S(1)} %collective-permute-done.3.g2.b2_, ...), custom_call_target="tpu_custom_call" | custom-call | tf_op jit(solution)/shard_map/pallas_call | solution.py:257
  67.4 3.6 %collective-permute-done.8.lo = bf16[2,20,32,128]{3,2,1,0:T(8,128)(2,1)S(1)} collective-permute-done((bf16[2,20,32,128]{3,2,1,0:T(8,128)(2,1)S(1)}, bf16[2,20,32,128]{3,2,1,0:T(8,128)(2,1)S(1)}, u32[]{:S(2)}, u32[]{:S(2)}) %collective-permute-start.8) | collective-permute-done | bytes 327712 | tf_op jit(solution)/shard_map/ppermute | solution.py:142
  71.0 7.5 %shard_map.78 = (bf16[4,8,32,128]{3,2,1,0:T(8,128)(2,1)S(1)}, bf16[4,14,32,128]{3,2,1,0:T(8,128)(2,1)S(1)}, bf16[4,8,32,128]{3,2,1,0:T(8,128)(2,1)S(1)}, bf16[2,...) custom-call(s32[3]{0:T(128)S(1)} %pad_add_fusion.idx, bf16[2,20,32,128]{3,2,1,0:T(8,128)(2,1)S(1)} %get-tuple-element.52.own, ...), custom_call_target="tpu_custom_call" | custom-call | tf_op jit(solution)/shard_map/pallas_call | solution.py:300
  78.9 1.2 collective-permute-start.13
  80.1 0.8 shard_map.79
  81.0 2.1 %collective-permute-start.11 = (bf16[6,8,32,128]{3,2,1,0:T(8,128)(2,1)S(1)}, bf16[6,8,32,128]{3,2,1,0:T(8,128)(2,1)S(1)}, u32[]{:S(2)}, u32[]{:S(2)}) collective-permute-start(bf16[6,8,32,128]{3,2,1,0:T(8,128)(2,1)S(1)} %get-tuple-element.60), channel_id=1, source_target_pairs={{0,32},{16,48},{32,0},{48,16},{1,33},{17,49},{33,1},{49,17},{2,34}... | collective-permute-start | bytes 1179656 | tf_op jit(solution)/shard_map/ppermute | solution.py:139
  83.6 0.8 collective-permute-done.14.hi
  84.4 3.6 %collective-permute-done.13.lo = bf16[2,16,32,128]{3,2,1,0:T(8,128)(2,1)S(1)} collective-permute-done((bf16[2,16,32,128]{3,2,1,0:T(8,128)(2,1)S(1)}, bf16[2,16,32,128]{3,2,1,0:T(8,128)(2,1)S(1)}, u32[]{:S(2)}, u32[]{:S(2)}) %collective-permute-start.13) | collective-permute-done | bytes 262176 | tf_op jit(solution)/shard_map/ppermute | solution.py:142
  88.1 5.5 %shard_map.80 = (bf16[2,8,32,128]{3,2,1,0:T(8,128)(2,1)S(1)}, bf16[2,8,32,128]{3,2,1,0:T(8,128)(2,1)S(1)}, bf16[2,8,32,128]{3,2,1,0:T(8,128)(2,1)S(1)}, bf16[2,12,32,128]{3,2,1,0:T(8,128)(2,1)S(1)}) custom-call(s32[3]{0:T(128)S(1)} %pad_add_fusion.idx, bf16[2,16,32,128]{3,2,1,0:T(8,128)(2,1)S(1)} %get-tuple-element.62.own.e3, ...), custom_call_target="tpu_custom_call" | custom-call | tf_op jit(solution)/shard_map/pallas_call | solution.py:379
  93.9 1.2 collective-permute-start.15
  95.1 3.3 %collective-permute-done.16.hi = bf16[2,12,32,128]{3,2,1,0:T(8,128)(2,1)S(1)} collective-permute-done((bf16[2,12,32,128]{3,2,1,0:T(8,128)(2,1)S(1)}, bf16[2,12,32,128]{3,2,1,0:T(8,128)(2,1)S(1)}, u32[]{:S(2)}, u32[]{:S(2)}) %collective-permute-start.16) | collective-permute-done | bytes 196640 | tf_op jit(solution)/shard_map/ppermute | solution.py:142
  98.4 3.3 %collective-permute-done.15.lo = bf16[2,12,32,128]{3,2,1,0:T(8,128)(2,1)S(1)} collective-permute-done((bf16[2,12,32,128]{3,2,1,0:T(8,128)(2,1)S(1)}, bf16[2,12,32,128]{3,2,1,0:T(8,128)(2,1)S(1)}, u32[]{:S(2)}, u32[]{:S(2)}) %collective-permute-start.15) | collective-permute-done | bytes 196640 | tf_op jit(solution)/shard_map/ppermute | solution.py:142
  101.7 3.3 %shard_map.81 = (bf16[2,8,32,128]{3,2,1,0:T(8,128)(2,1)S(1)}, bf16[4,10,32,128]{3,2,1,0:T(8,128)(2,1)S(1)}, bf16[2,8,32,128]{3,2,1,0:T(8,128)(2,1)S(1)}, bf16[2,...) custom-call(s32[3]{0:T(128)S(1)} %pad_add_fusion.idx, ...), custom_call_target="tpu_custom_call" | custom-call | tf_op jit(solution)/shard_map/pallas_call | solution.py:414
  105.1 2.1 %collective-permute-start.21 = (bf16[2,8,32,128]{3,2,1,0:T(8,128)(2,1)S(1)}, bf16[2,8,32,128]{3,2,1,0:T(8,128)(2,1)S(1)}, u32[]{:S(2)}, u32[]{:S(2)}) collective-permute-start(bf16[2,8,32,128]{3,2,1,0:T(8,128)(2,1)S(1)} %get-tuple-element.79), channel_id=1, source_target_pairs={{0,32},{16,48},{32,0},{48,16},{1,33},{17,49},{33,1},{49,17},{2,34}... | collective-permute-start | bytes 393224 | tf_op jit(solution)/shard_map/ppermute | solution.py:139
  107.2 1.3 collective-permute-start.22
  109.1 2.4 %collective-permute-done.20.e1 = bf16[2,8,32,128]{3,2,1,0:T(8,128)(2,1)S(1)} collective-permute-done((bf16[2,8,32,128]{3,2,1,0:T(8,128)(2,1)S(1)}, bf16[2,8,32,128]{3,2,1,0:T(8,128)(2,1)S(1)}, u32[]{:S(2)}, u32[]{:S(2)}) %collective-permute-start.20) | collective-permute-done | bytes 131104 | tf_op jit(solution)/shard_map/ppermute | solution.py:139
  112.1 4.1 %shard_map.84 = (f32[1792,128]{1,0:T(8,128)S(1)}, bf16[1792,128]{1,0:T(8,128)(2,1)S(1)}) custom-call(s32[3]{0:T(128)S(1)} %pad_add_fusion.idx, bf16[4,34,32,128]{3,2,1,0:T(8,128)(2,1)S(1)} %shard_map.83.x, bf16[2,8,32,128]{3,2,1,0:T(8,128)(2,1)S(1)} %get-tuple-element.77.e0, bf16[2,8,32,128]{3,2,1,0:T(8,128)(2,1)S(1)} %collective-permute-done.20.e1, ...), custom_call_target="tpu_custom_call" | custom-call | tf_op jit(solution)/shard_map/pallas_call | solution.py:489
  116.2 5.5 %collective-permute-start.23 = (bf16[1792,128]{1,0:T(8,128)(2,1)S(1)}, bf16[1792,128]{1,0:T(8,128)(2,1)S(1)}, u32[]{:S(2)}, u32[]{:S(2)}) collective-permute-start(bf16[1792,128]{1,0:T(8,128)(2,1)S(1)} %get-tuple-element.82), channel_id=1, source_target_pairs={{0,64},{64,0},{1,65},{65,1},{2,66},{66,2},{3,67},{67,3},{4,68},{68... | collective-permute-start | bytes 1376264 | tf_op jit(solution)/shard_map/ppermute | solution.py:145
  121.7 1.4 collective-permute-done.23.recv
  124.1 2.6 %collective-permute-start.26 = (bf16[448,128]{1,0:T(8,128)(2,1)S(1)}, bf16[448,128]{1,0:T(8,128)(2,1)S(1)}, u32[]{:S(2)}, u32[]{:S(2)}) collective-permute-start(bf16[448,128]{1,0:T(8,128)(2,1)S(1)} %get-tuple-element.86), channel_id=1, source_target_pairs={{0,3},{1,0},{2,1},{3,2},{4,7},{5,4},{6,5},{7,6},{8,11},{9,8},{10,9... | collective-permute-start | bytes 344072 | tf_op jit(solution)/shard_map/ppermute | solution.py:148
  126.6 5.7 %collective-permute-done.24 = bf16[448,128]{1,0:T(8,128)(2,1)S(1)} collective-permute-done((bf16[448,128]{1,0:T(8,128)(2,1)S(1)}, bf16[448,128]{1,0:T(8,128)(2,1)S(1)}, u32[]{:S(2)}, u32[]{:S(2)}) %collective-permute-start.24) | collective-permute-done | bytes 114720 | tf_op jit(solution)/shard_map/ppermute | solution.py:148
  132.6 1.4 collective-permute-start.27
  133.9 2.2 %collective-permute-done.29.q3 = bf16[448,128]{1,0:T(8,128)(2,1)S(1)} collective-permute-done((bf16[448,128]{1,0:T(8,128)(2,1)S(1)}, bf16[448,128]{1,0:T(8,128)(2,1)S(1)}, u32[]{:S(2)}, u32[]{:S(2)}) %collective-permute-start.29) | collective-permute-done | bytes 114720 | tf_op jit(solution)/shard_map/ppermute | solution.py:151
  136.1 1.6 collective-permute-done.28.q2
  137.7 2.1 %collective-permute-done.27.q1 = bf16[448,128]{1,0:T(8,128)(2,1)S(1)} collective-permute-done((bf16[448,128]{1,0:T(8,128)(2,1)S(1)}, bf16[448,128]{1,0:T(8,128)(2,1)S(1)}, u32[]{:S(2)}, u32[]{:S(2)}) %collective-permute-start.27) | collective-permute-done | bytes 114720 | tf_op jit(solution)/shard_map/ppermute | solution.py:151
  140.5 4.5 %collective-permute-start.32 = (bf16[448,128]{1,0:T(8,128)(2,1)S(1)}, bf16[448,128]{1,0:T(8,128)(2,1)S(1)}, u32[]{:S(2)}, u32[]{:S(2)}) collective-permute-start(bf16[448,128]{1,0:T(8,128)(2,1)S(1)} %shard_map.86.q0), channel_id=1, source_target_pairs={{0,3},{1,0},{2,1},{3,2},{4,7},{5,4},{6,5},{7,6},{8,11},{9,8},{10,9... | collective-permute-start | bytes 344072 | tf_op jit(solution)/shard_map/ppermute | solution.py:148
  145.6 3.9 %collective-permute-done.32.q3 = bf16[448,128]{1,0:T(8,128)(2,1)S(1)} collective-permute-done((bf16[448,128]{1,0:T(8,128)(2,1)S(1)}, bf16[448,128]{1,0:T(8,128)(2,1)S(1)}, u32[]{:S(2)}, u32[]{:S(2)}) %collective-permute-start.32) | collective-permute-done | bytes 114720 | tf_op jit(solution)/shard_map/ppermute | solution.py:148
  150.2 3.2 %collective-permute-done.30.q1 = bf16[448,128]{1,0:T(8,128)(2,1)S(1)} collective-permute-done((bf16[448,128]{1,0:T(8,128)(2,1)S(1)}, bf16[448,128]{1,0:T(8,128)(2,1)S(1)}, u32[]{:S(2)}, u32[]{:S(2)}) %collective-permute-start.30) | collective-permute-done | bytes 114720 | tf_op jit(solution)/shard_map/ppermute | solution.py:148
  154.0 0.9 collective-permute-start.33
  154.9 1.6 shard_map.82
  156.5 1.3 collective-permute-start.17
  157.8 2.4 %collective-permute-start.18 = (bf16[2,8,32,128]{3,2,1,0:T(8,128)(2,1)S(1)}, bf16[2,8,32,128]{3,2,1,0:T(8,128)(2,1)S(1)}, u32[]{:S(2)}, u32[]{:S(2)}) collective-permute-start(bf16[2,8,32,128]{3,2,1,0:T(8,128)(2,1)S(1)} %get-tuple-element.75), channel_id=1, source_target_pairs={{0,32},{16,48},{32,0},{48,16},{1,33},{17,49},{33,1},{49,17},{2,34}... | collective-permute-start | bytes 393224 | tf_op jit(solution)/shard_map/ppermute | solution.py:139
  160.5 2.3 %collective-permute-done.17.b1 = bf16[2,8,32,128]{3,2,1,0:T(8,128)(2,1)S(1)} collective-permute-done((bf16[2,8,32,128]{3,2,1,0:T(8,128)(2,1)S(1)}, bf16[2,8,32,128]{3,2,1,0:T(8,128)(2,1)S(1)}, u32[]{:S(2)}, u32[]{:S(2)}) %collective-permute-start.17) | collective-permute-done | bytes 131104 | tf_op jit(solution)/shard_map/ppermute | solution.py:139
  162.8 3.7 %collective-permute-done.18.b2 = bf16[2,8,32,128]{3,2,1,0:T(8,128)(2,1)S(1)} collective-permute-done((bf16[2,8,32,128]{3,2,1,0:T(8,128)(2,1)S(1)}, bf16[2,8,32,128]{3,2,1,0:T(8,128)(2,1)S(1)}, u32[]{:S(2)}, u32[]{:S(2)}) %collective-permute-start.18) | collective-permute-done | bytes 131104 | tf_op jit(solution)/shard_map/ppermute | solution.py:139
  166.5 1.9 %shard_map.88 = (bf16[2,32,32,128]{3,2,1,0:T(8,128)(2,1)}, bf16[2,32,32,128]{3,2,1,0:T(8,128)(2,1)}, f32[3456,128]{1,0:T(8,128)}) custom-call(s32[3]{0:T(128)S(1)} %pad_add_fusion.idx, bf16[6,8,32,128]{3,2,1,0:T(8,128)(2,1)S(1)} %get-tuple-element.58.x0.a0, bf16[6,8,32,128]{3,2,1,0:T(8,128)(2,1)S(1)} %collective-permute-done.10.x1.a1, ...), custom_call_target="tpu_custom_call" | custom-call | tf_op jit(solution)/shard_map/pallas_call | solution.py:562
  168.4 2.0 %finish.1 = (f32[3456,128]{1,0:T(8,128)}, f32[1,128]{1,0:T(1,128)}) custom-call(s32[3]{0:T(128)S(1)} %pad_add_fusion.idx, bf16[4,448,128]{2,1,0:T(8,128)(2,1)S(1)} %shard_map.87.mine, bf16[4,448,128]{2,1,0:T(8,128)(2,1)S(1)} %collective-permute-done.33.theirs, f32[3456,128]{1,0:T(8,128)} %get-tuple-element.89.w_in), custom_call_target="tpu_custom_call", output_to_operand_aliasing={{0}: (3, {})} | custom-call | tf_op jit(solution)/shard_map/finish/pallas_call | solution.py:608
  (47 shorter events, 8.7 us)
Async XLA Ops:
  0.6 48.2 %copy-start = (bf16[1,3456,128]{2,1,0:T(8,128)(2,1)S(1)}, bf16[1,3456,128]{2,1,0:T(8,128)(2,1)}, u32[]{:S(2)}) copy-start(bf16[1,3456,128]{2,1,0:T(8,128)(2,1)} %param.5) | copy-start | bytes 2654212
  2.0 23.0 %collective-permute-start.4 = (bf16[1744,128]{1,0:T(8,128)(2,1)S(1)}, bf16[1744,128]{1,0:T(8,128)(2,1)S(1)}, u32[]{:S(2)}, u32[]{:S(2)}) collective-permute-start(bf16[1744,128]{1,0:T(8,128)(2,1)S(1)} %get-tuple-element.49.ob), channel_id=1, source_target_pairs={{0,48},{16,0},{32,16},{48,32},{1,49},{17,1},{33,17},{49,33},{2,50}... | collective-permute-start | bytes 1339400 | tf_op jit(solution)/shard_map/ppermute | solution.py:139
  6.6 20.0 %collective-permute-start.3 = (bf16[1744,128]{1,0:T(8,128)(2,1)S(1)}, bf16[1744,128]{1,0:T(8,128)(2,1)S(1)}, u32[]{:S(2)}, u32[]{:S(2)}) collective-permute-start(bf16[1744,128]{1,0:T(8,128)(2,1)S(1)} %get-tuple-element.49.ob), channel_id=1, source_target_pairs={{0,32},{16,48},{32,0},{48,16},{1,33},{17,49},{33,1},{49,17},{2,34}... | collective-permute-start | bytes 1339400 | tf_op jit(solution)/shard_map/ppermute | solution.py:139
  6.6 22.7 %collective-permute-start.2 = (bf16[1744,128]{1,0:T(8,128)(2,1)S(1)}, bf16[1744,128]{1,0:T(8,128)(2,1)S(1)}, u32[]{:S(2)}, u32[]{:S(2)}) collective-permute-start(bf16[1744,128]{1,0:T(8,128)(2,1)S(1)} %get-tuple-element.49.ob), channel_id=1, source_target_pairs={{0,16},{16,32},{32,48},{48,0},{1,17},{17,33},{33,49},{49,1},{2,18}... | collective-permute-start | bytes 1339400 | tf_op jit(solution)/shard_map/ppermute | solution.py:139
  7.3 0.8 copy-start.1
  25.0 23.8 %collective-permute-start.7 = (bf16[1744,128]{1,0:T(8,128)(2,1)S(1)}, bf16[1744,128]{1,0:T(8,128)(2,1)S(1)}, u32[]{:S(2)}, u32[]{:S(2)}) collective-permute-start(bf16[1744,128]{1,0:T(8,128)(2,1)S(1)} %collective-permute-done.4.g3.b3_), channel_id=1, source_target_pairs={{0,64},{64,0},{1,65},{65,1},{2,66},{66,2},{3,67},{67,3},{4,68},{68... | collective-permute-start | bytes 1339400 | tf_op jit(solution)/shard_map/ppermute | solution.py:145
  26.6 22.2 %collective-permute-start.6 = (bf16[1744,128]{1,0:T(8,128)(2,1)S(1)}, bf16[1744,128]{1,0:T(8,128)(2,1)S(1)}, u32[]{:S(2)}, u32[]{:S(2)}) collective-permute-start(bf16[1744,128]{1,0:T(8,128)(2,1)S(1)} %collective-permute-done.3.g2.b2_), channel_id=1, source_target_pairs={{0,64},{64,0},{1,65},{65,1},{2,66},{66,2},{3,67},{67,3},{4,68},{68... | collective-permute-start | bytes 1339400 | tf_op jit(solution)/shard_map/ppermute | solution.py:145
  29.3 19.5 %collective-permute-start.5 = (bf16[1744,128]{1,0:T(8,128)(2,1)S(1)}, bf16[1744,128]{1,0:T(8,128)(2,1)}, u32[]{:S(2)}, u32[]{:S(2)}) collective-permute-start(bf16[1744,128]{1,0:T(8,128)(2,1)S(1)} %collective-permute-done.2.g1.b1_), channel_id=1, source_target_pairs={{0,64},{64,0},{1,65},{65,1},{2,66},{66,2},{3,67},{67,3},{4,68},{68... | collective-permute-start | bytes 1339400 | tf_op jit(solution)/shard_map/ppermute | solution.py:145
  30.1 13.4 %collective-permute-start.1 = (bf16[2,24,32,128]{3,2,1,0:T(8,128)(2,1)S(1)}, bf16[2,24,32,128]{3,2,1,0:T(8,128)(2,1)}, u32[]{:S(2)}, u32[]{:S(2)}) collective-permute-start(bf16[2,24,32,128]{3,2,1,0:T(8,128)(2,1)S(1)} %get-tuple-element.48.own), channel_id=1, source_target_pairs={{0,15},{1,0},{2,1},{3,2},{4,3},{5,4},{6,5},{7,6},{8,7},{9,8},{10,9... | collective-permute-start | bytes 1179656 | tf_op jit(solution)/shard_map/ppermute | solution.py:142
  35.0 13.8 %collective-permute-start = (bf16[2,24,32,128]{3,2,1,0:T(8,128)(2,1)S(1)}, bf16[2,24,32,128]{3,2,1,0:T(8,128)(2,1)}, u32[]{:S(2)}, u32[]{:S(2)}) collective-permute-start(bf16[2,24,32,128]{3,2,1,0:T(8,128)(2,1)S(1)} %get-tuple-element.48.own), channel_id=1, source_target_pairs={{0,1},{1,2},{2,3},{3,4},{4,5},{5,6},{6,7},{7,8},{8,9},{9,10},{10,1... | collective-permute-start | bytes 1179656 | tf_op jit(solution)/shard_map/ppermute | solution.py:142
  48.8 1.0 copy-start.2
  59.2 11.8 %copy-start.3 = (bf16[1744,128]{1,0:T(8,128)(2,1)S(1)}, bf16[1744,128]{1,0:T(8,128)(2,1)}, u32[]{:S(2)}) copy-start(bf16[1744,128]{1,0:T(8,128)(2,1)} %copy-done.1) | copy-start | bytes 1339396
  59.2 11.8 %copy-start.4 = (bf16[1,2,32,32,128]{4,3,2,1,0:T(8,128)(2,1)S(1)}, bf16[1,2,32,32,128]{4,3,2,1,0:T(8,128)(2,1)}, u32[]{:S(2)}) copy-start(bf16[1,2,32,32,128]{4,3,2,1,0:T(8,128)(2,1)} %param.7) | copy-start | bytes 1572868
  59.2 8.2 %collective-permute-start.9 = (bf16[2,20,32,128]{3,2,1,0:T(8,128)(2,1)S(1)}, bf16[2,20,32,128]{3,2,1,0:T(8,128)(2,1)S(1)}, u32[]{:S(2)}, u32[]{:S(2)}) collective-permute-start(bf16[2,20,32,128]{3,2,1,0:T(8,128)(2,1)S(1)} %get-tuple-element.52.own), channel_id=1, source_target_pairs={{0,15},{1,0},{2,1},{3,2},{4,3},{5,4},{6,5},{7,6},{8,7},{9,8},{10,9... | collective-permute-start | bytes 983048 | tf_op jit(solution)/shard_map/ppermute | solution.py:142
  59.5 11.4 %collective-permute-start.8 = (bf16[2,20,32,128]{3,2,1,0:T(8,128)(2,1)S(1)}, bf16[2,20,32,128]{3,2,1,0:T(8,128)(2,1)S(1)}, u32[]{:S(2)}, u32[]{:S(2)}) collective-permute-start(bf16[2,20,32,128]{3,2,1,0:T(8,128)(2,1)S(1)} %get-tuple-element.52.own), channel_id=1, source_target_pairs={{0,1},{1,2},{2,3},{3,4},{4,5},{5,6},{6,7},{7,8},{8,9},{9,10},{10,1... | collective-permute-start | bytes 983048 | tf_op jit(solution)/shard_map/ppermute | solution.py:142
  78.5 5.9 %collective-permute-start.14 = (bf16[2,16,32,128]{3,2,1,0:T(8,128)(2,1)S(1)}, bf16[2,16,32,128]{3,2,1,0:T(8,128)(2,1)S(1)}, u32[]{:S(2)}, u32[]{:S(2)}) collective-permute-start(bf16[2,16,32,128]{3,2,1,0:T(8,128)(2,1)S(1)} %get-tuple-element.62.own.e3), channel_id=1, source_target_pairs={{0,15},{1,0},{2,1},{3,2},{4,3},{5,4},{6,5},{7,6},{8,7},{9,8},{10,9... | collective-permute-start | bytes 786440 | tf_op jit(solution)/shard_map/ppermute | solution.py:142
  78.9 9.2 %collective-permute-start.13 = (bf16[2,16,32,128]{3,2,1,0:T(8,128)(2,1)S(1)}, bf16[2,16,32,128]{3,2,1,0:T(8,128)(2,1)S(1)}, u32[]{:S(2)}, u32[]{:S(2)}) collective-permute-start(bf16[2,16,32,128]{3,2,1,0:T(8,128)(2,1)S(1)} %get-tuple-element.62.own.e3), channel_id=1, source_target_pairs={{0,1},{1,2},{2,3},{3,4},{4,5},{5,6},{6,7},{7,8},{8,9},{9,10},{10,1... | collective-permute-start | bytes 786440 | tf_op jit(solution)/shard_map/ppermute | solution.py:142
  80.9 26.3 %collective-permute-start.10 = (bf16[6,8,32,128]{3,2,1,0:T(8,128)(2,1)S(1)}, bf16[6,8,32,128]{3,2,1,0:T(8,128)(2,1)S(1)}, u32[]{:S(2)}, u32[]{:S(2)}) collective-permute-start(bf16[6,8,32,128]{3,2,1,0:T(8,128)(2,1)S(1)} %get-tuple-element.59), channel_id=1, source_target_pairs={{0,16},{16,32},{32,48},{48,0},{1,17},{17,33},{33,49},{49,1},{2,18}... | collective-permute-start | bytes 1179656 | tf_op jit(solution)/shard_map/ppermute | solution.py:139
  81.0 27.5 %collective-permute-start.11 = (bf16[6,8,32,128]{3,2,1,0:T(8,128)(2,1)S(1)}, bf16[6,8,32,128]{3,2,1,0:T(8,128)(2,1)S(1)}, u32[]{:S(2)}, u32[]{:S(2)}) collective-permute-start(bf16[6,8,32,128]{3,2,1,0:T(8,128)(2,1)S(1)} %get-tuple-element.60), channel_id=1, source_target_pairs={{0,32},{16,48},{32,0},{48,16},{1,33},{17,49},{33,1},{49,17},{2,34}... | collective-permute-start | bytes 1179656 | tf_op jit(solution)/shard_map/ppermute | solution.py:139
  83.0 25.4 %collective-permute-start.12 = (bf16[6,8,32,128]{3,2,1,0:T(8,128)(2,1)S(1)}, bf16[6,8,32,128]{3,2,1,0:T(8,128)(2,1)S(1)}, u32[]{:S(2)}, u32[]{:S(2)}) collective-permute-start(bf16[6,8,32,128]{3,2,1,0:T(8,128)(2,1)S(1)} %get-tuple-element.61), channel_id=1, source_target_pairs={{0,48},{16,0},{32,16},{48,32},{1,49},{17,1},{33,17},{49,33},{2,50}... | collective-permute-start | bytes 1179656 | tf_op jit(solution)/shard_map/ppermute | solution.py:139
  93.5 4.9 %collective-permute-start.16 = (bf16[2,12,32,128]{3,2,1,0:T(8,128)(2,1)S(1)}, bf16[2,12,32,128]{3,2,1,0:T(8,128)(2,1)S(1)}, u32[]{:S(2)}, u32[]{:S(2)}) collective-permute-start(bf16[2,12,32,128]{3,2,1,0:T(8,128)(2,1)S(1)} %get-tuple-element.66.own.e1), channel_id=1, source_target_pairs={{0,15},{1,0},{2,1},{3,2},{4,3},{5,4},{6,5},{7,6},{8,7},{9,8},{10,9... | collective-permute-start | bytes 589832 | tf_op jit(solution)/shard_map/ppermute | solution.py:142
  93.9 7.8 %collective-permute-start.15 = (bf16[2,12,32,128]{3,2,1,0:T(8,128)(2,1)S(1)}, bf16[2,12,32,128]{3,2,1,0:T(8,128)(2,1)S(1)}, u32[]{:S(2)}, u32[]{:S(2)}) collective-permute-start(bf16[2,12,32,128]{3,2,1,0:T(8,128)(2,1)S(1)} %get-tuple-element.66.own.e1), channel_id=1, source_target_pairs={{0,1},{1,2},{2,3},{3,4},{4,5},{5,6},{6,7},{7,8},{8,9},{9,10},{10,1... | collective-permute-start | bytes 589832 | tf_op jit(solution)/shard_map/ppermute | solution.py:142
  105.0 6.5 %collective-permute-start.20 = (bf16[2,8,32,128]{3,2,1,0:T(8,128)(2,1)S(1)}, bf16[2,8,32,128]{3,2,1,0:T(8,128)(2,1)S(1)}, u32[]{:S(2)}, u32[]{:S(2)}) collective-permute-start(bf16[2,8,32,128]{3,2,1,0:T(8,128)(2,1)S(1)} %get-tuple-element.78), channel_id=1, source_target_pairs={{0,16},{16,32},{32,48},{48,0},{1,17},{17,33},{33,49},{49,1},{2,18}... | collective-permute-start | bytes 393224 | tf_op jit(solution)/shard_map/ppermute | solution.py:139
  105.1 6.4 %collective-permute-start.21 = (bf16[2,8,32,128]{3,2,1,0:T(8,128)(2,1)S(1)}, bf16[2,8,32,128]{3,2,1,0:T(8,128)(2,1)S(1)}, u32[]{:S(2)}, u32[]{:S(2)}) collective-permute-start(bf16[2,8,32,128]{3,2,1,0:T(8,128)(2,1)S(1)} %get-tuple-element.79), channel_id=1, source_target_pairs={{0,32},{16,48},{32,0},{48,16},{1,33},{17,49},{33,1},{49,17},{2,34}... | collective-permute-start | bytes 393224 | tf_op jit(solution)/shard_map/ppermute | solution.py:139
  107.2 4.9 %collective-permute-start.22 = (bf16[2,8,32,128]{3,2,1,0:T(8,128)(2,1)S(1)}, bf16[2,8,32,128]{3,2,1,0:T(8,128)(2,1)S(1)}, u32[]{:S(2)}, u32[]{:S(2)}) collective-permute-start(bf16[2,8,32,128]{3,2,1,0:T(8,128)(2,1)S(1)} %get-tuple-element.80), channel_id=1, source_target_pairs={{0,48},{16,0},{32,16},{48,32},{1,49},{17,1},{33,17},{49,33},{2,50}... | collective-permute-start | bytes 393224 | tf_op jit(solution)/shard_map/ppermute | solution.py:139
  116.2 7.0 %collective-permute-start.23 = (bf16[1792,128]{1,0:T(8,128)(2,1)S(1)}, bf16[1792,128]{1,0:T(8,128)(2,1)S(1)}, u32[]{:S(2)}, u32[]{:S(2)}) collective-permute-start(bf16[1792,128]{1,0:T(8,128)(2,1)S(1)} %get-tuple-element.82), channel_id=1, source_target_pairs={{0,64},{64,0},{1,65},{65,1},{2,66},{66,2},{3,67},{67,3},{4,68},{68... | collective-permute-start | bytes 1376264 | tf_op jit(solution)/shard_map/ppermute | solution.py:145
  123.9 8.4 %collective-permute-start.24 = (bf16[448,128]{1,0:T(8,128)(2,1)S(1)}, bf16[448,128]{1,0:T(8,128)(2,1)S(1)}, u32[]{:S(2)}, u32[]{:S(2)}) collective-permute-start(bf16[448,128]{1,0:T(8,128)(2,1)S(1)} %get-tuple-element.84), channel_id=1, source_target_pairs={{0,1},{1,2},{2,3},{3,0},{4,5},{5,6},{6,7},{7,4},{8,9},{9,10},{10,1... | collective-permute-start | bytes 344072 | tf_op jit(solution)/shard_map/ppermute | solution.py:148
  124.0 8.3 %collective-permute-start.25 = (bf16[448,128]{1,0:T(8,128)(2,1)S(1)}, bf16[448,128]{1,0:T(8,128)(2,1)S(1)}, u32[]{:S(2)}, u32[]{:S(2)}) collective-permute-start(bf16[448,128]{1,0:T(8,128)(2,1)S(1)} %get-tuple-element.85), channel_id=1, source_target_pairs={{0,2},{1,3},{2,0},{3,1},{4,6},{5,7},{6,4},{7,5},{8,10},{9,11},{10,... | collective-permute-start | bytes 344072 | tf_op jit(solution)/shard_map/ppermute | solution.py:148
  124.1 8.3 %collective-permute-start.26 = (bf16[448,128]{1,0:T(8,128)(2,1)S(1)}, bf16[448,128]{1,0:T(8,128)(2,1)S(1)}, u32[]{:S(2)}, u32[]{:S(2)}) collective-permute-start(bf16[448,128]{1,0:T(8,128)(2,1)S(1)} %get-tuple-element.86), channel_id=1, source_target_pairs={{0,3},{1,0},{2,1},{3,2},{4,7},{5,4},{6,5},{7,6},{8,11},{9,8},{10,9... | collective-permute-start | bytes 344072 | tf_op jit(solution)/shard_map/ppermute | solution.py:148
  132.4 3.7 %collective-permute-start.29 = (bf16[448,128]{1,0:T(8,128)(2,1)S(1)}, bf16[448,128]{1,0:T(8,128)(2,1)S(1)}, u32[]{:S(2)}, u32[]{:S(2)}) collective-permute-start(bf16[448,128]{1,0:T(8,128)(2,1)S(1)} %add_convert_fusion.q0), channel_id=1, source_target_pairs={{0,12},{1,13},{2,14},{3,15},{4,0},{5,1},{6,2},{7,3},{8,4},{9,5},{1... | collective-permute-start | bytes 344072 | tf_op jit(solution)/shard_map/ppermute | solution.py:151
  132.5 5.3 %collective-permute-start.28 = (bf16[448,128]{1,0:T(8,128)(2,1)S(1)}, bf16[448,128]{1,0:T(8,128)(2,1)S(1)}, u32[]{:S(2)}, u32[]{:S(2)}) collective-permute-start(bf16[448,128]{1,0:T(8,128)(2,1)S(1)} %add_convert_fusion.q0), channel_id=1, source_target_pairs={{0,8},{1,9},{2,10},{3,11},{4,12},{5,13},{6,14},{7,15},{8,0},{9,1},... | collective-permute-start | bytes 344072 | tf_op jit(solution)/shard_map/ppermute | solution.py:151
  132.6 7.2 %collective-permute-start.27 = (bf16[448,128]{1,0:T(8,128)(2,1)S(1)}, bf16[448,128]{1,0:T(8,128)(2,1)S(1)}, u32[]{:S(2)}, u32[]{:S(2)}) collective-permute-start(bf16[448,128]{1,0:T(8,128)(2,1)S(1)} %add_convert_fusion.q0), channel_id=1, source_target_pairs={{0,4},{1,5},{2,6},{3,7},{4,8},{5,9},{6,10},{7,11},{8,12},{9,13},{1... | collective-permute-start | bytes 344072 | tf_op jit(solution)/shard_map/ppermute | solution.py:151
  140.5 9.1 %collective-permute-start.32 = (bf16[448,128]{1,0:T(8,128)(2,1)S(1)}, bf16[448,128]{1,0:T(8,128)(2,1)S(1)}, u32[]{:S(2)}, u32[]{:S(2)}) collective-permute-start(bf16[448,128]{1,0:T(8,128)(2,1)S(1)} %shard_map.86.q0), channel_id=1, source_target_pairs={{0,3},{1,0},{2,1},{3,2},{4,7},{5,4},{6,5},{7,6},{8,11},{9,8},{10,9... | collective-permute-start | bytes 344072 | tf_op jit(solution)/shard_map/ppermute | solution.py:148
  145.0 5.2 %collective-permute-start.31 = (bf16[448,128]{1,0:T(8,128)(2,1)S(1)}, bf16[448,128]{1,0:T(8,128)(2,1)S(1)}, u32[]{:S(2)}, u32[]{:S(2)}) collective-permute-start(bf16[448,128]{1,0:T(8,128)(2,1)S(1)} %shard_map.86.q0), channel_id=1, source_target_pairs={{0,2},{1,3},{2,0},{3,1},{4,6},{5,7},{6,4},{7,5},{8,10},{9,11},{10,... | collective-permute-start | bytes 344072 | tf_op jit(solution)/shard_map/ppermute | solution.py:148
  145.0 8.4 %collective-permute-start.30 = (bf16[448,128]{1,0:T(8,128)(2,1)S(1)}, bf16[448,128]{1,0:T(8,128)(2,1)S(1)}, u32[]{:S(2)}, u32[]{:S(2)}) collective-permute-start(bf16[448,128]{1,0:T(8,128)(2,1)S(1)} %shard_map.86.q0), channel_id=1, source_target_pairs={{0,1},{1,2},{2,3},{3,0},{4,5},{5,6},{6,7},{7,4},{8,9},{9,10},{10,1... | collective-permute-start | bytes 344072 | tf_op jit(solution)/shard_map/ppermute | solution.py:148
  154.0 14.4 %collective-permute-start.33 = (bf16[4,448,128]{2,1,0:T(8,128)(2,1)S(1)}, bf16[4,448,128]{2,1,0:T(8,128)(2,1)S(1)}, u32[]{:S(2)}, u32[]{:S(2)}) collective-permute-start(bf16[4,448,128]{2,1,0:T(8,128)(2,1)S(1)} %shard_map.87.mine), channel_id=1, source_target_pairs={{0,64},{64,0},{1,65},{65,1},{2,66},{66,2},{3,67},{67,3},{4,68},{68... | collective-permute-start | bytes 1376264 | tf_op jit(solution)/shard_map/ppermute | solution.py:145
  156.5 6.3 %collective-permute-start.17 = (bf16[2,8,32,128]{3,2,1,0:T(8,128)(2,1)S(1)}, bf16[2,8,32,128]{3,2,1,0:T(8,128)(2,1)S(1)}, u32[]{:S(2)}, u32[]{:S(2)}) collective-permute-start(bf16[2,8,32,128]{3,2,1,0:T(8,128)(2,1)S(1)} %get-tuple-element.74), channel_id=1, source_target_pairs={{0,16},{16,32},{32,48},{48,0},{1,17},{17,33},{33,49},{49,1},{2,18}... | collective-permute-start | bytes 393224 | tf_op jit(solution)/shard_map/ppermute | solution.py:139
  157.8 8.7 %collective-permute-start.18 = (bf16[2,8,32,128]{3,2,1,0:T(8,128)(2,1)S(1)}, bf16[2,8,32,128]{3,2,1,0:T(8,128)(2,1)S(1)}, u32[]{:S(2)}, u32[]{:S(2)}) collective-permute-start(bf16[2,8,32,128]{3,2,1,0:T(8,128)(2,1)S(1)} %get-tuple-element.75), channel_id=1, source_target_pairs={{0,32},{16,48},{32,0},{48,16},{1,33},{17,49},{33,1},{49,17},{2,34}... | collective-permute-start | bytes 393224 | tf_op jit(solution)/shard_map/ppermute | solution.py:139
  160.1 6.4 %collective-permute-start.19 = (bf16[2,8,32,128]{3,2,1,0:T(8,128)(2,1)S(1)}, bf16[2,8,32,128]{3,2,1,0:T(8,128)(2,1)S(1)}, u32[]{:S(2)}, u32[]{:S(2)}) collective-permute-start(bf16[2,8,32,128]{3,2,1,0:T(8,128)(2,1)S(1)} %get-tuple-element.76), channel_id=1, source_target_pairs={{0,48},{16,0},{32,16},{48,32},{1,49},{17,1},{33,17},{49,33},{2,50}... | collective-permute-start | bytes 393224 | tf_op jit(solution)/shard_map/ppermute | solution.py:139

commit v2 on v1

--- a/solution.py
+++ b/solution.py
@@ -70,39 +70,42 @@
     return q * (1.0 + pre * (1.0 - q))
 
 
-def assemble(dst, lo, own, hi, d, last):
-    zero = jnp.zeros(lo.shape, BF)
-    dst[0:2] = jnp.where(d > 0, lo[...], zero)
+def assemble(dst, far, own, near, d, last):
+    odd = d % 2
+    zero = jnp.zeros(far.shape, BF)
+    dst[pl.ds(4 * odd, 2)] = jnp.where((d > 0) & (d < last), far[...], zero)
     dst[2:4] = own[...]
-    dst[4:6] = jnp.where(d < last, hi[...], zero)
-
-
-def halves(s, c, t, own, got, swp, dst, sem, half):
-    mine = pl.multiple_of(c * half, 16)
-    other = pl.multiple_of((1 - c) * half, 16)
+    dst[pl.ds(4 - 4 * odd, 2)] = near[...]
+
+
+def layer_copies(s, c, t, own, got, swp, dst, sem, rows):
     k = (s + 4 - t) % 4
 
-    def pair(first, second):
-        return (
-            pltpu.make_async_copy(first, dst.at[pl.ds(mine, half)], sem.at[0]),
-            pltpu.make_async_copy(second, dst.at[pl.ds(other, half)], sem.at[1]),
-        )
+    def four(parts):
+        out = []
+        for i, part in enumerate(parts):
+            at = pl.multiple_of((2 * c + i if i < 2 else 2 * (1 - c) + i - 2) * rows, 16)
+            out.append((part, at, i))
+        return [
+            pltpu.make_async_copy(own.at[pl.ds(at, rows)] if part is None else part.at[pl.ds(0, rows)], dst.at[pl.ds(at, rows)], sem.at[i])
+            for part, at, i in out
+        ]
 
     def start():
         @pl.when(k == 0)
         def _():
-            for cp in pair(own.at[pl.ds(mine, half)], own.at[pl.ds(other, half)]):
+            for cp in four((None,) * 4):
                 cp.start()
 
         for i in range(3):
 
             @pl.when(k == i + 1)
             def _():
-                for cp in pair(got[i].at[pl.ds(0, half)], swp[i].at[pl.ds(0, half)]):
+                for cp in four((*got[2 * i : 2 * i + 2], *swp[2 * i : 2 * i + 2])):
                     cp.start()
 
     def wait():
-        for cp in pair(own.at[pl.ds(mine, half)], own.at[pl.ds(other, half)]):
+        for cp in four((None,) * 4):
             cp.wait()
 
     return start, wait
@@ -133,61 +136,76 @@
     idx = jnp.stack([s, d, c]).astype(jnp.int32)
     TAP = 27 * C
     HALF = TAP // 2
-    HB = HALF + 16
+    QR = HALF // 2
+    QB = QR + 16
 
     def sec(v, k):
-        return lax.ppermute(v, "section", [(i, (i + k) % n_sec) for i in range(n_sec)])
-
-    def dep(v, k):
-        return lax.ppermute(v, "depth", [(i, (i + k) % n_dep) for i in range(n_dep)])
+        return lax.ppermute(v, "section", [(i, i ^ k) for i in range(n_sec)])
+
+    def both(v):
+        result = []
+        for first in (1, 0):
+            pairs = [(i, i + 1) for i in range(first, n_dep - 1, 2)]
+            result.append(lax.ppermute(v, "depth", pairs + [(b, a) for a, b in pairs]))
+        return result
 
     def swap(v):
         return lax.ppermute(v, "dp", [(0, 1), (1, 0)])
 
     def xdep(v, k):
-        return lax.ppermute(v, "depth", [(i, i // 4 * 4 + (i + k) % 4) for i in range(n_dep)])
+        return lax.ppermute(v, "depth", [(i, i ^ k) for i in range(n_dep)])
 
     def ydep(v, k):
-        return lax.ppermute(v, "depth", [(i, (i + 4 * k) % n_dep) for i in range(n_dep)])
+        return lax.ppermute(v, "depth", [(i, i ^ (4 * k)) for i in range(n_dep)])
 
     own_w = weights[0]
 
-    def prepare(vol, w, b, h0, half, pad, row, sem):
+    def prepare(vol, w, b, h0, part_a, part_b, own_b, pad, row, sem):
         s_, c_ = lax.axis_index("section"), lax.axis_index("dp")
-        pull_w = pltpu.make_async_copy(w.at[c_], half.at[pl.ds(0, HALF)], sem.at[0])
-        pull_v = pltpu.make_async_copy(vol, pad.at[:, pl.ds(8, H)], sem.at[1])
-        pull_b = pltpu.make_async_copy(b, row, sem.at[2])
-        pull_w.start()
-        pull_v.start()
-        pull_b.start()
+        pulls = [
+            pltpu.make_async_copy(w.at[2 * c_], part_a.at[pl.ds(0, QR)], sem.at[0]),
+            pltpu.make_async_copy(w.at[2 * c_ + 1], part_b.at[pl.ds(0, QR)], sem.at[1]),
+            pltpu.make_async_copy(b, row, sem.at[2]),
+            pltpu.make_async_copy(vol, pad.at[:, pl.ds(8, H)], sem.at[3]),
+        ]
+        for cp in pulls:
+            cp.start()
         pad[:, 0:8] = jnp.zeros((PL, 8, W, C), BF)
         pad[:, H + 8 :] = jnp.zeros((PL, 8, W, C), BF)
-        pull_b.wait()
-        half[HALF:] = jnp.broadcast_to(row[...], (16, C))
-        pull_v.wait()
+        for cp in pulls:
+            cp.wait()
+        bias = jnp.broadcast_to(row[...], (16, C))
+        part_a[QR:] = bias
+        part_b[QR:] = bias
+        own_b[...] = bias
         h0[...] = pad[:, pl.ds(s_ * R, R + 16)]
-        pull_w.wait()
-
-    h0, own_half = call(
+
+    h0, part_a, part_b, own_b = call(
         prepare,
-        (sds((PL, R + 16, W, C)), sds((HB, C))),
+        (sds((PL, R + 16, W, C)), sds((QB, C)), sds((QB, C)), sds((16, C))),
         [HBM, HBM, HBM],
-        [pltpu.VMEM((PL, H + 16, W, C), BF), pltpu.VMEM((1, C), BF), pltpu.SemaphoreType.DMA((3,))],
-    )(in_hbm(volume[0]), in_hbm(own_w.reshape(2, HALF, C)), in_hbm(biases))
-    h0_lo, h0_hi = dep(h0, 1), dep(h0, -1)
-
-    near = [sec(own_half, k) for k in (1, 3)]
-    got = [near[0], sec(own_half, 2), near[1]]
+        [pltpu.VMEM((PL, H + 16, W, C), BF), pltpu.VMEM((1, C), BF), pltpu.SemaphoreType.DMA((4,))],
+    )(in_hbm(volume[0]), in_hbm(own_w.reshape(4, QR, C)), in_hbm(biases))
+    h0_lo, h0_hi = both(h0)
+
+    def ring(v, k):
+        return lax.ppermute(v, "section", [(i, (i + k) % n_sec) for i in range(n_sec)])
+
+    a1, b3 = ring(part_a, 1), ring(part_b, 3)
+    b1, a3 = ring(part_b, 1), ring(part_a, 3)
+    a2, b2 = ring(a1, 1), ring(b3, 3)
+    got = (a1, b1, a2, b2, a3, b3)
     swapped = [swap(g) for g in got]
     all_w = (own_w, *got, *swapped)
-    W_SPECS = [HBM] + [ANY] * 6
-    all_b = (own_half, *got)
-    tail_rows = pl.BlockSpec((16, C), lambda _: (HALF // 16, 0))
-    B_SPECS = [tail_rows] * 4
-
-    def turn(idx, own, g1, g2, g3, s1, s2, s3, out, buf, sem):
+    W_SPECS = [HBM] + [ANY] * 12
+    all_b = (own_b, a1, a2, a3)
+    tail_rows = pl.BlockSpec((16, C), lambda _: (QR // 16, 0))
+    B_SPECS = [VMEM] + [tail_rows] * 3
+
+    def turn(idx, own, *rest):
+        got_, swp_, (out, buf, sem) = rest[:6], rest[6:12], rest[12:]
         steps = [
-            halves(idx[0], idx[2], t, own, (g1, g2, g3), (s1, s2, s3), buf.at[t], sem.at[t], HALF) for t in range(4)
+            layer_copies(idx[0], idx[2], t, own, got_, swp_, buf.at[t], sem.at[t], QR) for t in range(4)
         ]
         for start, _ in steps:
             start()
@@ -200,10 +218,12 @@
 
             lax.fori_loop(0, 27, one, 0, unroll=3)
 
-    def k1(idx, own, lo, hi, ow, g1, g2, g3, s1, s2, s3, ob, b1_, b2_, b3_, h0e, pre0, h1e, pre1, h2, x, h1, w, sem):
+    def k1(idx, own, lo, hi, ow, *rest):
+        got_, swp_, rest = rest[:6], rest[6:12], rest[12:]
+        ob, b1_, b2_, b3_, h0e, pre0, h1e, pre1, h2, x, h1, w, sem = rest
         s_, d_ = idx[0], idx[1]
         steps = [
-            halves(s_, idx[2], t, ow, (g1, g2, g3), (s1, s2, s3), w.at[t], sem.at[t], HALF) for t in range(2)
+            layer_copies(s_, idx[2], t, ow, got_, swp_, w.at[t], sem.at[t], QR) for t in range(2)
         ]
         for start, _ in steps:
             start()
@@ -248,21 +268,23 @@
             pltpu.VMEM((6, R + 16, W, C), BF),
             pltpu.VMEM((4, R + 14, W, C), BF),
             pltpu.VMEM((2, TAP, C), BF),
-            pltpu.SemaphoreType.DMA((2, 2)),
+            pltpu.SemaphoreType.DMA((2, 4)),
         ],
     )(idx, h0, h0_lo, h0_hi, *all_w, *all_b)
 
-    h2_lo, h2_hi = dep(h2, 1), dep(h2, -1)
+    h2_lo, h2_hi = both(h2)
 
     wturn = call(
-        turn, sds((4, TAP, C)), [SMEM] + W_SPECS, [pltpu.VMEM((4, TAP, C), BF), pltpu.SemaphoreType.DMA((4, 2))], VMEM
+        turn, sds((4, TAP, C)), [SMEM] + W_SPECS, [pltpu.VMEM((4, TAP, C), BF), pltpu.SemaphoreType.DMA((4, 4))], VMEM
     )(idx, *all_w)
     h2_lo, h2_hi, wturn = lax.optimization_barrier((h2_lo, h2_hi, wturn))
 
-    def k2(idx, own, lo, hi, ow, g1, g2, g3, s1, s2, s3, ob, b1_, b2_, b3_, cot, h2e, pre2, h3e, h4, d3, x, h3, w, gpad, sem):
+    def k2(idx, own, lo, hi, ow, *rest):
+        got_, swp_, rest = rest[:6], rest[6:12], rest[12:]
+        ob, b1_, b2_, b3_, cot, h2e, pre2, h3e, h4, d3, x, h3, w, gpad, sem = rest
         s_, d_ = idx[0], idx[1]
         steps = [
-            halves(s_, idx[2], t + 2, ow, (g1, g2, g3), (s1, s2, s3), w.at[t], sem.at[t], HALF) for t in range(2)
+            layer_copies(s_, idx[2], t + 2, ow, got_, swp_, w.at[t], sem.at[t], QR) for t in range(2)
         ]
         for start, _ in steps:
             start()
@@ -312,18 +334,18 @@
             pltpu.VMEM((4, R + 10, W, C), BF),
             pltpu.VMEM((2, TAP, C), BF),
             pltpu.VMEM((PL, H + 8, W, C), BF),
-            pltpu.SemaphoreType.DMA((2, 2)),
+            pltpu.SemaphoreType.DMA((2, 4)),
         ],
     )(idx, h2, h2_lo, h2_hi, *all_w, *all_b, cotangent[0])
 
-    d3_lo, d3_hi = dep(d3, 1), dep(d3, -1)
+    d3_lo, d3_hi = both(d3)
 
     def pack(idx, x0, x1, x2, x3, x4, own, a1, a2, a3):
         xs = (x0, x1, x2, x3)
         for k, out in enumerate((own, a1, a2, a3)):
             for t in range(4):
 
-                @pl.when((idx[0] + k) % 4 == t)
+                @pl.when((idx[0] ^ k) == t)
                 def _():
                     out[0:4] = xs[t][...]
                     out[4:6] = x4[...] if t == 3 else xs[t + 1][1:3]
@@ -346,7 +368,7 @@
         for k in range(4):
             for t in range(4):
 
-                @pl.when((s_ + k) % 4 == t)
+                @pl.when((s_ ^ k) == t)
                 def _():
                     outs[k][...] = values[t]()
 
@@ -382,7 +404,7 @@
         [SMEM, VMEM, VMEM, VMEM, wturn_of(3), wturn_of(2), VMEM, VMEM],
         [pltpu.VMEM((6, R + 8, W, C), BF), pltpu.VMEM((4, R + 6, W, C), BF)],
     )(idx, d3, d3_lo, d3_hi, wturn, wturn, pre2, pre1)
-    d1_lo, d1_hi = dep(d1, 1), dep(d1, -1)
+    d1_lo, d1_hi = both(d1)
 
     def k4a(idx, own, lo, hi, wa, pre_a, e1, e2, e3, g1, dbuf, *rest):
         *sends, x = rest
@@ -441,7 +463,7 @@
         x[:, 0] = jnp.zeros((4, W, C), BF)
         x[:, H + 1] = jnp.zeros((4, W, C), BF)
         for k, xs in enumerate((x0, x1, x2, x3)):
-            x[:, pl.ds(((idx[0] + 4 - k) % 4) * R + 1, R)] = xs[0:4]
+            x[:, pl.ds((idx[0] ^ k) * R + 1, R)] = xs[0:4]
 
     x_all = call(kx, sds((4, H + 2, W, C)), [SMEM] + [VMEM] * 4, [], VMEM)(idx, h_own, *h_got)
 
@@ -450,7 +472,7 @@
     def kw(idx, x, e0, e1, e2, e3, keep, away, dl, wide, out):
         s_ = idx[0]
         for k, es in enumerate((e0, e1, e2, e3)):
-            dl[:, pl.ds(((s_ + 4 - k) % 4) * R, R)] = es[...]
+            dl[:, pl.ds((s_ ^ k) * R, R)] = es[...]
         m = 4 * W
         pos = lax.broadcasted_iota(jnp.int32, (m, C), 0) % W
 
@@ -504,7 +526,7 @@
         buf[...] = keep[...].reshape(4, RQ, C) + recv[...].reshape(4, RQ, C).astype(F32)
         mine[...] = buf[x]
         for k, q in enumerate((q1, q2, q3), 1):
-            q[...] = buf[(x + k) % 4].astype(BF)
+            q[...] = buf[x ^ k].astype(BF)
 
     quart = sds((RQ, C))
     q, *qs = call(
@@ -520,9 +542,9 @@
         y = idx[1] // 4
         for k, r in enumerate((q0, q1, q2, q3)):
             buf[k] = r[...].astype(F32)
-        acc = buf[y % 4]
+        acc = buf[y]
         for j in range(1, 4):
-            acc = acc + buf[(y + 4 - j) % 4]
+            acc = acc + buf[y ^ j]
         out[...] = acc.astype(BF)
 
     q = call(ordered, sds((RQ, C)), [SMEM] + [VMEM] * 4, [pltpu.VMEM((4, RQ, C), F32)], VMEM)(idx, q, *ys)
@@ -531,7 +553,7 @@
     def join(idx, q0, q1, q2, q3, out):
         x = idx[1] % 4
         for k, r in enumerate((q0, q1, q2, q3)):
-            out[(x + 4 - k) % 4] = r[...]
+            out[x ^ k] = r[...]
 
     half = call(join, sds((4, RQ, C)), [SMEM] + [VMEM] * 4, [], VMEM)(idx, *qs)
     other = swap(half)
@@ -539,7 +561,7 @@
     def place(idx, a0, a1, a2, a3, b0, b1, b2, b3, mine, oa, ob, w_out, buf, sem):
         copies = []
         for k, (va, vb) in enumerate(((a0, b0), (a1, b1), (a2, b2), (a3, b3))):
-            row = ((idx[0] + 4 - k) % 4) * R
+            row = (idx[0] ^ k) * R
             copies.append(pltpu.make_async_copy(va.at[4:6], oa.at[:, pl.ds(row, R)], sem.at[2 * k]))
             copies.append(pltpu.make_async_copy(vb, ob.at[:, pl.ds(row, R)], sem.at[2 * k + 1]))
         for cp in copies:

time: 171 us -> 162 us (0.947)
  waiting for transfers between devices: 77.8 us -> 38.6 us
  starting transfers between devices: 43.3 us -> 65.6 us
  Pallas kernels: 46.5 us -> 50.6 us
  local copies, waits for them, and re-layouts: 1.79 us -> 5.23 us
    ppermute x29 -> x32, waiting for transfers between devices: 76.4 us -> 36 us  [the longest x6 11.6 us: xdep(): return lax.ppermute(v, 'depth', [(i, i ^ k) for i in range(n_dep)])]
    ppermute x29 -> x32, starting transfers between devices: 34.4 us -> 51.7 us  [the longest x8 13.9 us: both(): result.append(lax.ppermute(v, 'depth', pairs + [(b, a) for a, b in pairs]))]
    ppermute x5 -> x8, starting transfers between devices: 8.86 us -> 13.9 us  [swap(): return lax.ppermute(v, 'dp', [(0, 1), (1, 0)])]
    unnamed x10 -> x16, local copies, waits for them, and re-layouts: 1.79 us -> 5.23 us
    pallas_call x1, Pallas kernels: 6.61 us -> 8.51 us  [shards(): call(turn, sds((4, TAP, C)), [SMEM] + W_SPECS, [pltpu.VMEM((4, TAP, C), B...]
  transfers between devices with their start and end apart: 34 -> 40, of which waited for: 21 -> 20; matrix products, arithmetic and copies ran while one was open for 0% -> 0% of each run, Pallas kernels for 12% -> 14%
where the time goes in v2:
time: 162 us; the launch traced here: 161 us
  starting transfers between devices  65.6 us (40%)
  Pallas kernels  50.6 us (31%)
  waiting for transfers between devices  38.6 us (24%)
  local copies, waits for them, and re-layouts  5.23 us (3%)
    ppermute x8, starting transfers between devices, both(): result.append(lax.ppermute(v, 'depth', pairs + [(b, a) for a, b in pairs]))  13.9 us
    ppermute x8, starting transfers between devices, swap(): return lax.ppermute(v, 'dp', [(0, 1), (1, 0)])  13.9 us
    ppermute x9, starting transfers between devices, sec(): return lax.ppermute(v, 'section', [(i, i ^ k) for i in range(n_sec)])  13 us
    ppermute x6, starting transfers between devices, xdep(): return lax.ppermute(v, 'depth', [(i, i ^ k) for i in range(n_dep)])  13 us
    ppermute x6, waiting for transfers between devices, xdep(): return lax.ppermute(v, 'depth', [(i, i ^ k) for i in range(n_dep)])  11.6 us
    ppermute x9, waiting for transfers between devices, sec(): return lax.ppermute(v, 'section', [(i, i ^ k) for i in range(n_sec)])  11.2 us
    pallas_call x1, Pallas kernels, shards(): call(k1, (sds((4, R, W, C)), sds((4, R + 2, W, C)), sds((4, R, W, C)), sd...  10.1 us
    pallas_call x1, Pallas kernels, shards(): call(k2, (sds((4, R, W, C)), sds((4, R + 6, W, C)), sds((4, R, W, C)), sd...  9.02 us
  transfers between devices with their start and end apart: 40, of which 20 were waited for; matrix products, arithmetic and copies ran while one was open for 0% of the time, Pallas kernels for 14%

profile of v2, /device:TPU:1, one launch (start us, length us, event | category | flops | bytes accessed | tf_op | source)
XLA Modules:
  0.0 161.2 jit_solution(3833168576402866435)
XLA Ops:
  0.6 1.4 shard_map.75
  2.1 4.6 %collective-permute-start.7 = (bf16[880,128]{1,0:T(8,128)(2,1)S(1)}, bf16[880,128]{1,0:T(8,128)(2,1)S(1)}, u32[]{:S(2)}, u32[]{:S(2)}) collective-permute-start(bf16[880,128]{1,0:T(8,128)(2,1)S(1)} %get-tuple-element.51), channel_id=1, source_target_pairs={{0,48},{16,0},{32,16},{48,32},{1,49},{17,1},{33,17},{49,33},{2,50}... | collective-permute-start | bytes 675848 | tf_op jit(solution)/shard_map/ppermute | solution.py:192
  6.7 2.7 %collective-permute-start.5 = (bf16[880,128]{1,0:T(8,128)(2,1)S(1)}, bf16[880,128]{1,0:T(8,128)(2,1)S(1)}, u32[]{:S(2)}, u32[]{:S(2)}) collective-permute-start(bf16[880,128]{1,0:T(8,128)(2,1)S(1)} %get-tuple-element.52), channel_id=1, source_target_pairs={{0,48},{16,0},{32,16},{48,32},{1,49},{17,1},{33,17},{49,33},{2,50}... | collective-permute-start | bytes 675848 | tf_op jit(solution)/shard_map/ppermute | solution.py:192
  9.4 1.2 collective-permute-start.1
  12.3 1.7 %collective-permute-done.2.rest_0_.rest_13_ = bf16[880,128]{1,0:T(8,128)(2,1)S(1)} collective-permute-done((bf16[880,128]{1,0:T(8,128)(2,1)S(1)}, bf16[880,128]{1,0:T(8,128)(2,1)S(1)}, u32[]{:S(2)}, u32[]{:S(2)}) %collective-permute-start.2) | collective-permute-done | bytes 225312 | tf_op jit(solution)/shard_map/ppermute | solution.py:192
  14.0 3.2 %collective-permute-start.12 = (bf16[880,128]{1,0:T(8,128)(2,1)S(1)}, bf16[880,128]{1,0:T(8,128)(2,1)S(1)}, u32[]{:S(2)}, u32[]{:S(2)}) collective-permute-start(bf16[880,128]{1,0:T(8,128)(2,1)S(1)} %collective-permute-done.7.rest_4_.rest_15_), channel_id=1, source_target_pairs={{0,64},{64,0},{1,65},{65,1},{2,66},{66,2},{3,67},{67,3},{4,68},{68... | collective-permute-start | bytes 675848 | tf_op jit(solution)/shard_map/ppermute | solution.py:153
  17.3 1.6 collective-permute-done.3.rest_1_
  18.9 1.1 collective-permute-start.6
  20.7 1.0 collective-permute-start.8
  23.0 2.1 %collective-permute-done.4.rest_2_.rest_14_ = bf16[880,128]{1,0:T(8,128)(2,1)S(1)} collective-permute-done((bf16[880,128]{1,0:T(8,128)(2,1)S(1)}, bf16[880,128]{1,0:T(8,128)(2,1)S(1)}, u32[]{:S(2)}, u32[]{:S(2)}) %collective-permute-start.4) | collective-permute-done | bytes 225312 | tf_op jit(solution)/shard_map/ppermute | solution.py:192
  25.1 1.3 collective-permute-start.10
  31.0 10.1 %shard_map.76 = (bf16[4,8,32,128]{3,2,1,0:T(8,128)(2,1)S(1)}, bf16[4,10,32,128]{3,2,1,0:T(8,128)(2,1)S(1)}, bf16[4,8,32,128]{3,2,1,0:T(8,128)(2,1)S(1)}, bf16[2,...) custom-call(s32[3]{0:T(128)S(1)} %pad_add_fusion.idx, bf16[2,24,32,128]{3,2,1,0:T(8,128)(2,1)S(1)} %copy-done.3, ...), custom_call_target="tpu_custom_call" | custom-call | tf_op jit(solution)/shard_map/pallas_call | solution.py:257
  41.1 2.5 %collective-permute-start.15 = (bf16[2,20,32,128]{3,2,1,0:T(8,128)(2,1)S(1)}, bf16[2,20,32,128]{3,2,1,0:T(8,128)(2,1)S(1)}, u32[]{:S(2)}, u32[]{:S(2)}) collective-permute-start(bf16[2,20,32,128]{3,2,1,0:T(8,128)(2,1)S(1)} %get-tuple-element.56.own), channel_id=1, source_target_pairs={{0,1},{2,3},{4,5},{6,7},{8,9},{10,11},{12,13},{14,15},{1,0},{3,2},... | collective-permute-start | bytes 983048 | tf_op jit(solution)/shard_map/ppermute | solution.py:149
  44.3 8.5 %shard_map.77.wa.wb = bf16[4,3456,128]{2,1,0:T(8,128)(2,1)S(1)} custom-call(s32[3]{0:T(128)S(1)} %pad_add_fusion.idx, bf16[3456,128]{1,0:T(8,128)(2,1)S(1)} %bitcast.12, bf16[880,128]{1,0:T(8,128)(2,1)S(1)} %collective-permute-done.2.rest_0_.rest_13_, bf16[880,128]{1,0:T(8,128)(2,1)S(1)} %collective-permute-done.3.rest_1_, ...), custom_call_target="tpu_custom_call" | custom-call | tf_op jit(solution)/shard_map/pallas_call | solution.py:277
  52.8 9.0 %shard_map.78 = (bf16[4,8,32,128]{3,2,1,0:T(8,128)(2,1)S(1)}, bf16[4,14,32,128]{3,2,1,0:T(8,128)(2,1)S(1)}, bf16[4,8,32,128]{3,2,1,0:T(8,128)(2,1)S(1)}, bf16[2,...) custom-call(s32[3]{0:T(128)S(1)} %pad_add_fusion.idx, bf16[2,20,32,128]{3,2,1,0:T(8,128)(2,1)S(1)} %get-tuple-element.56.own, ...), custom_call_target="tpu_custom_call" | custom-call | tf_op jit(solution)/shard_map/pallas_call | solution.py:322
  61.8 3.7 %collective-permute-start.20 = (bf16[2,16,32,128]{3,2,1,0:T(8,128)(2,1)S(1)}, bf16[2,16,32,128]{3,2,1,0:T(8,128)(2,1)S(1)}, u32[]{:S(2)}, u32[]{:S(2)}) collective-permute-start(bf16[2,16,32,128]{3,2,1,0:T(8,128)(2,1)S(1)} %get-tuple-element.66.own.e3), channel_id=1, source_target_pairs={{0,1},{2,3},{4,5},{6,7},{8,9},{10,11},{12,13},{14,15},{1,0},{3,2},... | collective-permute-start | bytes 786440 | tf_op jit(solution)/shard_map/ppermute | solution.py:149
  66.9 1.5 collective-permute-start.16
  68.4 3.2 %collective-permute-start.17 = (bf16[6,8,32,128]{3,2,1,0:T(8,128)(2,1)S(1)}, bf16[6,8,32,128]{3,2,1,0:T(8,128)(2,1)S(1)}, u32[]{:S(2)}, u32[]{:S(2)}) collective-permute-start(bf16[6,8,32,128]{3,2,1,0:T(8,128)(2,1)S(1)} %get-tuple-element.64), channel_id=1, source_target_pairs={{0,32},{16,48},{32,0},{48,16},{1,33},{17,49},{33,1},{49,17},{2,34}... | collective-permute-start | bytes 1179656 | tf_op jit(solution)/shard_map/ppermute | solution.py:143
  71.6 5.5 %shard_map.80 = (bf16[2,8,32,128]{3,2,1,0:T(8,128)(2,1)S(1)}, bf16[2,8,32,128]{3,2,1,0:T(8,128)(2,1)S(1)}, bf16[2,8,32,128]{3,2,1,0:T(8,128)(2,1)S(1)}, bf16[2,12,32,128]{3,2,1,0:T(8,128)(2,1)S(1)}) custom-call(s32[3]{0:T(128)S(1)} %pad_add_fusion.idx, bf16[2,16,32,128]{3,2,1,0:T(8,128)(2,1)S(1)} %get-tuple-element.66.own.e3, ...), custom_call_target="tpu_custom_call" | custom-call | tf_op jit(solution)/shard_map/pallas_call | solution.py:401
  77.1 3.9 %collective-permute-start.22 = (bf16[2,12,32,128]{3,2,1,0:T(8,128)(2,1)S(1)}, bf16[2,12,32,128]{3,2,1,0:T(8,128)(2,1)S(1)}, u32[]{:S(2)}, u32[]{:S(2)}) collective-permute-start(bf16[2,12,32,128]{3,2,1,0:T(8,128)(2,1)S(1)} %get-tuple-element.70.own.e1), channel_id=1, source_target_pairs={{0,1},{2,3},{4,5},{6,7},{8,9},{10,11},{12,13},{14,15},{1,0},{3,2},... | collective-permute-start | bytes 589832 | tf_op jit(solution)/shard_map/ppermute | solution.py:149
  81.7 2.7 %collective-permute-done.22.hi = bf16[2,12,32,128]{3,2,1,0:T(8,128)(2,1)S(1)} collective-permute-done((bf16[2,12,32,128]{3,2,1,0:T(8,128)(2,1)S(1)}, bf16[2,12,32,128]{3,2,1,0:T(8,128)(2,1)S(1)}, u32[]{:S(2)}, u32[]{:S(2)}) %collective-permute-start.22) | collective-permute-done | bytes 196640 | tf_op jit(solution)/shard_map/ppermute | solution.py:149
  84.4 3.3 %shard_map.81 = (bf16[2,8,32,128]{3,2,1,0:T(8,128)(2,1)S(1)}, bf16[4,10,32,128]{3,2,1,0:T(8,128)(2,1)S(1)}, bf16[2,8,32,128]{3,2,1,0:T(8,128)(2,1)S(1)}, bf16[2,...) custom-call(s32[3]{0:T(128)S(1)} %pad_add_fusion.idx, ...), custom_call_target="tpu_custom_call" | custom-call | tf_op jit(solution)/shard_map/pallas_call | solution.py:436
  87.6 1.7 %collective-permute-start.26 = (bf16[2,8,32,128]{3,2,1,0:T(8,128)(2,1)S(1)}, bf16[2,8,32,128]{3,2,1,0:T(8,128)(2,1)S(1)}, u32[]{:S(2)}, u32[]{:S(2)}) collective-permute-start(bf16[2,8,32,128]{3,2,1,0:T(8,128)(2,1)S(1)} %get-tuple-element.82), channel_id=1, source_target_pairs={{0,16},{16,0},{32,48},{48,32},{1,17},{17,1},{33,49},{49,33},{2,18}... | collective-permute-start | bytes 393224 | tf_op jit(solution)/shard_map/ppermute | solution.py:143
  89.3 2.7 %collective-permute-start.27 = (bf16[2,8,32,128]{3,2,1,0:T(8,128)(2,1)S(1)}, bf16[2,8,32,128]{3,2,1,0:T(8,128)(2,1)S(1)}, u32[]{:S(2)}, u32[]{:S(2)}) collective-permute-start(bf16[2,8,32,128]{3,2,1,0:T(8,128)(2,1)S(1)} %get-tuple-element.83), channel_id=1, source_target_pairs={{0,32},{16,48},{32,0},{48,16},{1,33},{17,49},{33,1},{49,17},{2,34}... | collective-permute-start | bytes 393224 | tf_op jit(solution)/shard_map/ppermute | solution.py:143
  92.7 3.1 %collective-permute-done.27.e2 = bf16[2,8,32,128]{3,2,1,0:T(8,128)(2,1)S(1)} collective-permute-done((bf16[2,8,32,128]{3,2,1,0:T(8,128)(2,1)S(1)}, bf16[2,8,32,128]{3,2,1,0:T(8,128)(2,1)S(1)}, u32[]{:S(2)}, u32[]{:S(2)}) %collective-permute-start.27) | collective-permute-done | bytes 131104 | tf_op jit(solution)/shard_map/ppermute | solution.py:143
  95.8 1.4 collective-permute-done.28.e3
  97.2 4.1 %shard_map.84 = (f32[1792,128]{1,0:T(8,128)S(1)}, bf16[1792,128]{1,0:T(8,128)(2,1)S(1)}) custom-call(s32[3]{0:T(128)S(1)} %pad_add_fusion.idx, bf16[4,34,32,128]{3,2,1,0:T(8,128)(2,1)S(1)} %shard_map.83.x, bf16[2,8,32,128]{3,2,1,0:T(8,128)(2,1)S(1)} %get-tuple-element.81.e0, bf16[2,8,32,128]{3,2,1,0:T(8,128)(2,1)S(1)} %collective-permute-done.26.e1, ...), custom_call_target="tpu_custom_call" | custom-call | tf_op jit(solution)/shard_map/pallas_call | solution.py:511
  101.3 4.3 %collective-permute-start.29 = (bf16[1792,128]{1,0:T(8,128)(2,1)S(1)}, bf16[1792,128]{1,0:T(8,128)(2,1)S(1)}, u32[]{:S(2)}, u32[]{:S(2)}) collective-permute-start(bf16[1792,128]{1,0:T(8,128)(2,1)S(1)} %get-tuple-element.86), channel_id=1, source_target_pairs={{0,64},{64,0},{1,65},{65,1},{2,66},{66,2},{3,67},{67,3},{4,68},{68... | collective-permute-start | bytes 1376264 | tf_op jit(solution)/shard_map/ppermute | solution.py:153
  105.6 1.4 collective-permute-done.29.recv
  107.8 5.8 %collective-permute-start.30 = (bf16[448,128]{1,0:T(8,128)(2,1)S(1)}, bf16[448,128]{1,0:T(8,128)(2,1)S(1)}, u32[]{:S(2)}, u32[]{:S(2)}) collective-permute-start(bf16[448,128]{1,0:T(8,128)(2,1)S(1)} %get-tuple-element.88), channel_id=1, source_target_pairs={{0,1},{1,0},{2,3},{3,2},{4,5},{5,4},{6,7},{7,6},{8,9},{9,8},{10,11... | collective-permute-start | bytes 344072 | tf_op jit(solution)/shard_map/ppermute | solution.py:156
  113.6 3.9 %collective-permute-start.31 = (bf16[448,128]{1,0:T(8,128)(2,1)S(1)}, bf16[448,128]{1,0:T(8,128)(2,1)S(1)}, u32[]{:S(2)}, u32[]{:S(2)}) collective-permute-start(bf16[448,128]{1,0:T(8,128)(2,1)S(1)} %get-tuple-element.89), channel_id=1, source_target_pairs={{0,2},{1,3},{2,0},{3,1},{4,6},{5,7},{6,4},{7,5},{8,10},{9,11},{10,... | collective-permute-start | bytes 344072 | tf_op jit(solution)/shard_map/ppermute | solution.py:156
  117.5 5.3 %collective-permute-done.31 = bf16[448,128]{1,0:T(8,128)(2,1)S(1)} collective-permute-done((bf16[448,128]{1,0:T(8,128)(2,1)S(1)}, bf16[448,128]{1,0:T(8,128)(2,1)S(1)}, u32[]{:S(2)}, u32[]{:S(2)}) %collective-permute-start.31) | collective-permute-done | bytes 114720 | tf_op jit(solution)/shard_map/ppermute | solution.py:156
  122.8 2.6 %collective-permute-done.32 = bf16[448,128]{1,0:T(8,128)(2,1)S(1)} collective-permute-done((bf16[448,128]{1,0:T(8,128)(2,1)S(1)}, bf16[448,128]{1,0:T(8,128)(2,1)S(1)}, u32[]{:S(2)}, u32[]{:S(2)}) %collective-permute-start.32) | collective-permute-done | bytes 114720 | tf_op jit(solution)/shard_map/ppermute | solution.py:156
  126.0 2.6 %collective-permute-start.34 = (bf16[448,128]{1,0:T(8,128)(2,1)S(1)}, bf16[448,128]{1,0:T(8,128)(2,1)S(1)}, u32[]{:S(2)}, u32[]{:S(2)}) collective-permute-start(bf16[448,128]{1,0:T(8,128)(2,1)S(1)} %add_convert_fusion.q0), channel_id=1, source_target_pairs={{0,8},{1,9},{2,10},{3,11},{4,12},{5,13},{6,14},{7,15},{8,0},{9,1},... | collective-permute-start | bytes 344072 | tf_op jit(solution)/shard_map/ppermute | solution.py:159
  128.8 4.7 %collective-permute-done.35.q3 = bf16[448,128]{1,0:T(8,128)(2,1)S(1)} collective-permute-done((bf16[448,128]{1,0:T(8,128)(2,1)S(1)}, bf16[448,128]{1,0:T(8,128)(2,1)S(1)}, u32[]{:S(2)}, u32[]{:S(2)}) %collective-permute-start.35) | collective-permute-done | bytes 114720 | tf_op jit(solution)/shard_map/ppermute | solution.py:159
  134.2 1.1 collective-permute-start.38
  135.3 2.2 %collective-permute-start.36 = (bf16[448,128]{1,0:T(8,128)(2,1)S(1)}, bf16[448,128]{1,0:T(8,128)(2,1)S(1)}, u32[]{:S(2)}, u32[]{:S(2)}) collective-permute-start(bf16[448,128]{1,0:T(8,128)(2,1)S(1)} %shard_map.86.q0), channel_id=1, source_target_pairs={{0,1},{1,0},{2,3},{3,2},{4,5},{5,4},{6,7},{7,6},{8,9},{9,8},{10,11... | collective-permute-start | bytes 344072 | tf_op jit(solution)/shard_map/ppermute | solution.py:156
  137.5 1.6 collective-permute-done.38.q3
  139.1 1.3 collective-permute-done.37.q2
  141.8 3.1 %collective-permute-start.39 = (bf16[4,448,128]{2,1,0:T(8,128)(2,1)S(1)}, bf16[4,448,128]{2,1,0:T(8,128)(2,1)S(1)}, u32[]{:S(2)}, u32[]{:S(2)}) collective-permute-start(bf16[4,448,128]{2,1,0:T(8,128)(2,1)S(1)} %shard_map.87.mine), channel_id=1, source_target_pairs={{0,64},{64,0},{1,65},{65,1},{2,66},{66,2},{3,67},{67,3},{4,68},{68... | collective-permute-start | bytes 1376264 | tf_op jit(solution)/shard_map/ppermute | solution.py:153
  144.9 1.6 shard_map.82
  146.6 1.6 collective-permute-start.24
  148.2 2.3 %collective-permute-start.25 = (bf16[2,8,32,128]{3,2,1,0:T(8,128)(2,1)S(1)}, bf16[2,8,32,128]{3,2,1,0:T(8,128)(2,1)S(1)}, u32[]{:S(2)}, u32[]{:S(2)}) collective-permute-start(bf16[2,8,32,128]{3,2,1,0:T(8,128)(2,1)S(1)} %get-tuple-element.80), channel_id=1, source_target_pairs={{0,48},{16,32},{32,16},{48,0},{1,49},{17,33},{33,17},{49,1},{2,50}... | collective-permute-start | bytes 393224 | tf_op jit(solution)/shard_map/ppermute | solution.py:143
  150.5 1.2 collective-permute-done.23.b1
  151.7 3.0 %collective-permute-done.24.b2 = bf16[2,8,32,128]{3,2,1,0:T(8,128)(2,1)S(1)} collective-permute-done((bf16[2,8,32,128]{3,2,1,0:T(8,128)(2,1)S(1)}, bf16[2,8,32,128]{3,2,1,0:T(8,128)(2,1)S(1)}, u32[]{:S(2)}, u32[]{:S(2)}) %collective-permute-start.24) | collective-permute-done | bytes 131104 | tf_op jit(solution)/shard_map/ppermute | solution.py:143
  154.6 2.5 %collective-permute-done.25.b3 = bf16[2,8,32,128]{3,2,1,0:T(8,128)(2,1)S(1)} collective-permute-done((bf16[2,8,32,128]{3,2,1,0:T(8,128)(2,1)S(1)}, bf16[2,8,32,128]{3,2,1,0:T(8,128)(2,1)S(1)}, u32[]{:S(2)}, u32[]{:S(2)}) %collective-permute-start.25) | collective-permute-done | bytes 131104 | tf_op jit(solution)/shard_map/ppermute | solution.py:143
  157.2 1.9 %shard_map.88 = (bf16[2,32,32,128]{3,2,1,0:T(8,128)(2,1)}, bf16[2,32,32,128]{3,2,1,0:T(8,128)(2,1)}, f32[3456,128]{1,0:T(8,128)}) custom-call(s32[3]{0:T(128)S(1)} %pad_add_fusion.idx, bf16[6,8,32,128]{3,2,1,0:T(8,128)(2,1)S(1)} %get-tuple-element.62.x0.a0, bf16[6,8,32,128]{3,2,1,0:T(8,128)(2,1)S(1)} %collective-permute-done.16.x1.a1, ...), custom_call_target="tpu_custom_call" | custom-call | tf_op jit(solution)/shard_map/pallas_call | solution.py:584
  159.1 2.0 %finish.1 = (f32[3456,128]{1,0:T(8,128)}, f32[1,128]{1,0:T(1,128)}) custom-call(s32[3]{0:T(128)S(1)} %pad_add_fusion.idx, bf16[4,448,128]{2,1,0:T(8,128)(2,1)S(1)} %shard_map.87.mine, bf16[4,448,128]{2,1,0:T(8,128)(2,1)S(1)} %collective-permute-done.39.theirs, f32[3456,128]{1,0:T(8,128)} %get-tuple-element.93.w_in), custom_call_target="tpu_custom_call", output_to_operand_aliasing={{0}: (3, {})} | custom-call | tf_op jit(solution)/shard_map/finish/pallas_call | solution.py:630
  (65 shorter events, 15.4 us)
Async XLA Ops:
  0.6 27.4 %copy-start = (bf16[1,3456,128]{2,1,0:T(8,128)(2,1)S(1)}, bf16[1,3456,128]{2,1,0:T(8,128)(2,1)}, u32[]{:S(2)}) copy-start(bf16[1,3456,128]{2,1,0:T(8,128)(2,1)} %param.5) | copy-start | bytes 2654212
  2.1 8.8 %collective-permute-start.7 = (bf16[880,128]{1,0:T(8,128)(2,1)S(1)}, bf16[880,128]{1,0:T(8,128)(2,1)S(1)}, u32[]{:S(2)}, u32[]{:S(2)}) collective-permute-start(bf16[880,128]{1,0:T(8,128)(2,1)S(1)} %get-tuple-element.51), channel_id=1, source_target_pairs={{0,48},{16,0},{32,16},{48,32},{1,49},{17,1},{33,17},{49,33},{2,50}... | collective-permute-start | bytes 675848 | tf_op jit(solution)/shard_map/ppermute | solution.py:192
  6.7 7.3 %collective-permute-start.2 = (bf16[880,128]{1,0:T(8,128)(2,1)S(1)}, bf16[880,128]{1,0:T(8,128)(2,1)S(1)}, u32[]{:S(2)}, u32[]{:S(2)}) collective-permute-start(bf16[880,128]{1,0:T(8,128)(2,1)S(1)} %get-tuple-element.51), channel_id=1, source_target_pairs={{0,16},{16,32},{32,48},{48,0},{1,17},{17,33},{33,49},{49,1},{2,18}... | collective-permute-start | bytes 675848 | tf_op jit(solution)/shard_map/ppermute | solution.py:192
  6.7 10.6 %collective-permute-start.5 = (bf16[880,128]{1,0:T(8,128)(2,1)S(1)}, bf16[880,128]{1,0:T(8,128)(2,1)S(1)}, u32[]{:S(2)}, u32[]{:S(2)}) collective-permute-start(bf16[880,128]{1,0:T(8,128)(2,1)S(1)} %get-tuple-element.52), channel_id=1, source_target_pairs={{0,48},{16,0},{32,16},{48,32},{1,49},{17,1},{33,17},{49,33},{2,50}... | collective-permute-start | bytes 675848 | tf_op jit(solution)/shard_map/ppermute | solution.py:192
  9.4 9.5 %collective-permute-start.3 = (bf16[880,128]{1,0:T(8,128)(2,1)S(1)}, bf16[880,128]{1,0:T(8,128)(2,1)S(1)}, u32[]{:S(2)}, u32[]{:S(2)}) collective-permute-start(bf16[880,128]{1,0:T(8,128)(2,1)S(1)} %get-tuple-element.52), channel_id=1, source_target_pairs={{0,16},{16,32},{32,48},{48,0},{1,17},{17,33},{33,49},{49,1},{2,18}... | collective-permute-start | bytes 675848 | tf_op jit(solution)/shard_map/ppermute | solution.py:192
  9.4 10.6 %collective-permute-start.1 = (bf16[2,24,32,128]{3,2,1,0:T(8,128)(2,1)S(1)}, bf16[2,24,32,128]{3,2,1,0:T(8,128)(2,1)S(1)}, u32[]{:S(2)}, u32[]{:S(2)}) collective-permute-start(bf16[2,24,32,128]{3,2,1,0:T(8,128)(2,1)S(1)} %get-tuple-element.50.own), channel_id=1, source_target_pairs={{0,1},{2,3},{4,5},{6,7},{8,9},{10,11},{12,13},{14,15},{1,0},{3,2},... | collective-permute-start | bytes 1179656 | tf_op jit(solution)/shard_map/ppermute | solution.py:149
  10.9 10.8 %collective-permute-start = (bf16[2,24,32,128]{3,2,1,0:T(8,128)(2,1)S(1)}, bf16[2,24,32,128]{3,2,1,0:T(8,128)(2,1)S(1)}, u32[]{:S(2)}, u32[]{:S(2)}) collective-permute-start(bf16[2,24,32,128]{3,2,1,0:T(8,128)(2,1)S(1)} %get-tuple-element.50.own), channel_id=1, source_target_pairs={{1,2},{3,4},{5,6},{7,8},{9,10},{11,12},{13,14},{2,1},{4,3},{6,5},{... | collective-permute-start | bytes 1179656 | tf_op jit(solution)/shard_map/ppermute | solution.py:149
  11.6 0.7 copy-start.2
  14.0 8.4 %collective-permute-start.12 = (bf16[880,128]{1,0:T(8,128)(2,1)S(1)}, bf16[880,128]{1,0:T(8,128)(2,1)S(1)}, u32[]{:S(2)}, u32[]{:S(2)}) collective-permute-start(bf16[880,128]{1,0:T(8,128)(2,1)S(1)} %collective-permute-done.7.rest_4_.rest_15_), channel_id=1, source_target_pairs={{0,64},{64,0},{1,65},{65,1},{2,66},{66,2},{3,67},{67,3},{4,68},{68... | collective-permute-start | bytes 675848 | tf_op jit(solution)/shard_map/ppermute | solution.py:153
  17.3 7.8 %collective-permute-start.4 = (bf16[880,128]{1,0:T(8,128)(2,1)S(1)}, bf16[880,128]{1,0:T(8,128)(2,1)S(1)}, u32[]{:S(2)}, u32[]{:S(2)}) collective-permute-start(bf16[880,128]{1,0:T(8,128)(2,1)S(1)} %collective-permute-done.2.rest_0_.rest_13_), channel_id=1, source_target_pairs={{0,16},{16,32},{32,48},{48,0},{1,17},{17,33},{33,49},{49,1},{2,18}... | collective-permute-start | bytes 675848 | tf_op jit(solution)/shard_map/ppermute | solution.py:192
  18.9 7.5 %collective-permute-start.6 = (bf16[880,128]{1,0:T(8,128)(2,1)S(1)}, bf16[880,128]{1,0:T(8,128)(2,1)S(1)}, u32[]{:S(2)}, u32[]{:S(2)}) collective-permute-start(bf16[880,128]{1,0:T(8,128)(2,1)S(1)} %collective-permute-done.5.rest_5_), channel_id=1, source_target_pairs={{0,48},{16,0},{32,16},{48,32},{1,49},{17,1},{33,17},{49,33},{2,50}... | collective-permute-start | bytes 675848 | tf_op jit(solution)/shard_map/ppermute | solution.py:192
  20.0 0.7 copy-start.4
  20.7 6.2 %collective-permute-start.8 = (bf16[880,128]{1,0:T(8,128)(2,1)S(1)}, bf16[880,128]{1,0:T(8,128)(2,1)S(1)}, u32[]{:S(2)}, u32[]{:S(2)}) collective-permute-start(bf16[880,128]{1,0:T(8,128)(2,1)S(1)} %collective-permute-done.2.rest_0_.rest_13_), channel_id=1, source_target_pairs={{0,64},{64,0},{1,65},{65,1},{2,66},{66,2},{3,67},{67,3},{4,68},{68... | collective-permute-start | bytes 675848 | tf_op jit(solution)/shard_map/ppermute | solution.py:153
  21.7 0.7 copy-start.6
  22.5 4.4 %collective-permute-start.13 = (bf16[880,128]{1,0:T(8,128)(2,1)S(1)}, bf16[880,128]{1,0:T(8,128)(2,1)S(1)}, u32[]{:S(2)}, u32[]{:S(2)}) collective-permute-start(bf16[880,128]{1,0:T(8,128)(2,1)S(1)} %collective-permute-done.5.rest_5_), channel_id=1, source_target_pairs={{0,64},{64,0},{1,65},{65,1},{2,66},{66,2},{3,67},{67,3},{4,68},{68... | collective-permute-start | bytes 675848 | tf_op jit(solution)/shard_map/ppermute | solution.py:153
  22.5 4.4 %collective-permute-start.9 = (bf16[880,128]{1,0:T(8,128)(2,1)S(1)}, bf16[880,128]{1,0:T(8,128)(2,1)S(1)}, u32[]{:S(2)}, u32[]{:S(2)}) collective-permute-start(bf16[880,128]{1,0:T(8,128)(2,1)S(1)} %collective-permute-done.3.rest_1_), channel_id=1, source_target_pairs={{0,64},{64,0},{1,65},{65,1},{2,66},{66,2},{3,67},{67,3},{4,68},{68... | collective-permute-start | bytes 675848 | tf_op jit(solution)/shard_map/ppermute | solution.py:153
  25.1 2.4 %collective-permute-start.10 = (bf16[880,128]{1,0:T(8,128)(2,1)S(1)}, bf16[880,128]{1,0:T(8,128)(2,1)S(1)}, u32[]{:S(2)}, u32[]{:S(2)}) collective-permute-start(bf16[880,128]{1,0:T(8,128)(2,1)S(1)} %collective-permute-done.4.rest_2_.rest_14_), channel_id=1, source_target_pairs={{0,64},{64,0},{1,65},{65,1},{2,66},{66,2},{3,67},{67,3},{4,68},{68... | collective-permute-start | bytes 675848 | tf_op jit(solution)/shard_map/ppermute | solution.py:153
  26.4 1.6 %collective-permute-start.11 = (bf16[880,128]{1,0:T(8,128)(2,1)S(1)}, bf16[880,128]{1,0:T(8,128)(2,1)}, u32[]{:S(2)}, u32[]{:S(2)}) collective-permute-start(bf16[880,128]{1,0:T(8,128)(2,1)S(1)} %collective-permute-done.6.rest_3_), channel_id=1, source_target_pairs={{0,64},{64,0},{1,65},{65,1},{2,66},{66,2},{3,67},{67,3},{4,68},{68... | collective-permute-start | bytes 675848 | tf_op jit(solution)/shard_map/ppermute | solution.py:153
  28.0 1.0 copy-start.3
  29.0 1.0 copy-start.5
  30.0 1.0 copy-start.7
  41.1 11.7 %copy-start.1 = (bf16[1,2,32,32,128]{4,3,2,1,0:T(8,128)(2,1)S(1)}, bf16[1,2,32,32,128]{4,3,2,1,0:T(8,128)(2,1)}, u32[]{:S(2)}) copy-start(bf16[1,2,32,32,128]{4,3,2,1,0:T(8,128)(2,1)} %param.7) | copy-start | bytes 1572868
  41.1 11.7 %collective-permute-start.15 = (bf16[2,20,32,128]{3,2,1,0:T(8,128)(2,1)S(1)}, bf16[2,20,32,128]{3,2,1,0:T(8,128)(2,1)S(1)}, u32[]{:S(2)}, u32[]{:S(2)}) collective-permute-start(bf16[2,20,32,128]{3,2,1,0:T(8,128)(2,1)S(1)} %get-tuple-element.56.own), channel_id=1, source_target_pairs={{0,1},{2,3},{4,5},{6,7},{8,9},{10,11},{12,13},{14,15},{1,0},{3,2},... | collective-permute-start | bytes 983048 | tf_op jit(solution)/shard_map/ppermute | solution.py:149
  43.6 9.2 %collective-permute-start.14 = (bf16[2,20,32,128]{3,2,1,0:T(8,128)(2,1)S(1)}, bf16[2,20,32,128]{3,2,1,0:T(8,128)(2,1)S(1)}, u32[]{:S(2)}, u32[]{:S(2)}) collective-permute-start(bf16[2,20,32,128]{3,2,1,0:T(8,128)(2,1)S(1)} %get-tuple-element.56.own), channel_id=1, source_target_pairs={{1,2},{3,4},{5,6},{7,8},{9,10},{11,12},{13,14},{2,1},{4,3},{6,5},{... | collective-permute-start | bytes 983048 | tf_op jit(solution)/shard_map/ppermute | solution.py:149
  61.8 9.8 %collective-permute-start.20 = (bf16[2,16,32,128]{3,2,1,0:T(8,128)(2,1)S(1)}, bf16[2,16,32,128]{3,2,1,0:T(8,128)(2,1)S(1)}, u32[]{:S(2)}, u32[]{:S(2)}) collective-permute-start(bf16[2,16,32,128]{3,2,1,0:T(8,128)(2,1)S(1)} %get-tuple-element.66.own.e3), channel_id=1, source_target_pairs={{0,1},{2,3},{4,5},{6,7},{8,9},{10,11},{12,13},{14,15},{1,0},{3,2},... | collective-permute-start | bytes 786440 | tf_op jit(solution)/shard_map/ppermute | solution.py:149
  65.5 6.1 %collective-permute-start.19 = (bf16[2,16,32,128]{3,2,1,0:T(8,128)(2,1)S(1)}, bf16[2,16,32,128]{3,2,1,0:T(8,128)(2,1)S(1)}, u32[]{:S(2)}, u32[]{:S(2)}) collective-permute-start(bf16[2,16,32,128]{3,2,1,0:T(8,128)(2,1)S(1)} %get-tuple-element.66.own.e3), channel_id=1, source_target_pairs={{1,2},{3,4},{5,6},{7,8},{9,10},{11,12},{13,14},{2,1},{4,3},{6,5},{... | collective-permute-start | bytes 786440 | tf_op jit(solution)/shard_map/ppermute | solution.py:149
  66.9 25.1 %collective-permute-start.16 = (bf16[6,8,32,128]{3,2,1,0:T(8,128)(2,1)S(1)}, bf16[6,8,32,128]{3,2,1,0:T(8,128)(2,1)S(1)}, u32[]{:S(2)}, u32[]{:S(2)}) collective-permute-start(bf16[6,8,32,128]{3,2,1,0:T(8,128)(2,1)S(1)} %get-tuple-element.63), channel_id=1, source_target_pairs={{0,16},{16,0},{32,48},{48,32},{1,17},{17,1},{33,49},{49,33},{2,18}... | collective-permute-start | bytes 1179656 | tf_op jit(solution)/shard_map/ppermute | solution.py:143
  68.4 23.6 %collective-permute-start.17 = (bf16[6,8,32,128]{3,2,1,0:T(8,128)(2,1)S(1)}, bf16[6,8,32,128]{3,2,1,0:T(8,128)(2,1)S(1)}, u32[]{:S(2)}, u32[]{:S(2)}) collective-permute-start(bf16[6,8,32,128]{3,2,1,0:T(8,128)(2,1)S(1)} %get-tuple-element.64), channel_id=1, source_target_pairs={{0,32},{16,48},{32,0},{48,16},{1,33},{17,49},{33,1},{49,17},{2,34}... | collective-permute-start | bytes 1179656 | tf_op jit(solution)/shard_map/ppermute | solution.py:143
  71.6 20.4 %collective-permute-start.18 = (bf16[6,8,32,128]{3,2,1,0:T(8,128)(2,1)S(1)}, bf16[6,8,32,128]{3,2,1,0:T(8,128)(2,1)S(1)}, u32[]{:S(2)}, u32[]{:S(2)}) collective-permute-start(bf16[6,8,32,128]{3,2,1,0:T(8,128)(2,1)S(1)} %get-tuple-element.65), channel_id=1, source_target_pairs={{0,48},{16,32},{32,16},{48,0},{1,49},{17,33},{33,17},{49,1},{2,50}... | collective-permute-start | bytes 1179656 | tf_op jit(solution)/shard_map/ppermute | solution.py:143
  77.1 7.3 %collective-permute-start.22 = (bf16[2,12,32,128]{3,2,1,0:T(8,128)(2,1)S(1)}, bf16[2,12,32,128]{3,2,1,0:T(8,128)(2,1)S(1)}, u32[]{:S(2)}, u32[]{:S(2)}) collective-permute-start(bf16[2,12,32,128]{3,2,1,0:T(8,128)(2,1)S(1)} %get-tuple-element.70.own.e1), channel_id=1, source_target_pairs={{0,1},{2,3},{4,5},{6,7},{8,9},{10,11},{12,13},{14,15},{1,0},{3,2},... | collective-permute-start | bytes 589832 | tf_op jit(solution)/shard_map/ppermute | solution.py:149
  81.0 3.4 %collective-permute-start.21 = (bf16[2,12,32,128]{3,2,1,0:T(8,128)(2,1)S(1)}, bf16[2,12,32,128]{3,2,1,0:T(8,128)(2,1)S(1)}, u32[]{:S(2)}, u32[]{:S(2)}) collective-permute-start(bf16[2,12,32,128]{3,2,1,0:T(8,128)(2,1)S(1)} %get-tuple-element.70.own.e1), channel_id=1, source_target_pairs={{1,2},{3,4},{5,6},{7,8},{9,10},{11,12},{13,14},{2,1},{4,3},{6,5},{... | collective-permute-start | bytes 589832 | tf_op jit(solution)/shard_map/ppermute | solution.py:149
  87.6 5.1 %collective-permute-start.26 = (bf16[2,8,32,128]{3,2,1,0:T(8,128)(2,1)S(1)}, bf16[2,8,32,128]{3,2,1,0:T(8,128)(2,1)S(1)}, u32[]{:S(2)}, u32[]{:S(2)}) collective-permute-start(bf16[2,8,32,128]{3,2,1,0:T(8,128)(2,1)S(1)} %get-tuple-element.82), channel_id=1, source_target_pairs={{0,16},{16,0},{32,48},{48,32},{1,17},{17,1},{33,49},{49,33},{2,18}... | collective-permute-start | bytes 393224 | tf_op jit(solution)/shard_map/ppermute | solution.py:143
  89.3 6.5 %collective-permute-start.27 = (bf16[2,8,32,128]{3,2,1,0:T(8,128)(2,1)S(1)}, bf16[2,8,32,128]{3,2,1,0:T(8,128)(2,1)S(1)}, u32[]{:S(2)}, u32[]{:S(2)}) collective-permute-start(bf16[2,8,32,128]{3,2,1,0:T(8,128)(2,1)S(1)} %get-tuple-element.83), channel_id=1, source_target_pairs={{0,32},{16,48},{32,0},{48,16},{1,33},{17,49},{33,1},{49,17},{2,34}... | collective-permute-start | bytes 393224 | tf_op jit(solution)/shard_map/ppermute | solution.py:143
  92.0 5.2 %collective-permute-start.28 = (bf16[2,8,32,128]{3,2,1,0:T(8,128)(2,1)S(1)}, bf16[2,8,32,128]{3,2,1,0:T(8,128)(2,1)S(1)}, u32[]{:S(2)}, u32[]{:S(2)}) collective-permute-start(bf16[2,8,32,128]{3,2,1,0:T(8,128)(2,1)S(1)} %get-tuple-element.84), channel_id=1, source_target_pairs={{0,48},{16,32},{32,16},{48,0},{1,49},{17,33},{33,17},{49,1},{2,50}... | collective-permute-start | bytes 393224 | tf_op jit(solution)/shard_map/ppermute | solution.py:143
  101.3 5.8 %collective-permute-start.29 = (bf16[1792,128]{1,0:T(8,128)(2,1)S(1)}, bf16[1792,128]{1,0:T(8,128)(2,1)S(1)}, u32[]{:S(2)}, u32[]{:S(2)}) collective-permute-start(bf16[1792,128]{1,0:T(8,128)(2,1)S(1)} %get-tuple-element.86), channel_id=1, source_target_pairs={{0,64},{64,0},{1,65},{65,1},{2,66},{66,2},{3,67},{67,3},{4,68},{68... | collective-permute-start | bytes 1376264 | tf_op jit(solution)/shard_map/ppermute | solution.py:153
  107.8 9.7 %collective-permute-start.30 = (bf16[448,128]{1,0:T(8,128)(2,1)S(1)}, bf16[448,128]{1,0:T(8,128)(2,1)S(1)}, u32[]{:S(2)}, u32[]{:S(2)}) collective-permute-start(bf16[448,128]{1,0:T(8,128)(2,1)S(1)} %get-tuple-element.88), channel_id=1, source_target_pairs={{0,1},{1,0},{2,3},{3,2},{4,5},{5,4},{6,7},{7,6},{8,9},{9,8},{10,11... | collective-permute-start | bytes 344072 | tf_op jit(solution)/shard_map/ppermute | solution.py:156
  113.6 9.2 %collective-permute-start.31 = (bf16[448,128]{1,0:T(8,128)(2,1)S(1)}, bf16[448,128]{1,0:T(8,128)(2,1)S(1)}, u32[]{:S(2)}, u32[]{:S(2)}) collective-permute-start(bf16[448,128]{1,0:T(8,128)(2,1)S(1)} %get-tuple-element.89), channel_id=1, source_target_pairs={{0,2},{1,3},{2,0},{3,1},{4,6},{5,7},{6,4},{7,5},{8,10},{9,11},{10,... | collective-permute-start | bytes 344072 | tf_op jit(solution)/shard_map/ppermute | solution.py:156
  117.5 7.9 %collective-permute-start.32 = (bf16[448,128]{1,0:T(8,128)(2,1)S(1)}, bf16[448,128]{1,0:T(8,128)(2,1)S(1)}, u32[]{:S(2)}, u32[]{:S(2)}) collective-permute-start(bf16[448,128]{1,0:T(8,128)(2,1)S(1)} %get-tuple-element.90), channel_id=1, source_target_pairs={{0,3},{1,2},{2,1},{3,0},{4,7},{5,6},{6,5},{7,4},{8,11},{9,10},{10,... | collective-permute-start | bytes 344072 | tf_op jit(solution)/shard_map/ppermute | solution.py:156
  125.4 8.0 %collective-permute-start.35 = (bf16[448,128]{1,0:T(8,128)(2,1)S(1)}, bf16[448,128]{1,0:T(8,128)(2,1)S(1)}, u32[]{:S(2)}, u32[]{:S(2)}) collective-permute-start(bf16[448,128]{1,0:T(8,128)(2,1)S(1)} %add_convert_fusion.q0), channel_id=1, source_target_pairs={{0,12},{1,13},{2,14},{3,15},{4,8},{5,9},{6,10},{7,11},{8,4},{9,5},... | collective-permute-start | bytes 344072 | tf_op jit(solution)/shard_map/ppermute | solution.py:159
  126.0 7.4 %collective-permute-start.34 = (bf16[448,128]{1,0:T(8,128)(2,1)S(1)}, bf16[448,128]{1,0:T(8,128)(2,1)S(1)}, u32[]{:S(2)}, u32[]{:S(2)}) collective-permute-start(bf16[448,128]{1,0:T(8,128)(2,1)S(1)} %add_convert_fusion.q0), channel_id=1, source_target_pairs={{0,8},{1,9},{2,10},{3,11},{4,12},{5,13},{6,14},{7,15},{8,0},{9,1},... | collective-permute-start | bytes 344072 | tf_op jit(solution)/shard_map/ppermute | solution.py:159
  128.6 4.9 %collective-permute-start.33 = (bf16[448,128]{1,0:T(8,128)(2,1)S(1)}, bf16[448,128]{1,0:T(8,128)(2,1)S(1)}, u32[]{:S(2)}, u32[]{:S(2)}) collective-permute-start(bf16[448,128]{1,0:T(8,128)(2,1)S(1)} %add_convert_fusion.q0), channel_id=1, source_target_pairs={{0,4},{1,5},{2,6},{3,7},{4,0},{5,1},{6,2},{7,3},{8,12},{9,13},{10,... | collective-permute-start | bytes 344072 | tf_op jit(solution)/shard_map/ppermute | solution.py:159
  134.2 4.9 %collective-permute-start.38 = (bf16[448,128]{1,0:T(8,128)(2,1)S(1)}, bf16[448,128]{1,0:T(8,128)(2,1)S(1)}, u32[]{:S(2)}, u32[]{:S(2)}) collective-permute-start(bf16[448,128]{1,0:T(8,128)(2,1)S(1)} %shard_map.86.q0), channel_id=1, source_target_pairs={{0,3},{1,2},{2,1},{3,0},{4,7},{5,6},{6,5},{7,4},{8,11},{9,10},{10,... | collective-permute-start | bytes 344072 | tf_op jit(solution)/shard_map/ppermute | solution.py:156
  135.3 5.2 %collective-permute-start.37 = (bf16[448,128]{1,0:T(8,128)(2,1)S(1)}, bf16[448,128]{1,0:T(8,128)(2,1)S(1)}, u32[]{:S(2)}, u32[]{:S(2)}) collective-permute-start(bf16[448,128]{1,0:T(8,128)(2,1)S(1)} %shard_map.86.q0), channel_id=1, source_target_pairs={{0,2},{1,3},{2,0},{3,1},{4,6},{5,7},{6,4},{7,5},{8,10},{9,11},{10,... | collective-permute-start | bytes 344072 | tf_op jit(solution)/shard_map/ppermute | solution.py:156
  135.3 5.9 %collective-permute-start.36 = (bf16[448,128]{1,0:T(8,128)(2,1)S(1)}, bf16[448,128]{1,0:T(8,128)(2,1)S(1)}, u32[]{:S(2)}, u32[]{:S(2)}) collective-permute-start(bf16[448,128]{1,0:T(8,128)(2,1)S(1)} %shard_map.86.q0), channel_id=1, source_target_pairs={{0,1},{1,0},{2,3},{3,2},{4,5},{5,4},{6,7},{7,6},{8,9},{9,8},{10,11... | collective-permute-start | bytes 344072 | tf_op jit(solution)/shard_map/ppermute | solution.py:156
  141.8 17.2 %collective-permute-start.39 = (bf16[4,448,128]{2,1,0:T(8,128)(2,1)S(1)}, bf16[4,448,128]{2,1,0:T(8,128)(2,1)S(1)}, u32[]{:S(2)}, u32[]{:S(2)}) collective-permute-start(bf16[4,448,128]{2,1,0:T(8,128)(2,1)S(1)} %shard_map.87.mine), channel_id=1, source_target_pairs={{0,64},{64,0},{1,65},{65,1},{2,66},{66,2},{3,67},{67,3},{4,68},{68... | collective-permute-start | bytes 1376264 | tf_op jit(solution)/shard_map/ppermute | solution.py:153
  146.5 5.1 %collective-permute-start.23 = (bf16[2,8,32,128]{3,2,1,0:T(8,128)(2,1)S(1)}, bf16[2,8,32,128]{3,2,1,0:T(8,128)(2,1)S(1)}, u32[]{:S(2)}, u32[]{:S(2)}) collective-permute-start(bf16[2,8,32,128]{3,2,1,0:T(8,128)(2,1)S(1)} %get-tuple-element.78), channel_id=1, source_target_pairs={{0,16},{16,0},{32,48},{48,32},{1,17},{17,1},{33,49},{49,33},{2,18}... | collective-permute-start | bytes 393224 | tf_op jit(solution)/shard_map/ppermute | solution.py:143
  146.6 8.0 %collective-permute-start.24 = (bf16[2,8,32,128]{3,2,1,0:T(8,128)(2,1)S(1)}, bf16[2,8,32,128]{3,2,1,0:T(8,128)(2,1)S(1)}, u32[]{:S(2)}, u32[]{:S(2)}) collective-permute-start(bf16[2,8,32,128]{3,2,1,0:T(8,128)(2,1)S(1)} %get-tuple-element.79), channel_id=1, source_target_pairs={{0,32},{16,48},{32,0},{48,16},{1,33},{17,49},{33,1},{49,17},{2,34}... | collective-permute-start | bytes 393224 | tf_op jit(solution)/shard_map/ppermute | solution.py:143
  148.2 9.0 %collective-permute-start.25 = (bf16[2,8,32,128]{3,2,1,0:T(8,128)(2,1)S(1)}, bf16[2,8,32,128]{3,2,1,0:T(8,128)(2,1)S(1)}, u32[]{:S(2)}, u32[]{:S(2)}) collective-permute-start(bf16[2,8,32,128]{3,2,1,0:T(8,128)(2,1)S(1)} %get-tuple-element.80), channel_id=1, source_target_pairs={{0,48},{16,32},{32,16},{48,0},{1,49},{17,33},{33,17},{49,1},{2,50}... | collective-permute-start | bytes 393224 | tf_op jit(solution)/shard_map/ppermute | solution.py:143

commit v3 on v2

--- a/solution.py
+++ b/solution.py
@@ -78,37 +78,20 @@
     dst[pl.ds(4 - 4 * odd, 2)] = near[...]
 
 
-def layer_copies(s, c, t, own, got, swp, dst, sem, rows):
+def load_layer(s, c, t, own, got, swp, dst, rows):
     k = (s + 4 - t) % 4
 
-    def four(parts):
-        out = []
-        for i, part in enumerate(parts):
-            at = pl.multiple_of((2 * c + i if i < 2 else 2 * (1 - c) + i - 2) * rows, 16)
-            out.append((part, at, i))
-        return [
-            pltpu.make_async_copy(own.at[pl.ds(at, rows)] if part is None else part.at[pl.ds(0, rows)], dst.at[pl.ds(at, rows)], sem.at[i])
-            for part, at, i in out
-        ]
-
-    def start():
-        @pl.when(k == 0)
+    @pl.when(k == 0)
+    def _():
+        dst[...] = own[...]
+
+    for i in range(3):
+
+        @pl.when(k == i + 1)
         def _():
-            for cp in four((None,) * 4):
-                cp.start()
-
-        for i in range(3):
-
-            @pl.when(k == i + 1)
-            def _():
-                for cp in four((*got[2 * i : 2 * i + 2], *swp[2 * i : 2 * i + 2])):
-                    cp.start()
-
-    def wait():
-        for cp in four((None,) * 4):
-            cp.wait()
-
-    return start, wait
+            for j in range(2):
+                dst[pl.ds(pl.multiple_of((2 * c + j) * rows, 16), rows)] = got[2 * i + j][0:rows]
+                dst[pl.ds(pl.multiple_of((2 - 2 * c + j) * rows, 16), rows)] = swp[2 * i + j][0:rows]
 
 
 def bias_of(s, t, own_bias, got_bias):
@@ -197,20 +180,15 @@
     got = (a1, b1, a2, b2, a3, b3)
     swapped = [swap(g) for g in got]
     all_w = (own_w, *got, *swapped)
-    W_SPECS = [HBM] + [ANY] * 12
+    W_SPECS = [VMEM] * 13
     all_b = (own_b, a1, a2, a3)
     tail_rows = pl.BlockSpec((16, C), lambda _: (QR // 16, 0))
     B_SPECS = [VMEM] + [tail_rows] * 3
 
     def turn(idx, own, *rest):
-        got_, swp_, (out, buf, sem) = rest[:6], rest[6:12], rest[12:]
-        steps = [
-            layer_copies(idx[0], idx[2], t, own, got_, swp_, buf.at[t], sem.at[t], QR) for t in range(4)
-        ]
-        for start, _ in steps:
-            start()
+        got_, swp_, (out, buf) = rest[:6], rest[6:12], rest[12:]
         for t in (3, 2, 1, 0):
-            steps[t][1]()
+            load_layer(idx[0], idx[2], t, own, got_, swp_, buf.at[t], QR)
 
             def one(j, _):
                 out[t, pl.ds(pl.multiple_of(j * C, C), C)] = buf[t, pl.ds(pl.multiple_of((26 - j) * C, C), C)].T
@@ -220,16 +198,12 @@
 
     def k1(idx, own, lo, hi, ow, *rest):
         got_, swp_, rest = rest[:6], rest[6:12], rest[12:]
-        ob, b1_, b2_, b3_, h0e, pre0, h1e, pre1, h2, x, h1, w, sem = rest
+        ob, b1_, b2_, b3_, h0e, pre0, h1e, pre1, h2, x, h1, w = rest
         s_, d_ = idx[0], idx[1]
-        steps = [
-            layer_copies(s_, idx[2], t, ow, got_, swp_, w.at[t], sem.at[t], QR) for t in range(2)
-        ]
-        for start, _ in steps:
-            start()
+        for t in range(2):
+            load_layer(s_, idx[2], t, ow, got_, swp_, w.at[t], QR)
         assemble(x, lo, own, hi, d_, last)
         h0e[...] = x[1:5, 8 : 8 + R]
-        steps[0][1]()
         b0 = bias_of(s_, 0, ob, (b1_, b2_, b3_))
 
         def one(p, _):
@@ -242,7 +216,6 @@
             return 0
 
         lax.fori_loop(0, 4, one, 0)
-        steps[1][1]()
         b1 = bias_of(s_, 1, ob, (b1_, b2_, b3_))
 
         def two(p, _):
@@ -268,30 +241,23 @@
             pltpu.VMEM((6, R + 16, W, C), BF),
             pltpu.VMEM((4, R + 14, W, C), BF),
             pltpu.VMEM((2, TAP, C), BF),
-            pltpu.SemaphoreType.DMA((2, 4)),
         ],
     )(idx, h0, h0_lo, h0_hi, *all_w, *all_b)
 
     h2_lo, h2_hi = both(h2)
 
-    wturn = call(
-        turn, sds((4, TAP, C)), [SMEM] + W_SPECS, [pltpu.VMEM((4, TAP, C), BF), pltpu.SemaphoreType.DMA((4, 4))], VMEM
-    )(idx, *all_w)
+    wturn = call(turn, sds((4, TAP, C)), [SMEM] + W_SPECS, [pltpu.VMEM((4, TAP, C), BF)], VMEM)(idx, *all_w)
     h2_lo, h2_hi, wturn = lax.optimization_barrier((h2_lo, h2_hi, wturn))
 
     def k2(idx, own, lo, hi, ow, *rest):
         got_, swp_, rest = rest[:6], rest[6:12], rest[12:]
-        ob, b1_, b2_, b3_, cot, h2e, pre2, h3e, h4, d3, x, h3, w, gpad, sem = rest
+        ob, b1_, b2_, b3_, cot, h2e, pre2, h3e, h4, d3, x, h3, w, gpad = rest
         s_, d_ = idx[0], idx[1]
-        steps = [
-            layer_copies(s_, idx[2], t + 2, ow, got_, swp_, w.at[t], sem.at[t], QR) for t in range(2)
-        ]
-        for start, _ in steps:
-            start()
+        for t in range(2):
+            load_layer(s_, idx[2], t + 2, ow, got_, swp_, w.at[t], QR)
         assemble(x, lo, own, hi, d_, last)
         h2e[...] = x[1:5, 6 : 6 + R]
         gpad[:, 4 : 4 + H] = cot[...]
-        steps[0][1]()
         b0 = bias_of(s_, 2, ob, (b1_, b2_, b3_))
 
         def one(p, _):
@@ -304,7 +270,6 @@
             return 0
 
         lax.fori_loop(0, 4, one, 0)
-        steps[1][1]()
         b1 = bias_of(s_, 3, ob, (b1_, b2_, b3_))
 
         def two(p, _):
@@ -334,7 +299,6 @@
             pltpu.VMEM((4, R + 10, W, C), BF),
             pltpu.VMEM((2, TAP, C), BF),
             pltpu.VMEM((PL, H + 8, W, C), BF),
-            pltpu.SemaphoreType.DMA((2, 4)),
         ],
     )(idx, h2, h2_lo, h2_hi, *all_w, *all_b, cotangent[0])
 

time: 162 us -> 158 us (0.975)
  Pallas kernels: 50.6 us -> 42.8 us
  waiting for transfers between devices: 38.6 us -> 41.3 us
    pallas_call x1, Pallas kernels: 8.51 us -> 4.4 us  [shards(): call(turn, sds((4, TAP, C)), [SMEM] + W_SPECS, [pltpu.VMEM((4, TAP, C), B...]
    ppermute x8, waiting for transfers between devices: 2.7 us -> 5.38 us  [both(): result.append(lax.ppermute(v, 'depth', pairs + [(b, a) for a, b in pairs]))]
    pallas_call x1, Pallas kernels: 10.1 us -> 8.14 us  [shards(): call(k1, (sds((4, R, W, C)), sds((4, R + 2, W, C)), sds((4, R, W, C)), sd...]
    pallas_call x1, Pallas kernels: 9.02 us -> 7.21 us  [shards(): call(k2, (sds((4, R, W, C)), sds((4, R + 6, W, C)), sds((4, R, W, C)), sd...]
  transfers between devices with their start and end apart: 40 -> 40, of which waited for: 20 -> 19; matrix products, arithmetic and copies ran while one was open for 0% -> 0% of each run, Pallas kernels for 14% -> 11%
where the time goes in v3:
time: 158 us; the launch traced here: 157 us
  starting transfers between devices  67 us (42%)
  Pallas kernels  42.8 us (27%)
  waiting for transfers between devices  41.3 us (26%)
  local copies, waits for them, and re-layouts  5.23 us (3%)
    ppermute x8, starting transfers between devices, both(): result.append(lax.ppermute(v, 'depth', pairs + [(b, a) for a, b in pairs]))  15.4 us
    ppermute x8, starting transfers between devices, swap(): return lax.ppermute(v, 'dp', [(0, 1), (1, 0)])  13.8 us
    ppermute x9, starting transfers between devices, sec(): return lax.ppermute(v, 'section', [(i, i ^ k) for i in range(n_sec)])  13.1 us
    ppermute x6, starting transfers between devices, xdep(): return lax.ppermute(v, 'depth', [(i, i ^ k) for i in range(n_dep)])  13 us
    ppermute x6, waiting for transfers between devices, xdep(): return lax.ppermute(v, 'depth', [(i, i ^ k) for i in range(n_dep)])  11.6 us
    ppermute x9, waiting for transfers between devices, sec(): return lax.ppermute(v, 'section', [(i, i ^ k) for i in range(n_sec)])  11.2 us
    ppermute x6, starting transfers between devices, ring(): lax.ppermute(v, 'section', [(i, (i + k) % n_sec) for i in range(n_sec)])  8.4 us
    pallas_call x1, Pallas kernels, shards(): call(k1, (sds((4, R, W, C)), sds((4, R + 2, W, C)), sds((4, R, W, C)), sd...  8.14 us
  transfers between devices with their start and end apart: 40, of which 19 were waited for; matrix products, arithmetic and copies ran while one was open for 0% of the time, Pallas kernels for 11%

profile of v3, /device:TPU:1, one launch (start us, length us, event | category | flops | bytes accessed | tf_op | source)
XLA Modules:
  0.0 157.5 jit_solution(17282955384184259849)
XLA Ops:
  0.6 1.4 shard_map.75
  2.1 4.6 %collective-permute-start.7 = (bf16[880,128]{1,0:T(8,128)(2,1)S(1)}, bf16[880,128]{1,0:T(8,128)(2,1)S(1)}, u32[]{:S(2)}, u32[]{:S(2)}) collective-permute-start(bf16[880,128]{1,0:T(8,128)(2,1)S(1)} %get-tuple-element.51), channel_id=1, source_target_pairs={{0,48},{16,0},{32,16},{48,32},{1,49},{17,1},{33,17},{49,33},{2,50}... | collective-permute-start | bytes 675848 | tf_op jit(solution)/shard_map/ppermute | solution.py:175
  6.7 2.7 %collective-permute-start.5 = (bf16[880,128]{1,0:T(8,128)(2,1)S(1)}, bf16[880,128]{1,0:T(8,128)(2,1)S(1)}, u32[]{:S(2)}, u32[]{:S(2)}) collective-permute-start(bf16[880,128]{1,0:T(8,128)(2,1)S(1)} %get-tuple-element.52), channel_id=1, source_target_pairs={{0,48},{16,0},{32,16},{48,32},{1,49},{17,1},{33,17},{49,33},{2,50}... | collective-permute-start | bytes 675848 | tf_op jit(solution)/shard_map/ppermute | solution.py:175
  9.4 1.2 collective-permute-start.1
  12.3 1.7 %collective-permute-done.2.rest_0_.rest_13_ = bf16[880,128]{1,0:T(8,128)(2,1)S(1)} collective-permute-done((bf16[880,128]{1,0:T(8,128)(2,1)S(1)}, bf16[880,128]{1,0:T(8,128)(2,1)S(1)}, u32[]{:S(2)}, u32[]{:S(2)}) %collective-permute-start.2) | collective-permute-done | bytes 225312 | tf_op jit(solution)/shard_map/ppermute | solution.py:175
  14.0 3.2 %collective-permute-start.12 = (bf16[880,128]{1,0:T(8,128)(2,1)S(1)}, bf16[880,128]{1,0:T(8,128)(2,1)S(1)}, u32[]{:S(2)}, u32[]{:S(2)}) collective-permute-start(bf16[880,128]{1,0:T(8,128)(2,1)S(1)} %collective-permute-done.7.rest_4_.rest_15_), channel_id=1, source_target_pairs={{0,64},{64,0},{1,65},{65,1},{2,66},{66,2},{3,67},{67,3},{4,68},{68... | collective-permute-start | bytes 675848 | tf_op jit(solution)/shard_map/ppermute | solution.py:136
  17.3 1.6 %collective-permute-done.3.rest_1_ = bf16[880,128]{1,0:T(8,128)(2,1)S(1)} collective-permute-done((bf16[880,128]{1,0:T(8,128)(2,1)S(1)}, bf16[880,128]{1,0:T(8,128)(2,1)S(1)}, u32[]{:S(2)}, u32[]{:S(2)}) %collective-permute-start.3) | collective-permute-done | bytes 225312 | tf_op jit(solution)/shard_map/ppermute | solution.py:175
  18.9 1.1 collective-permute-start.6
  20.7 1.0 collective-permute-start.8
  23.0 2.1 %collective-permute-done.4.rest_2_.rest_14_ = bf16[880,128]{1,0:T(8,128)(2,1)S(1)} collective-permute-done((bf16[880,128]{1,0:T(8,128)(2,1)S(1)}, bf16[880,128]{1,0:T(8,128)(2,1)S(1)}, u32[]{:S(2)}, u32[]{:S(2)}) %collective-permute-start.4) | collective-permute-done | bytes 225312 | tf_op jit(solution)/shard_map/ppermute | solution.py:175
  25.1 1.3 collective-permute-start.10
  28.1 1.0 copy-done.3
  29.0 1.0 copy-done.5
  30.0 1.0 copy-done.7
  31.0 8.1 %shard_map.76 = (bf16[4,8,32,128]{3,2,1,0:T(8,128)(2,1)S(1)}, bf16[4,10,32,128]{3,2,1,0:T(8,128)(2,1)S(1)}, bf16[4,8,32,128]{3,2,1,0:T(8,128)(2,1)S(1)}, bf16[2,...) custom-call(s32[3]{0:T(128)S(1)} %pad_add_fusion.idx, bf16[2,24,32,128]{3,2,1,0:T(8,128)(2,1)S(1)} %copy-done.3, ...), custom_call_target="tpu_custom_call" | custom-call | tf_op jit(solution)/shard_map/pallas_call | solution.py:230
  39.2 2.5 %collective-permute-start.15 = (bf16[2,20,32,128]{3,2,1,0:T(8,128)(2,1)S(1)}, bf16[2,20,32,128]{3,2,1,0:T(8,128)(2,1)S(1)}, u32[]{:S(2)}, u32[]{:S(2)}) collective-permute-start(bf16[2,20,32,128]{3,2,1,0:T(8,128)(2,1)S(1)} %get-tuple-element.56.own), channel_id=1, source_target_pairs={{0,1},{2,3},{4,5},{6,7},{8,9},{10,11},{12,13},{14,15},{1,0},{3,2},... | collective-permute-start | bytes 983048 | tf_op jit(solution)/shard_map/ppermute | solution.py:132
  42.4 4.4 %shard_map.77.wa.wb = bf16[4,3456,128]{2,1,0:T(8,128)(2,1)S(1)} custom-call(s32[3]{0:T(128)S(1)} %pad_add_fusion.idx, bf16[3456,128]{1,0:T(8,128)(2,1)S(1)} %bitcast.12, bf16[880,128]{1,0:T(8,128)(2,1)S(1)} %collective-permute-done.2.rest_0_.rest_13_, bf16[880,128]{1,0:T(8,128)(2,1)S(1)} %collective-permute-done.3.rest_1_, ...), custom_call_target="tpu_custom_call" | custom-call | tf_op jit(solution)/shard_map/pallas_call | solution.py:249
  46.8 2.7 %collective-permute-done.15.hi = bf16[2,20,32,128]{3,2,1,0:T(8,128)(2,1)S(1)} collective-permute-done((bf16[2,20,32,128]{3,2,1,0:T(8,128)(2,1)S(1)}, bf16[2,20,32,128]{3,2,1,0:T(8,128)(2,1)S(1)}, u32[]{:S(2)}, u32[]{:S(2)}) %collective-permute-start.15) | collective-permute-done | bytes 327712 | tf_op jit(solution)/shard_map/ppermute | solution.py:132
  49.4 7.2 %shard_map.78 = (bf16[4,8,32,128]{3,2,1,0:T(8,128)(2,1)S(1)}, bf16[4,14,32,128]{3,2,1,0:T(8,128)(2,1)S(1)}, bf16[4,8,32,128]{3,2,1,0:T(8,128)(2,1)S(1)}, bf16[2,...) custom-call(s32[3]{0:T(128)S(1)} %pad_add_fusion.idx, bf16[2,20,32,128]{3,2,1,0:T(8,128)(2,1)S(1)} %get-tuple-element.56.own, ...), custom_call_target="tpu_custom_call" | custom-call | tf_op jit(solution)/shard_map/pallas_call | solution.py:287
  56.7 4.0 %collective-permute-start.20 = (bf16[2,16,32,128]{3,2,1,0:T(8,128)(2,1)S(1)}, bf16[2,16,32,128]{3,2,1,0:T(8,128)(2,1)S(1)}, u32[]{:S(2)}, u32[]{:S(2)}) collective-permute-start(bf16[2,16,32,128]{3,2,1,0:T(8,128)(2,1)S(1)} %get-tuple-element.66.own.e3), channel_id=1, source_target_pairs={{0,1},{2,3},{4,5},{6,7},{8,9},{10,11},{12,13},{14,15},{1,0},{3,2},... | collective-permute-start | bytes 786440 | tf_op jit(solution)/shard_map/ppermute | solution.py:132
  62.7 4.1 %collective-permute-start.17 = (bf16[6,8,32,128]{3,2,1,0:T(8,128)(2,1)S(1)}, bf16[6,8,32,128]{3,2,1,0:T(8,128)(2,1)S(1)}, u32[]{:S(2)}, u32[]{:S(2)}) collective-permute-start(bf16[6,8,32,128]{3,2,1,0:T(8,128)(2,1)S(1)} %get-tuple-element.64), channel_id=1, source_target_pairs={{0,32},{16,48},{32,0},{48,16},{1,33},{17,49},{33,1},{49,17},{2,34}... | collective-permute-start | bytes 1179656 | tf_op jit(solution)/shard_map/ppermute | solution.py:126
  66.8 5.5 %shard_map.80 = (bf16[2,8,32,128]{3,2,1,0:T(8,128)(2,1)S(1)}, bf16[2,8,32,128]{3,2,1,0:T(8,128)(2,1)S(1)}, bf16[2,8,32,128]{3,2,1,0:T(8,128)(2,1)S(1)}, bf16[2,12,32,128]{3,2,1,0:T(8,128)(2,1)S(1)}) custom-call(s32[3]{0:T(128)S(1)} %pad_add_fusion.idx, bf16[2,16,32,128]{3,2,1,0:T(8,128)(2,1)S(1)} %get-tuple-element.66.own.e3, ...), custom_call_target="tpu_custom_call" | custom-call | tf_op jit(solution)/shard_map/pallas_call | solution.py:365
  72.3 5.0 %collective-permute-start.22 = (bf16[2,12,32,128]{3,2,1,0:T(8,128)(2,1)S(1)}, bf16[2,12,32,128]{3,2,1,0:T(8,128)(2,1)S(1)}, u32[]{:S(2)}, u32[]{:S(2)}) collective-permute-start(bf16[2,12,32,128]{3,2,1,0:T(8,128)(2,1)S(1)} %get-tuple-element.70.own.e1), channel_id=1, source_target_pairs={{0,1},{2,3},{4,5},{6,7},{8,9},{10,11},{12,13},{14,15},{1,0},{3,2},... | collective-permute-start | bytes 589832 | tf_op jit(solution)/shard_map/ppermute | solution.py:132
  78.0 2.7 %collective-permute-done.22.hi = bf16[2,12,32,128]{3,2,1,0:T(8,128)(2,1)S(1)} collective-permute-done((bf16[2,12,32,128]{3,2,1,0:T(8,128)(2,1)S(1)}, bf16[2,12,32,128]{3,2,1,0:T(8,128)(2,1)S(1)}, u32[]{:S(2)}, u32[]{:S(2)}) %collective-permute-start.22) | collective-permute-done | bytes 196640 | tf_op jit(solution)/shard_map/ppermute | solution.py:132
  80.7 3.3 %shard_map.81 = (bf16[2,8,32,128]{3,2,1,0:T(8,128)(2,1)S(1)}, bf16[4,10,32,128]{3,2,1,0:T(8,128)(2,1)S(1)}, bf16[2,8,32,128]{3,2,1,0:T(8,128)(2,1)S(1)}, bf16[2,...) custom-call(s32[3]{0:T(128)S(1)} %pad_add_fusion.idx, ...), custom_call_target="tpu_custom_call" | custom-call | tf_op jit(solution)/shard_map/pallas_call | solution.py:400
  84.2 4.1 %collective-permute-start.27 = (bf16[2,8,32,128]{3,2,1,0:T(8,128)(2,1)S(1)}, bf16[2,8,32,128]{3,2,1,0:T(8,128)(2,1)S(1)}, u32[]{:S(2)}, u32[]{:S(2)}) collective-permute-start(bf16[2,8,32,128]{3,2,1,0:T(8,128)(2,1)S(1)} %get-tuple-element.83), channel_id=1, source_target_pairs={{0,32},{16,48},{32,0},{48,16},{1,33},{17,49},{33,1},{49,17},{2,34}... | collective-permute-start | bytes 393224 | tf_op jit(solution)/shard_map/ppermute | solution.py:126
  89.0 3.1 %collective-permute-done.27.e2 = bf16[2,8,32,128]{3,2,1,0:T(8,128)(2,1)S(1)} collective-permute-done((bf16[2,8,32,128]{3,2,1,0:T(8,128)(2,1)S(1)}, bf16[2,8,32,128]{3,2,1,0:T(8,128)(2,1)S(1)}, u32[]{:S(2)}, u32[]{:S(2)}) %collective-permute-start.27) | collective-permute-done | bytes 131104 | tf_op jit(solution)/shard_map/ppermute | solution.py:126
  92.1 1.4 collective-permute-done.28.e3
  93.5 4.1 %shard_map.84 = (f32[1792,128]{1,0:T(8,128)S(1)}, bf16[1792,128]{1,0:T(8,128)(2,1)S(1)}) custom-call(s32[3]{0:T(128)S(1)} %pad_add_fusion.idx, bf16[4,34,32,128]{3,2,1,0:T(8,128)(2,1)S(1)} %shard_map.83.x, bf16[2,8,32,128]{3,2,1,0:T(8,128)(2,1)S(1)} %get-tuple-element.81.e0, bf16[2,8,32,128]{3,2,1,0:T(8,128)(2,1)S(1)} %collective-permute-done.26.e1, ...), custom_call_target="tpu_custom_call" | custom-call | tf_op jit(solution)/shard_map/pallas_call | solution.py:475
  97.6 4.3 %collective-permute-start.29 = (bf16[1792,128]{1,0:T(8,128)(2,1)S(1)}, bf16[1792,128]{1,0:T(8,128)(2,1)S(1)}, u32[]{:S(2)}, u32[]{:S(2)}) collective-permute-start(bf16[1792,128]{1,0:T(8,128)(2,1)S(1)} %get-tuple-element.86), channel_id=1, source_target_pairs={{0,64},{64,0},{1,65},{65,1},{2,66},{66,2},{3,67},{67,3},{4,68},{68... | collective-permute-start | bytes 1376264 | tf_op jit(solution)/shard_map/ppermute | solution.py:136
  101.9 1.4 collective-permute-done.29.recv
  104.1 5.8 %collective-permute-start.30 = (bf16[448,128]{1,0:T(8,128)(2,1)S(1)}, bf16[448,128]{1,0:T(8,128)(2,1)S(1)}, u32[]{:S(2)}, u32[]{:S(2)}) collective-permute-start(bf16[448,128]{1,0:T(8,128)(2,1)S(1)} %get-tuple-element.88), channel_id=1, source_target_pairs={{0,1},{1,0},{2,3},{3,2},{4,5},{5,4},{6,7},{7,6},{8,9},{9,8},{10,11... | collective-permute-start | bytes 344072 | tf_op jit(solution)/shard_map/ppermute | solution.py:139
  109.9 3.9 %collective-permute-start.31 = (bf16[448,128]{1,0:T(8,128)(2,1)S(1)}, bf16[448,128]{1,0:T(8,128)(2,1)S(1)}, u32[]{:S(2)}, u32[]{:S(2)}) collective-permute-start(bf16[448,128]{1,0:T(8,128)(2,1)S(1)} %get-tuple-element.89), channel_id=1, source_target_pairs={{0,2},{1,3},{2,0},{3,1},{4,6},{5,7},{6,4},{7,5},{8,10},{9,11},{10,... | collective-permute-start | bytes 344072 | tf_op jit(solution)/shard_map/ppermute | solution.py:139
  113.8 5.3 %collective-permute-done.31 = bf16[448,128]{1,0:T(8,128)(2,1)S(1)} collective-permute-done((bf16[448,128]{1,0:T(8,128)(2,1)S(1)}, bf16[448,128]{1,0:T(8,128)(2,1)S(1)}, u32[]{:S(2)}, u32[]{:S(2)}) %collective-permute-start.31) | collective-permute-done | bytes 114720 | tf_op jit(solution)/shard_map/ppermute | solution.py:139
  119.1 2.6 %collective-permute-done.32 = bf16[448,128]{1,0:T(8,128)(2,1)S(1)} collective-permute-done((bf16[448,128]{1,0:T(8,128)(2,1)S(1)}, bf16[448,128]{1,0:T(8,128)(2,1)S(1)}, u32[]{:S(2)}, u32[]{:S(2)}) %collective-permute-start.32) | collective-permute-done | bytes 114720 | tf_op jit(solution)/shard_map/ppermute | solution.py:139
  122.2 2.7 %collective-permute-start.34 = (bf16[448,128]{1,0:T(8,128)(2,1)S(1)}, bf16[448,128]{1,0:T(8,128)(2,1)S(1)}, u32[]{:S(2)}, u32[]{:S(2)}) collective-permute-start(bf16[448,128]{1,0:T(8,128)(2,1)S(1)} %add_convert_fusion.q0), channel_id=1, source_target_pairs={{0,8},{1,9},{2,10},{3,11},{4,12},{5,13},{6,14},{7,15},{8,0},{9,1},... | collective-permute-start | bytes 344072 | tf_op jit(solution)/shard_map/ppermute | solution.py:142
  125.1 4.8 %collective-permute-done.35.q3 = bf16[448,128]{1,0:T(8,128)(2,1)S(1)} collective-permute-done((bf16[448,128]{1,0:T(8,128)(2,1)S(1)}, bf16[448,128]{1,0:T(8,128)(2,1)S(1)}, u32[]{:S(2)}, u32[]{:S(2)}) %collective-permute-start.35) | collective-permute-done | bytes 114720 | tf_op jit(solution)/shard_map/ppermute | solution.py:142
  131.2 2.6 %collective-permute-start.36 = (bf16[448,128]{1,0:T(8,128)(2,1)S(1)}, bf16[448,128]{1,0:T(8,128)(2,1)S(1)}, u32[]{:S(2)}, u32[]{:S(2)}) collective-permute-start(bf16[448,128]{1,0:T(8,128)(2,1)S(1)} %shard_map.86.q0), channel_id=1, source_target_pairs={{0,1},{1,0},{2,3},{3,2},{4,5},{5,4},{6,7},{7,6},{8,9},{9,8},{10,11... | collective-permute-start | bytes 344072 | tf_op jit(solution)/shard_map/ppermute | solution.py:139
  133.8 3.3 %collective-permute-done.38.q3 = bf16[448,128]{1,0:T(8,128)(2,1)S(1)} collective-permute-done((bf16[448,128]{1,0:T(8,128)(2,1)S(1)}, bf16[448,128]{1,0:T(8,128)(2,1)S(1)}, u32[]{:S(2)}, u32[]{:S(2)}) %collective-permute-start.38) | collective-permute-done | bytes 114720 | tf_op jit(solution)/shard_map/ppermute | solution.py:139
  138.1 3.0 %collective-permute-start.39 = (bf16[4,448,128]{2,1,0:T(8,128)(2,1)S(1)}, bf16[4,448,128]{2,1,0:T(8,128)(2,1)S(1)}, u32[]{:S(2)}, u32[]{:S(2)}) collective-permute-start(bf16[4,448,128]{2,1,0:T(8,128)(2,1)S(1)} %shard_map.87.mine), channel_id=1, source_target_pairs={{0,64},{64,0},{1,65},{65,1},{2,66},{66,2},{3,67},{67,3},{4,68},{68... | collective-permute-start | bytes 1376264 | tf_op jit(solution)/shard_map/ppermute | solution.py:136
  141.2 1.6 %shard_map.82 = (bf16[2,8,32,128]{3,2,1,0:T(8,128)(2,1)S(1)}, bf16[2,8,32,128]{3,2,1,0:T(8,128)(2,1)S(1)}, bf16[2,8,32,128]{3,2,1,0:T(8,128)(2,1)S(1)}, bf16[2,8,32,128]{3,2,1,0:T(8,128)(2,1)S(1)}) custom-call(s32[3]{0:T(128)S(1)} %pad_add_fusion.idx, bf16[4,10,32,128]{3,2,1,0:T(8,128)(2,1)S(1)} %get-tuple-element.73.dbuf, ...), custom_call_target="tpu_custom_call" | custom-call | tf_op jit(solution)/shard_map/pallas_call | solution.py:419
  142.9 1.5 collective-permute-start.24
  144.4 2.3 %collective-permute-start.25 = (bf16[2,8,32,128]{3,2,1,0:T(8,128)(2,1)S(1)}, bf16[2,8,32,128]{3,2,1,0:T(8,128)(2,1)S(1)}, u32[]{:S(2)}, u32[]{:S(2)}) collective-permute-start(bf16[2,8,32,128]{3,2,1,0:T(8,128)(2,1)S(1)} %get-tuple-element.80), channel_id=1, source_target_pairs={{0,48},{16,32},{32,16},{48,0},{1,49},{17,33},{33,17},{49,1},{2,50}... | collective-permute-start | bytes 393224 | tf_op jit(solution)/shard_map/ppermute | solution.py:126
  146.7 1.2 collective-permute-done.23.b1
  147.9 2.9 %collective-permute-done.24.b2 = bf16[2,8,32,128]{3,2,1,0:T(8,128)(2,1)S(1)} collective-permute-done((bf16[2,8,32,128]{3,2,1,0:T(8,128)(2,1)S(1)}, bf16[2,8,32,128]{3,2,1,0:T(8,128)(2,1)S(1)}, u32[]{:S(2)}, u32[]{:S(2)}) %collective-permute-start.24) | collective-permute-done | bytes 131104 | tf_op jit(solution)/shard_map/ppermute | solution.py:126
  150.9 2.5 %collective-permute-done.25.b3 = bf16[2,8,32,128]{3,2,1,0:T(8,128)(2,1)S(1)} collective-permute-done((bf16[2,8,32,128]{3,2,1,0:T(8,128)(2,1)S(1)}, bf16[2,8,32,128]{3,2,1,0:T(8,128)(2,1)S(1)}, u32[]{:S(2)}, u32[]{:S(2)}) %collective-permute-start.25) | collective-permute-done | bytes 131104 | tf_op jit(solution)/shard_map/ppermute | solution.py:126
  153.4 1.9 %shard_map.88 = (bf16[2,32,32,128]{3,2,1,0:T(8,128)(2,1)}, bf16[2,32,32,128]{3,2,1,0:T(8,128)(2,1)}, f32[3456,128]{1,0:T(8,128)}) custom-call(s32[3]{0:T(128)S(1)} %pad_add_fusion.idx, bf16[6,8,32,128]{3,2,1,0:T(8,128)(2,1)S(1)} %get-tuple-element.62.x0.a0, bf16[6,8,32,128]{3,2,1,0:T(8,128)(2,1)S(1)} %collective-permute-done.16.x1.a1, ...), custom_call_target="tpu_custom_call" | custom-call | tf_op jit(solution)/shard_map/pallas_call | solution.py:548
  155.3 2.0 %finish.1 = (f32[3456,128]{1,0:T(8,128)}, f32[1,128]{1,0:T(1,128)}) custom-call(s32[3]{0:T(128)S(1)} %pad_add_fusion.idx, bf16[4,448,128]{2,1,0:T(8,128)(2,1)S(1)} %shard_map.87.mine, bf16[4,448,128]{2,1,0:T(8,128)(2,1)S(1)} %collective-permute-done.39.theirs, f32[3456,128]{1,0:T(8,128)} %get-tuple-element.93.w_in), custom_call_target="tpu_custom_call", output_to_operand_aliasing={{0}: (3, {})} | custom-call | tf_op jit(solution)/shard_map/finish/pallas_call | solution.py:594
  (65 shorter events, 13.5 us)
Async XLA Ops:
  0.6 27.4 %copy-start = (bf16[1,3456,128]{2,1,0:T(8,128)(2,1)S(1)}, bf16[1,3456,128]{2,1,0:T(8,128)(2,1)}, u32[]{:S(2)}) copy-start(bf16[1,3456,128]{2,1,0:T(8,128)(2,1)} %param.5) | copy-start | bytes 2654212
  2.1 8.8 %collective-permute-start.7 = (bf16[880,128]{1,0:T(8,128)(2,1)S(1)}, bf16[880,128]{1,0:T(8,128)(2,1)S(1)}, u32[]{:S(2)}, u32[]{:S(2)}) collective-permute-start(bf16[880,128]{1,0:T(8,128)(2,1)S(1)} %get-tuple-element.51), channel_id=1, source_target_pairs={{0,48},{16,0},{32,16},{48,32},{1,49},{17,1},{33,17},{49,33},{2,50}... | collective-permute-start | bytes 675848 | tf_op jit(solution)/shard_map/ppermute | solution.py:175
  6.7 7.3 %collective-permute-start.2 = (bf16[880,128]{1,0:T(8,128)(2,1)S(1)}, bf16[880,128]{1,0:T(8,128)(2,1)S(1)}, u32[]{:S(2)}, u32[]{:S(2)}) collective-permute-start(bf16[880,128]{1,0:T(8,128)(2,1)S(1)} %get-tuple-element.51), channel_id=1, source_target_pairs={{0,16},{16,32},{32,48},{48,0},{1,17},{17,33},{33,49},{49,1},{2,18}... | collective-permute-start | bytes 675848 | tf_op jit(solution)/shard_map/ppermute | solution.py:175
  6.7 10.6 %collective-permute-start.5 = (bf16[880,128]{1,0:T(8,128)(2,1)S(1)}, bf16[880,128]{1,0:T(8,128)(2,1)S(1)}, u32[]{:S(2)}, u32[]{:S(2)}) collective-permute-start(bf16[880,128]{1,0:T(8,128)(2,1)S(1)} %get-tuple-element.52), channel_id=1, source_target_pairs={{0,48},{16,0},{32,16},{48,32},{1,49},{17,1},{33,17},{49,33},{2,50}... | collective-permute-start | bytes 675848 | tf_op jit(solution)/shard_map/ppermute | solution.py:175
  9.4 9.5 %collective-permute-start.3 = (bf16[880,128]{1,0:T(8,128)(2,1)S(1)}, bf16[880,128]{1,0:T(8,128)(2,1)S(1)}, u32[]{:S(2)}, u32[]{:S(2)}) collective-permute-start(bf16[880,128]{1,0:T(8,128)(2,1)S(1)} %get-tuple-element.52), channel_id=1, source_target_pairs={{0,16},{16,32},{32,48},{48,0},{1,17},{17,33},{33,49},{49,1},{2,18}... | collective-permute-start | bytes 675848 | tf_op jit(solution)/shard_map/ppermute | solution.py:175
  9.4 10.6 %collective-permute-start.1 = (bf16[2,24,32,128]{3,2,1,0:T(8,128)(2,1)S(1)}, bf16[2,24,32,128]{3,2,1,0:T(8,128)(2,1)S(1)}, u32[]{:S(2)}, u32[]{:S(2)}) collective-permute-start(bf16[2,24,32,128]{3,2,1,0:T(8,128)(2,1)S(1)} %get-tuple-element.50.own), channel_id=1, source_target_pairs={{0,1},{2,3},{4,5},{6,7},{8,9},{10,11},{12,13},{14,15},{1,0},{3,2},... | collective-permute-start | bytes 1179656 | tf_op jit(solution)/shard_map/ppermute | solution.py:132
  10.9 10.8 %collective-permute-start = (bf16[2,24,32,128]{3,2,1,0:T(8,128)(2,1)S(1)}, bf16[2,24,32,128]{3,2,1,0:T(8,128)(2,1)S(1)}, u32[]{:S(2)}, u32[]{:S(2)}) collective-permute-start(bf16[2,24,32,128]{3,2,1,0:T(8,128)(2,1)S(1)} %get-tuple-element.50.own), channel_id=1, source_target_pairs={{1,2},{3,4},{5,6},{7,8},{9,10},{11,12},{13,14},{2,1},{4,3},{6,5},{... | collective-permute-start | bytes 1179656 | tf_op jit(solution)/shard_map/ppermute | solution.py:132
  11.6 0.7 copy-start.2
  14.0 8.4 %collective-permute-start.12 = (bf16[880,128]{1,0:T(8,128)(2,1)S(1)}, bf16[880,128]{1,0:T(8,128)(2,1)S(1)}, u32[]{:S(2)}, u32[]{:S(2)}) collective-permute-start(bf16[880,128]{1,0:T(8,128)(2,1)S(1)} %collective-permute-done.7.rest_4_.rest_15_), channel_id=1, source_target_pairs={{0,64},{64,0},{1,65},{65,1},{2,66},{66,2},{3,67},{67,3},{4,68},{68... | collective-permute-start | bytes 675848 | tf_op jit(solution)/shard_map/ppermute | solution.py:136
  17.3 7.8 %collective-permute-start.4 = (bf16[880,128]{1,0:T(8,128)(2,1)S(1)}, bf16[880,128]{1,0:T(8,128)(2,1)S(1)}, u32[]{:S(2)}, u32[]{:S(2)}) collective-permute-start(bf16[880,128]{1,0:T(8,128)(2,1)S(1)} %collective-permute-done.2.rest_0_.rest_13_), channel_id=1, source_target_pairs={{0,16},{16,32},{32,48},{48,0},{1,17},{17,33},{33,49},{49,1},{2,18}... | collective-permute-start | bytes 675848 | tf_op jit(solution)/shard_map/ppermute | solution.py:175
  18.9 7.5 %collective-permute-start.6 = (bf16[880,128]{1,0:T(8,128)(2,1)S(1)}, bf16[880,128]{1,0:T(8,128)(2,1)S(1)}, u32[]{:S(2)}, u32[]{:S(2)}) collective-permute-start(bf16[880,128]{1,0:T(8,128)(2,1)S(1)} %collective-permute-done.5.rest_5_), channel_id=1, source_target_pairs={{0,48},{16,0},{32,16},{48,32},{1,49},{17,1},{33,17},{49,33},{2,50}... | collective-permute-start | bytes 675848 | tf_op jit(solution)/shard_map/ppermute | solution.py:175
  20.0 0.7 copy-start.4
  20.7 6.2 %collective-permute-start.8 = (bf16[880,128]{1,0:T(8,128)(2,1)S(1)}, bf16[880,128]{1,0:T(8,128)(2,1)S(1)}, u32[]{:S(2)}, u32[]{:S(2)}) collective-permute-start(bf16[880,128]{1,0:T(8,128)(2,1)S(1)} %collective-permute-done.2.rest_0_.rest_13_), channel_id=1, source_target_pairs={{0,64},{64,0},{1,65},{65,1},{2,66},{66,2},{3,67},{67,3},{4,68},{68... | collective-permute-start | bytes 675848 | tf_op jit(solution)/shard_map/ppermute | solution.py:136
  21.7 0.7 copy-start.6
  22.5 4.4 %collective-permute-start.13 = (bf16[880,128]{1,0:T(8,128)(2,1)S(1)}, bf16[880,128]{1,0:T(8,128)(2,1)S(1)}, u32[]{:S(2)}, u32[]{:S(2)}) collective-permute-start(bf16[880,128]{1,0:T(8,128)(2,1)S(1)} %collective-permute-done.5.rest_5_), channel_id=1, source_target_pairs={{0,64},{64,0},{1,65},{65,1},{2,66},{66,2},{3,67},{67,3},{4,68},{68... | collective-permute-start | bytes 675848 | tf_op jit(solution)/shard_map/ppermute | solution.py:136
  22.5 4.4 %collective-permute-start.9 = (bf16[880,128]{1,0:T(8,128)(2,1)S(1)}, bf16[880,128]{1,0:T(8,128)(2,1)S(1)}, u32[]{:S(2)}, u32[]{:S(2)}) collective-permute-start(bf16[880,128]{1,0:T(8,128)(2,1)S(1)} %collective-permute-done.3.rest_1_), channel_id=1, source_target_pairs={{0,64},{64,0},{1,65},{65,1},{2,66},{66,2},{3,67},{67,3},{4,68},{68... | collective-permute-start | bytes 675848 | tf_op jit(solution)/shard_map/ppermute | solution.py:136
  25.1 2.4 %collective-permute-start.10 = (bf16[880,128]{1,0:T(8,128)(2,1)S(1)}, bf16[880,128]{1,0:T(8,128)(2,1)S(1)}, u32[]{:S(2)}, u32[]{:S(2)}) collective-permute-start(bf16[880,128]{1,0:T(8,128)(2,1)S(1)} %collective-permute-done.4.rest_2_.rest_14_), channel_id=1, source_target_pairs={{0,64},{64,0},{1,65},{65,1},{2,66},{66,2},{3,67},{67,3},{4,68},{68... | collective-permute-start | bytes 675848 | tf_op jit(solution)/shard_map/ppermute | solution.py:136
  26.4 1.6 %collective-permute-start.11 = (bf16[880,128]{1,0:T(8,128)(2,1)S(1)}, bf16[880,128]{1,0:T(8,128)(2,1)}, u32[]{:S(2)}, u32[]{:S(2)}) collective-permute-start(bf16[880,128]{1,0:T(8,128)(2,1)S(1)} %collective-permute-done.6.rest_3_), channel_id=1, source_target_pairs={{0,64},{64,0},{1,65},{65,1},{2,66},{66,2},{3,67},{67,3},{4,68},{68... | collective-permute-start | bytes 675848 | tf_op jit(solution)/shard_map/ppermute | solution.py:136
  28.0 1.0 copy-start.3
  29.0 1.0 copy-start.5
  30.0 1.0 copy-start.7
  39.2 10.3 %copy-start.1 = (bf16[1,2,32,32,128]{4,3,2,1,0:T(8,128)(2,1)S(1)}, bf16[1,2,32,32,128]{4,3,2,1,0:T(8,128)(2,1)}, u32[]{:S(2)}) copy-start(bf16[1,2,32,32,128]{4,3,2,1,0:T(8,128)(2,1)} %param.7) | copy-start | bytes 1572868
  39.2 10.2 %collective-permute-start.15 = (bf16[2,20,32,128]{3,2,1,0:T(8,128)(2,1)S(1)}, bf16[2,20,32,128]{3,2,1,0:T(8,128)(2,1)S(1)}, u32[]{:S(2)}, u32[]{:S(2)}) collective-permute-start(bf16[2,20,32,128]{3,2,1,0:T(8,128)(2,1)S(1)} %get-tuple-element.56.own), channel_id=1, source_target_pairs={{0,1},{2,3},{4,5},{6,7},{8,9},{10,11},{12,13},{14,15},{1,0},{3,2},... | collective-permute-start | bytes 983048 | tf_op jit(solution)/shard_map/ppermute | solution.py:132
  41.7 7.8 %collective-permute-start.14 = (bf16[2,20,32,128]{3,2,1,0:T(8,128)(2,1)S(1)}, bf16[2,20,32,128]{3,2,1,0:T(8,128)(2,1)S(1)}, u32[]{:S(2)}, u32[]{:S(2)}) collective-permute-start(bf16[2,20,32,128]{3,2,1,0:T(8,128)(2,1)S(1)} %get-tuple-element.56.own), channel_id=1, source_target_pairs={{1,2},{3,4},{5,6},{7,8},{9,10},{11,12},{13,14},{2,1},{4,3},{6,5},{... | collective-permute-start | bytes 983048 | tf_op jit(solution)/shard_map/ppermute | solution.py:132
  56.7 10.2 %collective-permute-start.20 = (bf16[2,16,32,128]{3,2,1,0:T(8,128)(2,1)S(1)}, bf16[2,16,32,128]{3,2,1,0:T(8,128)(2,1)S(1)}, u32[]{:S(2)}, u32[]{:S(2)}) collective-permute-start(bf16[2,16,32,128]{3,2,1,0:T(8,128)(2,1)S(1)} %get-tuple-element.66.own.e3), channel_id=1, source_target_pairs={{0,1},{2,3},{4,5},{6,7},{8,9},{10,11},{12,13},{14,15},{1,0},{3,2},... | collective-permute-start | bytes 786440 | tf_op jit(solution)/shard_map/ppermute | solution.py:132
  60.7 6.1 %collective-permute-start.19 = (bf16[2,16,32,128]{3,2,1,0:T(8,128)(2,1)S(1)}, bf16[2,16,32,128]{3,2,1,0:T(8,128)(2,1)S(1)}, u32[]{:S(2)}, u32[]{:S(2)}) collective-permute-start(bf16[2,16,32,128]{3,2,1,0:T(8,128)(2,1)S(1)} %get-tuple-element.66.own.e3), channel_id=1, source_target_pairs={{1,2},{3,4},{5,6},{7,8},{9,10},{11,12},{13,14},{2,1},{4,3},{6,5},{... | collective-permute-start | bytes 786440 | tf_op jit(solution)/shard_map/ppermute | solution.py:132
  62.1 26.2 %collective-permute-start.16 = (bf16[6,8,32,128]{3,2,1,0:T(8,128)(2,1)S(1)}, bf16[6,8,32,128]{3,2,1,0:T(8,128)(2,1)S(1)}, u32[]{:S(2)}, u32[]{:S(2)}) collective-permute-start(bf16[6,8,32,128]{3,2,1,0:T(8,128)(2,1)S(1)} %get-tuple-element.63), channel_id=1, source_target_pairs={{0,16},{16,0},{32,48},{48,32},{1,17},{17,1},{33,49},{49,33},{2,18}... | collective-permute-start | bytes 1179656 | tf_op jit(solution)/shard_map/ppermute | solution.py:126
  62.7 25.7 %collective-permute-start.17 = (bf16[6,8,32,128]{3,2,1,0:T(8,128)(2,1)S(1)}, bf16[6,8,32,128]{3,2,1,0:T(8,128)(2,1)S(1)}, u32[]{:S(2)}, u32[]{:S(2)}) collective-permute-start(bf16[6,8,32,128]{3,2,1,0:T(8,128)(2,1)S(1)} %get-tuple-element.64), channel_id=1, source_target_pairs={{0,32},{16,48},{32,0},{48,16},{1,33},{17,49},{33,1},{49,17},{2,34}... | collective-permute-start | bytes 1179656 | tf_op jit(solution)/shard_map/ppermute | solution.py:126
  66.8 21.6 %collective-permute-start.18 = (bf16[6,8,32,128]{3,2,1,0:T(8,128)(2,1)S(1)}, bf16[6,8,32,128]{3,2,1,0:T(8,128)(2,1)S(1)}, u32[]{:S(2)}, u32[]{:S(2)}) collective-permute-start(bf16[6,8,32,128]{3,2,1,0:T(8,128)(2,1)S(1)} %get-tuple-element.65), channel_id=1, source_target_pairs={{0,48},{16,32},{32,16},{48,0},{1,49},{17,33},{33,17},{49,1},{2,50}... | collective-permute-start | bytes 1179656 | tf_op jit(solution)/shard_map/ppermute | solution.py:126
  72.3 8.4 %collective-permute-start.22 = (bf16[2,12,32,128]{3,2,1,0:T(8,128)(2,1)S(1)}, bf16[2,12,32,128]{3,2,1,0:T(8,128)(2,1)S(1)}, u32[]{:S(2)}, u32[]{:S(2)}) collective-permute-start(bf16[2,12,32,128]{3,2,1,0:T(8,128)(2,1)S(1)} %get-tuple-element.70.own.e1), channel_id=1, source_target_pairs={{0,1},{2,3},{4,5},{6,7},{8,9},{10,11},{12,13},{14,15},{1,0},{3,2},... | collective-permute-start | bytes 589832 | tf_op jit(solution)/shard_map/ppermute | solution.py:132
  77.3 3.4 %collective-permute-start.21 = (bf16[2,12,32,128]{3,2,1,0:T(8,128)(2,1)S(1)}, bf16[2,12,32,128]{3,2,1,0:T(8,128)(2,1)S(1)}, u32[]{:S(2)}, u32[]{:S(2)}) collective-permute-start(bf16[2,12,32,128]{3,2,1,0:T(8,128)(2,1)S(1)} %get-tuple-element.70.own.e1), channel_id=1, source_target_pairs={{1,2},{3,4},{5,6},{7,8},{9,10},{11,12},{13,14},{2,1},{4,3},{6,5},{... | collective-permute-start | bytes 589832 | tf_op jit(solution)/shard_map/ppermute | solution.py:132
  83.9 5.1 %collective-permute-start.26 = (bf16[2,8,32,128]{3,2,1,0:T(8,128)(2,1)S(1)}, bf16[2,8,32,128]{3,2,1,0:T(8,128)(2,1)S(1)}, u32[]{:S(2)}, u32[]{:S(2)}) collective-permute-start(bf16[2,8,32,128]{3,2,1,0:T(8,128)(2,1)S(1)} %get-tuple-element.82), channel_id=1, source_target_pairs={{0,16},{16,0},{32,48},{48,32},{1,17},{17,1},{33,49},{49,33},{2,18}... | collective-permute-start | bytes 393224 | tf_op jit(solution)/shard_map/ppermute | solution.py:126
  84.2 7.9 %collective-permute-start.27 = (bf16[2,8,32,128]{3,2,1,0:T(8,128)(2,1)S(1)}, bf16[2,8,32,128]{3,2,1,0:T(8,128)(2,1)S(1)}, u32[]{:S(2)}, u32[]{:S(2)}) collective-permute-start(bf16[2,8,32,128]{3,2,1,0:T(8,128)(2,1)S(1)} %get-tuple-element.83), channel_id=1, source_target_pairs={{0,32},{16,48},{32,0},{48,16},{1,33},{17,49},{33,1},{49,17},{2,34}... | collective-permute-start | bytes 393224 | tf_op jit(solution)/shard_map/ppermute | solution.py:126
  88.4 5.2 %collective-permute-start.28 = (bf16[2,8,32,128]{3,2,1,0:T(8,128)(2,1)S(1)}, bf16[2,8,32,128]{3,2,1,0:T(8,128)(2,1)S(1)}, u32[]{:S(2)}, u32[]{:S(2)}) collective-permute-start(bf16[2,8,32,128]{3,2,1,0:T(8,128)(2,1)S(1)} %get-tuple-element.84), channel_id=1, source_target_pairs={{0,48},{16,32},{32,16},{48,0},{1,49},{17,33},{33,17},{49,1},{2,50}... | collective-permute-start | bytes 393224 | tf_op jit(solution)/shard_map/ppermute | solution.py:126
  97.6 5.8 %collective-permute-start.29 = (bf16[1792,128]{1,0:T(8,128)(2,1)S(1)}, bf16[1792,128]{1,0:T(8,128)(2,1)S(1)}, u32[]{:S(2)}, u32[]{:S(2)}) collective-permute-start(bf16[1792,128]{1,0:T(8,128)(2,1)S(1)} %get-tuple-element.86), channel_id=1, source_target_pairs={{0,64},{64,0},{1,65},{65,1},{2,66},{66,2},{3,67},{67,3},{4,68},{68... | collective-permute-start | bytes 1376264 | tf_op jit(solution)/shard_map/ppermute | solution.py:136
  104.1 9.7 %collective-permute-start.30 = (bf16[448,128]{1,0:T(8,128)(2,1)S(1)}, bf16[448,128]{1,0:T(8,128)(2,1)S(1)}, u32[]{:S(2)}, u32[]{:S(2)}) collective-permute-start(bf16[448,128]{1,0:T(8,128)(2,1)S(1)} %get-tuple-element.88), channel_id=1, source_target_pairs={{0,1},{1,0},{2,3},{3,2},{4,5},{5,4},{6,7},{7,6},{8,9},{9,8},{10,11... | collective-permute-start | bytes 344072 | tf_op jit(solution)/shard_map/ppermute | solution.py:139
  109.9 9.2 %collective-permute-start.31 = (bf16[448,128]{1,0:T(8,128)(2,1)S(1)}, bf16[448,128]{1,0:T(8,128)(2,1)S(1)}, u32[]{:S(2)}, u32[]{:S(2)}) collective-permute-start(bf16[448,128]{1,0:T(8,128)(2,1)S(1)} %get-tuple-element.89), channel_id=1, source_target_pairs={{0,2},{1,3},{2,0},{3,1},{4,6},{5,7},{6,4},{7,5},{8,10},{9,11},{10,... | collective-permute-start | bytes 344072 | tf_op jit(solution)/shard_map/ppermute | solution.py:139
  113.8 7.9 %collective-permute-start.32 = (bf16[448,128]{1,0:T(8,128)(2,1)S(1)}, bf16[448,128]{1,0:T(8,128)(2,1)S(1)}, u32[]{:S(2)}, u32[]{:S(2)}) collective-permute-start(bf16[448,128]{1,0:T(8,128)(2,1)S(1)} %get-tuple-element.90), channel_id=1, source_target_pairs={{0,3},{1,2},{2,1},{3,0},{4,7},{5,6},{6,5},{7,4},{8,11},{9,10},{10,... | collective-permute-start | bytes 344072 | tf_op jit(solution)/shard_map/ppermute | solution.py:139
  121.7 8.1 %collective-permute-start.35 = (bf16[448,128]{1,0:T(8,128)(2,1)S(1)}, bf16[448,128]{1,0:T(8,128)(2,1)S(1)}, u32[]{:S(2)}, u32[]{:S(2)}) collective-permute-start(bf16[448,128]{1,0:T(8,128)(2,1)S(1)} %add_convert_fusion.q0), channel_id=1, source_target_pairs={{0,12},{1,13},{2,14},{3,15},{4,8},{5,9},{6,10},{7,11},{8,4},{9,5},... | collective-permute-start | bytes 344072 | tf_op jit(solution)/shard_map/ppermute | solution.py:142
  122.2 7.6 %collective-permute-start.34 = (bf16[448,128]{1,0:T(8,128)(2,1)S(1)}, bf16[448,128]{1,0:T(8,128)(2,1)S(1)}, u32[]{:S(2)}, u32[]{:S(2)}) collective-permute-start(bf16[448,128]{1,0:T(8,128)(2,1)S(1)} %add_convert_fusion.q0), channel_id=1, source_target_pairs={{0,8},{1,9},{2,10},{3,11},{4,12},{5,13},{6,14},{7,15},{8,0},{9,1},... | collective-permute-start | bytes 344072 | tf_op jit(solution)/shard_map/ppermute | solution.py:142
  124.9 5.0 %collective-permute-start.33 = (bf16[448,128]{1,0:T(8,128)(2,1)S(1)}, bf16[448,128]{1,0:T(8,128)(2,1)S(1)}, u32[]{:S(2)}, u32[]{:S(2)}) collective-permute-start(bf16[448,128]{1,0:T(8,128)(2,1)S(1)} %add_convert_fusion.q0), channel_id=1, source_target_pairs={{0,4},{1,5},{2,6},{3,7},{4,0},{5,1},{6,2},{7,3},{8,12},{9,13},{10,... | collective-permute-start | bytes 344072 | tf_op jit(solution)/shard_map/ppermute | solution.py:142
  130.5 6.6 %collective-permute-start.38 = (bf16[448,128]{1,0:T(8,128)(2,1)S(1)}, bf16[448,128]{1,0:T(8,128)(2,1)S(1)}, u32[]{:S(2)}, u32[]{:S(2)}) collective-permute-start(bf16[448,128]{1,0:T(8,128)(2,1)S(1)} %shard_map.86.q0), channel_id=1, source_target_pairs={{0,3},{1,2},{2,1},{3,0},{4,7},{5,6},{6,5},{7,4},{8,11},{9,10},{10,... | collective-permute-start | bytes 344072 | tf_op jit(solution)/shard_map/ppermute | solution.py:139
  131.2 5.9 %collective-permute-start.37 = (bf16[448,128]{1,0:T(8,128)(2,1)S(1)}, bf16[448,128]{1,0:T(8,128)(2,1)S(1)}, u32[]{:S(2)}, u32[]{:S(2)}) collective-permute-start(bf16[448,128]{1,0:T(8,128)(2,1)S(1)} %shard_map.86.q0), channel_id=1, source_target_pairs={{0,2},{1,3},{2,0},{3,1},{4,6},{5,7},{6,4},{7,5},{8,10},{9,11},{10,... | collective-permute-start | bytes 344072 | tf_op jit(solution)/shard_map/ppermute | solution.py:139
  131.2 6.3 %collective-permute-start.36 = (bf16[448,128]{1,0:T(8,128)(2,1)S(1)}, bf16[448,128]{1,0:T(8,128)(2,1)S(1)}, u32[]{:S(2)}, u32[]{:S(2)}) collective-permute-start(bf16[448,128]{1,0:T(8,128)(2,1)S(1)} %shard_map.86.q0), channel_id=1, source_target_pairs={{0,1},{1,0},{2,3},{3,2},{4,5},{5,4},{6,7},{7,6},{8,9},{9,8},{10,11... | collective-permute-start | bytes 344072 | tf_op jit(solution)/shard_map/ppermute | solution.py:139
  138.1 17.2 %collective-permute-start.39 = (bf16[4,448,128]{2,1,0:T(8,128)(2,1)S(1)}, bf16[4,448,128]{2,1,0:T(8,128)(2,1)S(1)}, u32[]{:S(2)}, u32[]{:S(2)}) collective-permute-start(bf16[4,448,128]{2,1,0:T(8,128)(2,1)S(1)} %shard_map.87.mine), channel_id=1, source_target_pairs={{0,64},{64,0},{1,65},{65,1},{2,66},{66,2},{3,67},{67,3},{4,68},{68... | collective-permute-start | bytes 1376264 | tf_op jit(solution)/shard_map/ppermute | solution.py:136
  142.8 5.1 %collective-permute-start.23 = (bf16[2,8,32,128]{3,2,1,0:T(8,128)(2,1)S(1)}, bf16[2,8,32,128]{3,2,1,0:T(8,128)(2,1)S(1)}, u32[]{:S(2)}, u32[]{:S(2)}) collective-permute-start(bf16[2,8,32,128]{3,2,1,0:T(8,128)(2,1)S(1)} %get-tuple-element.78), channel_id=1, source_target_pairs={{0,16},{16,0},{32,48},{48,32},{1,17},{17,1},{33,49},{49,33},{2,18}... | collective-permute-start | bytes 393224 | tf_op jit(solution)/shard_map/ppermute | solution.py:126
  142.9 8.0 %collective-permute-start.24 = (bf16[2,8,32,128]{3,2,1,0:T(8,128)(2,1)S(1)}, bf16[2,8,32,128]{3,2,1,0:T(8,128)(2,1)S(1)}, u32[]{:S(2)}, u32[]{:S(2)}) collective-permute-start(bf16[2,8,32,128]{3,2,1,0:T(8,128)(2,1)S(1)} %get-tuple-element.79), channel_id=1, source_target_pairs={{0,32},{16,48},{32,0},{48,16},{1,33},{17,49},{33,1},{49,17},{2,34}... | collective-permute-start | bytes 393224 | tf_op jit(solution)/shard_map/ppermute | solution.py:126
  144.4 9.0 %collective-permute-start.25 = (bf16[2,8,32,128]{3,2,1,0:T(8,128)(2,1)S(1)}, bf16[2,8,32,128]{3,2,1,0:T(8,128)(2,1)S(1)}, u32[]{:S(2)}, u32[]{:S(2)}) collective-permute-start(bf16[2,8,32,128]{3,2,1,0:T(8,128)(2,1)S(1)} %get-tuple-element.80), channel_id=1, source_target_pairs={{0,48},{16,32},{32,16},{48,0},{1,49},{17,33},{33,17},{49,1},{2,50}... | collective-permute-start | bytes 393224 | tf_op jit(solution)/shard_map/ppermute | solution.py:126

commit v4 on v3

--- a/solution.py
+++ b/solution.py
@@ -125,6 +125,12 @@
     def sec(v, k):
         return lax.ppermute(v, "section", [(i, i ^ k) for i in range(n_sec)])
 
+    def three(send, values):
+        got = {}
+        for k in (2, 1, 3):
+            got[k] = send(values[k], k)
+        return [got[k] for k in (1, 2, 3)]
+
     def both(v):
         result = []
         for first in (1, 0):
@@ -143,32 +149,40 @@
 
     own_w = weights[0]
 
-    def prepare(vol, w, b, h0, part_a, part_b, own_b, pad, row, sem):
-        s_, c_ = lax.axis_index("section"), lax.axis_index("dp")
+    def prepare(w, b, part_a, part_b, own_b, row, sem):
+        c_ = lax.axis_index("dp")
         pulls = [
             pltpu.make_async_copy(w.at[2 * c_], part_a.at[pl.ds(0, QR)], sem.at[0]),
             pltpu.make_async_copy(w.at[2 * c_ + 1], part_b.at[pl.ds(0, QR)], sem.at[1]),
             pltpu.make_async_copy(b, row, sem.at[2]),
-            pltpu.make_async_copy(vol, pad.at[:, pl.ds(8, H)], sem.at[3]),
         ]
         for cp in pulls:
             cp.start()
-        pad[:, 0:8] = jnp.zeros((PL, 8, W, C), BF)
-        pad[:, H + 8 :] = jnp.zeros((PL, 8, W, C), BF)
         for cp in pulls:
             cp.wait()
         bias = jnp.broadcast_to(row[...], (16, C))
         part_a[QR:] = bias
         part_b[QR:] = bias
         own_b[...] = bias
-        h0[...] = pad[:, pl.ds(s_ * R, R + 16)]
-
-    h0, part_a, part_b, own_b = call(
+
+    part_a, part_b, own_b = call(
         prepare,
-        (sds((PL, R + 16, W, C)), sds((QB, C)), sds((QB, C)), sds((16, C))),
-        [HBM, HBM, HBM],
-        [pltpu.VMEM((PL, H + 16, W, C), BF), pltpu.VMEM((1, C), BF), pltpu.SemaphoreType.DMA((4,))],
-    )(in_hbm(volume[0]), in_hbm(own_w.reshape(4, QR, C)), in_hbm(biases))
+        (sds((QB, C)), sds((QB, C)), sds((16, C))),
+        [HBM, HBM],
+        [pltpu.VMEM((1, C), BF), pltpu.SemaphoreType.DMA((3,))],
+    )(in_hbm(own_w.reshape(4, QR, C)), in_hbm(biases))
+
+    def rows_of(vol, h0, pad, sem):
+        pull = pltpu.make_async_copy(vol, pad.at[:, pl.ds(8, H)], sem)
+        pull.start()
+        pad[:, 0:8] = jnp.zeros((PL, 8, W, C), BF)
+        pad[:, H + 8 :] = jnp.zeros((PL, 8, W, C), BF)
+        pull.wait()
+        h0[...] = pad[:, pl.ds(lax.axis_index("section") * R, R + 16)]
+
+    h0 = call(
+        rows_of, sds((PL, R + 16, W, C)), [HBM], [pltpu.VMEM((PL, H + 16, W, C), BF), pltpu.SemaphoreType.DMA], VMEM
+    )(in_hbm(volume[0]))
     h0_lo, h0_hi = both(h0)
 
     def ring(v, k):
@@ -403,8 +417,7 @@
         [SMEM, VMEM, VMEM, VMEM, wturn_of(1), VMEM, VMEM, VMEM, VMEM],
         [pltpu.VMEM((6, R + 4, W, C), BF)],
     )(idx, d1, d1_lo, d1_hi, wturn, pre0, d1, d2, d3)
-    d_got = [sec(d_send[k], k) for k in (1, 3, 2)]
-    d_got = [d_got[0], d_got[2], d_got[1]]
+    d_got = three(sec, d_send)
 
     def k4b(idx, dbuf, wb, g1, g2, g3, *rest):
         *sends, g0 = rest
@@ -496,11 +509,11 @@
     q, *qs = call(
         split, (sds((RQ, C), F32), quart, quart, quart), [SMEM, VMEM, VMEM], [pltpu.VMEM((4, RQ, C), F32)]
     )(idx, keep, recv)
-    xs = [xdep(qs[k - 1], k) for k in (1, 2, 3)]
+    xs = three(xdep, [None, *qs])
     for v in xs:
         q = q + v.astype(F32)
     q = q.astype(BF)
-    ys = [ydep(q, k) for k in (1, 2, 3)]
+    ys = three(ydep, [q] * 4)
 
     def ordered(idx, q0, q1, q2, q3, out, buf):
         y = idx[1] // 4
@@ -512,17 +525,15 @@
         out[...] = acc.astype(BF)
 
     q = call(ordered, sds((RQ, C)), [SMEM] + [VMEM] * 4, [pltpu.VMEM((4, RQ, C), F32)], VMEM)(idx, q, *ys)
-    qs = [q] + [xdep(q, k) for k in (1, 2, 3)]
-
-    def join(idx, q0, q1, q2, q3, out):
-        x = idx[1] % 4
-        for k, r in enumerate((q0, q1, q2, q3)):
-            out[x ^ k] = r[...]
-
-    half = call(join, sds((4, RQ, C)), [SMEM] + [VMEM] * 4, [], VMEM)(idx, *qs)
-    other = swap(half)
-
-    def place(idx, a0, a1, a2, a3, b0, b1, b2, b3, mine, oa, ob, w_out, buf, sem):
+    qs = [q] + three(xdep, [q] * 4)
+
+    others = [swap(v) for v in qs]
+
+    def fill(buf, x, pieces):
+        for k, q in enumerate(pieces):
+            buf[pl.ds(pl.multiple_of((x ^ k) * RQ, 8), RQ)] = q[...].astype(F32) * grad_scale
+
+    def place(idx, a0, a1, a2, a3, b0, b1, b2, b3, q0, q1, q2, q3, oa, ob, w_out, b_own, buf, sem):
         copies = []
         for k, (va, vb) in enumerate(((a0, b0), (a1, b1), (a2, b2), (a3, b3))):
             row = (idx[0] ^ k) * R
@@ -530,7 +541,8 @@
             copies.append(pltpu.make_async_copy(vb, ob.at[:, pl.ds(row, R)], sem.at[2 * k + 1]))
         for cp in copies:
             cp.start()
-        buf[...] = mine[...].reshape(RH, C).astype(F32) * grad_scale
+        fill(buf, idx[1] % 4, (q0, q1, q2, q3))
+        b_own[...] = buf[TAP - RH : TAP - RH + 8]
         for c_, n in ((0, RH), (1, TAP - RH)):
 
             @pl.when(idx[2] == c_)
@@ -545,21 +557,21 @@
             cp.wait()
 
     full = sds((2, H, W, C))
-    out_h, out_g, w_part = call(
+    out_h, out_g, w_part, b_own = call(
         place,
-        (full, full, sds((TAP, C), F32)),
-        [SMEM] + [ANY] * 8 + [VMEM],
+        (full, full, sds((TAP, C), F32), sds((8, C), F32)),
+        [SMEM] + [ANY] * 8 + [VMEM] * 4,
         [pltpu.VMEM((RH, C), F32), pltpu.SemaphoreType.DMA((9,))],
-        (ANY, ANY, ANY),
-    )(idx, h_own, *h_got, g_send[0], *g_got, half)
-
-    def finish(idx, mine, theirs, w_in, w_out, b_out, buf, sem):
+        (ANY, ANY, ANY, VMEM),
+    )(idx, h_own, *h_got, g_send[0], *g_got, *qs)
+
+    def finish(idx, q0, q1, q2, q3, b_own, w_in, w_out, b_out, buf, sem):
         parts = 4
         row = TAP - RH
         c_ = idx[2]
         step = RH // parts
+        fill(buf, idx[1] % 4, (q0, q1, q2, q3))
         for i in range(parts):
-            buf[i * step : (i + 1) * step] = theirs[...].reshape(RH, C)[i * step : (i + 1) * step].astype(F32) * grad_scale
             n = min(step, row - i * step)
 
             @pl.when(c_ == 1)
@@ -574,8 +586,7 @@
                     buf.at[pl.ds(i * step, n)], w_out.at[pl.ds(RH + i * step, n)], sem.at[i]
                 ).start()
 
-        own_b = mine[3, RQ - C : RQ - C + 8].astype(F32) * grad_scale
-        b_out[...] = jnp.where(c_ == 1, own_b, buf[row : row + 8])[0:1]
+        b_out[...] = jnp.where(c_ == 1, b_own[...], buf[row : row + 8])[0:1]
         for i in range(parts):
             n = min(step, row - i * step)
 
@@ -596,12 +607,12 @@
         name="finish",
         grid=(1,),
         out_shape=(sds((TAP, C), F32), sds((1, C), F32)),
-        in_specs=[SMEM, VMEM, VMEM, ANY],
+        in_specs=[SMEM] + [VMEM] * 5 + [ANY],
         out_specs=(ANY, VMEM),
         scratch_shapes=[pltpu.VMEM((RH, C), F32), pltpu.SemaphoreType.DMA((4,))],
-        input_output_aliases={3: 0},
+        input_output_aliases={6: 0},
         compiler_params=pltpu.CompilerParams(vmem_limit_bytes=20 * 1024 * 1024),
-    )(idx, half, other, w_part)
+    )(idx, *others, b_own, w_part)
     return out_h[None, None], out_g[None, None], w_grad[None], b_grad
 
 

time: 158 us -> 146 us (0.924)
  waiting for transfers between devices: 41.3 us -> 25.8 us
  starting transfers between devices: 67 us -> 69.2 us
    ppermute x9, waiting for transfers between devices: 11.2 us -> 4.52 us  [sec(): return lax.ppermute(v, 'section', [(i, i ^ k) for i in range(n_sec)])]
    ppermute x8 -> x11, starting transfers between devices: 13.8 us -> 17.8 us  [swap(): return lax.ppermute(v, 'dp', [(0, 1), (1, 0)])]
    ppermute x6, waiting for transfers between devices: 11.6 us -> 7.91 us  [xdep(): return lax.ppermute(v, 'depth', [(i, i ^ k) for i in range(n_dep)])]
    ppermute x3, waiting for transfers between devices: 4.79 us -> 1.88 us  [ydep(): return lax.ppermute(v, 'depth', [(i, i ^ 4 * k) for i in range(n_dep)])]
    ppermute x6, waiting for transfers between devices: 5.72 us -> 3.45 us  [ring(): lax.ppermute(v, 'section', [(i, (i + k) % n_sec) for i in range(n_sec)])]
    ppermute x9, starting transfers between devices: 13.1 us -> 11 us  [sec(): return lax.ppermute(v, 'section', [(i, i ^ k) for i in range(n_sec)])]
  transfers between devices with their start and end apart: 40 -> 43, of which waited for: 19 -> 13; matrix products, arithmetic and copies ran while one was open for 0% -> 0% of each run, Pallas kernels for 11% -> 14%
where the time goes in v4:
time: 146 us; the launch traced here: 144 us
  starting transfers between devices  69.2 us (47%)
  Pallas kernels  43.1 us (30%)
  waiting for transfers between devices  25.8 us (18%)
  local copies, waits for them, and re-layouts  5.23 us (4%)
    ppermute x11, starting transfers between devices, swap(): return lax.ppermute(v, 'dp', [(0, 1), (1, 0)])  17.8 us
    ppermute x8, starting transfers between devices, both(): result.append(lax.ppermute(v, 'depth', pairs + [(b, a) for a, b in pairs]))  15.7 us
    ppermute x6, starting transfers between devices, xdep(): return lax.ppermute(v, 'depth', [(i, i ^ k) for i in range(n_dep)])  13 us
    ppermute x9, starting transfers between devices, sec(): return lax.ppermute(v, 'section', [(i, i ^ k) for i in range(n_sec)])  11 us
    ppermute x6, starting transfers between devices, ring(): lax.ppermute(v, 'section', [(i, (i + k) % n_sec) for i in range(n_sec)])  8.4 us
    pallas_call x1, Pallas kernels, shards(): call(k1, (sds((4, R, W, C)), sds((4, R + 2, W, C)), sds((4, R, W, C)), sd...  8.14 us
    ppermute x6, waiting for transfers between devices, xdep(): return lax.ppermute(v, 'depth', [(i, i ^ k) for i in range(n_dep)])  7.91 us
    pallas_call x1, Pallas kernels, shards(): call(k2, (sds((4, R, W, C)), sds((4, R + 6, W, C)), sds((4, R, W, C)), sd...  7.21 us
  transfers between devices with their start and end apart: 43, of which 13 were waited for; matrix products, arithmetic and copies ran while one was open for 0% of the time, Pallas kernels for 14%

profile of v4, /device:TPU:1, one launch (start us, length us, event | category | flops | bytes accessed | tf_op | source)
XLA Modules:
  0.0 144.4 jit_solution(9460455814719295225)
XLA Ops:
  0.6 1.2 shard_map.76
  1.8 4.6 %collective-permute-start.7 = (bf16[880,128]{1,0:T(8,128)(2,1)S(1)}, bf16[880,128]{1,0:T(8,128)(2,1)S(1)}, u32[]{:S(2)}, u32[]{:S(2)}) collective-permute-start(bf16[880,128]{1,0:T(8,128)(2,1)S(1)} %get-tuple-element.50), channel_id=1, source_target_pairs={{0,48},{16,0},{32,16},{48,32},{1,49},{17,1},{33,17},{49,33},{2,50}... | collective-permute-start | bytes 675848 | tf_op jit(solution)/shard_map/ppermute | solution.py:189
  6.5 2.7 %collective-permute-start.5 = (bf16[880,128]{1,0:T(8,128)(2,1)S(1)}, bf16[880,128]{1,0:T(8,128)(2,1)S(1)}, u32[]{:S(2)}, u32[]{:S(2)}) collective-permute-start(bf16[880,128]{1,0:T(8,128)(2,1)S(1)} %get-tuple-element.51), channel_id=1, source_target_pairs={{0,48},{16,0},{32,16},{48,32},{1,49},{17,1},{33,17},{49,33},{2,50}... | collective-permute-start | bytes 675848 | tf_op jit(solution)/shard_map/ppermute | solution.py:189
  9.1 1.1 shard_map.75.own
  10.2 1.3 collective-permute-start.1
  12.9 0.8 collective-permute-done.2.rest_0_.rest_13_
  13.8 3.2 %collective-permute-start.12 = (bf16[880,128]{1,0:T(8,128)(2,1)S(1)}, bf16[880,128]{1,0:T(8,128)(2,1)S(1)}, u32[]{:S(2)}, u32[]{:S(2)}) collective-permute-start(bf16[880,128]{1,0:T(8,128)(2,1)S(1)} %collective-permute-done.7.rest_4_.rest_15_), channel_id=1, source_target_pairs={{0,64},{64,0},{1,65},{65,1},{2,66},{66,2},{3,67},{67,3},{4,68},{68... | collective-permute-start | bytes 675848 | tf_op jit(solution)/shard_map/ppermute | solution.py:142
  17.0 1.6 %collective-permute-done.3.rest_1_ = bf16[880,128]{1,0:T(8,128)(2,1)S(1)} collective-permute-done((bf16[880,128]{1,0:T(8,128)(2,1)S(1)}, bf16[880,128]{1,0:T(8,128)(2,1)S(1)}, u32[]{:S(2)}, u32[]{:S(2)}) %collective-permute-start.3) | collective-permute-done | bytes 225312 | tf_op jit(solution)/shard_map/ppermute | solution.py:189
  18.6 1.1 collective-permute-start.6
  19.7 0.7 copy-done.4
  20.4 2.1 %collective-permute-start.8 = (bf16[880,128]{1,0:T(8,128)(2,1)S(1)}, bf16[880,128]{1,0:T(8,128)(2,1)S(1)}, u32[]{:S(2)}, u32[]{:S(2)}) collective-permute-start(bf16[880,128]{1,0:T(8,128)(2,1)S(1)} %collective-permute-done.2.rest_0_.rest_13_), channel_id=1, source_target_pairs={{0,64},{64,0},{1,65},{65,1},{2,66},{66,2},{3,67},{67,3},{4,68},{68... | collective-permute-start | bytes 675848 | tf_op jit(solution)/shard_map/ppermute | solution.py:142
  23.8 1.0 collective-permute-done.4.rest_2_.rest_14_
  24.8 1.3 collective-permute-start.10
  27.8 1.0 copy-done.2
  28.8 1.0 copy-done.5
  29.8 1.0 copy-done.7
  30.8 8.1 %shard_map.77 = (bf16[4,8,32,128]{3,2,1,0:T(8,128)(2,1)S(1)}, bf16[4,10,32,128]{3,2,1,0:T(8,128)(2,1)S(1)}, bf16[4,8,32,128]{3,2,1,0:T(8,128)(2,1)S(1)}, bf16[2,...) custom-call(s32[3]{0:T(128)S(1)} %pad_add_fusion.idx, bf16[2,24,32,128]{3,2,1,0:T(8,128)(2,1)S(1)} %copy-done.2, ...), custom_call_target="tpu_custom_call" | custom-call | tf_op jit(solution)/shard_map/pallas_call | solution.py:244
  38.9 2.5 %collective-permute-start.15 = (bf16[2,20,32,128]{3,2,1,0:T(8,128)(2,1)S(1)}, bf16[2,20,32,128]{3,2,1,0:T(8,128)(2,1)S(1)}, u32[]{:S(2)}, u32[]{:S(2)}) collective-permute-start(bf16[2,20,32,128]{3,2,1,0:T(8,128)(2,1)S(1)} %get-tuple-element.55.own), channel_id=1, source_target_pairs={{0,1},{2,3},{4,5},{6,7},{8,9},{10,11},{12,13},{14,15},{1,0},{3,2},... | collective-permute-start | bytes 983048 | tf_op jit(solution)/shard_map/ppermute | solution.py:138
  42.1 4.4 %shard_map.78.wa.wb = bf16[4,3456,128]{2,1,0:T(8,128)(2,1)S(1)} custom-call(s32[3]{0:T(128)S(1)} %pad_add_fusion.idx, bf16[3456,128]{1,0:T(8,128)(2,1)S(1)} %bitcast.12, bf16[880,128]{1,0:T(8,128)(2,1)S(1)} %collective-permute-done.2.rest_0_.rest_13_, bf16[880,128]{1,0:T(8,128)(2,1)S(1)} %collective-permute-done.3.rest_1_, ...), custom_call_target="tpu_custom_call" | custom-call | tf_op jit(solution)/shard_map/pallas_call | solution.py:263
  46.5 2.7 %collective-permute-done.15.hi = bf16[2,20,32,128]{3,2,1,0:T(8,128)(2,1)S(1)} collective-permute-done((bf16[2,20,32,128]{3,2,1,0:T(8,128)(2,1)S(1)}, bf16[2,20,32,128]{3,2,1,0:T(8,128)(2,1)S(1)}, u32[]{:S(2)}, u32[]{:S(2)}) %collective-permute-start.15) | collective-permute-done | bytes 327712 | tf_op jit(solution)/shard_map/ppermute | solution.py:138
  49.2 7.2 %shard_map.79 = (bf16[4,8,32,128]{3,2,1,0:T(8,128)(2,1)S(1)}, bf16[4,14,32,128]{3,2,1,0:T(8,128)(2,1)S(1)}, bf16[4,8,32,128]{3,2,1,0:T(8,128)(2,1)S(1)}, bf16[2,...) custom-call(s32[3]{0:T(128)S(1)} %pad_add_fusion.idx, bf16[2,20,32,128]{3,2,1,0:T(8,128)(2,1)S(1)} %get-tuple-element.55.own, ...), custom_call_target="tpu_custom_call" | custom-call | tf_op jit(solution)/shard_map/pallas_call | solution.py:301
  56.4 4.2 %collective-permute-start.20 = (bf16[2,16,32,128]{3,2,1,0:T(8,128)(2,1)S(1)}, bf16[2,16,32,128]{3,2,1,0:T(8,128)(2,1)S(1)}, u32[]{:S(2)}, u32[]{:S(2)}) collective-permute-start(bf16[2,16,32,128]{3,2,1,0:T(8,128)(2,1)S(1)} %get-tuple-element.65.own.e3), channel_id=1, source_target_pairs={{0,1},{2,3},{4,5},{6,7},{8,9},{10,11},{12,13},{14,15},{1,0},{3,2},... | collective-permute-start | bytes 786440 | tf_op jit(solution)/shard_map/ppermute | solution.py:138
  61.3 0.8 shard_map.80
  62.4 4.2 %collective-permute-start.17 = (bf16[6,8,32,128]{3,2,1,0:T(8,128)(2,1)S(1)}, bf16[6,8,32,128]{3,2,1,0:T(8,128)(2,1)S(1)}, u32[]{:S(2)}, u32[]{:S(2)}) collective-permute-start(bf16[6,8,32,128]{3,2,1,0:T(8,128)(2,1)S(1)} %get-tuple-element.63), channel_id=1, source_target_pairs={{0,32},{16,48},{32,0},{48,16},{1,33},{17,49},{33,1},{49,17},{2,34}... | collective-permute-start | bytes 1179656 | tf_op jit(solution)/shard_map/ppermute | solution.py:126
  66.6 5.5 %shard_map.81 = (bf16[2,8,32,128]{3,2,1,0:T(8,128)(2,1)S(1)}, bf16[2,8,32,128]{3,2,1,0:T(8,128)(2,1)S(1)}, bf16[2,8,32,128]{3,2,1,0:T(8,128)(2,1)S(1)}, bf16[2,12,32,128]{3,2,1,0:T(8,128)(2,1)S(1)}) custom-call(s32[3]{0:T(128)S(1)} %pad_add_fusion.idx, bf16[2,16,32,128]{3,2,1,0:T(8,128)(2,1)S(1)} %get-tuple-element.65.own.e3, ...), custom_call_target="tpu_custom_call" | custom-call | tf_op jit(solution)/shard_map/pallas_call | solution.py:379
  72.0 5.0 %collective-permute-start.22 = (bf16[2,12,32,128]{3,2,1,0:T(8,128)(2,1)S(1)}, bf16[2,12,32,128]{3,2,1,0:T(8,128)(2,1)S(1)}, u32[]{:S(2)}, u32[]{:S(2)}) collective-permute-start(bf16[2,12,32,128]{3,2,1,0:T(8,128)(2,1)S(1)} %get-tuple-element.69.own.e1), channel_id=1, source_target_pairs={{0,1},{2,3},{4,5},{6,7},{8,9},{10,11},{12,13},{14,15},{1,0},{3,2},... | collective-permute-start | bytes 589832 | tf_op jit(solution)/shard_map/ppermute | solution.py:138
  77.7 2.7 %collective-permute-done.22.hi = bf16[2,12,32,128]{3,2,1,0:T(8,128)(2,1)S(1)} collective-permute-done((bf16[2,12,32,128]{3,2,1,0:T(8,128)(2,1)S(1)}, bf16[2,12,32,128]{3,2,1,0:T(8,128)(2,1)S(1)}, u32[]{:S(2)}, u32[]{:S(2)}) %collective-permute-start.22) | collective-permute-done | bytes 196640 | tf_op jit(solution)/shard_map/ppermute | solution.py:138
  80.4 3.3 %shard_map.82 = (bf16[2,8,32,128]{3,2,1,0:T(8,128)(2,1)S(1)}, bf16[4,10,32,128]{3,2,1,0:T(8,128)(2,1)S(1)}, bf16[2,8,32,128]{3,2,1,0:T(8,128)(2,1)S(1)}, bf16[2,...) custom-call(s32[3]{0:T(128)S(1)} %pad_add_fusion.idx, ...), custom_call_target="tpu_custom_call" | custom-call | tf_op jit(solution)/shard_map/pallas_call | solution.py:414
  83.9 4.2 %collective-permute-start.27 = (bf16[2,8,32,128]{3,2,1,0:T(8,128)(2,1)S(1)}, bf16[2,8,32,128]{3,2,1,0:T(8,128)(2,1)S(1)}, u32[]{:S(2)}, u32[]{:S(2)}) collective-permute-start(bf16[2,8,32,128]{3,2,1,0:T(8,128)(2,1)S(1)} %get-tuple-element.82), channel_id=1, source_target_pairs={{0,32},{16,48},{32,0},{48,16},{1,33},{17,49},{33,1},{49,17},{2,34}... | collective-permute-start | bytes 393224 | tf_op jit(solution)/shard_map/ppermute | solution.py:126
  88.8 3.1 %collective-permute-done.27.e2 = bf16[2,8,32,128]{3,2,1,0:T(8,128)(2,1)S(1)} collective-permute-done((bf16[2,8,32,128]{3,2,1,0:T(8,128)(2,1)S(1)}, bf16[2,8,32,128]{3,2,1,0:T(8,128)(2,1)S(1)}, u32[]{:S(2)}, u32[]{:S(2)}) %collective-permute-start.27) | collective-permute-done | bytes 131104 | tf_op jit(solution)/shard_map/ppermute | solution.py:126
  91.9 1.4 collective-permute-done.28.e3
  93.3 4.1 %shard_map.85 = (f32[1792,128]{1,0:T(8,128)S(1)}, bf16[1792,128]{1,0:T(8,128)(2,1)S(1)}) custom-call(s32[3]{0:T(128)S(1)} %pad_add_fusion.idx, bf16[4,34,32,128]{3,2,1,0:T(8,128)(2,1)S(1)} %shard_map.84.x, bf16[2,8,32,128]{3,2,1,0:T(8,128)(2,1)S(1)} %get-tuple-element.80.e0, bf16[2,8,32,128]{3,2,1,0:T(8,128)(2,1)S(1)} %collective-permute-done.26.e1, ...), custom_call_target="tpu_custom_call" | custom-call | tf_op jit(solution)/shard_map/pallas_call | solution.py:488
  97.3 4.3 %collective-permute-start.29 = (bf16[1792,128]{1,0:T(8,128)(2,1)S(1)}, bf16[1792,128]{1,0:T(8,128)(2,1)S(1)}, u32[]{:S(2)}, u32[]{:S(2)}) collective-permute-start(bf16[1792,128]{1,0:T(8,128)(2,1)S(1)} %get-tuple-element.85), channel_id=1, source_target_pairs={{0,64},{64,0},{1,65},{65,1},{2,66},{66,2},{3,67},{67,3},{4,68},{68... | collective-permute-start | bytes 1376264 | tf_op jit(solution)/shard_map/ppermute | solution.py:142
  101.7 1.4 collective-permute-done.29.recv
  103.8 5.8 %collective-permute-start.30 = (bf16[448,128]{1,0:T(8,128)(2,1)S(1)}, bf16[448,128]{1,0:T(8,128)(2,1)S(1)}, u32[]{:S(2)}, u32[]{:S(2)}) collective-permute-start(bf16[448,128]{1,0:T(8,128)(2,1)S(1)} %get-tuple-element.87), channel_id=1, source_target_pairs={{0,1},{1,0},{2,3},{3,2},{4,5},{5,4},{6,7},{7,6},{8,9},{9,8},{10,11... | collective-permute-start | bytes 344072 | tf_op jit(solution)/shard_map/ppermute | solution.py:145
  109.6 3.9 %collective-permute-start.31 = (bf16[448,128]{1,0:T(8,128)(2,1)S(1)}, bf16[448,128]{1,0:T(8,128)(2,1)S(1)}, u32[]{:S(2)}, u32[]{:S(2)}) collective-permute-start(bf16[448,128]{1,0:T(8,128)(2,1)S(1)} %get-tuple-element.88), channel_id=1, source_target_pairs={{0,2},{1,3},{2,0},{3,1},{4,6},{5,7},{6,4},{7,5},{8,10},{9,11},{10,... | collective-permute-start | bytes 344072 | tf_op jit(solution)/shard_map/ppermute | solution.py:145
  113.5 5.3 %collective-permute-done.31 = bf16[448,128]{1,0:T(8,128)(2,1)S(1)} collective-permute-done((bf16[448,128]{1,0:T(8,128)(2,1)S(1)}, bf16[448,128]{1,0:T(8,128)(2,1)S(1)}, u32[]{:S(2)}, u32[]{:S(2)}) %collective-permute-start.31) | collective-permute-done | bytes 114720 | tf_op jit(solution)/shard_map/ppermute | solution.py:145
  118.8 2.6 %collective-permute-done.32 = bf16[448,128]{1,0:T(8,128)(2,1)S(1)} collective-permute-done((bf16[448,128]{1,0:T(8,128)(2,1)S(1)}, bf16[448,128]{1,0:T(8,128)(2,1)S(1)}, u32[]{:S(2)}, u32[]{:S(2)}) %collective-permute-start.32) | collective-permute-done | bytes 114720 | tf_op jit(solution)/shard_map/ppermute | solution.py:145
  121.9 2.7 %collective-permute-start.34 = (bf16[448,128]{1,0:T(8,128)(2,1)S(1)}, bf16[448,128]{1,0:T(8,128)(2,1)S(1)}, u32[]{:S(2)}, u32[]{:S(2)}) collective-permute-start(bf16[448,128]{1,0:T(8,128)(2,1)S(1)} %add_convert_fusion.q0), channel_id=1, source_target_pairs={{0,8},{1,9},{2,10},{3,11},{4,12},{5,13},{6,14},{7,15},{8,0},{9,1},... | collective-permute-start | bytes 344072 | tf_op jit(solution)/shard_map/ppermute | solution.py:148
  124.8 1.6 %shard_map.83 = (bf16[2,8,32,128]{3,2,1,0:T(8,128)(2,1)S(1)}, bf16[2,8,32,128]{3,2,1,0:T(8,128)(2,1)S(1)}, bf16[2,8,32,128]{3,2,1,0:T(8,128)(2,1)S(1)}, bf16[2,8,32,128]{3,2,1,0:T(8,128)(2,1)S(1)}) custom-call(s32[3]{0:T(128)S(1)} %pad_add_fusion.idx, bf16[4,10,32,128]{3,2,1,0:T(8,128)(2,1)S(1)} %get-tuple-element.72.dbuf, ...), custom_call_target="tpu_custom_call" | custom-call | tf_op jit(solution)/shard_map/pallas_call | solution.py:432
  126.5 1.2 collective-permute-start.24
  127.7 1.9 %collective-permute-done.35.q3 = bf16[448,128]{1,0:T(8,128)(2,1)S(1)} collective-permute-done((bf16[448,128]{1,0:T(8,128)(2,1)S(1)}, bf16[448,128]{1,0:T(8,128)(2,1)S(1)}, u32[]{:S(2)}, u32[]{:S(2)}) %collective-permute-start.35) | collective-permute-done | bytes 114720 | tf_op jit(solution)/shard_map/ppermute | solution.py:148
  131.0 2.6 %collective-permute-start.36 = (bf16[448,128]{1,0:T(8,128)(2,1)S(1)}, bf16[448,128]{1,0:T(8,128)(2,1)S(1)}, u32[]{:S(2)}, u32[]{:S(2)}) collective-permute-start(bf16[448,128]{1,0:T(8,128)(2,1)S(1)} %shard_map.87.q0), channel_id=1, source_target_pairs={{0,1},{1,0},{2,3},{3,2},{4,5},{5,4},{6,7},{7,6},{8,9},{9,8},{10,11... | collective-permute-start | bytes 344072 | tf_op jit(solution)/shard_map/ppermute | solution.py:145
  133.6 0.8 collective-permute-start.25
  134.4 3.3 %collective-permute-start.39 = (bf16[448,128]{1,0:T(8,128)(2,1)S(1)}, bf16[448,128]{1,0:T(8,128)(2,1)S(1)}, u32[]{:S(2)}, u32[]{:S(2)}) collective-permute-start(bf16[448,128]{1,0:T(8,128)(2,1)S(1)} %shard_map.87.q0), channel_id=1, source_target_pairs={{0,64},{64,0},{1,65},{65,1},{2,66},{66,2},{3,67},{67,3},{4,68},{68... | collective-permute-start | bytes 344072 | tf_op jit(solution)/shard_map/ppermute | solution.py:142
  138.3 1.9 %collective-permute-start.41 = (bf16[448,128]{1,0:T(8,128)(2,1)S(1)}, bf16[448,128]{1,0:T(8,128)(2,1)S(1)}, u32[]{:S(2)}, u32[]{:S(2)}) collective-permute-start(bf16[448,128]{1,0:T(8,128)(2,1)S(1)} %collective-permute-done.37.q2), channel_id=1, source_target_pairs={{0,64},{64,0},{1,65},{65,1},{2,66},{66,2},{3,67},{67,3},{4,68},{68... | collective-permute-start | bytes 344072 | tf_op jit(solution)/shard_map/ppermute | solution.py:142
  140.3 1.9 %shard_map.88 = (bf16[2,32,32,128]{3,2,1,0:T(8,128)(2,1)}, bf16[2,32,32,128]{3,2,1,0:T(8,128)(2,1)}, f32[3456,128]{1,0:T(8,128)}, f32[8,128]{1,0:T(8,128)S(1)}) custom-call(s32[3]{0:T(128)S(1)} %pad_add_fusion.idx, bf16[6,8,32,128]{3,2,1,0:T(8,128)(2,1)S(1)} %get-tuple-element.61.x0.a0, bf16[6,8,32,128]{3,2,1,0:T(8,128)(2,1)S(1)} %collective-permute-done.16.x1.a1, ...), custom_call_target="tpu_custom_call" | custom-call | tf_op jit(solution)/shard_map/pallas_call | solution.py:560
  142.2 2.1 %finish.1 = (f32[3456,128]{1,0:T(8,128)}, f32[1,128]{1,0:T(1,128)}) custom-call(s32[3]{0:T(128)S(1)} %pad_add_fusion.idx, bf16[448,128]{1,0:T(8,128)(2,1)S(1)} %collective-permute-done.39.q0, bf16[448,128]{1,0:T(8,128)(2,1)S(1)} %collective-permute-done.40.q1, bf16[448,128]{1,0:T(8,128)(2,1)S(1)} %collective-permute-done.41.q2, ...), custom_call_target="tpu_custom_call", output_to_operand_aliasing={{0}: (6, {})} | custom-call | tf_op jit(solution)/shard_map/finish/pallas_call | solution.py:605
  (71 shorter events, 11.1 us)
Async XLA Ops:
  0.6 27.2 %copy-start = (bf16[1,3456,128]{2,1,0:T(8,128)(2,1)S(1)}, bf16[1,3456,128]{2,1,0:T(8,128)(2,1)}, u32[]{:S(2)}) copy-start(bf16[1,3456,128]{2,1,0:T(8,128)(2,1)} %param.5) | copy-start | bytes 2654212
  1.8 9.7 %collective-permute-start.7 = (bf16[880,128]{1,0:T(8,128)(2,1)S(1)}, bf16[880,128]{1,0:T(8,128)(2,1)S(1)}, u32[]{:S(2)}, u32[]{:S(2)}) collective-permute-start(bf16[880,128]{1,0:T(8,128)(2,1)S(1)} %get-tuple-element.50), channel_id=1, source_target_pairs={{0,48},{16,0},{32,16},{48,32},{1,49},{17,1},{33,17},{49,33},{2,50}... | collective-permute-start | bytes 675848 | tf_op jit(solution)/shard_map/ppermute | solution.py:189
  6.5 7.3 %collective-permute-start.2 = (bf16[880,128]{1,0:T(8,128)(2,1)S(1)}, bf16[880,128]{1,0:T(8,128)(2,1)S(1)}, u32[]{:S(2)}, u32[]{:S(2)}) collective-permute-start(bf16[880,128]{1,0:T(8,128)(2,1)S(1)} %get-tuple-element.50), channel_id=1, source_target_pairs={{0,16},{16,32},{32,48},{48,0},{1,17},{17,33},{33,49},{49,1},{2,18}... | collective-permute-start | bytes 675848 | tf_op jit(solution)/shard_map/ppermute | solution.py:189
  6.5 10.6 %collective-permute-start.5 = (bf16[880,128]{1,0:T(8,128)(2,1)S(1)}, bf16[880,128]{1,0:T(8,128)(2,1)S(1)}, u32[]{:S(2)}, u32[]{:S(2)}) collective-permute-start(bf16[880,128]{1,0:T(8,128)(2,1)S(1)} %get-tuple-element.51), channel_id=1, source_target_pairs={{0,48},{16,0},{32,16},{48,32},{1,49},{17,1},{33,17},{49,33},{2,50}... | collective-permute-start | bytes 675848 | tf_op jit(solution)/shard_map/ppermute | solution.py:189
  9.1 9.5 %collective-permute-start.3 = (bf16[880,128]{1,0:T(8,128)(2,1)S(1)}, bf16[880,128]{1,0:T(8,128)(2,1)S(1)}, u32[]{:S(2)}, u32[]{:S(2)}) collective-permute-start(bf16[880,128]{1,0:T(8,128)(2,1)S(1)} %get-tuple-element.51), channel_id=1, source_target_pairs={{0,16},{16,32},{32,48},{48,0},{1,17},{17,33},{33,49},{49,1},{2,18}... | collective-permute-start | bytes 675848 | tf_op jit(solution)/shard_map/ppermute | solution.py:189
  10.2 9.5 %collective-permute-start.1 = (bf16[2,24,32,128]{3,2,1,0:T(8,128)(2,1)S(1)}, bf16[2,24,32,128]{3,2,1,0:T(8,128)(2,1)S(1)}, u32[]{:S(2)}, u32[]{:S(2)}) collective-permute-start(bf16[2,24,32,128]{3,2,1,0:T(8,128)(2,1)S(1)} %shard_map.75.own), channel_id=1, source_target_pairs={{0,1},{2,3},{4,5},{6,7},{8,9},{10,11},{12,13},{14,15},{1,0},{3,2},... | collective-permute-start | bytes 1179656 | tf_op jit(solution)/shard_map/ppermute | solution.py:138
  11.5 11.1 %collective-permute-start = (bf16[2,24,32,128]{3,2,1,0:T(8,128)(2,1)S(1)}, bf16[2,24,32,128]{3,2,1,0:T(8,128)(2,1)S(1)}, u32[]{:S(2)}, u32[]{:S(2)}) collective-permute-start(bf16[2,24,32,128]{3,2,1,0:T(8,128)(2,1)S(1)} %shard_map.75.own), channel_id=1, source_target_pairs={{1,2},{3,4},{5,6},{7,8},{9,10},{11,12},{13,14},{2,1},{4,3},{6,5},{... | collective-permute-start | bytes 1179656 | tf_op jit(solution)/shard_map/ppermute | solution.py:138
  13.8 9.5 %collective-permute-start.12 = (bf16[880,128]{1,0:T(8,128)(2,1)S(1)}, bf16[880,128]{1,0:T(8,128)(2,1)S(1)}, u32[]{:S(2)}, u32[]{:S(2)}) collective-permute-start(bf16[880,128]{1,0:T(8,128)(2,1)S(1)} %collective-permute-done.7.rest_4_.rest_15_), channel_id=1, source_target_pairs={{0,64},{64,0},{1,65},{65,1},{2,66},{66,2},{3,67},{67,3},{4,68},{68... | collective-permute-start | bytes 675848 | tf_op jit(solution)/shard_map/ppermute | solution.py:142
  17.0 7.8 %collective-permute-start.4 = (bf16[880,128]{1,0:T(8,128)(2,1)S(1)}, bf16[880,128]{1,0:T(8,128)(2,1)S(1)}, u32[]{:S(2)}, u32[]{:S(2)}) collective-permute-start(bf16[880,128]{1,0:T(8,128)(2,1)S(1)} %collective-permute-done.2.rest_0_.rest_13_), channel_id=1, source_target_pairs={{0,16},{16,32},{32,48},{48,0},{1,17},{17,33},{33,49},{49,1},{2,18}... | collective-permute-start | bytes 675848 | tf_op jit(solution)/shard_map/ppermute | solution.py:189
  18.6 7.5 %collective-permute-start.6 = (bf16[880,128]{1,0:T(8,128)(2,1)S(1)}, bf16[880,128]{1,0:T(8,128)(2,1)S(1)}, u32[]{:S(2)}, u32[]{:S(2)}) collective-permute-start(bf16[880,128]{1,0:T(8,128)(2,1)S(1)} %collective-permute-done.5.rest_5_), channel_id=1, source_target_pairs={{0,48},{16,0},{32,16},{48,32},{1,49},{17,1},{33,17},{49,33},{2,50}... | collective-permute-start | bytes 675848 | tf_op jit(solution)/shard_map/ppermute | solution.py:189
  20.4 6.2 %collective-permute-start.8 = (bf16[880,128]{1,0:T(8,128)(2,1)S(1)}, bf16[880,128]{1,0:T(8,128)(2,1)S(1)}, u32[]{:S(2)}, u32[]{:S(2)}) collective-permute-start(bf16[880,128]{1,0:T(8,128)(2,1)S(1)} %collective-permute-done.2.rest_0_.rest_13_), channel_id=1, source_target_pairs={{0,64},{64,0},{1,65},{65,1},{2,66},{66,2},{3,67},{67,3},{4,68},{68... | collective-permute-start | bytes 675848 | tf_op jit(solution)/shard_map/ppermute | solution.py:142
  23.3 3.3 %collective-permute-start.13 = (bf16[880,128]{1,0:T(8,128)(2,1)S(1)}, bf16[880,128]{1,0:T(8,128)(2,1)S(1)}, u32[]{:S(2)}, u32[]{:S(2)}) collective-permute-start(bf16[880,128]{1,0:T(8,128)(2,1)S(1)} %collective-permute-done.5.rest_5_), channel_id=1, source_target_pairs={{0,64},{64,0},{1,65},{65,1},{2,66},{66,2},{3,67},{67,3},{4,68},{68... | collective-permute-start | bytes 675848 | tf_op jit(solution)/shard_map/ppermute | solution.py:142
  23.3 3.3 %collective-permute-start.9 = (bf16[880,128]{1,0:T(8,128)(2,1)S(1)}, bf16[880,128]{1,0:T(8,128)(2,1)S(1)}, u32[]{:S(2)}, u32[]{:S(2)}) collective-permute-start(bf16[880,128]{1,0:T(8,128)(2,1)S(1)} %collective-permute-done.3.rest_1_), channel_id=1, source_target_pairs={{0,64},{64,0},{1,65},{65,1},{2,66},{66,2},{3,67},{67,3},{4,68},{68... | collective-permute-start | bytes 675848 | tf_op jit(solution)/shard_map/ppermute | solution.py:142
  24.8 2.4 %collective-permute-start.10 = (bf16[880,128]{1,0:T(8,128)(2,1)S(1)}, bf16[880,128]{1,0:T(8,128)(2,1)S(1)}, u32[]{:S(2)}, u32[]{:S(2)}) collective-permute-start(bf16[880,128]{1,0:T(8,128)(2,1)S(1)} %collective-permute-done.4.rest_2_.rest_14_), channel_id=1, source_target_pairs={{0,64},{64,0},{1,65},{65,1},{2,66},{66,2},{3,67},{67,3},{4,68},{68... | collective-permute-start | bytes 675848 | tf_op jit(solution)/shard_map/ppermute | solution.py:142
  26.2 1.6 %collective-permute-start.11 = (bf16[880,128]{1,0:T(8,128)(2,1)S(1)}, bf16[880,128]{1,0:T(8,128)(2,1)}, u32[]{:S(2)}, u32[]{:S(2)}) collective-permute-start(bf16[880,128]{1,0:T(8,128)(2,1)S(1)} %collective-permute-done.6.rest_3_), channel_id=1, source_target_pairs={{0,64},{64,0},{1,65},{65,1},{2,66},{66,2},{3,67},{67,3},{4,68},{68... | collective-permute-start | bytes 675848 | tf_op jit(solution)/shard_map/ppermute | solution.py:142
  27.8 1.0 copy-start.2
  28.8 1.0 copy-start.5
  29.8 1.0 copy-start.7
  38.9 10.3 %copy-start.3 = (bf16[1,2,32,32,128]{4,3,2,1,0:T(8,128)(2,1)S(1)}, bf16[1,2,32,32,128]{4,3,2,1,0:T(8,128)(2,1)}, u32[]{:S(2)}) copy-start(bf16[1,2,32,32,128]{4,3,2,1,0:T(8,128)(2,1)} %param.7) | copy-start | bytes 1572868
  38.9 10.3 %collective-permute-start.15 = (bf16[2,20,32,128]{3,2,1,0:T(8,128)(2,1)S(1)}, bf16[2,20,32,128]{3,2,1,0:T(8,128)(2,1)S(1)}, u32[]{:S(2)}, u32[]{:S(2)}) collective-permute-start(bf16[2,20,32,128]{3,2,1,0:T(8,128)(2,1)S(1)} %get-tuple-element.55.own), channel_id=1, source_target_pairs={{0,1},{2,3},{4,5},{6,7},{8,9},{10,11},{12,13},{14,15},{1,0},{3,2},... | collective-permute-start | bytes 983048 | tf_op jit(solution)/shard_map/ppermute | solution.py:138
  41.4 7.8 %collective-permute-start.14 = (bf16[2,20,32,128]{3,2,1,0:T(8,128)(2,1)S(1)}, bf16[2,20,32,128]{3,2,1,0:T(8,128)(2,1)S(1)}, u32[]{:S(2)}, u32[]{:S(2)}) collective-permute-start(bf16[2,20,32,128]{3,2,1,0:T(8,128)(2,1)S(1)} %get-tuple-element.55.own), channel_id=1, source_target_pairs={{1,2},{3,4},{5,6},{7,8},{9,10},{11,12},{13,14},{2,1},{4,3},{6,5},{... | collective-permute-start | bytes 983048 | tf_op jit(solution)/shard_map/ppermute | solution.py:138
  56.4 10.1 %collective-permute-start.20 = (bf16[2,16,32,128]{3,2,1,0:T(8,128)(2,1)S(1)}, bf16[2,16,32,128]{3,2,1,0:T(8,128)(2,1)S(1)}, u32[]{:S(2)}, u32[]{:S(2)}) collective-permute-start(bf16[2,16,32,128]{3,2,1,0:T(8,128)(2,1)S(1)} %get-tuple-element.65.own.e3), channel_id=1, source_target_pairs={{0,1},{2,3},{4,5},{6,7},{8,9},{10,11},{12,13},{14,15},{1,0},{3,2},... | collective-permute-start | bytes 786440 | tf_op jit(solution)/shard_map/ppermute | solution.py:138
  60.7 5.9 %collective-permute-start.19 = (bf16[2,16,32,128]{3,2,1,0:T(8,128)(2,1)S(1)}, bf16[2,16,32,128]{3,2,1,0:T(8,128)(2,1)S(1)}, u32[]{:S(2)}, u32[]{:S(2)}) collective-permute-start(bf16[2,16,32,128]{3,2,1,0:T(8,128)(2,1)S(1)} %get-tuple-element.65.own.e3), channel_id=1, source_target_pairs={{1,2},{3,4},{5,6},{7,8},{9,10},{11,12},{13,14},{2,1},{4,3},{6,5},{... | collective-permute-start | bytes 786440 | tf_op jit(solution)/shard_map/ppermute | solution.py:138
  62.1 26.0 %collective-permute-start.16 = (bf16[6,8,32,128]{3,2,1,0:T(8,128)(2,1)S(1)}, bf16[6,8,32,128]{3,2,1,0:T(8,128)(2,1)S(1)}, u32[]{:S(2)}, u32[]{:S(2)}) collective-permute-start(bf16[6,8,32,128]{3,2,1,0:T(8,128)(2,1)S(1)} %get-tuple-element.62), channel_id=1, source_target_pairs={{0,16},{16,0},{32,48},{48,32},{1,17},{17,1},{33,49},{49,33},{2,18}... | collective-permute-start | bytes 1179656 | tf_op jit(solution)/shard_map/ppermute | solution.py:126
  62.4 25.7 %collective-permute-start.17 = (bf16[6,8,32,128]{3,2,1,0:T(8,128)(2,1)S(1)}, bf16[6,8,32,128]{3,2,1,0:T(8,128)(2,1)S(1)}, u32[]{:S(2)}, u32[]{:S(2)}) collective-permute-start(bf16[6,8,32,128]{3,2,1,0:T(8,128)(2,1)S(1)} %get-tuple-element.63), channel_id=1, source_target_pairs={{0,32},{16,48},{32,0},{48,16},{1,33},{17,49},{33,1},{49,17},{2,34}... | collective-permute-start | bytes 1179656 | tf_op jit(solution)/shard_map/ppermute | solution.py:126
  66.6 21.6 %collective-permute-start.18 = (bf16[6,8,32,128]{3,2,1,0:T(8,128)(2,1)S(1)}, bf16[6,8,32,128]{3,2,1,0:T(8,128)(2,1)S(1)}, u32[]{:S(2)}, u32[]{:S(2)}) collective-permute-start(bf16[6,8,32,128]{3,2,1,0:T(8,128)(2,1)S(1)} %get-tuple-element.64), channel_id=1, source_target_pairs={{0,48},{16,32},{32,16},{48,0},{1,49},{17,33},{33,17},{49,1},{2,50}... | collective-permute-start | bytes 1179656 | tf_op jit(solution)/shard_map/ppermute | solution.py:126
  72.0 8.4 %collective-permute-start.22 = (bf16[2,12,32,128]{3,2,1,0:T(8,128)(2,1)S(1)}, bf16[2,12,32,128]{3,2,1,0:T(8,128)(2,1)S(1)}, u32[]{:S(2)}, u32[]{:S(2)}) collective-permute-start(bf16[2,12,32,128]{3,2,1,0:T(8,128)(2,1)S(1)} %get-tuple-element.69.own.e1), channel_id=1, source_target_pairs={{0,1},{2,3},{4,5},{6,7},{8,9},{10,11},{12,13},{14,15},{1,0},{3,2},... | collective-permute-start | bytes 589832 | tf_op jit(solution)/shard_map/ppermute | solution.py:138
  77.1 3.4 %collective-permute-start.21 = (bf16[2,12,32,128]{3,2,1,0:T(8,128)(2,1)S(1)}, bf16[2,12,32,128]{3,2,1,0:T(8,128)(2,1)S(1)}, u32[]{:S(2)}, u32[]{:S(2)}) collective-permute-start(bf16[2,12,32,128]{3,2,1,0:T(8,128)(2,1)S(1)} %get-tuple-element.69.own.e1), channel_id=1, source_target_pairs={{1,2},{3,4},{5,6},{7,8},{9,10},{11,12},{13,14},{2,1},{4,3},{6,5},{... | collective-permute-start | bytes 589832 | tf_op jit(solution)/shard_map/ppermute | solution.py:138
  83.7 5.1 %collective-permute-start.26 = (bf16[2,8,32,128]{3,2,1,0:T(8,128)(2,1)S(1)}, bf16[2,8,32,128]{3,2,1,0:T(8,128)(2,1)S(1)}, u32[]{:S(2)}, u32[]{:S(2)}) collective-permute-start(bf16[2,8,32,128]{3,2,1,0:T(8,128)(2,1)S(1)} %get-tuple-element.81), channel_id=1, source_target_pairs={{0,16},{16,0},{32,48},{48,32},{1,17},{17,1},{33,49},{49,33},{2,18}... | collective-permute-start | bytes 393224 | tf_op jit(solution)/shard_map/ppermute | solution.py:126
  83.9 8.0 %collective-permute-start.27 = (bf16[2,8,32,128]{3,2,1,0:T(8,128)(2,1)S(1)}, bf16[2,8,32,128]{3,2,1,0:T(8,128)(2,1)S(1)}, u32[]{:S(2)}, u32[]{:S(2)}) collective-permute-start(bf16[2,8,32,128]{3,2,1,0:T(8,128)(2,1)S(1)} %get-tuple-element.82), channel_id=1, source_target_pairs={{0,32},{16,48},{32,0},{48,16},{1,33},{17,49},{33,1},{49,17},{2,34}... | collective-permute-start | bytes 393224 | tf_op jit(solution)/shard_map/ppermute | solution.py:126
  88.1 5.2 %collective-permute-start.28 = (bf16[2,8,32,128]{3,2,1,0:T(8,128)(2,1)S(1)}, bf16[2,8,32,128]{3,2,1,0:T(8,128)(2,1)S(1)}, u32[]{:S(2)}, u32[]{:S(2)}) collective-permute-start(bf16[2,8,32,128]{3,2,1,0:T(8,128)(2,1)S(1)} %get-tuple-element.83), channel_id=1, source_target_pairs={{0,48},{16,32},{32,16},{48,0},{1,49},{17,33},{33,17},{49,1},{2,50}... | collective-permute-start | bytes 393224 | tf_op jit(solution)/shard_map/ppermute | solution.py:126
  97.3 5.8 %collective-permute-start.29 = (bf16[1792,128]{1,0:T(8,128)(2,1)S(1)}, bf16[1792,128]{1,0:T(8,128)(2,1)S(1)}, u32[]{:S(2)}, u32[]{:S(2)}) collective-permute-start(bf16[1792,128]{1,0:T(8,128)(2,1)S(1)} %get-tuple-element.85), channel_id=1, source_target_pairs={{0,64},{64,0},{1,65},{65,1},{2,66},{66,2},{3,67},{67,3},{4,68},{68... | collective-permute-start | bytes 1376264 | tf_op jit(solution)/shard_map/ppermute | solution.py:142
  103.8 9.7 %collective-permute-start.30 = (bf16[448,128]{1,0:T(8,128)(2,1)S(1)}, bf16[448,128]{1,0:T(8,128)(2,1)S(1)}, u32[]{:S(2)}, u32[]{:S(2)}) collective-permute-start(bf16[448,128]{1,0:T(8,128)(2,1)S(1)} %get-tuple-element.87), channel_id=1, source_target_pairs={{0,1},{1,0},{2,3},{3,2},{4,5},{5,4},{6,7},{7,6},{8,9},{9,8},{10,11... | collective-permute-start | bytes 344072 | tf_op jit(solution)/shard_map/ppermute | solution.py:145
  109.6 9.2 %collective-permute-start.31 = (bf16[448,128]{1,0:T(8,128)(2,1)S(1)}, bf16[448,128]{1,0:T(8,128)(2,1)S(1)}, u32[]{:S(2)}, u32[]{:S(2)}) collective-permute-start(bf16[448,128]{1,0:T(8,128)(2,1)S(1)} %get-tuple-element.88), channel_id=1, source_target_pairs={{0,2},{1,3},{2,0},{3,1},{4,6},{5,7},{6,4},{7,5},{8,10},{9,11},{10,... | collective-permute-start | bytes 344072 | tf_op jit(solution)/shard_map/ppermute | solution.py:145
  113.5 7.9 %collective-permute-start.32 = (bf16[448,128]{1,0:T(8,128)(2,1)S(1)}, bf16[448,128]{1,0:T(8,128)(2,1)S(1)}, u32[]{:S(2)}, u32[]{:S(2)}) collective-permute-start(bf16[448,128]{1,0:T(8,128)(2,1)S(1)} %get-tuple-element.89), channel_id=1, source_target_pairs={{0,3},{1,2},{2,1},{3,0},{4,7},{5,6},{6,5},{7,4},{8,11},{9,10},{10,... | collective-permute-start | bytes 344072 | tf_op jit(solution)/shard_map/ppermute | solution.py:145
  121.5 8.1 %collective-permute-start.35 = (bf16[448,128]{1,0:T(8,128)(2,1)S(1)}, bf16[448,128]{1,0:T(8,128)(2,1)S(1)}, u32[]{:S(2)}, u32[]{:S(2)}) collective-permute-start(bf16[448,128]{1,0:T(8,128)(2,1)S(1)} %add_convert_fusion.q0), channel_id=1, source_target_pairs={{0,12},{1,13},{2,14},{3,15},{4,8},{5,9},{6,10},{7,11},{8,4},{9,5},... | collective-permute-start | bytes 344072 | tf_op jit(solution)/shard_map/ppermute | solution.py:148
  121.9 7.7 %collective-permute-start.34 = (bf16[448,128]{1,0:T(8,128)(2,1)S(1)}, bf16[448,128]{1,0:T(8,128)(2,1)S(1)}, u32[]{:S(2)}, u32[]{:S(2)}) collective-permute-start(bf16[448,128]{1,0:T(8,128)(2,1)S(1)} %add_convert_fusion.q0), channel_id=1, source_target_pairs={{0,8},{1,9},{2,10},{3,11},{4,12},{5,13},{6,14},{7,15},{8,0},{9,1},... | collective-permute-start | bytes 344072 | tf_op jit(solution)/shard_map/ppermute | solution.py:148
  124.6 5.0 %collective-permute-start.33 = (bf16[448,128]{1,0:T(8,128)(2,1)S(1)}, bf16[448,128]{1,0:T(8,128)(2,1)S(1)}, u32[]{:S(2)}, u32[]{:S(2)}) collective-permute-start(bf16[448,128]{1,0:T(8,128)(2,1)S(1)} %add_convert_fusion.q0), channel_id=1, source_target_pairs={{0,4},{1,5},{2,6},{3,7},{4,0},{5,1},{6,2},{7,3},{8,12},{9,13},{10,... | collective-permute-start | bytes 344072 | tf_op jit(solution)/shard_map/ppermute | solution.py:148
  126.4 7.2 %collective-permute-start.23 = (bf16[2,8,32,128]{3,2,1,0:T(8,128)(2,1)S(1)}, bf16[2,8,32,128]{3,2,1,0:T(8,128)(2,1)S(1)}, u32[]{:S(2)}, u32[]{:S(2)}) collective-permute-start(bf16[2,8,32,128]{3,2,1,0:T(8,128)(2,1)S(1)} %get-tuple-element.77), channel_id=1, source_target_pairs={{0,16},{16,0},{32,48},{48,32},{1,17},{17,1},{33,49},{49,33},{2,18}... | collective-permute-start | bytes 393224 | tf_op jit(solution)/shard_map/ppermute | solution.py:126
  126.5 7.9 %collective-permute-start.24 = (bf16[2,8,32,128]{3,2,1,0:T(8,128)(2,1)S(1)}, bf16[2,8,32,128]{3,2,1,0:T(8,128)(2,1)S(1)}, u32[]{:S(2)}, u32[]{:S(2)}) collective-permute-start(bf16[2,8,32,128]{3,2,1,0:T(8,128)(2,1)S(1)} %get-tuple-element.78), channel_id=1, source_target_pairs={{0,32},{16,48},{32,0},{48,16},{1,33},{17,49},{33,1},{49,17},{2,34}... | collective-permute-start | bytes 393224 | tf_op jit(solution)/shard_map/ppermute | solution.py:126
  130.3 7.4 %collective-permute-start.38 = (bf16[448,128]{1,0:T(8,128)(2,1)S(1)}, bf16[448,128]{1,0:T(8,128)(2,1)S(1)}, u32[]{:S(2)}, u32[]{:S(2)}) collective-permute-start(bf16[448,128]{1,0:T(8,128)(2,1)S(1)} %shard_map.87.q0), channel_id=1, source_target_pairs={{0,3},{1,2},{2,1},{3,0},{4,7},{5,6},{6,5},{7,4},{8,11},{9,10},{10,... | collective-permute-start | bytes 344072 | tf_op jit(solution)/shard_map/ppermute | solution.py:145
  131.0 7.4 %collective-permute-start.37 = (bf16[448,128]{1,0:T(8,128)(2,1)S(1)}, bf16[448,128]{1,0:T(8,128)(2,1)S(1)}, u32[]{:S(2)}, u32[]{:S(2)}) collective-permute-start(bf16[448,128]{1,0:T(8,128)(2,1)S(1)} %shard_map.87.q0), channel_id=1, source_target_pairs={{0,2},{1,3},{2,0},{3,1},{4,6},{5,7},{6,4},{7,5},{8,10},{9,11},{10,... | collective-permute-start | bytes 344072 | tf_op jit(solution)/shard_map/ppermute | solution.py:145
  131.0 9.2 %collective-permute-start.36 = (bf16[448,128]{1,0:T(8,128)(2,1)S(1)}, bf16[448,128]{1,0:T(8,128)(2,1)S(1)}, u32[]{:S(2)}, u32[]{:S(2)}) collective-permute-start(bf16[448,128]{1,0:T(8,128)(2,1)S(1)} %shard_map.87.q0), channel_id=1, source_target_pairs={{0,1},{1,0},{2,3},{3,2},{4,5},{5,4},{6,7},{7,6},{8,9},{9,8},{10,11... | collective-permute-start | bytes 344072 | tf_op jit(solution)/shard_map/ppermute | solution.py:145
  133.6 6.7 %collective-permute-start.25 = (bf16[2,8,32,128]{3,2,1,0:T(8,128)(2,1)S(1)}, bf16[2,8,32,128]{3,2,1,0:T(8,128)(2,1)S(1)}, u32[]{:S(2)}, u32[]{:S(2)}) collective-permute-start(bf16[2,8,32,128]{3,2,1,0:T(8,128)(2,1)S(1)} %get-tuple-element.79), channel_id=1, source_target_pairs={{0,48},{16,32},{32,16},{48,0},{1,49},{17,33},{33,17},{49,1},{2,50}... | collective-permute-start | bytes 393224 | tf_op jit(solution)/shard_map/ppermute | solution.py:126
  134.4 7.8 %collective-permute-start.39 = (bf16[448,128]{1,0:T(8,128)(2,1)S(1)}, bf16[448,128]{1,0:T(8,128)(2,1)S(1)}, u32[]{:S(2)}, u32[]{:S(2)}) collective-permute-start(bf16[448,128]{1,0:T(8,128)(2,1)S(1)} %shard_map.87.q0), channel_id=1, source_target_pairs={{0,64},{64,0},{1,65},{65,1},{2,66},{66,2},{3,67},{67,3},{4,68},{68... | collective-permute-start | bytes 344072 | tf_op jit(solution)/shard_map/ppermute | solution.py:142
  137.7 4.5 %collective-permute-start.42 = (bf16[448,128]{1,0:T(8,128)(2,1)S(1)}, bf16[448,128]{1,0:T(8,128)(2,1)S(1)}, u32[]{:S(2)}, u32[]{:S(2)}) collective-permute-start(bf16[448,128]{1,0:T(8,128)(2,1)S(1)} %collective-permute-done.38.q3), channel_id=1, source_target_pairs={{0,64},{64,0},{1,65},{65,1},{2,66},{66,2},{3,67},{67,3},{4,68},{68... | collective-permute-start | bytes 344072 | tf_op jit(solution)/shard_map/ppermute | solution.py:142
  138.3 3.8 %collective-permute-start.41 = (bf16[448,128]{1,0:T(8,128)(2,1)S(1)}, bf16[448,128]{1,0:T(8,128)(2,1)S(1)}, u32[]{:S(2)}, u32[]{:S(2)}) collective-permute-start(bf16[448,128]{1,0:T(8,128)(2,1)S(1)} %collective-permute-done.37.q2), channel_id=1, source_target_pairs={{0,64},{64,0},{1,65},{65,1},{2,66},{66,2},{3,67},{67,3},{4,68},{68... | collective-permute-start | bytes 344072 | tf_op jit(solution)/shard_map/ppermute | solution.py:142
  140.2 2.0 %collective-permute-start.40 = (bf16[448,128]{1,0:T(8,128)(2,1)S(1)}, bf16[448,128]{1,0:T(8,128)(2,1)S(1)}, u32[]{:S(2)}, u32[]{:S(2)}) collective-permute-start(bf16[448,128]{1,0:T(8,128)(2,1)S(1)} %collective-permute-done.36.q1), channel_id=1, source_target_pairs={{0,64},{64,0},{1,65},{65,1},{2,66},{66,2},{3,67},{67,3},{4,68},{68... | collective-permute-start | bytes 344072 | tf_op jit(solution)/shard_map/ppermute | solution.py:142
  (3 other events, 2.2 us)

commit v5 on v4

--- a/solution.py
+++ b/solution.py
@@ -11,7 +11,6 @@
 BF = jnp.bfloat16
 F32 = jnp.float32
 
-SMEM = pl.BlockSpec(memory_space=pltpu.SMEM)
 VMEM = pl.BlockSpec(memory_space=pltpu.VMEM)
 ANY = pl.BlockSpec(memory_space=pl.ANY)
 HBM = pl.BlockSpec(memory_space=pltpu.HBM)
@@ -25,22 +24,29 @@
     return jax.ShapeDtypeStruct(shape, dtype)
 
 
-def call(body, out, n_any_or_specs, scratch, out_specs=None, vmem=20):
+def placed(body):
+    def inner(*refs):
+        return body(tuple(lax.axis_index(name) for name in ("section", "depth", "dp")), *refs)
+
+    return inner
+
+
+def call(body, out, in_specs, scratch, out_specs=None):
     return pl.pallas_call(
         body,
         grid=(1,),
         out_shape=out,
-        in_specs=n_any_or_specs,
+        in_specs=in_specs,
         out_specs=out_specs if out_specs is not None else jax.tree.map(lambda _: VMEM, out),
         scratch_shapes=scratch,
-        compiler_params=pltpu.CompilerParams(vmem_limit_bytes=vmem * 1024 * 1024),
+        compiler_params=pltpu.CompilerParams(vmem_limit_bytes=20 * 1024 * 1024),
     )
 
 
-def column(w_ref, t, C=128):
+def column(w_ref, C=128):
     return jnp.concatenate(
         [
-            jnp.concatenate([w_ref[t, (3 * k + c) * C : (3 * k + c + 1) * C] for c in range(3)], axis=1)
+            jnp.concatenate([w_ref[(3 * k + c) * C : (3 * k + c + 1) * C] for c in range(3)], axis=1)
             for k in range(9)
         ],
         axis=0,
@@ -94,11 +100,11 @@
                 dst[pl.ds(pl.multiple_of((2 - 2 * c + j) * rows, 16), rows)] = swp[2 * i + j][0:rows]
 
 
-def bias_of(s, t, own_bias, got_bias):
+def bias_of(s, t, own_bias, got, rows):
     k = (s + 4 - t) % 4
     row = own_bias[0:1].astype(F32)
     for i in range(3):
-        row = jnp.where(k == i + 1, got_bias[i][0:1].astype(F32), row)
+        row = jnp.where(k == i + 1, got[2 * i][rows : rows + 1].astype(F32), row)
     return row
 
 
@@ -106,9 +112,6 @@
     n_sec = lax.axis_size("section")
     n_dep = lax.axis_size("depth")
     n_dp = lax.axis_size("dp")
-    s = lax.axis_index("section")
-    d = lax.axis_index("depth")
-    c = lax.axis_index("dp")
     assert n_sec == 4 and n_dep == 16 and n_dp == 2
     PL, H, W, C = volume.shape[1:]
     assert PL == 2
@@ -116,7 +119,6 @@
     D = PL * n_dep
     last = n_dep - 1
     grad_scale = 1.0 / math.sqrt(n_dp * D * H * W)
-    idx = jnp.stack([s, d, c]).astype(jnp.int32)
     TAP = 27 * C
     HALF = TAP // 2
     QR = HALF // 2
@@ -195,33 +197,32 @@
     swapped = [swap(g) for g in got]
     all_w = (own_w, *got, *swapped)
     W_SPECS = [VMEM] * 13
-    all_b = (own_b, a1, a2, a3)
-    tail_rows = pl.BlockSpec((16, C), lambda _: (QR // 16, 0))
-    B_SPECS = [VMEM] + [tail_rows] * 3
-
+
+    @placed
     def turn(idx, own, *rest):
-        got_, swp_, (out, buf) = rest[:6], rest[6:12], rest[12:]
+        got_, swp_, (*outs, buf) = rest[:6], rest[6:12], rest[12:]
         for t in (3, 2, 1, 0):
             load_layer(idx[0], idx[2], t, own, got_, swp_, buf.at[t], QR)
 
             def one(j, _):
-                out[t, pl.ds(pl.multiple_of(j * C, C), C)] = buf[t, pl.ds(pl.multiple_of((26 - j) * C, C), C)].T
+                outs[t][pl.ds(pl.multiple_of(j * C, C), C)] = buf[t, pl.ds(pl.multiple_of((26 - j) * C, C), C)].T
                 return 0
 
             lax.fori_loop(0, 27, one, 0, unroll=3)
 
+    @placed
     def k1(idx, own, lo, hi, ow, *rest):
         got_, swp_, rest = rest[:6], rest[6:12], rest[12:]
-        ob, b1_, b2_, b3_, h0e, pre0, h1e, pre1, h2, x, h1, w = rest
+        ob, h0e, pre0, h1e, pre1, h2, x, h1, w = rest
         s_, d_ = idx[0], idx[1]
         for t in range(2):
             load_layer(s_, idx[2], t, ow, got_, swp_, w.at[t], QR)
         assemble(x, lo, own, hi, d_, last)
         h0e[...] = x[1:5, 8 : 8 + R]
-        b0 = bias_of(s_, 0, ob, (b1_, b2_, b3_))
+        b0 = bias_of(s_, 0, ob, got_, QR)
 
         def one(p, _):
-            pre = conv_plane(x, p, column(w, 0), R + 14) + b0
+            pre = conv_plane(x, p, column(w.at[0]), R + 14) + b0
             h = jnp.where(inside(R + 14, W, C, s_ * R - 7, H, 2 * d_ - 1 + p, D), pre * jax.nn.sigmoid(pre), 0.0)
             h = h.astype(BF).reshape(R + 14, W, C)
             h1[p] = h
@@ -230,10 +231,10 @@
             return 0
 
         lax.fori_loop(0, 4, one, 0)
-        b1 = bias_of(s_, 1, ob, (b1_, b2_, b3_))
+        b1 = bias_of(s_, 1, ob, got_, QR)
 
         def two(p, _):
-            pre = conv_plane(h1, p, column(w, 1), R + 12) + b1
+            pre = conv_plane(h1, p, column(w.at[1]), R + 12) + b1
             h = jnp.where(inside(R + 12, W, C, s_ * R - 6, H, 2 * d_ + p, D), pre * jax.nn.sigmoid(pre), 0.0)
             h2[p] = h.astype(BF).reshape(R + 12, W, C)
             pre1[p] = pre[4 * W : 16 * W].astype(BF).reshape(R + 4, W, C)
@@ -250,32 +251,33 @@
             sds((2, R + 4, W, C)),
             sds((2, R + 12, W, C)),
         ),
-        [SMEM, VMEM, VMEM, VMEM] + W_SPECS + B_SPECS,
+        [VMEM, VMEM, VMEM] + W_SPECS + [VMEM],
         [
             pltpu.VMEM((6, R + 16, W, C), BF),
             pltpu.VMEM((4, R + 14, W, C), BF),
             pltpu.VMEM((2, TAP, C), BF),
         ],
-    )(idx, h0, h0_lo, h0_hi, *all_w, *all_b)
+    )(h0, h0_lo, h0_hi, *all_w, own_b)
 
     h2_lo, h2_hi = both(h2)
 
-    wturn = call(turn, sds((4, TAP, C)), [SMEM] + W_SPECS, [pltpu.VMEM((4, TAP, C), BF)], VMEM)(idx, *all_w)
-    h2_lo, h2_hi, wturn = lax.optimization_barrier((h2_lo, h2_hi, wturn))
-
+    wturn = call(turn, (sds((TAP, C)),) * 4, W_SPECS, [pltpu.VMEM((4, TAP, C), BF)])(*all_w)
+    h2_lo, h2_hi, *wturn = lax.optimization_barrier((h2_lo, h2_hi, *wturn))
+
+    @placed
     def k2(idx, own, lo, hi, ow, *rest):
         got_, swp_, rest = rest[:6], rest[6:12], rest[12:]
-        ob, b1_, b2_, b3_, cot, h2e, pre2, h3e, h4, d3, x, h3, w, gpad = rest
+        ob, cot, h2e, pre2, h3e, h4, d3, x, h3, w, gpad = rest
         s_, d_ = idx[0], idx[1]
         for t in range(2):
             load_layer(s_, idx[2], t + 2, ow, got_, swp_, w.at[t], QR)
         assemble(x, lo, own, hi, d_, last)
         h2e[...] = x[1:5, 6 : 6 + R]
         gpad[:, 4 : 4 + H] = cot[...]
-        b0 = bias_of(s_, 2, ob, (b1_, b2_, b3_))
+        b0 = bias_of(s_, 2, ob, got_, QR)
 
         def one(p, _):
-            pre = conv_plane(x, p, column(w, 0), R + 10) + b0
+            pre = conv_plane(x, p, column(w.at[0]), R + 10) + b0
             h = jnp.where(inside(R + 10, W, C, s_ * R - 5, H, 2 * d_ - 1 + p, D), pre * jax.nn.sigmoid(pre), 0.0)
             h = h.astype(BF).reshape(R + 10, W, C)
             h3[p] = h
@@ -284,10 +286,10 @@
             return 0
 
         lax.fori_loop(0, 4, one, 0)
-        b1 = bias_of(s_, 3, ob, (b1_, b2_, b3_))
+        b1 = bias_of(s_, 3, ob, got_, QR)
 
         def two(p, _):
-            pre = conv_plane(h3, p, column(w, 1), R + 8) + b1
+            pre = conv_plane(h3, p, column(w.at[1]), R + 8) + b1
             h = (pre * jax.nn.sigmoid(pre)).astype(BF).reshape(R + 8, W, C)
             h4[p] = h[4 : 4 + R]
             g = gpad[p, pl.ds(s_ * R, R + 8)].reshape((R + 8) * W, C).astype(F32)
@@ -307,17 +309,18 @@
             sds((2, R, W, C)),
             sds((2, R + 8, W, C)),
         ),
-        [SMEM, VMEM, VMEM, VMEM] + W_SPECS + B_SPECS + [VMEM],
+        [VMEM, VMEM, VMEM] + W_SPECS + [VMEM] + [VMEM],
         [
             pltpu.VMEM((6, R + 12, W, C), BF),
             pltpu.VMEM((4, R + 10, W, C), BF),
             pltpu.VMEM((2, TAP, C), BF),
             pltpu.VMEM((PL, H + 8, W, C), BF),
         ],
-    )(idx, h2, h2_lo, h2_hi, *all_w, *all_b, cotangent[0])
+    )(h2, h2_lo, h2_hi, *all_w, own_b, cotangent[0])
 
     d3_lo, d3_hi = both(d3)
 
+    @placed
     def pack(idx, x0, x1, x2, x3, x4, own, a1, a2, a3):
         xs = (x0, x1, x2, x3)
         for k, out in enumerate((own, a1, a2, a3)):
@@ -329,11 +332,8 @@
                     out[4:6] = x4[...] if t == 3 else xs[t + 1][1:3]
 
     six = sds((6, R, W, C))
-    h_own, *h_send = call(pack, (six,) * 4, [SMEM] + [VMEM] * 5, [])(idx, h0e, h1e, h2e, h3e, h4)
+    h_own, *h_send = call(pack, (six,) * 4, [VMEM] * 5, [])(h0e, h1e, h2e, h3e, h4)
     h_got = [sec(h_send[k - 1], k) for k in (1, 2, 3)]
-
-    def wturn_of(t):
-        return pl.BlockSpec((1, TAP, C), lambda _: (t, 0, 0))
 
     piece = sds((2, R, W, C))
 
@@ -350,12 +350,13 @@
                 def _():
                     outs[k][...] = values[t]()
 
+    @placed
     def k3(idx, own, lo, hi, wa, wb, pre_a, pre_b, ga, da, gb, db, x, dbuf):
         s_, d_ = idx[0], idx[1]
         assemble(x, lo, own, hi, d_, last)
 
         def one(p, _):
-            g = conv_plane(x, p, column(wa, 0), R + 6).astype(BF)
+            g = conv_plane(x, p, column(wa), R + 6).astype(BF)
             dl = delta_of(g, pre_a, p, R + 6, s_ * R - 3, 2 * d_ - 1 + p)
             dbuf[p] = dl
 
@@ -369,7 +370,7 @@
         lax.fori_loop(0, 4, one, 0)
 
         def two(p, _):
-            g = conv_plane(dbuf, p, column(wb, 0), R + 4).astype(BF)
+            g = conv_plane(dbuf, p, column(wb), R + 4).astype(BF)
             gb[p] = g.reshape(R + 4, W, C)[2 : 2 + R]
             db[p] = delta_of(g, pre_b, p, R + 4, s_ * R - 2, 2 * d_ + p)
             return 0
@@ -379,18 +380,19 @@
     g3, d2, g2, d1 = call(
         k3,
         (piece, piece, piece, sds((2, R + 4, W, C))),
-        [SMEM, VMEM, VMEM, VMEM, wturn_of(3), wturn_of(2), VMEM, VMEM],
+        [VMEM, VMEM, VMEM, VMEM, VMEM, VMEM, VMEM],
         [pltpu.VMEM((6, R + 8, W, C), BF), pltpu.VMEM((4, R + 6, W, C), BF)],
-    )(idx, d3, d3_lo, d3_hi, wturn, wturn, pre2, pre1)
+    )(d3, d3_lo, d3_hi, wturn[3], wturn[2], pre2, pre1)
     d1_lo, d1_hi = both(d1)
 
+    @placed
     def k4a(idx, own, lo, hi, wa, pre_a, e1, e2, e3, g1, dbuf, *rest):
         *sends, x = rest
         s_, d_ = idx[0], idx[1]
         assemble(x, lo, own, hi, d_, last)
 
         def one(p, _):
-            g = conv_plane(x, p, column(wa, 0), R + 2).astype(BF)
+            g = conv_plane(x, p, column(wa), R + 2).astype(BF)
             dbuf[p] = delta_of(g, pre_a, p, R + 2, s_ * R - 1, 2 * d_ - 1 + p)
 
             @pl.when((p > 0) & (p < 3))
@@ -414,38 +416,41 @@
     g1, d0, *d_send = call(
         k4a,
         (piece, sds((4, R + 2, W, C))) + (piece,) * 4,
-        [SMEM, VMEM, VMEM, VMEM, wturn_of(1), VMEM, VMEM, VMEM, VMEM],
+        [VMEM, VMEM, VMEM, VMEM, VMEM, VMEM, VMEM, VMEM],
         [pltpu.VMEM((6, R + 4, W, C), BF)],
-    )(idx, d1, d1_lo, d1_hi, wturn, pre0, d1, d2, d3)
+    )(d1, d1_lo, d1_hi, wturn[1], pre0, d1, d2, d3)
     d_got = three(sec, d_send)
 
+    @placed
     def k4b(idx, dbuf, wb, g1, g2, g3, *rest):
         *sends, g0 = rest
 
         def two(p, _):
-            g0[p] = conv_plane(dbuf, p, column(wb, 0), R).astype(BF).reshape(R, W, C)
+            g0[p] = conv_plane(dbuf, p, column(wb), R).astype(BF).reshape(R, W, C)
             return 0
 
         lax.fori_loop(0, 2, two, 0)
         send_all(idx[0], sends, (lambda: g0[...], lambda: g1[...], lambda: g2[...], lambda: g3[...]))
 
     g_send = call(
-        k4b, (piece,) * 4, [SMEM, VMEM, wturn_of(0), VMEM, VMEM, VMEM], [pltpu.VMEM(piece.shape, BF)]
-    )(idx, d0, wturn, g1, g2, g3)
+        k4b, (piece,) * 4, [VMEM, VMEM, VMEM, VMEM, VMEM], [pltpu.VMEM(piece.shape, BF)]
+    )(d0, wturn[0], g1, g2, g3)
     g_got = []
     for k in (1, 2, 3):
         g_got.append(sec(g_send[k], k))
 
+    @placed
     def kx(idx, x0, x1, x2, x3, x):
         x[:, 0] = jnp.zeros((4, W, C), BF)
         x[:, H + 1] = jnp.zeros((4, W, C), BF)
         for k, xs in enumerate((x0, x1, x2, x3)):
             x[:, pl.ds((idx[0] ^ k) * R + 1, R)] = xs[0:4]
 
-    x_all = call(kx, sds((4, H + 2, W, C)), [SMEM] + [VMEM] * 4, [], VMEM)(idx, h_own, *h_got)
+    x_all = call(kx, sds((4, H + 2, W, C)), [VMEM] * 4, [], VMEM)(h_own, *h_got)
 
     ROWS = TAP + C
 
+    @placed
     def kw(idx, x, e0, e1, e2, e3, keep, away, dl, wide, out):
         s_ = idx[0]
         for k, es in enumerate((e0, e1, e2, e3)):
@@ -488,16 +493,17 @@
     keep, away = call(
         kw,
         (sds((RH, C), F32), sds((RH, C))),
-        [SMEM] + [VMEM] * 5,
+        [VMEM] * 5,
         [
             pltpu.VMEM((2, H, W, C), BF),
             pltpu.VMEM((2, H * W, 3 * C), BF),
             pltpu.VMEM((28, C, C), F32),
         ],
-    )(idx, x_all, d_send[0], *d_got)
+    )(x_all, d_send[0], *d_got)
 
     recv = swap(away)
 
+    @placed
     def split(idx, keep, recv, mine, q1, q2, q3, buf):
         x = idx[1] % 4
         buf[...] = keep[...].reshape(4, RQ, C) + recv[...].reshape(4, RQ, C).astype(F32)
@@ -507,14 +513,15 @@
 
     quart = sds((RQ, C))
     q, *qs = call(
-        split, (sds((RQ, C), F32), quart, quart, quart), [SMEM, VMEM, VMEM], [pltpu.VMEM((4, RQ, C), F32)]
-    )(idx, keep, recv)
+        split, (sds((RQ, C), F32), quart, quart, quart), [VMEM, VMEM], [pltpu.VMEM((4, RQ, C), F32)]
+    )(keep, recv)
     xs = three(xdep, [None, *qs])
     for v in xs:
         q = q + v.astype(F32)
     q = q.astype(BF)
     ys = three(ydep, [q] * 4)
 
+    @placed
     def ordered(idx, q0, q1, q2, q3, out, buf):
         y = idx[1] // 4
         for k, r in enumerate((q0, q1, q2, q3)):
@@ -524,7 +531,7 @@
             acc = acc + buf[y ^ j]
         out[...] = acc.astype(BF)
 
-    q = call(ordered, sds((RQ, C)), [SMEM] + [VMEM] * 4, [pltpu.VMEM((4, RQ, C), F32)], VMEM)(idx, q, *ys)
+    q = call(ordered, sds((RQ, C)), [VMEM] * 4, [pltpu.VMEM((4, RQ, C), F32)], VMEM)(q, *ys)
     qs = [q] + three(xdep, [q] * 4)
 
     others = [swap(v) for v in qs]
@@ -533,6 +540,7 @@
         for k, q in enumerate(pieces):
             buf[pl.ds(pl.multiple_of((x ^ k) * RQ, 8), RQ)] = q[...].astype(F32) * grad_scale
 
+    @placed
     def place(idx, a0, a1, a2, a3, b0, b1, b2, b3, q0, q1, q2, q3, oa, ob, w_out, b_own, buf, sem):
         copies = []
         for k, (va, vb) in enumerate(((a0, b0), (a1, b1), (a2, b2), (a3, b3))):
@@ -560,11 +568,12 @@
     out_h, out_g, w_part, b_own = call(
         place,
         (full, full, sds((TAP, C), F32), sds((8, C), F32)),
-        [SMEM] + [ANY] * 8 + [VMEM] * 4,
+        [ANY] * 8 + [VMEM] * 4,
         [pltpu.VMEM((RH, C), F32), pltpu.SemaphoreType.DMA((9,))],
         (ANY, ANY, ANY, VMEM),
-    )(idx, h_own, *h_got, g_send[0], *g_got, *qs)
-
+    )(h_own, *h_got, g_send[0], *g_got, *qs)
+
+    @placed
     def finish(idx, q0, q1, q2, q3, b_own, w_in, w_out, b_out, buf, sem):
         parts = 4
         row = TAP - RH
@@ -607,12 +616,12 @@
         name="finish",
         grid=(1,),
         out_shape=(sds((TAP, C), F32), sds((1, C), F32)),
-        in_specs=[SMEM] + [VMEM] * 5 + [ANY],
+        in_specs=[VMEM] * 5 + [ANY],
         out_specs=(ANY, VMEM),
         scratch_shapes=[pltpu.VMEM((RH, C), F32), pltpu.SemaphoreType.DMA((4,))],
-        input_output_aliases={6: 0},
+        input_output_aliases={5: 0},
         compiler_params=pltpu.CompilerParams(vmem_limit_bytes=20 * 1024 * 1024),
-    )(idx, *others, b_own, w_part)
+    )(*others, b_own, w_part)
     return out_h[None, None], out_g[None, None], w_grad[None], b_grad
 
 

time: 146 us -> 136 us (0.932)
  Pallas kernels: 43.1 us -> 34.8 us
  local copies, waits for them, and re-layouts: 5.23 us -> 0.01 us
  waiting for transfers between devices: 25.8 us -> 30 us
    pallas_call x10, Pallas kernels: 23.4 us -> 17.6 us  [the longest x1 4.91 us: shards(): call(k3, (piece, piece, piece, sds((2, R + 4, W, C))), [VMEM, VMEM, VMEM,...]
    unnamed x16 -> x4, local copies, waits for them, and re-layouts: 5.23 us -> 0.01 us
    ppermute x6, waiting for transfers between devices: 3.45 us -> 5.69 us  [ring(): lax.ppermute(v, 'section', [(i, (i + k) % n_sec) for i in range(n_sec)])]
  transfers between devices with their start and end apart: 43 -> 43, of which waited for: 13 -> 14; matrix products, arithmetic and copies ran while one was open for 0% -> 0% of each run, Pallas kernels for 14% -> 11%
where the time goes in v5:
time: 136 us; the launch traced here: 135 us
  starting transfers between devices  69 us (51%)
  Pallas kernels  34.8 us (26%)
  waiting for transfers between devices  30 us (22%)
    ppermute x11, starting transfers between devices, swap(): return lax.ppermute(v, 'dp', [(0, 1), (1, 0)])  18.3 us
    ppermute x8, starting transfers between devices, both(): result.append(lax.ppermute(v, 'depth', pairs + [(b, a) for a, b in pairs]))  15.4 us
    ppermute x6, starting transfers between devices, xdep(): return lax.ppermute(v, 'depth', [(i, i ^ k) for i in range(n_dep)])  13.1 us
    ppermute x9, starting transfers between devices, sec(): return lax.ppermute(v, 'section', [(i, i ^ k) for i in range(n_sec)])  10.6 us
    ppermute x6, starting transfers between devices, ring(): lax.ppermute(v, 'section', [(i, (i + k) % n_sec) for i in range(n_sec)])  8.4 us
    ppermute x6, waiting for transfers between devices, xdep(): return lax.ppermute(v, 'depth', [(i, i ^ k) for i in range(n_dep)])  7.91 us
    pallas_call x1, Pallas kernels, shards(): call(k1, (sds((4, R, W, C)), sds((4, R + 2, W, C)), sds((4, R, W, C)), sd...  7.18 us
    ppermute x8, waiting for transfers between devices, both(): result.append(lax.ppermute(v, 'depth', pairs + [(b, a) for a, b in pairs]))  6.4 us
  transfers between devices with their start and end apart: 43, of which 14 were waited for; matrix products, arithmetic and copies ran while one was open for 0% of the time, Pallas kernels for 11%

profile of v5, /device:TPU:1, one launch (start us, length us, event | category | flops | bytes accessed | tf_op | source)
XLA Modules:
  0.0 134.9 jit_solution(13096898752136838935)
XLA Ops:
  0.6 1.2 shard_map.76
  1.8 4.6 %collective-permute-start.7 = (bf16[880,128]{1,0:T(8,128)(2,1)S(1)}, bf16[880,128]{1,0:T(8,128)(2,1)S(1)}, u32[]{:S(2)}, u32[]{:S(2)}) collective-permute-start(bf16[880,128]{1,0:T(8,128)(2,1)S(1)} %get-tuple-element.57), channel_id=1, source_target_pairs={{0,48},{16,0},{32,16},{48,32},{1,49},{17,1},{33,17},{49,33},{2,50}... | collective-permute-start | bytes 675848 | tf_op jit(solution)/shard_map/ppermute | solution.py:191
  6.5 2.7 %collective-permute-start.5 = (bf16[880,128]{1,0:T(8,128)(2,1)S(1)}, bf16[880,128]{1,0:T(8,128)(2,1)S(1)}, u32[]{:S(2)}, u32[]{:S(2)}) collective-permute-start(bf16[880,128]{1,0:T(8,128)(2,1)S(1)} %get-tuple-element.58), channel_id=1, source_target_pairs={{0,48},{16,0},{32,16},{48,32},{1,49},{17,1},{33,17},{49,33},{2,50}... | collective-permute-start | bytes 675848 | tf_op jit(solution)/shard_map/ppermute | solution.py:191
  9.1 1.1 shard_map.75.refs_0_
  10.2 1.3 collective-permute-start.1
  11.5 0.7 collective-permute-start
  12.2 1.6 %collective-permute-done.2.refs_4_.refs_1_ = bf16[880,128]{1,0:T(8,128)(2,1)S(1)} collective-permute-done((bf16[880,128]{1,0:T(8,128)(2,1)S(1)}, bf16[880,128]{1,0:T(8,128)(2,1)S(1)}, u32[]{:S(2)}, u32[]{:S(2)}) %collective-permute-start.2) | collective-permute-done | bytes 225312 | tf_op jit(solution)/shard_map/ppermute | solution.py:191
  13.8 3.2 %collective-permute-start.12 = (bf16[880,128]{1,0:T(8,128)(2,1)S(1)}, bf16[880,128]{1,0:T(8,128)(2,1)S(1)}, u32[]{:S(2)}, u32[]{:S(2)}) collective-permute-start(bf16[880,128]{1,0:T(8,128)(2,1)S(1)} %collective-permute-done.7.refs_8_.refs_5_), channel_id=1, source_target_pairs={{0,64},{64,0},{1,65},{65,1},{2,66},{66,2},{3,67},{67,3},{4,68},{68... | collective-permute-start | bytes 675848 | tf_op jit(solution)/shard_map/ppermute | solution.py:144
  17.0 1.6 %collective-permute-done.3.refs_5_.refs_2_ = bf16[880,128]{1,0:T(8,128)(2,1)S(1)} collective-permute-done((bf16[880,128]{1,0:T(8,128)(2,1)S(1)}, bf16[880,128]{1,0:T(8,128)(2,1)S(1)}, u32[]{:S(2)}, u32[]{:S(2)}) %collective-permute-start.3) | collective-permute-done | bytes 225312 | tf_op jit(solution)/shard_map/ppermute | solution.py:191
  18.6 1.1 collective-permute-start.6
  19.7 2.1 %collective-permute-start.8 = (bf16[880,128]{1,0:T(8,128)(2,1)S(1)}, bf16[880,128]{1,0:T(8,128)(2,1)S(1)}, u32[]{:S(2)}, u32[]{:S(2)}) collective-permute-start(bf16[880,128]{1,0:T(8,128)(2,1)S(1)} %collective-permute-done.2.refs_4_.refs_1_), channel_id=1, source_target_pairs={{0,64},{64,0},{1,65},{65,1},{2,66},{66,2},{3,67},{67,3},{4,68},{68... | collective-permute-start | bytes 675848 | tf_op jit(solution)/shard_map/ppermute | solution.py:144
  22.3 2.5 %collective-permute-done.4.refs_6_.refs_3_ = bf16[880,128]{1,0:T(8,128)(2,1)S(1)} collective-permute-done((bf16[880,128]{1,0:T(8,128)(2,1)S(1)}, bf16[880,128]{1,0:T(8,128)(2,1)S(1)}, u32[]{:S(2)}, u32[]{:S(2)}) %collective-permute-start.4) | collective-permute-done | bytes 225312 | tf_op jit(solution)/shard_map/ppermute | solution.py:191
  24.8 1.3 collective-permute-start.10
  26.6 0.7 collective-permute-done.10.refs_12_.refs_9_
  27.7 7.2 %shard_map.77 = (bf16[4,8,32,128]{3,2,1,0:T(8,128)(2,1)S(1)}, bf16[4,10,32,128]{3,2,1,0:T(8,128)(2,1)S(1)}, bf16[4,8,32,128]{3,2,1,0:T(8,128)(2,1)S(1)}, bf16[2,...) custom-call(bf16[2,24,32,128]{3,2,1,0:T(8,128)(2,1)S(1)} %shard_map.75.refs_0_, ...), custom_call_target="tpu_custom_call" | custom-call | tf_op jit(solution)/shard_map/pallas_call | solution.py:245
  34.9 1.8 %collective-permute-start.15 = (bf16[2,20,32,128]{3,2,1,0:T(8,128)(2,1)S(1)}, bf16[2,20,32,128]{3,2,1,0:T(8,128)(2,1)S(1)}, u32[]{:S(2)}, u32[]{:S(2)}) collective-permute-start(bf16[2,20,32,128]{3,2,1,0:T(8,128)(2,1)S(1)} %get-tuple-element.62.refs_0_), channel_id=1, source_target_pairs={{0,1},{2,3},{4,5},{6,7},{8,9},{10,11},{12,13},{14,15},{1,0},{3,2},... | collective-permute-start | bytes 983048 | tf_op jit(solution)/shard_map/ppermute | solution.py:140
  36.7 0.7 collective-permute-start.14
  37.3 3.5 %shard_map.78 = (bf16[3456,128]{1,0:T(8,128)(2,1)S(1)}, bf16[3456,128]{1,0:T(8,128)(2,1)S(1)}, bf16[3456,128]{1,0:T(8,128)(2,1)S(1)}, bf16[3456,128]{1,0:T(8,128)(2,1)S(1)}) custom-call(bf16[3456,128]{1,0:T(8,128)(2,1)S(1)} %bitcast.9, bf16[880,128]{1,0:T(8,128)(2,1)S(1)} %collective-permute-done.2.refs_4_.refs_1_, ...), custom_call_target="tpu_custom_call" | custom-call | tf_op jit(solution)/shard_map/pallas_call | solution.py:264
  40.8 3.5 %collective-permute-done.15.refs_2_ = bf16[2,20,32,128]{3,2,1,0:T(8,128)(2,1)S(1)} collective-permute-done((bf16[2,20,32,128]{3,2,1,0:T(8,128)(2,1)S(1)}, bf16[2,20,32,128]{3,2,1,0:T(8,128)(2,1)S(1)}, u32[]{:S(2)}, u32[]{:S(2)}) %collective-permute-start.15) | collective-permute-done | bytes 327712 | tf_op jit(solution)/shard_map/ppermute | solution.py:140
  44.4 6.2 %shard_map.79 = (bf16[4,8,32,128]{3,2,1,0:T(8,128)(2,1)S(1)}, bf16[4,14,32,128]{3,2,1,0:T(8,128)(2,1)S(1)}, bf16[4,8,32,128]{3,2,1,0:T(8,128)(2,1)S(1)}, bf16[2,...) custom-call(bf16[2,20,32,128]{3,2,1,0:T(8,128)(2,1)S(1)} %get-tuple-element.62.refs_0_, ...), custom_call_target="tpu_custom_call" | custom-call | tf_op jit(solution)/shard_map/pallas_call | solution.py:303
  50.6 4.2 %collective-permute-start.20 = (bf16[2,16,32,128]{3,2,1,0:T(8,128)(2,1)S(1)}, bf16[2,16,32,128]{3,2,1,0:T(8,128)(2,1)S(1)}, u32[]{:S(2)}, u32[]{:S(2)}) collective-permute-start(bf16[2,16,32,128]{3,2,1,0:T(8,128)(2,1)S(1)} %get-tuple-element.76.refs_0_.refs_7_), channel_id=1, source_target_pairs={{0,1},{2,3},{4,5},{6,7},{8,9},{10,11},{12,13},{14,15},{1,0},{3,2},... | collective-permute-start | bytes 786440 | tf_op jit(solution)/shard_map/ppermute | solution.py:140
  54.8 0.7 collective-permute-start.19
  56.0 4.2 %collective-permute-start.17 = (bf16[6,8,32,128]{3,2,1,0:T(8,128)(2,1)S(1)}, bf16[6,8,32,128]{3,2,1,0:T(8,128)(2,1)S(1)}, u32[]{:S(2)}, u32[]{:S(2)}) collective-permute-start(bf16[6,8,32,128]{3,2,1,0:T(8,128)(2,1)S(1)} %get-tuple-element.74), channel_id=1, source_target_pairs={{0,32},{16,48},{32,0},{48,16},{1,33},{17,49},{33,1},{49,17},{2,34}... | collective-permute-start | bytes 1179656 | tf_op jit(solution)/shard_map/ppermute | solution.py:128
  60.3 4.9 %shard_map.81 = (bf16[2,8,32,128]{3,2,1,0:T(8,128)(2,1)S(1)}, bf16[2,8,32,128]{3,2,1,0:T(8,128)(2,1)S(1)}, bf16[2,8,32,128]{3,2,1,0:T(8,128)(2,1)S(1)}, bf16[2,12,32,128]{3,2,1,0:T(8,128)(2,1)S(1)}) custom-call(bf16[2,16,32,128]{3,2,1,0:T(8,128)(2,1)S(1)} %get-tuple-element.76.refs_0_.refs_7_, bf16[2,16,32,128]{3,2,1,0:T(8,128)(2,1)S(1)} %collective-permute-done.19.refs_1_, ...), custom_call_target="tpu_custom_call" | custom-call | tf_op jit(solution)/shard_map/pallas_call | solution.py:380
  65.2 5.4 %collective-permute-start.22 = (bf16[2,12,32,128]{3,2,1,0:T(8,128)(2,1)S(1)}, bf16[2,12,32,128]{3,2,1,0:T(8,128)(2,1)S(1)}, u32[]{:S(2)}, u32[]{:S(2)}) collective-permute-start(bf16[2,12,32,128]{3,2,1,0:T(8,128)(2,1)S(1)} %get-tuple-element.81.refs_0_.refs_5_), channel_id=1, source_target_pairs={{0,1},{2,3},{4,5},{6,7},{8,9},{10,11},{12,13},{14,15},{1,0},{3,2},... | collective-permute-start | bytes 589832 | tf_op jit(solution)/shard_map/ppermute | solution.py:140
  71.3 2.7 %collective-permute-done.22.refs_2_ = bf16[2,12,32,128]{3,2,1,0:T(8,128)(2,1)S(1)} collective-permute-done((bf16[2,12,32,128]{3,2,1,0:T(8,128)(2,1)S(1)}, bf16[2,12,32,128]{3,2,1,0:T(8,128)(2,1)S(1)}, u32[]{:S(2)}, u32[]{:S(2)}) %collective-permute-start.22) | collective-permute-done | bytes 196640 | tf_op jit(solution)/shard_map/ppermute | solution.py:140
  74.0 2.7 %shard_map.82 = (bf16[2,8,32,128]{3,2,1,0:T(8,128)(2,1)S(1)}, bf16[4,10,32,128]{3,2,1,0:T(8,128)(2,1)S(1)}, bf16[2,8,32,128]{3,2,1,0:T(8,128)(2,1)S(1)}, bf16[2,...) custom-call(bf16[2,12,32,128]{3,2,1,0:T(8,128)(2,1)S(1)} %get-tuple-element.81, ...), custom_call_target="tpu_custom_call" | custom-call | tf_op jit(solution)/shard_map/pallas_call | solution.py:416
  77.0 4.2 %collective-permute-start.27 = (bf16[2,8,32,128]{3,2,1,0:T(8,128)(2,1)S(1)}, bf16[2,8,32,128]{3,2,1,0:T(8,128)(2,1)S(1)}, u32[]{:S(2)}, u32[]{:S(2)}) collective-permute-start(bf16[2,8,32,128]{3,2,1,0:T(8,128)(2,1)S(1)} %get-tuple-element.96), channel_id=1, source_target_pairs={{0,32},{16,48},{32,0},{48,16},{1,33},{17,49},{33,1},{49,17},{2,34}... | collective-permute-start | bytes 393224 | tf_op jit(solution)/shard_map/ppermute | solution.py:128
  81.3 3.6 %collective-permute-done.27.refs_3_ = bf16[2,8,32,128]{3,2,1,0:T(8,128)(2,1)S(1)} collective-permute-done((bf16[2,8,32,128]{3,2,1,0:T(8,128)(2,1)S(1)}, bf16[2,8,32,128]{3,2,1,0:T(8,128)(2,1)S(1)}, u32[]{:S(2)}, u32[]{:S(2)}) %collective-permute-start.27) | collective-permute-done | bytes 131104 | tf_op jit(solution)/shard_map/ppermute | solution.py:128
  85.0 1.4 %collective-permute-done.28.refs_4_ = bf16[2,8,32,128]{3,2,1,0:T(8,128)(2,1)S(1)} collective-permute-done((bf16[2,8,32,128]{3,2,1,0:T(8,128)(2,1)S(1)}, bf16[2,8,32,128]{3,2,1,0:T(8,128)(2,1)S(1)}, u32[]{:S(2)}, u32[]{:S(2)}) %collective-permute-start.28) | collective-permute-done | bytes 131104 | tf_op jit(solution)/shard_map/ppermute | solution.py:128
  86.4 3.5 %shard_map.85 = (f32[1792,128]{1,0:T(8,128)S(1)}, bf16[1792,128]{1,0:T(8,128)(2,1)S(1)}) custom-call(bf16[4,34,32,128]{3,2,1,0:T(8,128)(2,1)S(1)} %shard_map.84.refs_0_, bf16[2,8,32,128]{3,2,1,0:T(8,128)(2,1)S(1)} %get-tuple-element.94.refs_1_, bf16[2,8,32,128]{3,2,1,0:T(8,128)(2,1)S(1)} %collective-permute-done.26.refs_2_, ...), custom_call_target="tpu_custom_call" | custom-call | tf_op jit(solution)/shard_map/pallas_call | solution.py:493
  89.9 4.3 %collective-permute-start.29 = (bf16[1792,128]{1,0:T(8,128)(2,1)S(1)}, bf16[1792,128]{1,0:T(8,128)(2,1)S(1)}, u32[]{:S(2)}, u32[]{:S(2)}) collective-permute-start(bf16[1792,128]{1,0:T(8,128)(2,1)S(1)} %get-tuple-element.99), channel_id=1, source_target_pairs={{0,64},{64,0},{1,65},{65,1},{2,66},{66,2},{3,67},{67,3},{4,68},{68... | collective-permute-start | bytes 1376264 | tf_op jit(solution)/shard_map/ppermute | solution.py:144
  94.2 1.4 %collective-permute-done.29.refs_1_ = bf16[1792,128]{1,0:T(8,128)(2,1)S(1)} collective-permute-done((bf16[1792,128]{1,0:T(8,128)(2,1)S(1)}, bf16[1792,128]{1,0:T(8,128)(2,1)S(1)}, u32[]{:S(2)}, u32[]{:S(2)}) %collective-permute-start.29) | collective-permute-done | bytes 458784 | tf_op jit(solution)/shard_map/ppermute | solution.py:144
  95.8 5.8 %collective-permute-start.30 = (bf16[448,128]{1,0:T(8,128)(2,1)S(1)}, bf16[448,128]{1,0:T(8,128)(2,1)S(1)}, u32[]{:S(2)}, u32[]{:S(2)}) collective-permute-start(bf16[448,128]{1,0:T(8,128)(2,1)S(1)} %get-tuple-element.101), channel_id=1, source_target_pairs={{0,1},{1,0},{2,3},{3,2},{4,5},{5,4},{6,7},{7,6},{8,9},{9,8},{10,11... | collective-permute-start | bytes 344072 | tf_op jit(solution)/shard_map/ppermute | solution.py:147
  101.6 3.9 %collective-permute-start.31 = (bf16[448,128]{1,0:T(8,128)(2,1)S(1)}, bf16[448,128]{1,0:T(8,128)(2,1)S(1)}, u32[]{:S(2)}, u32[]{:S(2)}) collective-permute-start(bf16[448,128]{1,0:T(8,128)(2,1)S(1)} %get-tuple-element.102), channel_id=1, source_target_pairs={{0,2},{1,3},{2,0},{3,1},{4,6},{5,7},{6,4},{7,5},{8,10},{9,11},{10,... | collective-permute-start | bytes 344072 | tf_op jit(solution)/shard_map/ppermute | solution.py:147
  105.5 5.3 %collective-permute-done.31 = bf16[448,128]{1,0:T(8,128)(2,1)S(1)} collective-permute-done((bf16[448,128]{1,0:T(8,128)(2,1)S(1)}, bf16[448,128]{1,0:T(8,128)(2,1)S(1)}, u32[]{:S(2)}, u32[]{:S(2)}) %collective-permute-start.31) | collective-permute-done | bytes 114720 | tf_op jit(solution)/shard_map/ppermute | solution.py:147
  110.9 2.6 %collective-permute-done.32 = bf16[448,128]{1,0:T(8,128)(2,1)S(1)} collective-permute-done((bf16[448,128]{1,0:T(8,128)(2,1)S(1)}, bf16[448,128]{1,0:T(8,128)(2,1)S(1)}, u32[]{:S(2)}, u32[]{:S(2)}) %collective-permute-start.32) | collective-permute-done | bytes 114720 | tf_op jit(solution)/shard_map/ppermute | solution.py:147
  114.0 2.6 %collective-permute-start.34 = (bf16[448,128]{1,0:T(8,128)(2,1)S(1)}, bf16[448,128]{1,0:T(8,128)(2,1)S(1)}, u32[]{:S(2)}, u32[]{:S(2)}) collective-permute-start(bf16[448,128]{1,0:T(8,128)(2,1)S(1)} %add_convert_fusion.refs_0_), channel_id=1, source_target_pairs={{0,8},{1,9},{2,10},{3,11},{4,12},{5,13},{6,14},{7,15},{8,0},{9,1},... | collective-permute-start | bytes 344072 | tf_op jit(solution)/shard_map/ppermute | solution.py:150
  116.8 1.1 shard_map.83
  118.0 1.2 collective-permute-start.24
  119.2 2.4 %collective-permute-done.35.refs_3_ = bf16[448,128]{1,0:T(8,128)(2,1)S(1)} collective-permute-done((bf16[448,128]{1,0:T(8,128)(2,1)S(1)}, bf16[448,128]{1,0:T(8,128)(2,1)S(1)}, u32[]{:S(2)}, u32[]{:S(2)}) %collective-permute-start.35) | collective-permute-done | bytes 114720 | tf_op jit(solution)/shard_map/ppermute | solution.py:150
  121.7 0.8 collective-permute-start.38
  122.5 2.5 %collective-permute-start.36 = (bf16[448,128]{1,0:T(8,128)(2,1)S(1)}, bf16[448,128]{1,0:T(8,128)(2,1)S(1)}, u32[]{:S(2)}, u32[]{:S(2)}) collective-permute-start(bf16[448,128]{1,0:T(8,128)(2,1)S(1)} %shard_map.87.refs_8_), channel_id=1, source_target_pairs={{0,1},{1,0},{2,3},{3,2},{4,5},{5,4},{6,7},{7,6},{8,9},{9,8},{10,11... | collective-permute-start | bytes 344072 | tf_op jit(solution)/shard_map/ppermute | solution.py:147
  125.3 3.3 %collective-permute-start.39 = (bf16[448,128]{1,0:T(8,128)(2,1)S(1)}, bf16[448,128]{1,0:T(8,128)(2,1)S(1)}, u32[]{:S(2)}, u32[]{:S(2)}) collective-permute-start(bf16[448,128]{1,0:T(8,128)(2,1)S(1)} %shard_map.87.refs_8_), channel_id=1, source_target_pairs={{0,64},{64,0},{1,65},{65,1},{2,66},{66,2},{3,67},{67,3},{4,68},{68... | collective-permute-start | bytes 344072 | tf_op jit(solution)/shard_map/ppermute | solution.py:144
  128.6 1.1 collective-permute-start.42
  129.8 2.0 %collective-permute-start.41 = (bf16[448,128]{1,0:T(8,128)(2,1)S(1)}, bf16[448,128]{1,0:T(8,128)(2,1)S(1)}, u32[]{:S(2)}, u32[]{:S(2)}) collective-permute-start(bf16[448,128]{1,0:T(8,128)(2,1)S(1)} %collective-permute-done.37.refs_10_), channel_id=1, source_target_pairs={{0,64},{64,0},{1,65},{65,1},{2,66},{66,2},{3,67},{67,3},{4,68},{68... | collective-permute-start | bytes 344072 | tf_op jit(solution)/shard_map/ppermute | solution.py:144
  131.8 1.3 %shard_map.88 = (bf16[2,32,32,128]{3,2,1,0:T(8,128)(2,1)}, bf16[2,32,32,128]{3,2,1,0:T(8,128)(2,1)}, f32[3456,128]{1,0:T(8,128)}, f32[8,128]{1,0:T(8,128)S(1)}) custom-call(bf16[6,8,32,128]{3,2,1,0:T(8,128)(2,1)S(1)} %get-tuple-element.72.refs_0_, bf16[6,8,32,128]{3,2,1,0:T(8,128)(2,1)S(1)} %collective-permute-done.16.refs_1_, ...), custom_call_target="tpu_custom_call" | custom-call | tf_op jit(solution)/shard_map/pallas_call | solution.py:568
  133.2 1.5 %finish.1 = (f32[3456,128]{1,0:T(8,128)}, f32[1,128]{1,0:T(1,128)}) custom-call(bf16[448,128]{1,0:T(8,128)(2,1)S(1)} %collective-permute-done.39.refs_0_, bf16[448,128]{1,0:T(8,128)(2,1)S(1)} %collective-permute-done.40.refs_1_, bf16[448,128]{1,0:T(8,128)(2,1)S(1)} %collective-permute-done.41.refs_2_, ...), custom_call_target="tpu_custom_call", output_to_operand_aliasing={{0}: (5, {})} | custom-call | tf_op jit(solution)/shard_map/finish/pallas_call | solution.py:614
  (58 shorter events, 4.6 us)
Async XLA Ops:
  0.6 27.0 %copy-start = (bf16[1,3456,128]{2,1,0:T(8,128)(2,1)S(1)}, bf16[1,3456,128]{2,1,0:T(8,128)(2,1)}, u32[]{:S(2)}) copy-start(bf16[1,3456,128]{2,1,0:T(8,128)(2,1)} %param.5) | copy-start | bytes 2654212
  1.8 9.7 %collective-permute-start.7 = (bf16[880,128]{1,0:T(8,128)(2,1)S(1)}, bf16[880,128]{1,0:T(8,128)(2,1)S(1)}, u32[]{:S(2)}, u32[]{:S(2)}) collective-permute-start(bf16[880,128]{1,0:T(8,128)(2,1)S(1)} %get-tuple-element.57), channel_id=1, source_target_pairs={{0,48},{16,0},{32,16},{48,32},{1,49},{17,1},{33,17},{49,33},{2,50}... | collective-permute-start | bytes 675848 | tf_op jit(solution)/shard_map/ppermute | solution.py:191
  6.5 7.3 %collective-permute-start.2 = (bf16[880,128]{1,0:T(8,128)(2,1)S(1)}, bf16[880,128]{1,0:T(8,128)(2,1)S(1)}, u32[]{:S(2)}, u32[]{:S(2)}) collective-permute-start(bf16[880,128]{1,0:T(8,128)(2,1)S(1)} %get-tuple-element.57), channel_id=1, source_target_pairs={{0,16},{16,32},{32,48},{48,0},{1,17},{17,33},{33,49},{49,1},{2,18}... | collective-permute-start | bytes 675848 | tf_op jit(solution)/shard_map/ppermute | solution.py:191
  6.5 10.6 %collective-permute-start.5 = (bf16[880,128]{1,0:T(8,128)(2,1)S(1)}, bf16[880,128]{1,0:T(8,128)(2,1)S(1)}, u32[]{:S(2)}, u32[]{:S(2)}) collective-permute-start(bf16[880,128]{1,0:T(8,128)(2,1)S(1)} %get-tuple-element.58), channel_id=1, source_target_pairs={{0,48},{16,0},{32,16},{48,32},{1,49},{17,1},{33,17},{49,33},{2,50}... | collective-permute-start | bytes 675848 | tf_op jit(solution)/shard_map/ppermute | solution.py:191
  9.1 9.5 %collective-permute-start.3 = (bf16[880,128]{1,0:T(8,128)(2,1)S(1)}, bf16[880,128]{1,0:T(8,128)(2,1)S(1)}, u32[]{:S(2)}, u32[]{:S(2)}) collective-permute-start(bf16[880,128]{1,0:T(8,128)(2,1)S(1)} %get-tuple-element.58), channel_id=1, source_target_pairs={{0,16},{16,32},{32,48},{48,0},{1,17},{17,33},{33,49},{49,1},{2,18}... | collective-permute-start | bytes 675848 | tf_op jit(solution)/shard_map/ppermute | solution.py:191
  10.2 9.5 %collective-permute-start.1 = (bf16[2,24,32,128]{3,2,1,0:T(8,128)(2,1)S(1)}, bf16[2,24,32,128]{3,2,1,0:T(8,128)(2,1)S(1)}, u32[]{:S(2)}, u32[]{:S(2)}) collective-permute-start(bf16[2,24,32,128]{3,2,1,0:T(8,128)(2,1)S(1)} %shard_map.75.refs_0_), channel_id=1, source_target_pairs={{0,1},{2,3},{4,5},{6,7},{8,9},{10,11},{12,13},{14,15},{1,0},{3,2},... | collective-permute-start | bytes 1179656 | tf_op jit(solution)/shard_map/ppermute | solution.py:140
  11.5 10.3 %collective-permute-start = (bf16[2,24,32,128]{3,2,1,0:T(8,128)(2,1)S(1)}, bf16[2,24,32,128]{3,2,1,0:T(8,128)(2,1)S(1)}, u32[]{:S(2)}, u32[]{:S(2)}) collective-permute-start(bf16[2,24,32,128]{3,2,1,0:T(8,128)(2,1)S(1)} %shard_map.75.refs_0_), channel_id=1, source_target_pairs={{1,2},{3,4},{5,6},{7,8},{9,10},{11,12},{13,14},{2,1},{4,3},{6,5},{... | collective-permute-start | bytes 1179656 | tf_op jit(solution)/shard_map/ppermute | solution.py:140
  13.8 8.1 %collective-permute-start.12 = (bf16[880,128]{1,0:T(8,128)(2,1)S(1)}, bf16[880,128]{1,0:T(8,128)(2,1)S(1)}, u32[]{:S(2)}, u32[]{:S(2)}) collective-permute-start(bf16[880,128]{1,0:T(8,128)(2,1)S(1)} %collective-permute-done.7.refs_8_.refs_5_), channel_id=1, source_target_pairs={{0,64},{64,0},{1,65},{65,1},{2,66},{66,2},{3,67},{67,3},{4,68},{68... | collective-permute-start | bytes 675848 | tf_op jit(solution)/shard_map/ppermute | solution.py:144
  17.0 7.8 %collective-permute-start.4 = (bf16[880,128]{1,0:T(8,128)(2,1)S(1)}, bf16[880,128]{1,0:T(8,128)(2,1)S(1)}, u32[]{:S(2)}, u32[]{:S(2)}) collective-permute-start(bf16[880,128]{1,0:T(8,128)(2,1)S(1)} %collective-permute-done.2.refs_4_.refs_1_), channel_id=1, source_target_pairs={{0,16},{16,32},{32,48},{48,0},{1,17},{17,33},{33,49},{49,1},{2,18}... | collective-permute-start | bytes 675848 | tf_op jit(solution)/shard_map/ppermute | solution.py:191
  18.6 7.5 %collective-permute-start.6 = (bf16[880,128]{1,0:T(8,128)(2,1)S(1)}, bf16[880,128]{1,0:T(8,128)(2,1)S(1)}, u32[]{:S(2)}, u32[]{:S(2)}) collective-permute-start(bf16[880,128]{1,0:T(8,128)(2,1)S(1)} %collective-permute-done.5.refs_9_.refs_6_), channel_id=1, source_target_pairs={{0,48},{16,0},{32,16},{48,32},{1,49},{17,1},{33,17},{49,33},{2,50}... | collective-permute-start | bytes 675848 | tf_op jit(solution)/shard_map/ppermute | solution.py:191
  19.7 6.9 %collective-permute-start.8 = (bf16[880,128]{1,0:T(8,128)(2,1)S(1)}, bf16[880,128]{1,0:T(8,128)(2,1)S(1)}, u32[]{:S(2)}, u32[]{:S(2)}) collective-permute-start(bf16[880,128]{1,0:T(8,128)(2,1)S(1)} %collective-permute-done.2.refs_4_.refs_1_), channel_id=1, source_target_pairs={{0,64},{64,0},{1,65},{65,1},{2,66},{66,2},{3,67},{67,3},{4,68},{68... | collective-permute-start | bytes 675848 | tf_op jit(solution)/shard_map/ppermute | solution.py:144
  21.8 4.7 %collective-permute-start.13 = (bf16[880,128]{1,0:T(8,128)(2,1)S(1)}, bf16[880,128]{1,0:T(8,128)(2,1)S(1)}, u32[]{:S(2)}, u32[]{:S(2)}) collective-permute-start(bf16[880,128]{1,0:T(8,128)(2,1)S(1)} %collective-permute-done.5.refs_9_.refs_6_), channel_id=1, source_target_pairs={{0,64},{64,0},{1,65},{65,1},{2,66},{66,2},{3,67},{67,3},{4,68},{68... | collective-permute-start | bytes 675848 | tf_op jit(solution)/shard_map/ppermute | solution.py:144
  21.8 4.7 %collective-permute-start.9 = (bf16[880,128]{1,0:T(8,128)(2,1)S(1)}, bf16[880,128]{1,0:T(8,128)(2,1)S(1)}, u32[]{:S(2)}, u32[]{:S(2)}) collective-permute-start(bf16[880,128]{1,0:T(8,128)(2,1)S(1)} %collective-permute-done.3.refs_5_.refs_2_), channel_id=1, source_target_pairs={{0,64},{64,0},{1,65},{65,1},{2,66},{66,2},{3,67},{67,3},{4,68},{68... | collective-permute-start | bytes 675848 | tf_op jit(solution)/shard_map/ppermute | solution.py:144
  24.8 2.4 %collective-permute-start.10 = (bf16[880,128]{1,0:T(8,128)(2,1)S(1)}, bf16[880,128]{1,0:T(8,128)(2,1)S(1)}, u32[]{:S(2)}, u32[]{:S(2)}) collective-permute-start(bf16[880,128]{1,0:T(8,128)(2,1)S(1)} %collective-permute-done.4.refs_6_.refs_3_), channel_id=1, source_target_pairs={{0,64},{64,0},{1,65},{65,1},{2,66},{66,2},{3,67},{67,3},{4,68},{68... | collective-permute-start | bytes 675848 | tf_op jit(solution)/shard_map/ppermute | solution.py:144
  26.2 1.5 %collective-permute-start.11 = (bf16[880,128]{1,0:T(8,128)(2,1)S(1)}, bf16[880,128]{1,0:T(8,128)(2,1)S(1)}, u32[]{:S(2)}, u32[]{:S(2)}) collective-permute-start(bf16[880,128]{1,0:T(8,128)(2,1)S(1)} %collective-permute-done.6.refs_7_.refs_4_), channel_id=1, source_target_pairs={{0,64},{64,0},{1,65},{65,1},{2,66},{66,2},{3,67},{67,3},{4,68},{68... | collective-permute-start | bytes 675848 | tf_op jit(solution)/shard_map/ppermute | solution.py:144
  34.8 9.5 %copy-start.1 = (bf16[1,2,32,32,128]{4,3,2,1,0:T(8,128)(2,1)S(1)}, bf16[1,2,32,32,128]{4,3,2,1,0:T(8,128)(2,1)}, u32[]{:S(2)}) copy-start(bf16[1,2,32,32,128]{4,3,2,1,0:T(8,128)(2,1)} %param.7) | copy-start | bytes 1572868
  34.9 9.5 %collective-permute-start.15 = (bf16[2,20,32,128]{3,2,1,0:T(8,128)(2,1)S(1)}, bf16[2,20,32,128]{3,2,1,0:T(8,128)(2,1)S(1)}, u32[]{:S(2)}, u32[]{:S(2)}) collective-permute-start(bf16[2,20,32,128]{3,2,1,0:T(8,128)(2,1)S(1)} %get-tuple-element.62.refs_0_), channel_id=1, source_target_pairs={{0,1},{2,3},{4,5},{6,7},{8,9},{10,11},{12,13},{14,15},{1,0},{3,2},... | collective-permute-start | bytes 983048 | tf_op jit(solution)/shard_map/ppermute | solution.py:140
  36.7 7.7 %collective-permute-start.14 = (bf16[2,20,32,128]{3,2,1,0:T(8,128)(2,1)S(1)}, bf16[2,20,32,128]{3,2,1,0:T(8,128)(2,1)S(1)}, u32[]{:S(2)}, u32[]{:S(2)}) collective-permute-start(bf16[2,20,32,128]{3,2,1,0:T(8,128)(2,1)S(1)} %get-tuple-element.62.refs_0_), channel_id=1, source_target_pairs={{1,2},{3,4},{5,6},{7,8},{9,10},{11,12},{13,14},{2,1},{4,3},{6,5},{... | collective-permute-start | bytes 983048 | tf_op jit(solution)/shard_map/ppermute | solution.py:140
  50.6 9.7 %collective-permute-start.20 = (bf16[2,16,32,128]{3,2,1,0:T(8,128)(2,1)S(1)}, bf16[2,16,32,128]{3,2,1,0:T(8,128)(2,1)S(1)}, u32[]{:S(2)}, u32[]{:S(2)}) collective-permute-start(bf16[2,16,32,128]{3,2,1,0:T(8,128)(2,1)S(1)} %get-tuple-element.76.refs_0_.refs_7_), channel_id=1, source_target_pairs={{0,1},{2,3},{4,5},{6,7},{8,9},{10,11},{12,13},{14,15},{1,0},{3,2},... | collective-permute-start | bytes 786440 | tf_op jit(solution)/shard_map/ppermute | solution.py:140
  54.8 5.5 %collective-permute-start.19 = (bf16[2,16,32,128]{3,2,1,0:T(8,128)(2,1)S(1)}, bf16[2,16,32,128]{3,2,1,0:T(8,128)(2,1)S(1)}, u32[]{:S(2)}, u32[]{:S(2)}) collective-permute-start(bf16[2,16,32,128]{3,2,1,0:T(8,128)(2,1)S(1)} %get-tuple-element.76.refs_0_.refs_7_), channel_id=1, source_target_pairs={{1,2},{3,4},{5,6},{7,8},{9,10},{11,12},{13,14},{2,1},{4,3},{6,5},{... | collective-permute-start | bytes 786440 | tf_op jit(solution)/shard_map/ppermute | solution.py:140
  55.7 25.5 %collective-permute-start.16 = (bf16[6,8,32,128]{3,2,1,0:T(8,128)(2,1)S(1)}, bf16[6,8,32,128]{3,2,1,0:T(8,128)(2,1)S(1)}, u32[]{:S(2)}, u32[]{:S(2)}) collective-permute-start(bf16[6,8,32,128]{3,2,1,0:T(8,128)(2,1)S(1)} %get-tuple-element.73), channel_id=1, source_target_pairs={{0,16},{16,0},{32,48},{48,32},{1,17},{17,1},{33,49},{49,33},{2,18}... | collective-permute-start | bytes 1179656 | tf_op jit(solution)/shard_map/ppermute | solution.py:128
  56.0 25.2 %collective-permute-start.17 = (bf16[6,8,32,128]{3,2,1,0:T(8,128)(2,1)S(1)}, bf16[6,8,32,128]{3,2,1,0:T(8,128)(2,1)S(1)}, u32[]{:S(2)}, u32[]{:S(2)}) collective-permute-start(bf16[6,8,32,128]{3,2,1,0:T(8,128)(2,1)S(1)} %get-tuple-element.74), channel_id=1, source_target_pairs={{0,32},{16,48},{32,0},{48,16},{1,33},{17,49},{33,1},{49,17},{2,34}... | collective-permute-start | bytes 1179656 | tf_op jit(solution)/shard_map/ppermute | solution.py:128
  60.2 21.1 %collective-permute-start.18 = (bf16[6,8,32,128]{3,2,1,0:T(8,128)(2,1)S(1)}, bf16[6,8,32,128]{3,2,1,0:T(8,128)(2,1)S(1)}, u32[]{:S(2)}, u32[]{:S(2)}) collective-permute-start(bf16[6,8,32,128]{3,2,1,0:T(8,128)(2,1)S(1)} %get-tuple-element.75), channel_id=1, source_target_pairs={{0,48},{16,32},{32,16},{48,0},{1,49},{17,33},{33,17},{49,1},{2,50}... | collective-permute-start | bytes 1179656 | tf_op jit(solution)/shard_map/ppermute | solution.py:128
  65.2 8.8 %collective-permute-start.22 = (bf16[2,12,32,128]{3,2,1,0:T(8,128)(2,1)S(1)}, bf16[2,12,32,128]{3,2,1,0:T(8,128)(2,1)S(1)}, u32[]{:S(2)}, u32[]{:S(2)}) collective-permute-start(bf16[2,12,32,128]{3,2,1,0:T(8,128)(2,1)S(1)} %get-tuple-element.81.refs_0_.refs_5_), channel_id=1, source_target_pairs={{0,1},{2,3},{4,5},{6,7},{8,9},{10,11},{12,13},{14,15},{1,0},{3,2},... | collective-permute-start | bytes 589832 | tf_op jit(solution)/shard_map/ppermute | solution.py:140
  70.6 3.4 %collective-permute-start.21 = (bf16[2,12,32,128]{3,2,1,0:T(8,128)(2,1)S(1)}, bf16[2,12,32,128]{3,2,1,0:T(8,128)(2,1)S(1)}, u32[]{:S(2)}, u32[]{:S(2)}) collective-permute-start(bf16[2,12,32,128]{3,2,1,0:T(8,128)(2,1)S(1)} %get-tuple-element.81.refs_0_.refs_5_), channel_id=1, source_target_pairs={{1,2},{3,4},{5,6},{7,8},{9,10},{11,12},{13,14},{2,1},{4,3},{6,5},{... | collective-permute-start | bytes 589832 | tf_op jit(solution)/shard_map/ppermute | solution.py:140
  76.7 4.6 %collective-permute-start.26 = (bf16[2,8,32,128]{3,2,1,0:T(8,128)(2,1)S(1)}, bf16[2,8,32,128]{3,2,1,0:T(8,128)(2,1)S(1)}, u32[]{:S(2)}, u32[]{:S(2)}) collective-permute-start(bf16[2,8,32,128]{3,2,1,0:T(8,128)(2,1)S(1)} %get-tuple-element.95), channel_id=1, source_target_pairs={{0,16},{16,0},{32,48},{48,32},{1,17},{17,1},{33,49},{49,33},{2,18}... | collective-permute-start | bytes 393224 | tf_op jit(solution)/shard_map/ppermute | solution.py:128
  77.0 7.9 %collective-permute-start.27 = (bf16[2,8,32,128]{3,2,1,0:T(8,128)(2,1)S(1)}, bf16[2,8,32,128]{3,2,1,0:T(8,128)(2,1)S(1)}, u32[]{:S(2)}, u32[]{:S(2)}) collective-permute-start(bf16[2,8,32,128]{3,2,1,0:T(8,128)(2,1)S(1)} %get-tuple-element.96), channel_id=1, source_target_pairs={{0,32},{16,48},{32,0},{48,16},{1,33},{17,49},{33,1},{49,17},{2,34}... | collective-permute-start | bytes 393224 | tf_op jit(solution)/shard_map/ppermute | solution.py:128
  81.2 5.2 %collective-permute-start.28 = (bf16[2,8,32,128]{3,2,1,0:T(8,128)(2,1)S(1)}, bf16[2,8,32,128]{3,2,1,0:T(8,128)(2,1)S(1)}, u32[]{:S(2)}, u32[]{:S(2)}) collective-permute-start(bf16[2,8,32,128]{3,2,1,0:T(8,128)(2,1)S(1)} %get-tuple-element.97), channel_id=1, source_target_pairs={{0,48},{16,32},{32,16},{48,0},{1,49},{17,33},{33,17},{49,1},{2,50}... | collective-permute-start | bytes 393224 | tf_op jit(solution)/shard_map/ppermute | solution.py:128
  89.9 5.7 %collective-permute-start.29 = (bf16[1792,128]{1,0:T(8,128)(2,1)S(1)}, bf16[1792,128]{1,0:T(8,128)(2,1)S(1)}, u32[]{:S(2)}, u32[]{:S(2)}) collective-permute-start(bf16[1792,128]{1,0:T(8,128)(2,1)S(1)} %get-tuple-element.99), channel_id=1, source_target_pairs={{0,64},{64,0},{1,65},{65,1},{2,66},{66,2},{3,67},{67,3},{4,68},{68... | collective-permute-start | bytes 1376264 | tf_op jit(solution)/shard_map/ppermute | solution.py:144
  95.8 9.7 %collective-permute-start.30 = (bf16[448,128]{1,0:T(8,128)(2,1)S(1)}, bf16[448,128]{1,0:T(8,128)(2,1)S(1)}, u32[]{:S(2)}, u32[]{:S(2)}) collective-permute-start(bf16[448,128]{1,0:T(8,128)(2,1)S(1)} %get-tuple-element.101), channel_id=1, source_target_pairs={{0,1},{1,0},{2,3},{3,2},{4,5},{5,4},{6,7},{7,6},{8,9},{9,8},{10,11... | collective-permute-start | bytes 344072 | tf_op jit(solution)/shard_map/ppermute | solution.py:147
  101.6 9.2 %collective-permute-start.31 = (bf16[448,128]{1,0:T(8,128)(2,1)S(1)}, bf16[448,128]{1,0:T(8,128)(2,1)S(1)}, u32[]{:S(2)}, u32[]{:S(2)}) collective-permute-start(bf16[448,128]{1,0:T(8,128)(2,1)S(1)} %get-tuple-element.102), channel_id=1, source_target_pairs={{0,2},{1,3},{2,0},{3,1},{4,6},{5,7},{6,4},{7,5},{8,10},{9,11},{10,... | collective-permute-start | bytes 344072 | tf_op jit(solution)/shard_map/ppermute | solution.py:147
  105.5 7.9 %collective-permute-start.32 = (bf16[448,128]{1,0:T(8,128)(2,1)S(1)}, bf16[448,128]{1,0:T(8,128)(2,1)S(1)}, u32[]{:S(2)}, u32[]{:S(2)}) collective-permute-start(bf16[448,128]{1,0:T(8,128)(2,1)S(1)} %get-tuple-element.103), channel_id=1, source_target_pairs={{0,3},{1,2},{2,1},{3,0},{4,7},{5,6},{6,5},{7,4},{8,11},{9,10},{10,... | collective-permute-start | bytes 344072 | tf_op jit(solution)/shard_map/ppermute | solution.py:147
  113.5 8.1 %collective-permute-start.35 = (bf16[448,128]{1,0:T(8,128)(2,1)S(1)}, bf16[448,128]{1,0:T(8,128)(2,1)S(1)}, u32[]{:S(2)}, u32[]{:S(2)}) collective-permute-start(bf16[448,128]{1,0:T(8,128)(2,1)S(1)} %add_convert_fusion.refs_0_), channel_id=1, source_target_pairs={{0,12},{1,13},{2,14},{3,15},{4,8},{5,9},{6,10},{7,11},{8,4},{9,5},... | collective-permute-start | bytes 344072 | tf_op jit(solution)/shard_map/ppermute | solution.py:150
  114.0 7.5 %collective-permute-start.34 = (bf16[448,128]{1,0:T(8,128)(2,1)S(1)}, bf16[448,128]{1,0:T(8,128)(2,1)S(1)}, u32[]{:S(2)}, u32[]{:S(2)}) collective-permute-start(bf16[448,128]{1,0:T(8,128)(2,1)S(1)} %add_convert_fusion.refs_0_), channel_id=1, source_target_pairs={{0,8},{1,9},{2,10},{3,11},{4,12},{5,13},{6,14},{7,15},{8,0},{9,1},... | collective-permute-start | bytes 344072 | tf_op jit(solution)/shard_map/ppermute | solution.py:150
  116.6 4.9 %collective-permute-start.33 = (bf16[448,128]{1,0:T(8,128)(2,1)S(1)}, bf16[448,128]{1,0:T(8,128)(2,1)S(1)}, u32[]{:S(2)}, u32[]{:S(2)}) collective-permute-start(bf16[448,128]{1,0:T(8,128)(2,1)S(1)} %add_convert_fusion.refs_0_), channel_id=1, source_target_pairs={{0,4},{1,5},{2,6},{3,7},{4,0},{5,1},{6,2},{7,3},{8,12},{9,13},{10,... | collective-permute-start | bytes 344072 | tf_op jit(solution)/shard_map/ppermute | solution.py:150
  117.9 7.1 %collective-permute-start.23 = (bf16[2,8,32,128]{3,2,1,0:T(8,128)(2,1)S(1)}, bf16[2,8,32,128]{3,2,1,0:T(8,128)(2,1)S(1)}, u32[]{:S(2)}, u32[]{:S(2)}) collective-permute-start(bf16[2,8,32,128]{3,2,1,0:T(8,128)(2,1)S(1)} %get-tuple-element.91), channel_id=1, source_target_pairs={{0,16},{16,0},{32,48},{48,32},{1,17},{17,1},{33,49},{49,33},{2,18}... | collective-permute-start | bytes 393224 | tf_op jit(solution)/shard_map/ppermute | solution.py:128
  118.0 7.3 %collective-permute-start.24 = (bf16[2,8,32,128]{3,2,1,0:T(8,128)(2,1)S(1)}, bf16[2,8,32,128]{3,2,1,0:T(8,128)(2,1)S(1)}, u32[]{:S(2)}, u32[]{:S(2)}) collective-permute-start(bf16[2,8,32,128]{3,2,1,0:T(8,128)(2,1)S(1)} %get-tuple-element.92), channel_id=1, source_target_pairs={{0,32},{16,48},{32,0},{48,16},{1,33},{17,49},{33,1},{49,17},{2,34}... | collective-permute-start | bytes 393224 | tf_op jit(solution)/shard_map/ppermute | solution.py:128
  121.7 7.0 %collective-permute-start.38 = (bf16[448,128]{1,0:T(8,128)(2,1)S(1)}, bf16[448,128]{1,0:T(8,128)(2,1)S(1)}, u32[]{:S(2)}, u32[]{:S(2)}) collective-permute-start(bf16[448,128]{1,0:T(8,128)(2,1)S(1)} %shard_map.87.refs_8_), channel_id=1, source_target_pairs={{0,3},{1,2},{2,1},{3,0},{4,7},{5,6},{6,5},{7,4},{8,11},{9,10},{10,... | collective-permute-start | bytes 344072 | tf_op jit(solution)/shard_map/ppermute | solution.py:147
  122.5 7.2 %collective-permute-start.37 = (bf16[448,128]{1,0:T(8,128)(2,1)S(1)}, bf16[448,128]{1,0:T(8,128)(2,1)S(1)}, u32[]{:S(2)}, u32[]{:S(2)}) collective-permute-start(bf16[448,128]{1,0:T(8,128)(2,1)S(1)} %shard_map.87.refs_8_), channel_id=1, source_target_pairs={{0,2},{1,3},{2,0},{3,1},{4,6},{5,7},{6,4},{7,5},{8,10},{9,11},{10,... | collective-permute-start | bytes 344072 | tf_op jit(solution)/shard_map/ppermute | solution.py:147
  122.5 9.2 %collective-permute-start.36 = (bf16[448,128]{1,0:T(8,128)(2,1)S(1)}, bf16[448,128]{1,0:T(8,128)(2,1)S(1)}, u32[]{:S(2)}, u32[]{:S(2)}) collective-permute-start(bf16[448,128]{1,0:T(8,128)(2,1)S(1)} %shard_map.87.refs_8_), channel_id=1, source_target_pairs={{0,1},{1,0},{2,3},{3,2},{4,5},{5,4},{6,7},{7,6},{8,9},{9,8},{10,11... | collective-permute-start | bytes 344072 | tf_op jit(solution)/shard_map/ppermute | solution.py:147
  125.0 6.7 %collective-permute-start.25 = (bf16[2,8,32,128]{3,2,1,0:T(8,128)(2,1)S(1)}, bf16[2,8,32,128]{3,2,1,0:T(8,128)(2,1)S(1)}, u32[]{:S(2)}, u32[]{:S(2)}) collective-permute-start(bf16[2,8,32,128]{3,2,1,0:T(8,128)(2,1)S(1)} %get-tuple-element.93), channel_id=1, source_target_pairs={{0,48},{16,32},{32,16},{48,0},{1,49},{17,33},{33,17},{49,1},{2,50}... | collective-permute-start | bytes 393224 | tf_op jit(solution)/shard_map/ppermute | solution.py:128
  125.3 7.8 %collective-permute-start.39 = (bf16[448,128]{1,0:T(8,128)(2,1)S(1)}, bf16[448,128]{1,0:T(8,128)(2,1)S(1)}, u32[]{:S(2)}, u32[]{:S(2)}) collective-permute-start(bf16[448,128]{1,0:T(8,128)(2,1)S(1)} %shard_map.87.refs_8_), channel_id=1, source_target_pairs={{0,64},{64,0},{1,65},{65,1},{2,66},{66,2},{3,67},{67,3},{4,68},{68... | collective-permute-start | bytes 344072 | tf_op jit(solution)/shard_map/ppermute | solution.py:144
  128.6 4.5 %collective-permute-start.42 = (bf16[448,128]{1,0:T(8,128)(2,1)S(1)}, bf16[448,128]{1,0:T(8,128)(2,1)S(1)}, u32[]{:S(2)}, u32[]{:S(2)}) collective-permute-start(bf16[448,128]{1,0:T(8,128)(2,1)S(1)} %collective-permute-done.38.refs_11_), channel_id=1, source_target_pairs={{0,64},{64,0},{1,65},{65,1},{2,66},{66,2},{3,67},{67,3},{4,68},{68... | collective-permute-start | bytes 344072 | tf_op jit(solution)/shard_map/ppermute | solution.py:144
  129.8 3.4 %collective-permute-start.41 = (bf16[448,128]{1,0:T(8,128)(2,1)S(1)}, bf16[448,128]{1,0:T(8,128)(2,1)S(1)}, u32[]{:S(2)}, u32[]{:S(2)}) collective-permute-start(bf16[448,128]{1,0:T(8,128)(2,1)S(1)} %collective-permute-done.37.refs_10_), channel_id=1, source_target_pairs={{0,64},{64,0},{1,65},{65,1},{2,66},{66,2},{3,67},{67,3},{4,68},{68... | collective-permute-start | bytes 344072 | tf_op jit(solution)/shard_map/ppermute | solution.py:144
  131.8 1.4 %collective-permute-start.40 = (bf16[448,128]{1,0:T(8,128)(2,1)S(1)}, bf16[448,128]{1,0:T(8,128)(2,1)S(1)}, u32[]{:S(2)}, u32[]{:S(2)}) collective-permute-start(bf16[448,128]{1,0:T(8,128)(2,1)S(1)} %collective-permute-done.36.refs_9_), channel_id=1, source_target_pairs={{0,64},{64,0},{1,65},{65,1},{2,66},{66,2},{3,67},{67,3},{4,68},{68... | collective-permute-start | bytes 344072 | tf_op jit(solution)/shard_map/ppermute | solution.py:144

commit v6 on v5

--- a/solution.py
+++ b/solution.py
@@ -516,9 +516,14 @@
         split, (sds((RQ, C), F32), quart, quart, quart), [VMEM, VMEM], [pltpu.VMEM((4, RQ, C), F32)]
     )(keep, recv)
     xs = three(xdep, [None, *qs])
-    for v in xs:
-        q = q + v.astype(F32)
-    q = q.astype(BF)
+
+    def add(own, q1, q2, q3, out):
+        acc = own[...]
+        for r in (q1, q2, q3):
+            acc = acc + r[...].astype(F32)
+        out[...] = acc.astype(BF)
+
+    q = call(add, quart, [VMEM] * 4, [], VMEM)(q, *xs)
     ys = three(ydep, [q] * 4)
 
     @placed

time: 136 us -> 136 us (level)
  no operation moved by 1% of the time
where the time goes in v6:
time: 136 us; the launch traced here: 135 us
  starting transfers between devices  69 us (51%)
  Pallas kernels  34.8 us (26%)
  waiting for transfers between devices  30 us (22%)
    ppermute x11, starting transfers between devices, swap(): return lax.ppermute(v, 'dp', [(0, 1), (1, 0)])  18.3 us
    ppermute x8, starting transfers between devices, both(): result.append(lax.ppermute(v, 'depth', pairs + [(b, a) for a, b in pairs]))  15.4 us
    ppermute x6, starting transfers between devices, xdep(): return lax.ppermute(v, 'depth', [(i, i ^ k) for i in range(n_dep)])  13.1 us
    ppermute x9, starting transfers between devices, sec(): return lax.ppermute(v, 'section', [(i, i ^ k) for i in range(n_sec)])  10.6 us
    ppermute x6, starting transfers between devices, ring(): lax.ppermute(v, 'section', [(i, (i + k) % n_sec) for i in range(n_sec)])  8.4 us
    ppermute x6, waiting for transfers between devices, xdep(): return lax.ppermute(v, 'depth', [(i, i ^ k) for i in range(n_dep)])  7.91 us
    pallas_call x1, Pallas kernels, shards(): call(k1, (sds((4, R, W, C)), sds((4, R + 2, W, C)), sds((4, R, W, C)), sd...  7.18 us
    ppermute x8, waiting for transfers between devices, both(): result.append(lax.ppermute(v, 'depth', pairs + [(b, a) for a, b in pairs]))  6.4 us
  transfers between devices with their start and end apart: 43, of which 14 were waited for; matrix products, arithmetic and copies ran while one was open for 0% of the time, Pallas kernels for 11%

profile of v6, /device:TPU:1, one launch (start us, length us, event | category | flops | bytes accessed | tf_op | source)
XLA Modules:
  0.0 134.9 jit_solution(7512518591319200631)
XLA Ops:
  0.6 1.2 shard_map.76
  1.8 4.6 %collective-permute-start.7 = (bf16[880,128]{1,0:T(8,128)(2,1)S(1)}, bf16[880,128]{1,0:T(8,128)(2,1)S(1)}, u32[]{:S(2)}, u32[]{:S(2)}) collective-permute-start(bf16[880,128]{1,0:T(8,128)(2,1)S(1)} %get-tuple-element.57), channel_id=1, source_target_pairs={{0,48},{16,0},{32,16},{48,32},{1,49},{17,1},{33,17},{49,33},{2,50}... | collective-permute-start | bytes 675848 | tf_op jit(solution)/shard_map/ppermute | solution.py:191
  6.5 2.7 %collective-permute-start.5 = (bf16[880,128]{1,0:T(8,128)(2,1)S(1)}, bf16[880,128]{1,0:T(8,128)(2,1)S(1)}, u32[]{:S(2)}, u32[]{:S(2)}) collective-permute-start(bf16[880,128]{1,0:T(8,128)(2,1)S(1)} %get-tuple-element.58), channel_id=1, source_target_pairs={{0,48},{16,0},{32,16},{48,32},{1,49},{17,1},{33,17},{49,33},{2,50}... | collective-permute-start | bytes 675848 | tf_op jit(solution)/shard_map/ppermute | solution.py:191
  9.1 1.1 shard_map.75.refs_0_
  10.2 1.3 collective-permute-start.1
  11.5 0.7 collective-permute-start
  12.2 1.6 %collective-permute-done.2.refs_4_.refs_1_ = bf16[880,128]{1,0:T(8,128)(2,1)S(1)} collective-permute-done((bf16[880,128]{1,0:T(8,128)(2,1)S(1)}, bf16[880,128]{1,0:T(8,128)(2,1)S(1)}, u32[]{:S(2)}, u32[]{:S(2)}) %collective-permute-start.2) | collective-permute-done | bytes 225312 | tf_op jit(solution)/shard_map/ppermute | solution.py:191
  13.8 3.2 %collective-permute-start.12 = (bf16[880,128]{1,0:T(8,128)(2,1)S(1)}, bf16[880,128]{1,0:T(8,128)(2,1)S(1)}, u32[]{:S(2)}, u32[]{:S(2)}) collective-permute-start(bf16[880,128]{1,0:T(8,128)(2,1)S(1)} %collective-permute-done.7.refs_8_.refs_5_), channel_id=1, source_target_pairs={{0,64},{64,0},{1,65},{65,1},{2,66},{66,2},{3,67},{67,3},{4,68},{68... | collective-permute-start | bytes 675848 | tf_op jit(solution)/shard_map/ppermute | solution.py:144
  17.0 1.6 %collective-permute-done.3.refs_5_.refs_2_ = bf16[880,128]{1,0:T(8,128)(2,1)S(1)} collective-permute-done((bf16[880,128]{1,0:T(8,128)(2,1)S(1)}, bf16[880,128]{1,0:T(8,128)(2,1)S(1)}, u32[]{:S(2)}, u32[]{:S(2)}) %collective-permute-start.3) | collective-permute-done | bytes 225312 | tf_op jit(solution)/shard_map/ppermute | solution.py:191
  18.6 1.1 collective-permute-start.6
  19.7 2.1 %collective-permute-start.8 = (bf16[880,128]{1,0:T(8,128)(2,1)S(1)}, bf16[880,128]{1,0:T(8,128)(2,1)S(1)}, u32[]{:S(2)}, u32[]{:S(2)}) collective-permute-start(bf16[880,128]{1,0:T(8,128)(2,1)S(1)} %collective-permute-done.2.refs_4_.refs_1_), channel_id=1, source_target_pairs={{0,64},{64,0},{1,65},{65,1},{2,66},{66,2},{3,67},{67,3},{4,68},{68... | collective-permute-start | bytes 675848 | tf_op jit(solution)/shard_map/ppermute | solution.py:144
  22.3 2.5 %collective-permute-done.4.refs_6_.refs_3_ = bf16[880,128]{1,0:T(8,128)(2,1)S(1)} collective-permute-done((bf16[880,128]{1,0:T(8,128)(2,1)S(1)}, bf16[880,128]{1,0:T(8,128)(2,1)S(1)}, u32[]{:S(2)}, u32[]{:S(2)}) %collective-permute-start.4) | collective-permute-done | bytes 225312 | tf_op jit(solution)/shard_map/ppermute | solution.py:191
  24.8 1.3 collective-permute-start.10
  26.6 0.7 collective-permute-done.10.refs_12_.refs_9_
  27.7 7.2 %shard_map.77 = (bf16[4,8,32,128]{3,2,1,0:T(8,128)(2,1)S(1)}, bf16[4,10,32,128]{3,2,1,0:T(8,128)(2,1)S(1)}, bf16[4,8,32,128]{3,2,1,0:T(8,128)(2,1)S(1)}, bf16[2,...) custom-call(bf16[2,24,32,128]{3,2,1,0:T(8,128)(2,1)S(1)} %shard_map.75.refs_0_, ...), custom_call_target="tpu_custom_call" | custom-call | tf_op jit(solution)/shard_map/pallas_call | solution.py:245
  34.9 1.8 %collective-permute-start.15 = (bf16[2,20,32,128]{3,2,1,0:T(8,128)(2,1)S(1)}, bf16[2,20,32,128]{3,2,1,0:T(8,128)(2,1)S(1)}, u32[]{:S(2)}, u32[]{:S(2)}) collective-permute-start(bf16[2,20,32,128]{3,2,1,0:T(8,128)(2,1)S(1)} %get-tuple-element.62.refs_0_), channel_id=1, source_target_pairs={{0,1},{2,3},{4,5},{6,7},{8,9},{10,11},{12,13},{14,15},{1,0},{3,2},... | collective-permute-start | bytes 983048 | tf_op jit(solution)/shard_map/ppermute | solution.py:140
  36.7 0.7 collective-permute-start.14
  37.3 3.5 %shard_map.78 = (bf16[3456,128]{1,0:T(8,128)(2,1)S(1)}, bf16[3456,128]{1,0:T(8,128)(2,1)S(1)}, bf16[3456,128]{1,0:T(8,128)(2,1)S(1)}, bf16[3456,128]{1,0:T(8,128)(2,1)S(1)}) custom-call(bf16[3456,128]{1,0:T(8,128)(2,1)S(1)} %bitcast.9, bf16[880,128]{1,0:T(8,128)(2,1)S(1)} %collective-permute-done.2.refs_4_.refs_1_, ...), custom_call_target="tpu_custom_call" | custom-call | tf_op jit(solution)/shard_map/pallas_call | solution.py:264
  40.8 3.5 %collective-permute-done.15.refs_2_ = bf16[2,20,32,128]{3,2,1,0:T(8,128)(2,1)S(1)} collective-permute-done((bf16[2,20,32,128]{3,2,1,0:T(8,128)(2,1)S(1)}, bf16[2,20,32,128]{3,2,1,0:T(8,128)(2,1)S(1)}, u32[]{:S(2)}, u32[]{:S(2)}) %collective-permute-start.15) | collective-permute-done | bytes 327712 | tf_op jit(solution)/shard_map/ppermute | solution.py:140
  44.4 6.2 %shard_map.79 = (bf16[4,8,32,128]{3,2,1,0:T(8,128)(2,1)S(1)}, bf16[4,14,32,128]{3,2,1,0:T(8,128)(2,1)S(1)}, bf16[4,8,32,128]{3,2,1,0:T(8,128)(2,1)S(1)}, bf16[2,...) custom-call(bf16[2,20,32,128]{3,2,1,0:T(8,128)(2,1)S(1)} %get-tuple-element.62.refs_0_, ...), custom_call_target="tpu_custom_call" | custom-call | tf_op jit(solution)/shard_map/pallas_call | solution.py:303
  50.6 4.2 %collective-permute-start.20 = (bf16[2,16,32,128]{3,2,1,0:T(8,128)(2,1)S(1)}, bf16[2,16,32,128]{3,2,1,0:T(8,128)(2,1)S(1)}, u32[]{:S(2)}, u32[]{:S(2)}) collective-permute-start(bf16[2,16,32,128]{3,2,1,0:T(8,128)(2,1)S(1)} %get-tuple-element.76.refs_0_.refs_7_), channel_id=1, source_target_pairs={{0,1},{2,3},{4,5},{6,7},{8,9},{10,11},{12,13},{14,15},{1,0},{3,2},... | collective-permute-start | bytes 786440 | tf_op jit(solution)/shard_map/ppermute | solution.py:140
  54.8 0.7 collective-permute-start.19
  56.0 4.2 %collective-permute-start.17 = (bf16[6,8,32,128]{3,2,1,0:T(8,128)(2,1)S(1)}, bf16[6,8,32,128]{3,2,1,0:T(8,128)(2,1)S(1)}, u32[]{:S(2)}, u32[]{:S(2)}) collective-permute-start(bf16[6,8,32,128]{3,2,1,0:T(8,128)(2,1)S(1)} %get-tuple-element.74), channel_id=1, source_target_pairs={{0,32},{16,48},{32,0},{48,16},{1,33},{17,49},{33,1},{49,17},{2,34}... | collective-permute-start | bytes 1179656 | tf_op jit(solution)/shard_map/ppermute | solution.py:128
  60.3 4.9 %shard_map.81 = (bf16[2,8,32,128]{3,2,1,0:T(8,128)(2,1)S(1)}, bf16[2,8,32,128]{3,2,1,0:T(8,128)(2,1)S(1)}, bf16[2,8,32,128]{3,2,1,0:T(8,128)(2,1)S(1)}, bf16[2,12,32,128]{3,2,1,0:T(8,128)(2,1)S(1)}) custom-call(bf16[2,16,32,128]{3,2,1,0:T(8,128)(2,1)S(1)} %get-tuple-element.76.refs_0_.refs_7_, bf16[2,16,32,128]{3,2,1,0:T(8,128)(2,1)S(1)} %collective-permute-done.19.refs_1_, ...), custom_call_target="tpu_custom_call" | custom-call | tf_op jit(solution)/shard_map/pallas_call | solution.py:380
  65.2 5.4 %collective-permute-start.22 = (bf16[2,12,32,128]{3,2,1,0:T(8,128)(2,1)S(1)}, bf16[2,12,32,128]{3,2,1,0:T(8,128)(2,1)S(1)}, u32[]{:S(2)}, u32[]{:S(2)}) collective-permute-start(bf16[2,12,32,128]{3,2,1,0:T(8,128)(2,1)S(1)} %get-tuple-element.81.refs_0_.refs_5_), channel_id=1, source_target_pairs={{0,1},{2,3},{4,5},{6,7},{8,9},{10,11},{12,13},{14,15},{1,0},{3,2},... | collective-permute-start | bytes 589832 | tf_op jit(solution)/shard_map/ppermute | solution.py:140
  71.3 2.7 %collective-permute-done.22.refs_2_ = bf16[2,12,32,128]{3,2,1,0:T(8,128)(2,1)S(1)} collective-permute-done((bf16[2,12,32,128]{3,2,1,0:T(8,128)(2,1)S(1)}, bf16[2,12,32,128]{3,2,1,0:T(8,128)(2,1)S(1)}, u32[]{:S(2)}, u32[]{:S(2)}) %collective-permute-start.22) | collective-permute-done | bytes 196640 | tf_op jit(solution)/shard_map/ppermute | solution.py:140
  74.0 2.7 %shard_map.82 = (bf16[2,8,32,128]{3,2,1,0:T(8,128)(2,1)S(1)}, bf16[4,10,32,128]{3,2,1,0:T(8,128)(2,1)S(1)}, bf16[2,8,32,128]{3,2,1,0:T(8,128)(2,1)S(1)}, bf16[2,...) custom-call(bf16[2,12,32,128]{3,2,1,0:T(8,128)(2,1)S(1)} %get-tuple-element.81, ...), custom_call_target="tpu_custom_call" | custom-call | tf_op jit(solution)/shard_map/pallas_call | solution.py:416
  77.0 4.2 %collective-permute-start.27 = (bf16[2,8,32,128]{3,2,1,0:T(8,128)(2,1)S(1)}, bf16[2,8,32,128]{3,2,1,0:T(8,128)(2,1)S(1)}, u32[]{:S(2)}, u32[]{:S(2)}) collective-permute-start(bf16[2,8,32,128]{3,2,1,0:T(8,128)(2,1)S(1)} %get-tuple-element.96), channel_id=1, source_target_pairs={{0,32},{16,48},{32,0},{48,16},{1,33},{17,49},{33,1},{49,17},{2,34}... | collective-permute-start | bytes 393224 | tf_op jit(solution)/shard_map/ppermute | solution.py:128
  81.3 3.6 %collective-permute-done.27.refs_3_ = bf16[2,8,32,128]{3,2,1,0:T(8,128)(2,1)S(1)} collective-permute-done((bf16[2,8,32,128]{3,2,1,0:T(8,128)(2,1)S(1)}, bf16[2,8,32,128]{3,2,1,0:T(8,128)(2,1)S(1)}, u32[]{:S(2)}, u32[]{:S(2)}) %collective-permute-start.27) | collective-permute-done | bytes 131104 | tf_op jit(solution)/shard_map/ppermute | solution.py:128
  85.0 1.4 %collective-permute-done.28.refs_4_ = bf16[2,8,32,128]{3,2,1,0:T(8,128)(2,1)S(1)} collective-permute-done((bf16[2,8,32,128]{3,2,1,0:T(8,128)(2,1)S(1)}, bf16[2,8,32,128]{3,2,1,0:T(8,128)(2,1)S(1)}, u32[]{:S(2)}, u32[]{:S(2)}) %collective-permute-start.28) | collective-permute-done | bytes 131104 | tf_op jit(solution)/shard_map/ppermute | solution.py:128
  86.4 3.5 %shard_map.85 = (f32[1792,128]{1,0:T(8,128)S(1)}, bf16[1792,128]{1,0:T(8,128)(2,1)S(1)}) custom-call(bf16[4,34,32,128]{3,2,1,0:T(8,128)(2,1)S(1)} %shard_map.84.refs_0_, bf16[2,8,32,128]{3,2,1,0:T(8,128)(2,1)S(1)} %get-tuple-element.94.refs_1_, bf16[2,8,32,128]{3,2,1,0:T(8,128)(2,1)S(1)} %collective-permute-done.26.refs_2_, ...), custom_call_target="tpu_custom_call" | custom-call | tf_op jit(solution)/shard_map/pallas_call | solution.py:493
  89.9 4.3 %collective-permute-start.29 = (bf16[1792,128]{1,0:T(8,128)(2,1)S(1)}, bf16[1792,128]{1,0:T(8,128)(2,1)S(1)}, u32[]{:S(2)}, u32[]{:S(2)}) collective-permute-start(bf16[1792,128]{1,0:T(8,128)(2,1)S(1)} %get-tuple-element.99), channel_id=1, source_target_pairs={{0,64},{64,0},{1,65},{65,1},{2,66},{66,2},{3,67},{67,3},{4,68},{68... | collective-permute-start | bytes 1376264 | tf_op jit(solution)/shard_map/ppermute | solution.py:144
  94.2 1.4 %collective-permute-done.29.refs_1_ = bf16[1792,128]{1,0:T(8,128)(2,1)S(1)} collective-permute-done((bf16[1792,128]{1,0:T(8,128)(2,1)S(1)}, bf16[1792,128]{1,0:T(8,128)(2,1)S(1)}, u32[]{:S(2)}, u32[]{:S(2)}) %collective-permute-start.29) | collective-permute-done | bytes 458784 | tf_op jit(solution)/shard_map/ppermute | solution.py:144
  95.8 5.8 %collective-permute-start.30 = (bf16[448,128]{1,0:T(8,128)(2,1)S(1)}, bf16[448,128]{1,0:T(8,128)(2,1)S(1)}, u32[]{:S(2)}, u32[]{:S(2)}) collective-permute-start(bf16[448,128]{1,0:T(8,128)(2,1)S(1)} %get-tuple-element.101), channel_id=1, source_target_pairs={{0,1},{1,0},{2,3},{3,2},{4,5},{5,4},{6,7},{7,6},{8,9},{9,8},{10,11... | collective-permute-start | bytes 344072 | tf_op jit(solution)/shard_map/ppermute | solution.py:147
  101.6 3.9 %collective-permute-start.31 = (bf16[448,128]{1,0:T(8,128)(2,1)S(1)}, bf16[448,128]{1,0:T(8,128)(2,1)S(1)}, u32[]{:S(2)}, u32[]{:S(2)}) collective-permute-start(bf16[448,128]{1,0:T(8,128)(2,1)S(1)} %get-tuple-element.102), channel_id=1, source_target_pairs={{0,2},{1,3},{2,0},{3,1},{4,6},{5,7},{6,4},{7,5},{8,10},{9,11},{10,... | collective-permute-start | bytes 344072 | tf_op jit(solution)/shard_map/ppermute | solution.py:147
  105.5 5.3 %collective-permute-done.31.q2 = bf16[448,128]{1,0:T(8,128)(2,1)S(1)} collective-permute-done((bf16[448,128]{1,0:T(8,128)(2,1)S(1)}, bf16[448,128]{1,0:T(8,128)(2,1)S(1)}, u32[]{:S(2)}, u32[]{:S(2)}) %collective-permute-start.31) | collective-permute-done | bytes 114720 | tf_op jit(solution)/shard_map/ppermute | solution.py:147
  110.9 2.6 %collective-permute-done.32.q3 = bf16[448,128]{1,0:T(8,128)(2,1)S(1)} collective-permute-done((bf16[448,128]{1,0:T(8,128)(2,1)S(1)}, bf16[448,128]{1,0:T(8,128)(2,1)S(1)}, u32[]{:S(2)}, u32[]{:S(2)}) %collective-permute-start.32) | collective-permute-done | bytes 114720 | tf_op jit(solution)/shard_map/ppermute | solution.py:147
  114.0 2.6 %collective-permute-start.34 = (bf16[448,128]{1,0:T(8,128)(2,1)S(1)}, bf16[448,128]{1,0:T(8,128)(2,1)S(1)}, u32[]{:S(2)}, u32[]{:S(2)}) collective-permute-start(bf16[448,128]{1,0:T(8,128)(2,1)S(1)} %shard_map.87.refs_0_), channel_id=1, source_target_pairs={{0,8},{1,9},{2,10},{3,11},{4,12},{5,13},{6,14},{7,15},{8,0},{9,1},... | collective-permute-start | bytes 344072 | tf_op jit(solution)/shard_map/ppermute | solution.py:150
  116.8 1.1 shard_map.83
  118.0 1.2 collective-permute-start.24
  119.2 2.4 %collective-permute-done.35.refs_3_ = bf16[448,128]{1,0:T(8,128)(2,1)S(1)} collective-permute-done((bf16[448,128]{1,0:T(8,128)(2,1)S(1)}, bf16[448,128]{1,0:T(8,128)(2,1)S(1)}, u32[]{:S(2)}, u32[]{:S(2)}) %collective-permute-start.35) | collective-permute-done | bytes 114720 | tf_op jit(solution)/shard_map/ppermute | solution.py:150
  121.7 0.8 collective-permute-start.38
  122.5 2.5 %collective-permute-start.36 = (bf16[448,128]{1,0:T(8,128)(2,1)S(1)}, bf16[448,128]{1,0:T(8,128)(2,1)S(1)}, u32[]{:S(2)}, u32[]{:S(2)}) collective-permute-start(bf16[448,128]{1,0:T(8,128)(2,1)S(1)} %shard_map.88.refs_8_), channel_id=1, source_target_pairs={{0,1},{1,0},{2,3},{3,2},{4,5},{5,4},{6,7},{7,6},{8,9},{9,8},{10,11... | collective-permute-start | bytes 344072 | tf_op jit(solution)/shard_map/ppermute | solution.py:147
  125.3 3.3 %collective-permute-start.39 = (bf16[448,128]{1,0:T(8,128)(2,1)S(1)}, bf16[448,128]{1,0:T(8,128)(2,1)S(1)}, u32[]{:S(2)}, u32[]{:S(2)}) collective-permute-start(bf16[448,128]{1,0:T(8,128)(2,1)S(1)} %shard_map.88.refs_8_), channel_id=1, source_target_pairs={{0,64},{64,0},{1,65},{65,1},{2,66},{66,2},{3,67},{67,3},{4,68},{68... | collective-permute-start | bytes 344072 | tf_op jit(solution)/shard_map/ppermute | solution.py:144
  128.6 1.1 collective-permute-start.42
  129.8 2.0 %collective-permute-start.41 = (bf16[448,128]{1,0:T(8,128)(2,1)S(1)}, bf16[448,128]{1,0:T(8,128)(2,1)S(1)}, u32[]{:S(2)}, u32[]{:S(2)}) collective-permute-start(bf16[448,128]{1,0:T(8,128)(2,1)S(1)} %collective-permute-done.37.refs_10_), channel_id=1, source_target_pairs={{0,64},{64,0},{1,65},{65,1},{2,66},{66,2},{3,67},{67,3},{4,68},{68... | collective-permute-start | bytes 344072 | tf_op jit(solution)/shard_map/ppermute | solution.py:144
  131.8 1.3 %shard_map.89 = (bf16[2,32,32,128]{3,2,1,0:T(8,128)(2,1)}, bf16[2,32,32,128]{3,2,1,0:T(8,128)(2,1)}, f32[3456,128]{1,0:T(8,128)}, f32[8,128]{1,0:T(8,128)S(1)}) custom-call(bf16[6,8,32,128]{3,2,1,0:T(8,128)(2,1)S(1)} %get-tuple-element.72.refs_0_, bf16[6,8,32,128]{3,2,1,0:T(8,128)(2,1)S(1)} %collective-permute-done.16.refs_1_, ...), custom_call_target="tpu_custom_call" | custom-call | tf_op jit(solution)/shard_map/pallas_call | solution.py:573
  133.2 1.5 %finish.1 = (f32[3456,128]{1,0:T(8,128)}, f32[1,128]{1,0:T(1,128)}) custom-call(bf16[448,128]{1,0:T(8,128)(2,1)S(1)} %collective-permute-done.39.refs_0_, bf16[448,128]{1,0:T(8,128)(2,1)S(1)} %collective-permute-done.40.refs_1_, bf16[448,128]{1,0:T(8,128)(2,1)S(1)} %collective-permute-done.41.refs_2_, ...), custom_call_target="tpu_custom_call", output_to_operand_aliasing={{0}: (5, {})} | custom-call | tf_op jit(solution)/shard_map/finish/pallas_call | solution.py:619
  (58 shorter events, 4.6 us)
Async XLA Ops:
  0.6 27.0 %copy-start = (bf16[1,3456,128]{2,1,0:T(8,128)(2,1)S(1)}, bf16[1,3456,128]{2,1,0:T(8,128)(2,1)}, u32[]{:S(2)}) copy-start(bf16[1,3456,128]{2,1,0:T(8,128)(2,1)} %param.5) | copy-start | bytes 2654212
  1.8 9.7 %collective-permute-start.7 = (bf16[880,128]{1,0:T(8,128)(2,1)S(1)}, bf16[880,128]{1,0:T(8,128)(2,1)S(1)}, u32[]{:S(2)}, u32[]{:S(2)}) collective-permute-start(bf16[880,128]{1,0:T(8,128)(2,1)S(1)} %get-tuple-element.57), channel_id=1, source_target_pairs={{0,48},{16,0},{32,16},{48,32},{1,49},{17,1},{33,17},{49,33},{2,50}... | collective-permute-start | bytes 675848 | tf_op jit(solution)/shard_map/ppermute | solution.py:191
  6.5 7.3 %collective-permute-start.2 = (bf16[880,128]{1,0:T(8,128)(2,1)S(1)}, bf16[880,128]{1,0:T(8,128)(2,1)S(1)}, u32[]{:S(2)}, u32[]{:S(2)}) collective-permute-start(bf16[880,128]{1,0:T(8,128)(2,1)S(1)} %get-tuple-element.57), channel_id=1, source_target_pairs={{0,16},{16,32},{32,48},{48,0},{1,17},{17,33},{33,49},{49,1},{2,18}... | collective-permute-start | bytes 675848 | tf_op jit(solution)/shard_map/ppermute | solution.py:191
  6.5 10.6 %collective-permute-start.5 = (bf16[880,128]{1,0:T(8,128)(2,1)S(1)}, bf16[880,128]{1,0:T(8,128)(2,1)S(1)}, u32[]{:S(2)}, u32[]{:S(2)}) collective-permute-start(bf16[880,128]{1,0:T(8,128)(2,1)S(1)} %get-tuple-element.58), channel_id=1, source_target_pairs={{0,48},{16,0},{32,16},{48,32},{1,49},{17,1},{33,17},{49,33},{2,50}... | collective-permute-start | bytes 675848 | tf_op jit(solution)/shard_map/ppermute | solution.py:191
  9.1 9.5 %collective-permute-start.3 = (bf16[880,128]{1,0:T(8,128)(2,1)S(1)}, bf16[880,128]{1,0:T(8,128)(2,1)S(1)}, u32[]{:S(2)}, u32[]{:S(2)}) collective-permute-start(bf16[880,128]{1,0:T(8,128)(2,1)S(1)} %get-tuple-element.58), channel_id=1, source_target_pairs={{0,16},{16,32},{32,48},{48,0},{1,17},{17,33},{33,49},{49,1},{2,18}... | collective-permute-start | bytes 675848 | tf_op jit(solution)/shard_map/ppermute | solution.py:191
  10.2 9.5 %collective-permute-start.1 = (bf16[2,24,32,128]{3,2,1,0:T(8,128)(2,1)S(1)}, bf16[2,24,32,128]{3,2,1,0:T(8,128)(2,1)S(1)}, u32[]{:S(2)}, u32[]{:S(2)}) collective-permute-start(bf16[2,24,32,128]{3,2,1,0:T(8,128)(2,1)S(1)} %shard_map.75.refs_0_), channel_id=1, source_target_pairs={{0,1},{2,3},{4,5},{6,7},{8,9},{10,11},{12,13},{14,15},{1,0},{3,2},... | collective-permute-start | bytes 1179656 | tf_op jit(solution)/shard_map/ppermute | solution.py:140
  11.5 10.3 %collective-permute-start = (bf16[2,24,32,128]{3,2,1,0:T(8,128)(2,1)S(1)}, bf16[2,24,32,128]{3,2,1,0:T(8,128)(2,1)S(1)}, u32[]{:S(2)}, u32[]{:S(2)}) collective-permute-start(bf16[2,24,32,128]{3,2,1,0:T(8,128)(2,1)S(1)} %shard_map.75.refs_0_), channel_id=1, source_target_pairs={{1,2},{3,4},{5,6},{7,8},{9,10},{11,12},{13,14},{2,1},{4,3},{6,5},{... | collective-permute-start | bytes 1179656 | tf_op jit(solution)/shard_map/ppermute | solution.py:140
  13.8 8.1 %collective-permute-start.12 = (bf16[880,128]{1,0:T(8,128)(2,1)S(1)}, bf16[880,128]{1,0:T(8,128)(2,1)S(1)}, u32[]{:S(2)}, u32[]{:S(2)}) collective-permute-start(bf16[880,128]{1,0:T(8,128)(2,1)S(1)} %collective-permute-done.7.refs_8_.refs_5_), channel_id=1, source_target_pairs={{0,64},{64,0},{1,65},{65,1},{2,66},{66,2},{3,67},{67,3},{4,68},{68... | collective-permute-start | bytes 675848 | tf_op jit(solution)/shard_map/ppermute | solution.py:144
  17.0 7.8 %collective-permute-start.4 = (bf16[880,128]{1,0:T(8,128)(2,1)S(1)}, bf16[880,128]{1,0:T(8,128)(2,1)S(1)}, u32[]{:S(2)}, u32[]{:S(2)}) collective-permute-start(bf16[880,128]{1,0:T(8,128)(2,1)S(1)} %collective-permute-done.2.refs_4_.refs_1_), channel_id=1, source_target_pairs={{0,16},{16,32},{32,48},{48,0},{1,17},{17,33},{33,49},{49,1},{2,18}... | collective-permute-start | bytes 675848 | tf_op jit(solution)/shard_map/ppermute | solution.py:191
  18.6 7.5 %collective-permute-start.6 = (bf16[880,128]{1,0:T(8,128)(2,1)S(1)}, bf16[880,128]{1,0:T(8,128)(2,1)S(1)}, u32[]{:S(2)}, u32[]{:S(2)}) collective-permute-start(bf16[880,128]{1,0:T(8,128)(2,1)S(1)} %collective-permute-done.5.refs_9_.refs_6_), channel_id=1, source_target_pairs={{0,48},{16,0},{32,16},{48,32},{1,49},{17,1},{33,17},{49,33},{2,50}... | collective-permute-start | bytes 675848 | tf_op jit(solution)/shard_map/ppermute | solution.py:191
  19.7 6.9 %collective-permute-start.8 = (bf16[880,128]{1,0:T(8,128)(2,1)S(1)}, bf16[880,128]{1,0:T(8,128)(2,1)S(1)}, u32[]{:S(2)}, u32[]{:S(2)}) collective-permute-start(bf16[880,128]{1,0:T(8,128)(2,1)S(1)} %collective-permute-done.2.refs_4_.refs_1_), channel_id=1, source_target_pairs={{0,64},{64,0},{1,65},{65,1},{2,66},{66,2},{3,67},{67,3},{4,68},{68... | collective-permute-start | bytes 675848 | tf_op jit(solution)/shard_map/ppermute | solution.py:144
  21.8 4.7 %collective-permute-start.13 = (bf16[880,128]{1,0:T(8,128)(2,1)S(1)}, bf16[880,128]{1,0:T(8,128)(2,1)S(1)}, u32[]{:S(2)}, u32[]{:S(2)}) collective-permute-start(bf16[880,128]{1,0:T(8,128)(2,1)S(1)} %collective-permute-done.5.refs_9_.refs_6_), channel_id=1, source_target_pairs={{0,64},{64,0},{1,65},{65,1},{2,66},{66,2},{3,67},{67,3},{4,68},{68... | collective-permute-start | bytes 675848 | tf_op jit(solution)/shard_map/ppermute | solution.py:144
  21.8 4.7 %collective-permute-start.9 = (bf16[880,128]{1,0:T(8,128)(2,1)S(1)}, bf16[880,128]{1,0:T(8,128)(2,1)S(1)}, u32[]{:S(2)}, u32[]{:S(2)}) collective-permute-start(bf16[880,128]{1,0:T(8,128)(2,1)S(1)} %collective-permute-done.3.refs_5_.refs_2_), channel_id=1, source_target_pairs={{0,64},{64,0},{1,65},{65,1},{2,66},{66,2},{3,67},{67,3},{4,68},{68... | collective-permute-start | bytes 675848 | tf_op jit(solution)/shard_map/ppermute | solution.py:144
  24.8 2.4 %collective-permute-start.10 = (bf16[880,128]{1,0:T(8,128)(2,1)S(1)}, bf16[880,128]{1,0:T(8,128)(2,1)S(1)}, u32[]{:S(2)}, u32[]{:S(2)}) collective-permute-start(bf16[880,128]{1,0:T(8,128)(2,1)S(1)} %collective-permute-done.4.refs_6_.refs_3_), channel_id=1, source_target_pairs={{0,64},{64,0},{1,65},{65,1},{2,66},{66,2},{3,67},{67,3},{4,68},{68... | collective-permute-start | bytes 675848 | tf_op jit(solution)/shard_map/ppermute | solution.py:144
  26.2 1.5 %collective-permute-start.11 = (bf16[880,128]{1,0:T(8,128)(2,1)S(1)}, bf16[880,128]{1,0:T(8,128)(2,1)S(1)}, u32[]{:S(2)}, u32[]{:S(2)}) collective-permute-start(bf16[880,128]{1,0:T(8,128)(2,1)S(1)} %collective-permute-done.6.refs_7_.refs_4_), channel_id=1, source_target_pairs={{0,64},{64,0},{1,65},{65,1},{2,66},{66,2},{3,67},{67,3},{4,68},{68... | collective-permute-start | bytes 675848 | tf_op jit(solution)/shard_map/ppermute | solution.py:144
  34.8 9.5 %copy-start.1 = (bf16[1,2,32,32,128]{4,3,2,1,0:T(8,128)(2,1)S(1)}, bf16[1,2,32,32,128]{4,3,2,1,0:T(8,128)(2,1)}, u32[]{:S(2)}) copy-start(bf16[1,2,32,32,128]{4,3,2,1,0:T(8,128)(2,1)} %param.7) | copy-start | bytes 1572868
  34.9 9.5 %collective-permute-start.15 = (bf16[2,20,32,128]{3,2,1,0:T(8,128)(2,1)S(1)}, bf16[2,20,32,128]{3,2,1,0:T(8,128)(2,1)S(1)}, u32[]{:S(2)}, u32[]{:S(2)}) collective-permute-start(bf16[2,20,32,128]{3,2,1,0:T(8,128)(2,1)S(1)} %get-tuple-element.62.refs_0_), channel_id=1, source_target_pairs={{0,1},{2,3},{4,5},{6,7},{8,9},{10,11},{12,13},{14,15},{1,0},{3,2},... | collective-permute-start | bytes 983048 | tf_op jit(solution)/shard_map/ppermute | solution.py:140
  36.7 7.7 %collective-permute-start.14 = (bf16[2,20,32,128]{3,2,1,0:T(8,128)(2,1)S(1)}, bf16[2,20,32,128]{3,2,1,0:T(8,128)(2,1)S(1)}, u32[]{:S(2)}, u32[]{:S(2)}) collective-permute-start(bf16[2,20,32,128]{3,2,1,0:T(8,128)(2,1)S(1)} %get-tuple-element.62.refs_0_), channel_id=1, source_target_pairs={{1,2},{3,4},{5,6},{7,8},{9,10},{11,12},{13,14},{2,1},{4,3},{6,5},{... | collective-permute-start | bytes 983048 | tf_op jit(solution)/shard_map/ppermute | solution.py:140
  50.6 9.7 %collective-permute-start.20 = (bf16[2,16,32,128]{3,2,1,0:T(8,128)(2,1)S(1)}, bf16[2,16,32,128]{3,2,1,0:T(8,128)(2,1)S(1)}, u32[]{:S(2)}, u32[]{:S(2)}) collective-permute-start(bf16[2,16,32,128]{3,2,1,0:T(8,128)(2,1)S(1)} %get-tuple-element.76.refs_0_.refs_7_), channel_id=1, source_target_pairs={{0,1},{2,3},{4,5},{6,7},{8,9},{10,11},{12,13},{14,15},{1,0},{3,2},... | collective-permute-start | bytes 786440 | tf_op jit(solution)/shard_map/ppermute | solution.py:140
  54.8 5.5 %collective-permute-start.19 = (bf16[2,16,32,128]{3,2,1,0:T(8,128)(2,1)S(1)}, bf16[2,16,32,128]{3,2,1,0:T(8,128)(2,1)S(1)}, u32[]{:S(2)}, u32[]{:S(2)}) collective-permute-start(bf16[2,16,32,128]{3,2,1,0:T(8,128)(2,1)S(1)} %get-tuple-element.76.refs_0_.refs_7_), channel_id=1, source_target_pairs={{1,2},{3,4},{5,6},{7,8},{9,10},{11,12},{13,14},{2,1},{4,3},{6,5},{... | collective-permute-start | bytes 786440 | tf_op jit(solution)/shard_map/ppermute | solution.py:140
  55.7 25.5 %collective-permute-start.16 = (bf16[6,8,32,128]{3,2,1,0:T(8,128)(2,1)S(1)}, bf16[6,8,32,128]{3,2,1,0:T(8,128)(2,1)S(1)}, u32[]{:S(2)}, u32[]{:S(2)}) collective-permute-start(bf16[6,8,32,128]{3,2,1,0:T(8,128)(2,1)S(1)} %get-tuple-element.73), channel_id=1, source_target_pairs={{0,16},{16,0},{32,48},{48,32},{1,17},{17,1},{33,49},{49,33},{2,18}... | collective-permute-start | bytes 1179656 | tf_op jit(solution)/shard_map/ppermute | solution.py:128
  56.0 25.2 %collective-permute-start.17 = (bf16[6,8,32,128]{3,2,1,0:T(8,128)(2,1)S(1)}, bf16[6,8,32,128]{3,2,1,0:T(8,128)(2,1)S(1)}, u32[]{:S(2)}, u32[]{:S(2)}) collective-permute-start(bf16[6,8,32,128]{3,2,1,0:T(8,128)(2,1)S(1)} %get-tuple-element.74), channel_id=1, source_target_pairs={{0,32},{16,48},{32,0},{48,16},{1,33},{17,49},{33,1},{49,17},{2,34}... | collective-permute-start | bytes 1179656 | tf_op jit(solution)/shard_map/ppermute | solution.py:128
  60.2 21.1 %collective-permute-start.18 = (bf16[6,8,32,128]{3,2,1,0:T(8,128)(2,1)S(1)}, bf16[6,8,32,128]{3,2,1,0:T(8,128)(2,1)S(1)}, u32[]{:S(2)}, u32[]{:S(2)}) collective-permute-start(bf16[6,8,32,128]{3,2,1,0:T(8,128)(2,1)S(1)} %get-tuple-element.75), channel_id=1, source_target_pairs={{0,48},{16,32},{32,16},{48,0},{1,49},{17,33},{33,17},{49,1},{2,50}... | collective-permute-start | bytes 1179656 | tf_op jit(solution)/shard_map/ppermute | solution.py:128
  65.2 8.8 %collective-permute-start.22 = (bf16[2,12,32,128]{3,2,1,0:T(8,128)(2,1)S(1)}, bf16[2,12,32,128]{3,2,1,0:T(8,128)(2,1)S(1)}, u32[]{:S(2)}, u32[]{:S(2)}) collective-permute-start(bf16[2,12,32,128]{3,2,1,0:T(8,128)(2,1)S(1)} %get-tuple-element.81.refs_0_.refs_5_), channel_id=1, source_target_pairs={{0,1},{2,3},{4,5},{6,7},{8,9},{10,11},{12,13},{14,15},{1,0},{3,2},... | collective-permute-start | bytes 589832 | tf_op jit(solution)/shard_map/ppermute | solution.py:140
  70.6 3.4 %collective-permute-start.21 = (bf16[2,12,32,128]{3,2,1,0:T(8,128)(2,1)S(1)}, bf16[2,12,32,128]{3,2,1,0:T(8,128)(2,1)S(1)}, u32[]{:S(2)}, u32[]{:S(2)}) collective-permute-start(bf16[2,12,32,128]{3,2,1,0:T(8,128)(2,1)S(1)} %get-tuple-element.81.refs_0_.refs_5_), channel_id=1, source_target_pairs={{1,2},{3,4},{5,6},{7,8},{9,10},{11,12},{13,14},{2,1},{4,3},{6,5},{... | collective-permute-start | bytes 589832 | tf_op jit(solution)/shard_map/ppermute | solution.py:140
  76.7 4.6 %collective-permute-start.26 = (bf16[2,8,32,128]{3,2,1,0:T(8,128)(2,1)S(1)}, bf16[2,8,32,128]{3,2,1,0:T(8,128)(2,1)S(1)}, u32[]{:S(2)}, u32[]{:S(2)}) collective-permute-start(bf16[2,8,32,128]{3,2,1,0:T(8,128)(2,1)S(1)} %get-tuple-element.95), channel_id=1, source_target_pairs={{0,16},{16,0},{32,48},{48,32},{1,17},{17,1},{33,49},{49,33},{2,18}... | collective-permute-start | bytes 393224 | tf_op jit(solution)/shard_map/ppermute | solution.py:128
  77.0 7.9 %collective-permute-start.27 = (bf16[2,8,32,128]{3,2,1,0:T(8,128)(2,1)S(1)}, bf16[2,8,32,128]{3,2,1,0:T(8,128)(2,1)S(1)}, u32[]{:S(2)}, u32[]{:S(2)}) collective-permute-start(bf16[2,8,32,128]{3,2,1,0:T(8,128)(2,1)S(1)} %get-tuple-element.96), channel_id=1, source_target_pairs={{0,32},{16,48},{32,0},{48,16},{1,33},{17,49},{33,1},{49,17},{2,34}... | collective-permute-start | bytes 393224 | tf_op jit(solution)/shard_map/ppermute | solution.py:128
  81.2 5.2 %collective-permute-start.28 = (bf16[2,8,32,128]{3,2,1,0:T(8,128)(2,1)S(1)}, bf16[2,8,32,128]{3,2,1,0:T(8,128)(2,1)S(1)}, u32[]{:S(2)}, u32[]{:S(2)}) collective-permute-start(bf16[2,8,32,128]{3,2,1,0:T(8,128)(2,1)S(1)} %get-tuple-element.97), channel_id=1, source_target_pairs={{0,48},{16,32},{32,16},{48,0},{1,49},{17,33},{33,17},{49,1},{2,50}... | collective-permute-start | bytes 393224 | tf_op jit(solution)/shard_map/ppermute | solution.py:128
  89.9 5.7 %collective-permute-start.29 = (bf16[1792,128]{1,0:T(8,128)(2,1)S(1)}, bf16[1792,128]{1,0:T(8,128)(2,1)S(1)}, u32[]{:S(2)}, u32[]{:S(2)}) collective-permute-start(bf16[1792,128]{1,0:T(8,128)(2,1)S(1)} %get-tuple-element.99), channel_id=1, source_target_pairs={{0,64},{64,0},{1,65},{65,1},{2,66},{66,2},{3,67},{67,3},{4,68},{68... | collective-permute-start | bytes 1376264 | tf_op jit(solution)/shard_map/ppermute | solution.py:144
  95.8 9.7 %collective-permute-start.30 = (bf16[448,128]{1,0:T(8,128)(2,1)S(1)}, bf16[448,128]{1,0:T(8,128)(2,1)S(1)}, u32[]{:S(2)}, u32[]{:S(2)}) collective-permute-start(bf16[448,128]{1,0:T(8,128)(2,1)S(1)} %get-tuple-element.101), channel_id=1, source_target_pairs={{0,1},{1,0},{2,3},{3,2},{4,5},{5,4},{6,7},{7,6},{8,9},{9,8},{10,11... | collective-permute-start | bytes 344072 | tf_op jit(solution)/shard_map/ppermute | solution.py:147
  101.6 9.2 %collective-permute-start.31 = (bf16[448,128]{1,0:T(8,128)(2,1)S(1)}, bf16[448,128]{1,0:T(8,128)(2,1)S(1)}, u32[]{:S(2)}, u32[]{:S(2)}) collective-permute-start(bf16[448,128]{1,0:T(8,128)(2,1)S(1)} %get-tuple-element.102), channel_id=1, source_target_pairs={{0,2},{1,3},{2,0},{3,1},{4,6},{5,7},{6,4},{7,5},{8,10},{9,11},{10,... | collective-permute-start | bytes 344072 | tf_op jit(solution)/shard_map/ppermute | solution.py:147
  105.5 7.9 %collective-permute-start.32 = (bf16[448,128]{1,0:T(8,128)(2,1)S(1)}, bf16[448,128]{1,0:T(8,128)(2,1)S(1)}, u32[]{:S(2)}, u32[]{:S(2)}) collective-permute-start(bf16[448,128]{1,0:T(8,128)(2,1)S(1)} %get-tuple-element.103), channel_id=1, source_target_pairs={{0,3},{1,2},{2,1},{3,0},{4,7},{5,6},{6,5},{7,4},{8,11},{9,10},{10,... | collective-permute-start | bytes 344072 | tf_op jit(solution)/shard_map/ppermute | solution.py:147
  113.5 8.1 %collective-permute-start.35 = (bf16[448,128]{1,0:T(8,128)(2,1)S(1)}, bf16[448,128]{1,0:T(8,128)(2,1)S(1)}, u32[]{:S(2)}, u32[]{:S(2)}) collective-permute-start(bf16[448,128]{1,0:T(8,128)(2,1)S(1)} %shard_map.87.refs_0_), channel_id=1, source_target_pairs={{0,12},{1,13},{2,14},{3,15},{4,8},{5,9},{6,10},{7,11},{8,4},{9,5},... | collective-permute-start | bytes 344072 | tf_op jit(solution)/shard_map/ppermute | solution.py:150
  114.0 7.5 %collective-permute-start.34 = (bf16[448,128]{1,0:T(8,128)(2,1)S(1)}, bf16[448,128]{1,0:T(8,128)(2,1)S(1)}, u32[]{:S(2)}, u32[]{:S(2)}) collective-permute-start(bf16[448,128]{1,0:T(8,128)(2,1)S(1)} %shard_map.87.refs_0_), channel_id=1, source_target_pairs={{0,8},{1,9},{2,10},{3,11},{4,12},{5,13},{6,14},{7,15},{8,0},{9,1},... | collective-permute-start | bytes 344072 | tf_op jit(solution)/shard_map/ppermute | solution.py:150
  116.6 4.9 %collective-permute-start.33 = (bf16[448,128]{1,0:T(8,128)(2,1)S(1)}, bf16[448,128]{1,0:T(8,128)(2,1)S(1)}, u32[]{:S(2)}, u32[]{:S(2)}) collective-permute-start(bf16[448,128]{1,0:T(8,128)(2,1)S(1)} %shard_map.87.refs_0_), channel_id=1, source_target_pairs={{0,4},{1,5},{2,6},{3,7},{4,0},{5,1},{6,2},{7,3},{8,12},{9,13},{10,... | collective-permute-start | bytes 344072 | tf_op jit(solution)/shard_map/ppermute | solution.py:150
  117.9 7.1 %collective-permute-start.23 = (bf16[2,8,32,128]{3,2,1,0:T(8,128)(2,1)S(1)}, bf16[2,8,32,128]{3,2,1,0:T(8,128)(2,1)S(1)}, u32[]{:S(2)}, u32[]{:S(2)}) collective-permute-start(bf16[2,8,32,128]{3,2,1,0:T(8,128)(2,1)S(1)} %get-tuple-element.91), channel_id=1, source_target_pairs={{0,16},{16,0},{32,48},{48,32},{1,17},{17,1},{33,49},{49,33},{2,18}... | collective-permute-start | bytes 393224 | tf_op jit(solution)/shard_map/ppermute | solution.py:128
  118.0 7.3 %collective-permute-start.24 = (bf16[2,8,32,128]{3,2,1,0:T(8,128)(2,1)S(1)}, bf16[2,8,32,128]{3,2,1,0:T(8,128)(2,1)S(1)}, u32[]{:S(2)}, u32[]{:S(2)}) collective-permute-start(bf16[2,8,32,128]{3,2,1,0:T(8,128)(2,1)S(1)} %get-tuple-element.92), channel_id=1, source_target_pairs={{0,32},{16,48},{32,0},{48,16},{1,33},{17,49},{33,1},{49,17},{2,34}... | collective-permute-start | bytes 393224 | tf_op jit(solution)/shard_map/ppermute | solution.py:128
  121.7 7.0 %collective-permute-start.38 = (bf16[448,128]{1,0:T(8,128)(2,1)S(1)}, bf16[448,128]{1,0:T(8,128)(2,1)S(1)}, u32[]{:S(2)}, u32[]{:S(2)}) collective-permute-start(bf16[448,128]{1,0:T(8,128)(2,1)S(1)} %shard_map.88.refs_8_), channel_id=1, source_target_pairs={{0,3},{1,2},{2,1},{3,0},{4,7},{5,6},{6,5},{7,4},{8,11},{9,10},{10,... | collective-permute-start | bytes 344072 | tf_op jit(solution)/shard_map/ppermute | solution.py:147
  122.5 7.2 %collective-permute-start.37 = (bf16[448,128]{1,0:T(8,128)(2,1)S(1)}, bf16[448,128]{1,0:T(8,128)(2,1)S(1)}, u32[]{:S(2)}, u32[]{:S(2)}) collective-permute-start(bf16[448,128]{1,0:T(8,128)(2,1)S(1)} %shard_map.88.refs_8_), channel_id=1, source_target_pairs={{0,2},{1,3},{2,0},{3,1},{4,6},{5,7},{6,4},{7,5},{8,10},{9,11},{10,... | collective-permute-start | bytes 344072 | tf_op jit(solution)/shard_map/ppermute | solution.py:147
  122.5 9.2 %collective-permute-start.36 = (bf16[448,128]{1,0:T(8,128)(2,1)S(1)}, bf16[448,128]{1,0:T(8,128)(2,1)S(1)}, u32[]{:S(2)}, u32[]{:S(2)}) collective-permute-start(bf16[448,128]{1,0:T(8,128)(2,1)S(1)} %shard_map.88.refs_8_), channel_id=1, source_target_pairs={{0,1},{1,0},{2,3},{3,2},{4,5},{5,4},{6,7},{7,6},{8,9},{9,8},{10,11... | collective-permute-start | bytes 344072 | tf_op jit(solution)/shard_map/ppermute | solution.py:147
  125.0 6.7 %collective-permute-start.25 = (bf16[2,8,32,128]{3,2,1,0:T(8,128)(2,1)S(1)}, bf16[2,8,32,128]{3,2,1,0:T(8,128)(2,1)S(1)}, u32[]{:S(2)}, u32[]{:S(2)}) collective-permute-start(bf16[2,8,32,128]{3,2,1,0:T(8,128)(2,1)S(1)} %get-tuple-element.93), channel_id=1, source_target_pairs={{0,48},{16,32},{32,16},{48,0},{1,49},{17,33},{33,17},{49,1},{2,50}... | collective-permute-start | bytes 393224 | tf_op jit(solution)/shard_map/ppermute | solution.py:128
  125.3 7.8 %collective-permute-start.39 = (bf16[448,128]{1,0:T(8,128)(2,1)S(1)}, bf16[448,128]{1,0:T(8,128)(2,1)S(1)}, u32[]{:S(2)}, u32[]{:S(2)}) collective-permute-start(bf16[448,128]{1,0:T(8,128)(2,1)S(1)} %shard_map.88.refs_8_), channel_id=1, source_target_pairs={{0,64},{64,0},{1,65},{65,1},{2,66},{66,2},{3,67},{67,3},{4,68},{68... | collective-permute-start | bytes 344072 | tf_op jit(solution)/shard_map/ppermute | solution.py:144
  128.6 4.5 %collective-permute-start.42 = (bf16[448,128]{1,0:T(8,128)(2,1)S(1)}, bf16[448,128]{1,0:T(8,128)(2,1)S(1)}, u32[]{:S(2)}, u32[]{:S(2)}) collective-permute-start(bf16[448,128]{1,0:T(8,128)(2,1)S(1)} %collective-permute-done.38.refs_11_), channel_id=1, source_target_pairs={{0,64},{64,0},{1,65},{65,1},{2,66},{66,2},{3,67},{67,3},{4,68},{68... | collective-permute-start | bytes 344072 | tf_op jit(solution)/shard_map/ppermute | solution.py:144
  129.8 3.4 %collective-permute-start.41 = (bf16[448,128]{1,0:T(8,128)(2,1)S(1)}, bf16[448,128]{1,0:T(8,128)(2,1)S(1)}, u32[]{:S(2)}, u32[]{:S(2)}) collective-permute-start(bf16[448,128]{1,0:T(8,128)(2,1)S(1)} %collective-permute-done.37.refs_10_), channel_id=1, source_target_pairs={{0,64},{64,0},{1,65},{65,1},{2,66},{66,2},{3,67},{67,3},{4,68},{68... | collective-permute-start | bytes 344072 | tf_op jit(solution)/shard_map/ppermute | solution.py:144
  131.8 1.4 %collective-permute-start.40 = (bf16[448,128]{1,0:T(8,128)(2,1)S(1)}, bf16[448,128]{1,0:T(8,128)(2,1)S(1)}, u32[]{:S(2)}, u32[]{:S(2)}) collective-permute-start(bf16[448,128]{1,0:T(8,128)(2,1)S(1)} %collective-permute-done.36.refs_9_), channel_id=1, source_target_pairs={{0,64},{64,0},{1,65},{65,1},{2,66},{66,2},{3,67},{67,3},{4,68},{68... | collective-permute-start | bytes 344072 | tf_op jit(solution)/shard_map/ppermute | solution.py:144
